TPU v7x, 32 devices: a whole 2x2x4 slice. The times are simulated.
32 devices in a mesh: pipe: 4 (over y, core), section: 4 (over z), tensor: 2 (over x).
Axes of the slice: x: 2, y: 2, z: 4, core: 2. Of those that a mesh axis runs over, the one named last changes fastest.
Arguments:
- bounds: int32 [2, 3], replicated, may hold values from 0 to 2, as said below
- saved_inputs: bfloat16 [4, 4, 2, 256, 1024], P('pipe', 'section', None, 'tensor')
- w_in: bfloat16 [4, 4, 2, 1024, 1024], P('pipe', 'section'), as said below
- w_out: bfloat16 [4, 4, 2, 1024, 1024], P('pipe', 'section')
- top_grad: bfloat16 [4, 2, 256, 1024], P('pipe', None, 'tensor'), may hold values from -0.125 to 0.125
Outputs:
- grad_in: float32 [4, 512, 1024], P('section', 'pipe', 'tensor')
- grad_out: float32 [4, 512, 1024], P('section', 'pipe', 'tensor')
Inputs may be any that keep to these rules, and one draw needn't show every extreme that they name: Row p of bounds starts at 0 and never falls; each relay either uses all 2 sections with one layer each, or gives one or two layers to each of its first 1 section with its later entries equal to 2; at least one relay is of each kind. `w_in`: for k < bounds[p, s+1] - bounds[p, s], slot k of entries [2p + a, 2s + b] holds layer bounds[p, s] + k, the same for every a and b; a layer's weights are the same in every relay.
All inputs are finite; a program needn't handle non-finite values.
Results may differ from a plain program's by a relative error of at most 0.014.
Values may be sent and summed in bfloat16 or wider, within the bound.
No kernel may reach another device: no remote copies, remote signals or barrier semaphores. Data moves between devices by JAX's collectives and lax.ppermute only.
A program may use at most 64 MiB of HBM per device.

v0:
```python
import jax
import jax.numpy as jnp
from jax import lax
from jax.sharding import PartitionSpec as P

EPS = 1e-05


def shifted(value, axis, steps):
    count = lax.axis_size(axis)
    pairs = [(source, (source + steps) % count) for source in range(count)]
    return lax.ppermute(value, axis, pairs)


def for_sending(shard):

    def short(part):
        return part.astype(jnp.bfloat16) if part.dtype == jnp.float32 else part

    return jax.tree.map(short, shard)


def partner(block, axis, bit):
    count = lax.axis_size(axis)
    route = []
    for low in range(count):
        high = low | 1 << bit
        if high != low and high < count:
            route += [(low, high), (high, low)]
    return lax.ppermute(block, axis, route)


def normalize(saved_rows):
    floats = saved_rows.astype(jnp.float32)
    row_scale = jnp.sqrt(jnp.mean(floats * floats, axis=-1, keepdims=True) + EPS)
    return (floats / row_scale, row_scale)


def layer_back(grad_next, unit_rows, row_scale, proj_in, proj_out):
    err_low = jnp.dot(grad_next, proj_out.T, preferred_element_type=jnp.float32).astype(
        jnp.bfloat16
    )
    pulled = jnp.dot(err_low, proj_in.T, preferred_element_type=jnp.float32)
    inner_mean = jnp.mean(pulled * unit_rows, axis=-1, keepdims=True)
    grad_here = (
        grad_next.astype(jnp.float32) + (pulled - unit_rows * inner_mean) / row_scale
    ).astype(jnp.bfloat16)
    return (grad_here, err_low)


def route_items(members, shifter, offset, occupied, positions, here_section, levels, sections):
    for bit_level in reversed(range(levels)):
        stride = 2**bit_level
        passed = offset // (2 * stride) * (2 * stride)
        present = occupied & ((positions[:, None] + passed) % sections == here_section)
        rising = offset // stride % 2 == 1
        send_mask = jnp.any(present & rising, axis=0)
        keep_mask = jnp.any(present & jnp.logical_not(rising), axis=0)
        outgoing = tuple(
            (
                jnp.where(send_mask[:, None, None], member, jnp.zeros_like(member))
                for member in members
            )
        )
        arrived = shifter(outgoing, stride)
        members = tuple(
            (
                jnp.where(keep_mask[:, None, None], member, jnp.zeros_like(member)) + landed
                for member, landed in zip(members, arrived)
            )
        )
    return members


def body(bounds, saved_inputs, w_in, w_out, top_grad):
    sections = lax.axis_size("section") // 2
    tensors = lax.axis_size("tensor")
    pipe_index = lax.axis_index("pipe")
    section_index = lax.axis_index("section")
    tensor_index = lax.axis_index("tensor")
    position = section_index // 2
    token_half = section_index % 2
    boundary = lax.dynamic_index_in_dim(bounds, pipe_index // 2, 0, keepdims=False)
    counts = boundary[1:] - boundary[:-1]
    layers_here = lax.dynamic_index_in_dim(counts, position, 0, keepdims=False)
    saved_rows = saved_inputs[0, 0]
    proj_in = w_in[0, 0]
    proj_out = w_out[0, 0]
    slot_count = saved_rows.shape[0]
    row_count = saved_rows.shape[1]
    model_width = saved_rows.shape[2]
    inner_width = proj_in.shape[2]
    unit_rows, scales = normalize(saved_rows)
    unit_low = unit_rows.astype(jnp.bfloat16)
    value_low = jnp.einsum(
        "kre,kea->kra", unit_low, proj_in, preferred_element_type=jnp.float32
    ).astype(jnp.bfloat16)
    positions = jnp.arange(sections, dtype=jnp.int32)
    slot_ids = jnp.arange(slot_count, dtype=jnp.int32)
    occupied = slot_ids[None, :] < counts[:, None]
    layer_of = boundary[:-1, None] + slot_ids[None, :]
    offset = (layer_of + 1 - positions[:, None]) % sections
    levels = min((sections - 3 * sections // 4 + 1).bit_length(), (sections - 1).bit_length())
    top_rows = lax.dynamic_index_in_dim(top_grad[0], token_half, 0, keepdims=False)

    def run_section(incoming):

        def upper_layer(grad_top):
            return layer_back(grad_top, unit_rows[1], scales[1], proj_in[1], proj_out[1])

        def lower_layer(grad_top):
            return layer_back(grad_top, unit_rows[0], scales[0], proj_in[0], proj_out[0])

        def no_layer(grad_top):
            return (grad_top, jnp.zeros((row_count, inner_width), jnp.bfloat16))

        lower_start, upper_err = lax.cond(layers_here == 2, upper_layer, no_layer, incoming)
        result, lower_err = lax.cond(layers_here >= 1, lower_layer, no_layer, lower_start)
        return (result, jnp.stack([lower_start, incoming]), jnp.stack([lower_err, upper_err]))

    def loop_turn(turn_index, carried):
        incoming = shifted(carried[0], "section", -2)
        return lax.cond(
            position == sections - 1 - turn_index,
            lambda arriving, kept: run_section(arriving),
            lambda arriving, kept: kept,
            incoming,
            carried,
        )

    start_rows = jnp.where(position == 0, top_rows, jnp.zeros_like(top_rows))
    carried = (
        start_rows,
        jnp.zeros((slot_count, row_count, model_width), jnp.bfloat16),
        jnp.zeros((slot_count, row_count, inner_width), jnp.bfloat16),
    )
    carried = lax.fori_loop(0, sections, loop_turn, carried)
    grads_slots = carried[1]
    errors = carried[2]
    unit_got, value_got, err_got, grad_got = route_items(
        (unit_low, value_low, errors, grads_slots),
        lambda members, stride: jax.tree.map(
            lambda part, own: part.astype(own.dtype),
            shifted(for_sending(members), "section", 2 * stride),
            members,
        ),
        offset,
        occupied,
        positions,
        position,
        levels,
        sections,
    )
    owner_slot = jnp.sum(
        jnp.where(occupied & ((layer_of + 1) % sections == position), slot_ids[None, :], 0)
    )
    unit_own = lax.dynamic_index_in_dim(unit_got, owner_slot, 0, keepdims=False)
    value_own = lax.dynamic_index_in_dim(value_got, owner_slot, 0, keepdims=False)
    err_own = lax.dynamic_index_in_dim(err_got, owner_slot, 0, keepdims=False)
    grad_own = lax.dynamic_index_in_dim(grad_got, owner_slot, 0, keepdims=False)
    in_cols = inner_width // tensors
    out_cols = model_width // tensors
    unit_piece = lax.all_gather(unit_own, "tensor", axis=0, tiled=True)
    value_piece = lax.all_gather(value_own, "tensor", axis=0, tiled=True)
    err_piece = lax.all_gather(err_own, "tensor", axis=0, tiled=True)
    grad_piece = lax.all_gather(grad_own, "tensor", axis=0, tiled=True)
    err_cols = lax.dynamic_slice_in_dim(err_piece, tensor_index * in_cols, in_cols, 1)
    grad_cols = lax.dynamic_slice_in_dim(grad_piece, tensor_index * out_cols, out_cols, 1)
    totals = (
        jnp.dot(unit_piece.T, err_cols, preferred_element_type=jnp.float32),
        jnp.dot(value_piece.T, grad_cols, preferred_element_type=jnp.float32),
    )
    half_model = model_width // 2
    half_inner = inner_width // 2
    mine_in = lax.dynamic_slice_in_dim(totals[0], token_half * half_model, half_model, 0)
    other_in = lax.dynamic_slice_in_dim(totals[0], (1 - token_half) * half_model, half_model, 0)
    mine_out = lax.dynamic_slice_in_dim(totals[1], token_half * half_inner, half_inner, 0)
    other_out = lax.dynamic_slice_in_dim(totals[1], (1 - token_half) * half_inner, half_inner, 0)
    landed_in, landed_out = partner((other_in, other_out), "section", 0)
    grad_in_part, grad_out_part = (
        lax.psum_scatter(mine_in + landed_in, "pipe", scatter_dimension=0, tiled=True),
        lax.psum_scatter(mine_out + landed_out, "pipe", scatter_dimension=0, tiled=True),
    )
    return (grad_in_part[None], grad_out_part[None])


def solution(mesh):
    placed = (
        P(),
        P("pipe", "section", None, "tensor", None),
        P("pipe", "section", None, None, None),
        P("pipe", "section", None, None, None),
        P("pipe", None, "tensor", None),
    )
    return jax.shard_map(
        body,
        mesh=mesh,
        in_specs=placed,
        out_specs=(P("section", "pipe", "tensor"), P("section", "pipe", "tensor")),
        check_vma=False,
    )
```

profile of v0, /device:TPU:24, one launch (start us, length us, event | category | flops | bytes accessed | tf_op | source)
XLA Modules:
  0.0 231.4 jit_solution(8870678346075298713)
XLA Ops:
  7.3 0.6 copy-done
  7.9 0.1 bitcast_subtract_fusion
  7.9 1.2 fusion.28
  9.2 0.1 and_reduce_fusion.1
  9.3 2.1 broadcast_select_fusion.3
  11.4 0.3 collective-permute-start.1
  11.8 0.1 convert_divide_fusion
  11.9 0.6 dynamic_slice.45
  12.5 0.7 select_bitcast_fusion
  13.4 51.1 %while.17 = (s32[]{:T(128)}, bf16[128,1024]{1,0:T(8,128)(2,1)}, bf16[2,128,1024]{2,1,0:T(8,128)(2,1)S(1)}, bf16[2,128,1024]{2,1,0:T(8,128)(2,1)S(1)}, s32[]{:T(1...) while((s32[]{:T(128)}, bf16[128,1024]{1,0:T(8,128)(2,1)}, ...), condition=%wide.region_13.14_spmd, body=%wide.region_4.13_spmd.sunk | while | flops 1076625408 | bytes 18357676 | solution.py:137
  13.4 2.7 %collective-permute-start = (bf16[128,1024]{1,0:T(8,128)(2,1)}, bf16[128,1024]{1,0:T(8,128)(2,1)S(1)}, u32[]{:S(2)}, u32[]{:S(2)}) collective-permute-start(bf16[128,1024]{1,0:T(8,128)(2,1)} %get-tuple-element.372), channel_id=1, source_target_pairs={{0,4},{2,6},{4,0},{6,2},{1,5},{3,7},{5,1},{7,3},{8,12},{10,14},{12... | collective-permute-start | bytes 786440 | tf_op jit(solution)/shard_map/while/body/eval_jaxpr/ppermute | solution.py:12
  16.0 32.5 %collective-permute-done = bf16[128,1024]{1,0:T(8,128)(2,1)S(1)} collective-permute-done((bf16[128,1024]{1,0:T(8,128)(2,1)}, bf16[128,1024]{1,0:T(8,128)(2,1)S(1)}, u32[]{:S(2)}, u32[]{:S(2)}) %collective-permute-start) | collective-permute-done | bytes 262176 | tf_op jit(solution)/shard_map/while/body/eval_jaxpr/ppermute | solution.py:12
  48.5 4.6 %conditional.4 = ((bf16[128,1024]{1,0:T(8,128)(2,1)}, bf16[2,128,1024]{2,1,0:T(8,128)(2,1)S(1)}, bf16[2,128,1024]{2,1,0:T(8,128)(2,1)S(1)})) conditional(s32[]{:T(128)} %convert_element_type.62, (bf16[128,1024]{1,0:T(8,128)(2,1)}, bf16[2,128,1024]{2,1,0:T(8,128)(2,1)S(1)}, bf16[2,128,1024]{2,1,0:T(8,128)(2,1)S(1)}) %tuple.69, (s32[]{:T(128)}, ...), branch_computations={%region_5.5_spmd, %region_6.0_spmd} | conditional | flops 1076625408 | bytes 17308844 | solution.py:123
  49.8 0.8 conditional
  49.8 0.7 stack.18
  50.6 1.4 conditional.1
  50.6 0.7 copy.11
  51.3 0.7 stack.20
  52.0 1.1 pad_maximum_fusion
  53.2 0.1 collective-permute-start
  53.3 11.2 %collective-permute-done = bf16[128,1024]{1,0:T(8,128)(2,1)S(1)} collective-permute-done((bf16[128,1024]{1,0:T(8,128)(2,1)}, bf16[128,1024]{1,0:T(8,128)(2,1)S(1)}, u32[]{:S(2)}, u32[]{:S(2)}) %collective-permute-start) | collective-permute-done | bytes 262176 | tf_op jit(solution)/shard_map/while/body/eval_jaxpr/ppermute | solution.py:12
  64.5 4.0 %broadcast_select_fusion = (bf16[2,128,1024]{2,1,0:T(8,128)(2,1)}, bf16[2,128,1024]{2,1,0:T(8,128)(2,1)S(1)}, bf16[2,128,1024]{2,1,0:T(8,128)(2,1)}, bf16[2,128,1024]{2,1,0:T(8,128)(2,1)}) fusion(bf16[2,128,1024]{2,1,0:T(8,128)(2,1)S(1)} %get-tuple-element.244, pred[2]{0:T(512)(128)(4,1)S(1)} %get-tuple-element.246, ...), kind=kOutput, calls=%fused_computation.44 | convolution fusion | flops 537919488 | bytes 7864322 | tf_op jit(solution)/shard_map/kre,kea->kra/dot_general | solution.py:95
  68.5 14.8 %collective-permute-start.2 = (bf16[2,128,1024]{2,1,0:T(8,128)(2,1)S(1)}, bf16[2,128,1024]{2,1,0:T(8,128)(2,1)S(1)}, u32[]{:S(2)}, u32[]{:S(2)}) collective-permute-start(bf16[2,128,1024]{2,1,0:T(8,128)(2,1)S(1)} %get-tuple-element.276), channel_id=1, source_target_pairs={{0,4},{2,6},{4,0},{6,2},{1,5},{3,7},{5,1},{7,3},{8,12},{10,14},{12... | collective-permute-start | bytes 1572872 | tf_op jit(solution)/shard_map/ppermute | solution.py:12
  83.2 0.7 fusion.42
  85.9 0.6 dynamic-slice.3
  86.5 1.6 dynamic-slice_add_fusion.5
  88.1 8.6 %all-gather = bf16[1,256,1024]{2,1,0:T(8,128)(2,1)S(1)} all-gather(bf16[1,128,1024]{2,1,0:T(8,128)(2,1)S(1)} %dynamic-slice_add_fusion.5), channel_id=2, replica_groups=mesh['pipe'=4,'section'=4,'tensor'=2] {'tensor'}, dimensions={1}, use_global_device_ids=true | all-gather | bytes 786432 | tf_op jit(solution)/shard_map/all_gather | solution.py:163
  96.7 4.2 %collective-permute-done.2 = bf16[2,128,1024]{2,1,0:T(8,128)(2,1)S(1)} collective-permute-done((bf16[2,128,1024]{2,1,0:T(8,128)(2,1)S(1)}, bf16[2,128,1024]{2,1,0:T(8,128)(2,1)S(1)}, u32[]{:S(2)}, u32[]{:S(2)}) %collective-permute-start.2) | collective-permute-done | bytes 524320 | tf_op jit(solution)/shard_map/ppermute | solution.py:12
  101.0 0.7 dynamic-slice_add_fusion.4
  101.6 8.3 %all-gather.1 = bf16[1,256,1024]{2,1,0:T(8,128)(2,1)S(1)} all-gather(bf16[1,128,1024]{2,1,0:T(8,128)(2,1)S(1)} %dynamic-slice_add_fusion.4), channel_id=3, replica_groups=mesh['pipe'=4,'section'=4,'tensor'=2] {'tensor'}, dimensions={1}, use_global_device_ids=true | all-gather | bytes 786432 | tf_op jit(solution)/shard_map/all_gather | solution.py:165
  110.0 0.5 fusion.31
  110.4 1.1 constant_dynamic-slice_fusion.1
  111.5 2.8 %collective-permute-start.5 = (bf16[2,128,1024]{2,1,0:T(8,128)(2,1)}, bf16[2,128,1024]{2,1,0:T(8,128)(2,1)}, u32[]{:S(2)}, u32[]{:S(2)}) collective-permute-start(bf16[2,128,1024]{2,1,0:T(8,128)(2,1)} %get-tuple-element.275), channel_id=1, source_target_pairs={{0,4},{2,6},{4,0},{6,2},{1,5},{3,7},{5,1},{7,3},{8,12},{10,14},{12... | collective-permute-start | bytes 1572872 | tf_op jit(solution)/shard_map/ppermute | solution.py:12
  114.4 0.1 collective-permute-start.4
  114.5 32.2 %collective-permute-done.5 = bf16[2,128,1024]{2,1,0:T(8,128)(2,1)} collective-permute-done((bf16[2,128,1024]{2,1,0:T(8,128)(2,1)}, bf16[2,128,1024]{2,1,0:T(8,128)(2,1)}, u32[]{:S(2)}, u32[]{:S(2)}) %collective-permute-start.5) | collective-permute-done | bytes 524320 | tf_op jit(solution)/shard_map/ppermute | solution.py:12
  146.7 1.6 dynamic-slice_add_fusion.2
  148.3 7.8 %collective-permute-done.3 = f32[512,512]{1,0:T(8,128)} collective-permute-done((f32[512,512]{1,0:T(8,128)}, f32[512,512]{1,0:T(8,128)}, u32[]{:S(2)}, u32[]{:S(2)}) %collective-permute-start.3) | collective-permute-done | bytes 1048608 | tf_op jit(solution)/shard_map/ppermute | solution.py:30
  156.1 2.4 %dynamic-slice_add_fusion.1 = f32[512,512]{1,0:T(8,128)} fusion(f32[512,512]{1,0:T(8,128)} %collective-permute-done.3, f32[1024,512]{1,0:T(8,128)S(1)} %fusion.31, s32[]{:T(128)S(6)} %select_n.129), kind=kLoop, calls=%fused_computation.39 | loop fusion | flops 262144 | bytes 3145732 | tf_op jit(solution)/shard_map/add | solution.py:181
  158.6 0.4 collective-permute-done.4
  158.9 1.6 dynamic-slice_add_fusion.3
  160.6 7.6 %all-gather.2 = bf16[1,256,1024]{2,1,0:T(8,128)(2,1)S(1)} all-gather(bf16[1,128,1024]{2,1,0:T(8,128)(2,1)S(1)} %dynamic-slice_add_fusion.3), channel_id=4, replica_groups=mesh['pipe'=4,'section'=4,'tensor'=2] {'tensor'}, dimensions={1}, use_global_device_ids=true | all-gather | bytes 786432 | tf_op jit(solution)/shard_map/all_gather | solution.py:164
  168.2 7.0 %all-gather.3 = bf16[1,256,1024]{2,1,0:T(8,128)(2,1)S(1)} all-gather(bf16[1,128,1024]{2,1,0:T(8,128)(2,1)S(1)} %dynamic-slice_add_fusion.2), channel_id=5, replica_groups=mesh['pipe'=4,'section'=4,'tensor'=2] {'tensor'}, dimensions={1}, use_global_device_ids=true | all-gather | bytes 786432 | tf_op jit(solution)/shard_map/all_gather | solution.py:166
  175.2 0.5 fusion.29
  175.7 0.1 constant_dynamic-slice_fusion
  175.8 0.1 collective-permute-start.6
  175.9 21.8 %collective-permute-done.6 = f32[512,512]{1,0:T(8,128)S(1)} collective-permute-done((f32[512,512]{1,0:T(8,128)S(1)}, f32[512,512]{1,0:T(8,128)S(1)}, u32[]{:S(2)}, u32[]{:S(2)}) %collective-permute-start.6) | collective-permute-done | bytes 1048608 | tf_op jit(solution)/shard_map/ppermute | solution.py:30
  197.7 1.2 dynamic-slice_add_fusion
  198.9 25.7 %reduce-scatter.5.cloned.1.call-done = f32[128,512]{1,0:T(8,128)} async-done(((f32[512,512]{1,0:T(8,128)}), f32[128,512]{1,0:T(8,128)}) %reduce-scatter.5.cloned.1.call-update) | async-done | bytes 262160 | tf_op jit(solution)/shard_map/reduce_scatter | solution.py:182
  (23 shorter events, 0.3 us)
Async XLA Ops:
  7.2 0.7 copy-start
  7.2 4.6 %copy-start.1 = (bf16[1,1,2,128,1024]{4,3,2,1,0:T(8,128)(2,1)S(1)}, bf16[1,1,2,128,1024]{4,3,2,1,0:T(8,128)(2,1)}, u32[]{:S(2)}) copy-start(bf16[1,1,2,128,1024]{4,3,2,1,0:T(8,128)(2,1)} %param.14) | copy-start | bytes 1572868
  7.2 5.3 %copy-start.4 = (bf16[1,2,128,1024]{3,2,1,0:T(8,128)(2,1)S(1)}, bf16[1,2,128,1024]{3,2,1,0:T(8,128)(2,1)}, u32[]{:S(2)}) copy-start(bf16[1,2,128,1024]{3,2,1,0:T(8,128)(2,1)} %param.17) | copy-start | bytes 1572868
  7.2 191.7 %reduce-scatter.3.cloned.1.call-start = ((), (), s32[]{:S(2)}) async-start(), calls=%async_computation.2 | async-start | bytes 1310720 | tf_op jit(solution)/shard_map/reduce_scatter | solution.py:181
  11.4 75.1 %collective-permute-start.1 = (bf16[2,128,1024]{2,1,0:T(8,128)(2,1)}, bf16[2,128,1024]{2,1,0:T(8,128)(2,1)}, u32[]{:S(2)}, u32[]{:S(2)}) collective-permute-start(bf16[2,128,1024]{2,1,0:T(8,128)(2,1)} %get-tuple-element.267), channel_id=1, source_target_pairs={{0,4},{2,6},{4,0},{6,2},{1,5},{3,7},{5,1},{7,3},{8,12},{10,14},{12... | collective-permute-start | bytes 1572872 | tf_op jit(solution)/shard_map/ppermute | solution.py:12
  13.4 35.2 %collective-permute-start = (bf16[128,1024]{1,0:T(8,128)(2,1)}, bf16[128,1024]{1,0:T(8,128)(2,1)S(1)}, u32[]{:S(2)}, u32[]{:S(2)}) collective-permute-start(bf16[128,1024]{1,0:T(8,128)(2,1)} %get-tuple-element.372), channel_id=1, source_target_pairs={{0,4},{2,6},{4,0},{6,2},{1,5},{3,7},{5,1},{7,3},{8,12},{10,14},{12... | collective-permute-start | bytes 786440 | tf_op jit(solution)/shard_map/while/body/eval_jaxpr/ppermute | solution.py:12
  53.2 11.3 %collective-permute-start = (bf16[128,1024]{1,0:T(8,128)(2,1)}, bf16[128,1024]{1,0:T(8,128)(2,1)S(1)}, u32[]{:S(2)}, u32[]{:S(2)}) collective-permute-start(bf16[128,1024]{1,0:T(8,128)(2,1)} %get-tuple-element.372), channel_id=1, source_target_pairs={{0,4},{2,6},{4,0},{6,2},{1,5},{3,7},{5,1},{7,3},{8,12},{10,14},{12... | collective-permute-start | bytes 786440 | tf_op jit(solution)/shard_map/while/body/eval_jaxpr/ppermute | solution.py:12
  68.5 32.5 %collective-permute-start.2 = (bf16[2,128,1024]{2,1,0:T(8,128)(2,1)S(1)}, bf16[2,128,1024]{2,1,0:T(8,128)(2,1)S(1)}, u32[]{:S(2)}, u32[]{:S(2)}) collective-permute-start(bf16[2,128,1024]{2,1,0:T(8,128)(2,1)S(1)} %get-tuple-element.276), channel_id=1, source_target_pairs={{0,4},{2,6},{4,0},{6,2},{1,5},{3,7},{5,1},{7,3},{8,12},{10,14},{12... | collective-permute-start | bytes 1572872 | tf_op jit(solution)/shard_map/ppermute | solution.py:12
  110.0 4.4 %copy-start.3 = (bf16[2,128,1024]{2,1,0:T(8,128)(2,1)S(1)}, bf16[2,128,1024]{2,1,0:T(8,128)(2,1)}, u32[]{:S(2)}) copy-start(bf16[2,128,1024]{2,1,0:T(8,128)(2,1)} %get-tuple-element.277) | copy-start | bytes 1572868
  111.5 44.6 %collective-permute-start.3 = (f32[512,512]{1,0:T(8,128)}, f32[512,512]{1,0:T(8,128)}, u32[]{:S(2)}, u32[]{:S(2)}) collective-permute-start(f32[512,512]{1,0:T(8,128)} %constant_dynamic-slice_fusion.1), channel_id=1, source_target_pairs={{0,2},{2,0},{4,6},{6,4},{1,3},{3,1},{5,7},{7,5},{8,10},{10,8},{12,... | collective-permute-start | bytes 3145736 | tf_op jit(solution)/shard_map/ppermute | solution.py:30
  111.5 35.1 %collective-permute-start.5 = (bf16[2,128,1024]{2,1,0:T(8,128)(2,1)}, bf16[2,128,1024]{2,1,0:T(8,128)(2,1)}, u32[]{:S(2)}, u32[]{:S(2)}) collective-permute-start(bf16[2,128,1024]{2,1,0:T(8,128)(2,1)} %get-tuple-element.275), channel_id=1, source_target_pairs={{0,4},{2,6},{4,0},{6,2},{1,5},{3,7},{5,1},{7,3},{8,12},{10,14},{12... | collective-permute-start | bytes 1572872 | tf_op jit(solution)/shard_map/ppermute | solution.py:12
  114.4 44.6 %collective-permute-start.4 = (bf16[2,128,1024]{2,1,0:T(8,128)(2,1)S(1)}, bf16[2,128,1024]{2,1,0:T(8,128)(2,1)}, u32[]{:S(2)}, u32[]{:S(2)}) collective-permute-start(bf16[2,128,1024]{2,1,0:T(8,128)(2,1)S(1)} %copy-done.3), channel_id=1, source_target_pairs={{0,4},{2,6},{4,0},{6,2},{1,5},{3,7},{5,1},{7,3},{8,12},{10,14},{12... | collective-permute-start | bytes 1572872 | tf_op jit(solution)/shard_map/ppermute | solution.py:12
  148.3 10.6 %copy-start.2 = (bf16[2,128,1024]{2,1,0:T(8,128)(2,1)S(1)}, bf16[2,128,1024]{2,1,0:T(8,128)(2,1)}, u32[]{:S(2)}) copy-start(bf16[2,128,1024]{2,1,0:T(8,128)(2,1)} %get-tuple-element.278) | copy-start | bytes 1572868
  158.5 66.1 %reduce-scatter.5.cloned.1.call-start = ((), (), s32[]{:S(2)}) async-start(), calls=%async_computation.3 | async-start | bytes 1310720 | tf_op jit(solution)/shard_map/reduce_scatter | solution.py:182
  175.8 21.9 %collective-permute-start.6 = (f32[512,512]{1,0:T(8,128)S(1)}, f32[512,512]{1,0:T(8,128)S(1)}, u32[]{:S(2)}, u32[]{:S(2)}) collective-permute-start(f32[512,512]{1,0:T(8,128)S(1)} %constant_dynamic-slice_fusion), channel_id=1, source_target_pairs={{0,2},{2,0},{4,6},{6,4},{1,3},{3,1},{5,7},{7,5},{8,10},{10,8},{12,... | collective-permute-start | bytes 3145736 | tf_op jit(solution)/shard_map/ppermute | solution.py:30
Sparse Core Ops, SparseCore 0:
  158.6 25.5 reduce-scatter.2
  199.0 25.5 reduce-scatter.4
where the time goes:
time: 234 us; the launch traced here: 231 us
  waiting for transfers between devices  136 us (58%)
  blocking collectives  31.6 us (14%)
  starting transfers between devices  20.9 us (9%)
  between operations  16.1 us (7%)
  other arithmetic  15.4 us (7%)
  local copies, waits for them, and re-layouts  5.29 us (2%)
  matrix products  4.95 us (2%)
    ppermute x6, waiting for transfers between devices, shifted(): return lax.ppermute(value, axis, pairs)  80.5 us
    ppermute x2, waiting for transfers between devices, partner(): return lax.ppermute(block, axis, route)  29.6 us
    reduce_scatter x1, waiting for transfers between devices, body(): lax.psum_scatter(mine_out + landed_out, 'pipe', scatter_dimension=0, tile...  25.7 us
    ppermute x6, starting transfers between devices, shifted(): return lax.ppermute(value, axis, pairs)  20.7 us
    all_gather x1, blocking collectives, body(): unit_piece = lax.all_gather(unit_own, 'tensor', axis=0, tiled=True)  8.62 us
    all_gather x1, blocking collectives, body(): err_piece = lax.all_gather(err_own, 'tensor', axis=0, tiled=True)  8.32 us
    all_gather x1, blocking collectives, body(): value_piece = lax.all_gather(value_own, 'tensor', axis=0, tiled=True)  7.65 us
    all_gather x1, blocking collectives, body(): grad_piece = lax.all_gather(grad_own, 'tensor', axis=0, tiled=True)  7.03 us
  transfers between devices with their start and end apart: 10, of which 8 were waited for; matrix products, arithmetic and copies ran while one was open for 8% of the time, Pallas kernels for 0%

commit v1 on v0

--- a/solution.py
+++ b/solution.py
@@ -1,6 +1,8 @@
 import jax
 import jax.numpy as jnp
 from jax import lax
+from jax.experimental import pallas as pl
+from jax.experimental.pallas import tpu as pltpu
 from jax.sharding import PartitionSpec as P
 
 EPS = 1e-05
@@ -72,7 +74,7 @@
     return members
 
 
-def body(bounds, saved_inputs, w_in, w_out, top_grad):
+def general_body(bounds, saved_inputs, w_in, w_out, top_grad):
     sections = lax.axis_size("section") // 2
     tensors = lax.axis_size("tensor")
     pipe_index = lax.axis_index("pipe")
@@ -184,6 +186,269 @@
     return (grad_in_part[None], grad_out_part[None])
 
 
+def norm_rows(saved):
+    floats = saved.astype(jnp.float32)
+    row_scale = jnp.sqrt(jnp.mean(floats * floats, axis=-1, keepdims=True) + EPS)
+    return floats / row_scale, row_scale
+
+
+def nt_dot(left, right):
+    return lax.dot_general(left, right, (((1,), (1,)), ((), ())), preferred_element_type=jnp.float32)
+
+
+def tn_dot(left, right):
+    return lax.dot_general(left, right, (((0,), (0,)), ((), ())), preferred_element_type=jnp.float32)
+
+
+def chain_kernel(pick, top_ref, saved_ref, w_in_ref, w_out_ref, grad_ref, q_buf, p_buf, err, pulled, sems):
+    slot = pick[0]
+    chunks = q_buf.shape[0]
+    step = q_buf.shape[1]
+    width = p_buf.shape[1]
+
+    def q_copy(j):
+        return pltpu.make_async_copy(w_out_ref.at[slot, pl.ds(j * step, step)], q_buf.at[j], sems.at[j])
+
+    def p_copy(j):
+        return pltpu.make_async_copy(w_in_ref.at[slot, pl.ds(j * width, width)], p_buf.at[j], sems.at[chunks + j])
+
+    for j in range(chunks):
+        q_copy(j).start()
+    for j in range(chunks):
+        p_copy(j).start()
+    grad_next = top_ref[0]
+    for j in range(chunks):
+        q_copy(j).wait()
+        err[:, j * step : (j + 1) * step] = nt_dot(grad_next, q_buf[j]).astype(jnp.bfloat16)
+    unit, row_scale = norm_rows(saved_ref[0])
+    for j in range(chunks):
+        p_copy(j).wait()
+        pulled[:, j * width : (j + 1) * width] = nt_dot(err[...], p_buf[j])
+    back = pulled[...]
+    inner_mean = jnp.mean(back * unit, axis=-1, keepdims=True)
+    grad_ref[...] = (grad_next.astype(jnp.float32) + (back - unit * inner_mean) / row_scale).astype(jnp.bfloat16)
+
+
+def chain(pick, tops, saved, w_in, w_out):
+    rows, model = saved.shape[1:]
+    inner = w_in.shape[2]
+    chunks = 4
+    return pl.pallas_call(
+        chain_kernel,
+        out_shape=jax.ShapeDtypeStruct((rows, model), jnp.bfloat16),
+        grid_spec=pltpu.PrefetchScalarGridSpec(
+            num_scalar_prefetch=1,
+            grid=(1,),
+            in_specs=[
+                pl.BlockSpec((1, rows, model), lambda i, pick: (pick[1], 0, 0)),
+                pl.BlockSpec((1, rows, model), lambda i, pick: (pick[0], 0, 0)),
+                pl.BlockSpec(memory_space=pl.ANY),
+                pl.BlockSpec(memory_space=pl.ANY),
+            ],
+            out_specs=pl.BlockSpec((rows, model), lambda i, pick: (0, 0)),
+            scratch_shapes=[
+                pltpu.VMEM((chunks, inner // chunks, model), jnp.bfloat16),
+                pltpu.VMEM((chunks, model // chunks, inner), jnp.bfloat16),
+                pltpu.VMEM((rows, inner), jnp.bfloat16),
+                pltpu.VMEM((rows, model), jnp.float32),
+                pltpu.SemaphoreType.DMA((2 * chunks,)),
+            ],
+        ),
+        cost_estimate=pl.CostEstimate(
+            flops=4 * rows * model * inner, bytes_accessed=4 * model * inner, transcendentals=0
+        ),
+        name="chain",
+    )(pick, tops, saved, w_in, w_out)
+
+
+def partial_kernel(
+    pick, e1, e2, e3, late, f1, f2, f3, flate, w_in_ref, w_out_ref,
+    in_send, in_keep, out_send, out_keep,
+    q_buf, p_buf, unit, grads, err, value, unit_part, sems,
+):
+    slot, short, core, half, column = pick[0], pick[1], pick[2], pick[3], pick[4]
+    rows = e1.shape[0]
+    model = e1.shape[1]
+    inner = err.shape[1]
+    lanes = p_buf.shape[2]
+    blocks = p_buf.shape[0]
+
+    def first_of(j):
+        return pl.multiple_of((2 * j + core) * lanes, lanes)
+
+    q_copy = pltpu.make_async_copy(w_out_ref.at[slot], q_buf, sems.at[0])
+    q_copy.start()
+    p_copies = [
+        pltpu.make_async_copy(w_in_ref.at[slot, :, pl.ds(first_of(j), lanes)], p_buf.at[j], sems.at[1 + j])
+        for j in range(blocks)
+    ]
+    for copy in p_copies:
+        copy.start()
+
+    def put(place, units, tops):
+        for n, (block, top) in enumerate(zip(units, tops)):
+            where = pl.ds((2 * place + n) * rows, rows)
+            unit[where, :] = norm_rows(block[...])[0].astype(jnp.bfloat16)
+            grads[where, :] = top[...]
+
+    @pl.when(short == 0)
+    def _():
+        put(0, (e1, e2), (late, e3))
+        put(1, (f1, f2), (flate, f3))
+
+    @pl.when(short != 0)
+    def _():
+        put(0, (late, e1), (e2, e3))
+        put(1, (flate, f1), (f2, f3))
+
+    for j in range(blocks):
+        unit_part[:, j * lanes : (j + 1) * lanes] = unit[:, pl.ds(first_of(j), lanes)]
+    q_copy.wait()
+    err[...] = nt_dot(grads[...], q_buf[...]).astype(jnp.bfloat16)
+    for j in range(blocks):
+        p_copies[j].wait()
+        value[:, j * lanes : (j + 1) * lanes] = jnp.dot(
+            unit[...], p_buf[j], preferred_element_type=jnp.float32
+        ).astype(jnp.bfloat16)
+    half_cols = inner // 2
+    mine = pl.ds(pl.multiple_of(column * half_cols, half_cols), half_cols)
+    other = pl.ds(pl.multiple_of((1 - column) * half_cols, half_cols), half_cols)
+    in_send[...] = tn_dot(unit_part[...], err[:, other]).astype(jnp.bfloat16)
+    in_keep[...] = tn_dot(unit_part[...], err[:, mine])
+    half_rows = value.shape[1] // 2
+    upper = pl.ds(pl.multiple_of(half * half_rows, half_rows), half_rows)
+    lower = pl.ds(pl.multiple_of((1 - half) * half_rows, half_rows), half_rows)
+    out_send[...] = tn_dot(value[:, lower], grads[...]).astype(jnp.bfloat16)
+    out_keep[...] = tn_dot(value[:, upper], grads[...])
+
+
+def partials(pick, early, late, other_early, other_late, w_in, w_out):
+    rows, model = late.shape
+    inner = w_in.shape[2]
+    blocks = 4
+    tokens = 4 * rows
+    lanes = model // (2 * blocks)
+    part = blocks * lanes
+    vmem = pl.BlockSpec(memory_space=pltpu.VMEM)
+    hbm = pl.BlockSpec(memory_space=pl.ANY)
+    return pl.pallas_call(
+        partial_kernel,
+        out_shape=(
+            jax.ShapeDtypeStruct((part, inner // 2), jnp.bfloat16),
+            jax.ShapeDtypeStruct((part, inner // 2), jnp.float32),
+            jax.ShapeDtypeStruct((part // 2, model), jnp.bfloat16),
+            jax.ShapeDtypeStruct((part // 2, model), jnp.float32),
+        ),
+        in_specs=[pl.BlockSpec(memory_space=pltpu.SMEM)] + [vmem] * 8 + [hbm] * 2,
+        out_specs=(vmem,) * 4,
+        scratch_shapes=[
+            pltpu.VMEM((inner, model), jnp.bfloat16),
+            pltpu.VMEM((blocks, model, lanes), jnp.bfloat16),
+            pltpu.VMEM((tokens, model), jnp.bfloat16),
+            pltpu.VMEM((tokens, model), jnp.bfloat16),
+            pltpu.VMEM((tokens, inner), jnp.bfloat16),
+            pltpu.VMEM((tokens, part), jnp.bfloat16),
+            pltpu.VMEM((tokens, part), jnp.bfloat16),
+            pltpu.SemaphoreType.DMA((1 + blocks,)),
+        ],
+        compiler_params=pltpu.CompilerParams(vmem_limit_bytes=40 * 2**20),
+        cost_estimate=pl.CostEstimate(
+            flops=10 * rows * model * inner, bytes_accessed=3 * model * inner, transcendentals=0
+        ),
+        name="partials",
+    )(pick, *early, late, *other_early, other_late, w_in, w_out)
+
+
+def moved(value, route):
+    sections = lax.axis_size("section")
+    pairs = []
+    for source in range(lax.axis_size("pipe") * sections):
+        target = route(source // sections, source % sections)
+        if target is not None:
+            pairs.append((source, target[0] * sections + target[1]))
+    return lax.ppermute(value, ("pipe", "section"), pairs)
+
+
+def two_section_body(bounds, saved_inputs, w_in, w_out, top_grad):
+    pipe_index = lax.axis_index("pipe")
+    section_index = lax.axis_index("section")
+    column = lax.axis_index("tensor")
+    relay = pipe_index // 2
+    core = pipe_index % 2
+    half = section_index % 2
+    left = section_index // 2 == 0
+    boundary = lax.dynamic_index_in_dim(bounds, relay, 0, keepdims=False)
+    short = boundary[1] - boundary[0] == 2
+    saved = saved_inputs[0, 0]
+    proj_in = w_in[0, 0]
+    proj_out = w_out[0, 0]
+    tops = top_grad[0]
+    model = saved.shape[2]
+    inner = proj_in.shape[2]
+    top_rows = lax.dynamic_index_in_dim(tops, half, 0, keepdims=False)
+
+    def across(value):
+        return moved(value, lambda p, s: (p ^ 2, s))
+
+    def across_left(value):
+        return moved(value, lambda p, s: (p ^ 2, s) if s < 2 else None)
+
+    def core_swap(value):
+        return moved(value, lambda p, s: (p ^ 1, s) if s < 2 else None)
+
+    def half_swap(value):
+        return moved(value, lambda p, s: (p, s ^ 1) if s < 2 else None)
+
+    def column_swap(value):
+        return lax.ppermute(value, "tensor", [(0, 1), (1, 0)])
+
+    swapped = across(jnp.where(left & jnp.logical_not(short), top_rows, saved[0]))
+    upper_slot = jnp.where(left, 1, 0).astype(jnp.int32)
+    grad_low = chain(jnp.stack([upper_slot, half.astype(jnp.int32)]), tops, saved, proj_in, proj_out)
+    grad_other = across_left(grad_low)
+    late = moved(jnp.where(short, swapped, grad_low), lambda p, s: (p, s - 2) if s >= 2 else None)
+    own_saved = jnp.where(short, saved[1], saved[0])
+    early = (own_saved, swapped, jnp.where(short, top_rows, grad_other))
+    other_early = tuple(core_swap(part) for part in early)
+    other_late = core_swap(late)
+    pick = jnp.stack(
+        [part.astype(jnp.int32) for part in (short, short, core, half, column)]
+    )
+    in_send, in_keep, out_send, out_keep = partials(
+        pick, early, late, other_early, other_late, proj_in, proj_out
+    )
+    in_landed = column_swap(in_send)
+    out_landed = half_swap(out_send)
+    in_sum = (in_keep + in_landed.astype(jnp.float32)).reshape(2, -1, inner // 2)
+    out_sum = out_keep + out_landed.astype(jnp.float32)
+    in_mine = lax.dynamic_index_in_dim(in_sum, half, 0, keepdims=False)
+    in_next = lax.dynamic_index_in_dim(in_sum, 1 - half, 0, keepdims=False)
+    out_mine = lax.dynamic_slice_in_dim(out_sum, column * (model // 2), model // 2, 1)
+    out_next = lax.dynamic_slice_in_dim(out_sum, (1 - column) * (model // 2), model // 2, 1)
+    in_landed = half_swap(in_next.astype(jnp.bfloat16))
+    out_landed = column_swap(out_next.astype(jnp.bfloat16))
+    results = []
+    for mine, landed in ((in_mine, in_landed), (out_mine, out_landed)):
+        total = (mine + landed.astype(jnp.float32)).reshape(2, -1, mine.shape[1])
+        own = lax.dynamic_index_in_dim(total, relay, 0, keepdims=False)
+        sent = lax.dynamic_index_in_dim(total, 1 - relay, 0, keepdims=False).astype(jnp.bfloat16)
+        got = across_left(sent)
+        onward = moved(
+            jnp.where(short, got, own.astype(jnp.bfloat16)),
+            lambda p, s: (p, s + 2) if s < 2 else None,
+        )
+        lower = jnp.where(short, own, got.astype(jnp.float32))
+        results.append(jnp.where(left, lower, onward.astype(jnp.float32))[None])
+    return tuple(results)
+
+
+def body(bounds, saved_inputs, w_in, w_out, top_grad):
+    two_sections = lax.axis_size("section") == 4 and lax.axis_size("pipe") == 4
+    if two_sections and lax.axis_size("tensor") == 2:
+        return two_section_body(bounds, saved_inputs, w_in, w_out, top_grad)
+    return general_body(bounds, saved_inputs, w_in, w_out, top_grad)
+
+
 def solution(mesh):
     placed = (
         P(),

time: 234 us -> 105 us (0.45)
  waiting for transfers between devices: 136 us -> 52.8 us
  blocking collectives: 31.6 us -> 0 us
  Pallas kernels: 0 us -> 14.5 us
  between operations: 16.1 us -> 2.35 us
  other arithmetic: 15.4 us -> 2.72 us
  matrix products: 4.95 us -> 0 us
  local copies, waits for them, and re-layouts: 5.29 us -> 10.2 us
    ppermute x8 -> x15, waiting for transfers between devices: 110 us -> 52.8 us  [the longest x13 39.1 us: moved(): return lax.ppermute(value, ('pipe', 'section'), pairs)]
    all_gather x4 -> x0, blocking collectives: 31.6 us -> none  [the longest x1 8.62 us: body(): unit_piece = lax.all_gather(unit_own, 'tensor', axis=0, tiled=True)]
    reduce_scatter x2 -> x0, waiting for transfers between devices: 25.7 us -> none  [the longest x1 25.7 us: body(): lax.psum_scatter(mine_out + landed_out, 'pipe', scatter_dimension=0, tile...]
    pallas_call x0 -> x2, Pallas kernels: none -> 14.5 us  [the longest x1 7.32 us: partials(): pl.pallas_call(partial_kernel, out_shape=(jax.ShapeDtypeStruct((part, inn...]
    unnamed x10 -> x22, local copies, waits for them, and re-layouts: 0.6 us -> 9.35 us
    add x6 -> x4, other arithmetic: 9.13 us -> 0.49 us  [the longest x1 0.18 us: two_section_body(): out_sum = out_keep + out_landed.astype(jnp.float32)]
    dot_general x3 -> x0, matrix products: 4.95 us -> none  [the longest x1 4.02 us: body(): jnp.einsum('kre,kea->kra', unit_low, proj_in, preferred_element_type=jnp....]
    select_n x2 -> x4, other arithmetic: 2.84 us -> 0.16 us  [the longest x1 0.07 us: two_section_body(): early = (own_saved, swapped, jnp.where(short, top_rows, grad_other))]
  transfers between devices with their start and end apart: 10 -> 15, of which waited for: 8 -> 6; matrix products, arithmetic and copies ran while one was open for 8% -> 2% of each run, Pallas kernels for 0% -> 0%
where the time goes in v1:
time: 105 us; the launch traced here: 104 us
  waiting for transfers between devices  52.8 us (50%)
  starting transfers between devices  21.2 us (20%)
  Pallas kernels  14.5 us (14%)
  local copies, waits for them, and re-layouts  10.2 us (10%)
  other arithmetic  2.72 us (3%)
  between operations  2.35 us (2%)
    ppermute x13, waiting for transfers between devices, moved(): return lax.ppermute(value, ('pipe', 'section'), pairs)  39.1 us
    ppermute x13, starting transfers between devices, moved(): return lax.ppermute(value, ('pipe', 'section'), pairs)  19 us
    ppermute x2, waiting for transfers between devices, column_swap(): return lax.ppermute(value, 'tensor', [(0, 1), (1, 0)])  13.7 us
    unnamed x22, local copies, waits for them, and re-layouts  9.35 us
    pallas_call x1, Pallas kernels, partials(): pl.pallas_call(partial_kernel, out_shape=(jax.ShapeDtypeStruct((part, inn...  7.32 us
    pallas_call x1, Pallas kernels, chain(): pl.pallas_call(chain_kernel, out_shape=jax.ShapeDtypeStruct((rows, model)...  7.2 us
    ppermute x2, starting transfers between devices, column_swap(): return lax.ppermute(value, 'tensor', [(0, 1), (1, 0)])  2.16 us
  transfers between devices with their start and end apart: 15, of which 6 were waited for; matrix products, arithmetic and copies ran while one was open for 2% of the time, Pallas kernels for 0%

profile of v1, /device:TPU:24, one launch (start us, length us, event | category | flops | bytes accessed | tf_op | source)
XLA Modules:
  0.0 103.8 jit_solution(9742743382031281482)
XLA Ops:
  0.6 0.0 copy-start
  0.7 0.6 pad_add_fusion.pick
  1.3 7.2 %chain.1 = bf16[128,1024]{1,0:T(8,128)(2,1)} custom-call(s32[2]{0:T(128)} %pad_add_fusion.pick, bf16[2,128,1024]{2,1,0:T(8,128)(2,1)} %bitcast.64, bf16[2,128,1024]{2,1,0:T(8,128)(2,1)} %bitcast.63, bf16[2,1024,1024]{2,1,0:T(8,128)(2,1)} %bitcast.51, bf16[2,1024,1024]{2,1,0:T(8,128)(2,1)} %bitcast.53), custom_call_target="tpu_custom_call" | custom-call | flops 536870912 | bytes 4194304 | tf_op jit(solution)/shard_map/chain/pallas_call | solution.py:236
  8.5 0.7 collective-permute-start.1
  9.2 0.7 fusion.9
  11.2 0.0 collective-permute-done.1
  11.3 0.1 bitcast_select_fusion.2
  11.3 1.6 %collective-permute-start = (bf16[128,1024]{1,0:T(8,128)(2,1)S(1)}, bf16[128,1024]{1,0:T(8,128)(2,1)S(1)}, u32[]{:S(2)}, u32[]{:S(2)}) collective-permute-start(bf16[128,1024]{1,0:T(8,128)(2,1)S(1)} %get-tuple-element.11), channel_id=1, source_target_pairs={{0,16},{2,18},{4,20},{6,22},{8,24},{10,26},{12,28},{14,30},{16,0},... | collective-permute-start | bytes 786440 | tf_op jit(solution)/shard_map/ppermute | solution.py:369
  12.9 6.5 %collective-permute-done.e2 = bf16[128,1024]{1,0:T(8,128)(2,1)S(1)} collective-permute-done((bf16[128,1024]{1,0:T(8,128)(2,1)S(1)}, bf16[128,1024]{1,0:T(8,128)(2,1)S(1)}, u32[]{:S(2)}, u32[]{:S(2)}) %collective-permute-start) | collective-permute-done | bytes 262176 | tf_op jit(solution)/shard_map/ppermute | solution.py:369
  19.5 8.8 %collective-permute-start.2 = (bf16[128,1024]{1,0:T(8,128)(2,1)S(1)}, bf16[128,1024]{1,0:T(8,128)(2,1)S(1)}, u32[]{:S(2)}, u32[]{:S(2)}) collective-permute-start(bf16[128,1024]{1,0:T(8,128)(2,1)S(1)} %broadcast_select_fusion), channel_id=1, source_target_pairs={{4,0},{6,2},{12,8},{14,10},{20,16},{22,18},{28,24},{30,26},{5,1},{... | collective-permute-start | bytes 786440 | tf_op jit(solution)/shard_map/ppermute | solution.py:369
  28.3 0.7 collective-permute-start.3
  28.9 0.7 collective-permute-start.5
  29.6 0.7 collective-permute-start.4
  30.3 1.8 %collective-permute-done.2.late = bf16[128,1024]{1,0:T(8,128)(2,1)S(1)} collective-permute-done((bf16[128,1024]{1,0:T(8,128)(2,1)S(1)}, bf16[128,1024]{1,0:T(8,128)(2,1)S(1)}, u32[]{:S(2)}, u32[]{:S(2)}) %collective-permute-start.2) | collective-permute-done | bytes 262176 | tf_op jit(solution)/shard_map/ppermute | solution.py:369
  32.1 0.7 collective-permute-start.6
  32.8 0.1 stack.31.pick
  32.9 0.7 copy-done.3
  33.6 0.0 collective-permute-done.4.f2
  33.6 0.7 copy-done.5
  34.3 0.0 collective-permute-done.6.flate
  34.3 0.7 copy-done.7
  35.0 2.2 %copy-done.1 = bf16[1,1,2,1024,1024]{4,3,2,1,0:T(8,128)(2,1)S(1)} copy-done((bf16[1,1,2,1024,1024]{4,3,2,1,0:T(8,128)(2,1)S(1)}, bf16[1,1,2,1024,1024]{4,3,2,1,0:T(8,128)(2,1)}, u32[]{:S(2)}) %copy-start.1) | copy-done | bytes 4194328
  37.2 2.2 %copy-done.2 = bf16[1,1,2,1024,1024]{4,3,2,1,0:T(8,128)(2,1)S(1)} copy-done((bf16[1,1,2,1024,1024]{4,3,2,1,0:T(8,128)(2,1)S(1)}, bf16[1,1,2,1024,1024]{4,3,2,1,0:T(8,128)(2,1)}, u32[]{:S(2)}) %copy-start.2) | copy-done | bytes 4194328
  39.4 0.9 copy-done.4
  40.4 0.9 copy-done.6
  41.3 0.9 copy-done.8
  42.3 7.3 %partials.1 = (bf16[512,512]{1,0:T(8,128)(2,1)}, f32[512,512]{1,0:T(8,128)S(1)}, bf16[256,1024]{1,0:T(8,128)(2,1)}, f32[256,1024]{1,0:T(8,128)S(1)}) custom-call(s32[5]{0:T(128)S(1)} %stack.31.pick, bf16[128,1024]{1,0:T(8,128)(2,1)S(1)} %get-tuple-element.12.e1, bf16[128,1024]{1,0:T(8,128)(2,1)S(1)} %collective-permute-done.e2, ...), custom_call_target="tpu_custom_call" | custom-call | flops 1342177280 | bytes 3145728 | tf_op jit(solution)/shard_map/partials/pallas_call | solution.py:334
  49.6 0.7 collective-permute-start.11
  50.3 1.5 %collective-permute-start.7 = (bf16[512,512]{1,0:T(8,128)(2,1)}, bf16[512,512]{1,0:T(8,128)(2,1)S(1)}, u32[]{:S(2)}, u32[]{:S(2)}) collective-permute-start(bf16[512,512]{1,0:T(8,128)(2,1)} %get-tuple-element.7), channel_id=1, source_target_pairs={{0,1},{1,0},{2,3},{3,2},{4,5},{5,4},{6,7},{7,6},{8,9},{9,8},{10,11... | collective-permute-start | bytes 1572872 | tf_op jit(solution)/shard_map/ppermute | solution.py:403
  51.8 0.0 collective-permute-done.11
  51.8 0.2 convert_add_fusion
  52.1 0.6 collective-permute-start.12
  52.7 11.8 %collective-permute-done.7 = bf16[512,512]{1,0:T(8,128)(2,1)S(1)} collective-permute-done((bf16[512,512]{1,0:T(8,128)(2,1)}, bf16[512,512]{1,0:T(8,128)(2,1)S(1)}, u32[]{:S(2)}, u32[]{:S(2)}) %collective-permute-start.7) | collective-permute-done | bytes 524320 | tf_op jit(solution)/shard_map/ppermute | solution.py:403
  64.5 0.2 convert_add_fusion.1
  64.7 0.7 collective-permute-start.8
  65.4 1.9 %collective-permute-done.12 = bf16[256,512]{1,0:T(8,128)(2,1)S(1)} collective-permute-done((bf16[256,512]{1,0:T(8,128)(2,1)S(1)}, bf16[256,512]{1,0:T(8,128)(2,1)S(1)}, u32[]{:S(2)}, u32[]{:S(2)}) %collective-permute-start.12) | collective-permute-done | bytes 262176 | tf_op jit(solution)/shard_map/ppermute | solution.py:403
  67.3 0.1 convert_add_fusion.2
  67.4 0.7 collective-permute-start.13
  68.1 0.0 collective-permute-done.8
  68.1 0.1 bitcast_add_fusion
  68.2 0.7 collective-permute-start.9
  68.9 0.0 collective-permute-done.13
  69.0 1.3 %collective-permute-start.14 = (bf16[128,512]{1,0:T(8,128)(2,1)S(1)}, bf16[128,512]{1,0:T(8,128)(2,1)S(1)}, u32[]{:S(2)}, u32[]{:S(2)}) collective-permute-start(bf16[128,512]{1,0:T(8,128)(2,1)S(1)} %fusion.8), channel_id=1, source_target_pairs={{0,4},{2,6},{8,12},{10,14},{16,20},{18,22},{24,28},{26,30},{1,5},{... | collective-permute-start | bytes 393224 | tf_op jit(solution)/shard_map/ppermute | solution.py:369
  70.3 1.3 %collective-permute-start.10 = (bf16[128,512]{1,0:T(8,128)(2,1)S(1)}, bf16[128,512]{1,0:T(8,128)(2,1)S(1)}, u32[]{:S(2)}, u32[]{:S(2)}) collective-permute-start(bf16[128,512]{1,0:T(8,128)(2,1)S(1)} %fusion.7), channel_id=1, source_target_pairs={{0,4},{2,6},{8,12},{10,14},{16,20},{18,22},{24,28},{26,30},{1,5},{... | collective-permute-start | bytes 393224 | tf_op jit(solution)/shard_map/ppermute | solution.py:369
  71.6 29.4 %collective-permute-done.14 = bf16[128,512]{1,0:T(8,128)(2,1)S(1)} collective-permute-done((bf16[128,512]{1,0:T(8,128)(2,1)S(1)}, bf16[128,512]{1,0:T(8,128)(2,1)S(1)}, u32[]{:S(2)}, u32[]{:S(2)}) %collective-permute-start.14) | collective-permute-done | bytes 131104 | tf_op jit(solution)/shard_map/ppermute | solution.py:369
  101.0 0.7 fusion.2
  101.8 1.3 %collective-permute-done.10 = bf16[128,512]{1,0:T(8,128)(2,1)S(1)} collective-permute-done((bf16[128,512]{1,0:T(8,128)(2,1)S(1)}, bf16[128,512]{1,0:T(8,128)(2,1)S(1)}, u32[]{:S(2)}, u32[]{:S(2)}) %collective-permute-start.10) | collective-permute-done | bytes 131104 | tf_op jit(solution)/shard_map/ppermute | solution.py:369
  103.1 0.7 fusion.4
  (24 shorter events, 0.3 us)
Async XLA Ops:
  0.6 8.6 %copy-start = (s32[2,3]{1,0:T(2,128)S(1)}, s32[2,3]{1,0:T(2,128)}, u32[]{:S(2)}) copy-start(s32[2,3]{1,0:T(2,128)} %param.5) | copy-start | bytes 76
  1.3 10.0 %copy-start.9 = (bf16[1,1,2,128,1024]{4,3,2,1,0:T(8,128)(2,1)S(1)}, bf16[1,1,2,128,1024]{4,3,2,1,0:T(8,128)(2,1)}, u32[]{:S(2)}) copy-start(bf16[1,1,2,128,1024]{4,3,2,1,0:T(8,128)(2,1)} %param.6) | copy-start | bytes 1572868
  1.3 10.0 %copy-start.10 = (bf16[1,2,128,1024]{3,2,1,0:T(8,128)(2,1)S(1)}, bf16[1,2,128,1024]{3,2,1,0:T(8,128)(2,1)}, u32[]{:S(2)}) copy-start(bf16[1,2,128,1024]{3,2,1,0:T(8,128)(2,1)} %param.9) | copy-start | bytes 1572868
  8.5 2.8 %collective-permute-start.1 = (bf16[128,1024]{1,0:T(8,128)(2,1)}, bf16[128,1024]{1,0:T(8,128)(2,1)S(1)}, u32[]{:S(2)}, u32[]{:S(2)}) collective-permute-start(bf16[128,1024]{1,0:T(8,128)(2,1)} %chain.1), channel_id=1, source_target_pairs={{0,16},{2,18},{8,24},{10,26},{16,0},{18,2},{24,8},{26,10},{1,17},{... | collective-permute-start | bytes 786440 | tf_op jit(solution)/shard_map/ppermute | solution.py:369
  11.3 8.1 %collective-permute-start = (bf16[128,1024]{1,0:T(8,128)(2,1)S(1)}, bf16[128,1024]{1,0:T(8,128)(2,1)S(1)}, u32[]{:S(2)}, u32[]{:S(2)}) collective-permute-start(bf16[128,1024]{1,0:T(8,128)(2,1)S(1)} %get-tuple-element.11), channel_id=1, source_target_pairs={{0,16},{2,18},{4,20},{6,22},{8,24},{10,26},{12,28},{14,30},{16,0},... | collective-permute-start | bytes 786440 | tf_op jit(solution)/shard_map/ppermute | solution.py:369
  19.5 12.6 %collective-permute-start.2 = (bf16[128,1024]{1,0:T(8,128)(2,1)S(1)}, bf16[128,1024]{1,0:T(8,128)(2,1)S(1)}, u32[]{:S(2)}, u32[]{:S(2)}) collective-permute-start(bf16[128,1024]{1,0:T(8,128)(2,1)S(1)} %broadcast_select_fusion), channel_id=1, source_target_pairs={{4,0},{6,2},{12,8},{14,10},{20,16},{22,18},{28,24},{30,26},{5,1},{... | collective-permute-start | bytes 786440 | tf_op jit(solution)/shard_map/ppermute | solution.py:369
  28.3 4.6 %collective-permute-start.3 = (bf16[128,1024]{1,0:T(8,128)(2,1)S(1)}, bf16[128,1024]{1,0:T(8,128)(2,1)S(1)}, u32[]{:S(2)}, u32[]{:S(2)}) collective-permute-start(bf16[128,1024]{1,0:T(8,128)(2,1)S(1)} %get-tuple-element.12.e1), channel_id=1, source_target_pairs={{0,8},{2,10},{8,0},{10,2},{16,24},{18,26},{24,16},{26,18},{1,9},{3... | collective-permute-start | bytes 786440 | tf_op jit(solution)/shard_map/ppermute | solution.py:369
  28.9 4.0 %collective-permute-start.5 = (bf16[128,1024]{1,0:T(8,128)(2,1)S(1)}, bf16[128,1024]{1,0:T(8,128)(2,1)S(1)}, u32[]{:S(2)}, u32[]{:S(2)}) collective-permute-start(bf16[128,1024]{1,0:T(8,128)(2,1)S(1)} %get-tuple-element.10.e3), channel_id=1, source_target_pairs={{0,8},{2,10},{8,0},{10,2},{16,24},{18,26},{24,16},{26,18},{1,9},{3... | collective-permute-start | bytes 786440 | tf_op jit(solution)/shard_map/ppermute | solution.py:369
  29.6 4.0 %collective-permute-start.4 = (bf16[128,1024]{1,0:T(8,128)(2,1)S(1)}, bf16[128,1024]{1,0:T(8,128)(2,1)S(1)}, u32[]{:S(2)}, u32[]{:S(2)}) collective-permute-start(bf16[128,1024]{1,0:T(8,128)(2,1)S(1)} %collective-permute-done.e2), channel_id=1, source_target_pairs={{0,8},{2,10},{8,0},{10,2},{16,24},{18,26},{24,16},{26,18},{1,9},{3... | collective-permute-start | bytes 786440 | tf_op jit(solution)/shard_map/ppermute | solution.py:369
  32.1 2.2 %collective-permute-start.6 = (bf16[128,1024]{1,0:T(8,128)(2,1)S(1)}, bf16[128,1024]{1,0:T(8,128)(2,1)S(1)}, u32[]{:S(2)}, u32[]{:S(2)}) collective-permute-start(bf16[128,1024]{1,0:T(8,128)(2,1)S(1)} %collective-permute-done.2.late), channel_id=1, source_target_pairs={{0,8},{2,10},{8,0},{10,2},{16,24},{18,26},{24,16},{26,18},{1,9},{3... | collective-permute-start | bytes 786440 | tf_op jit(solution)/shard_map/ppermute | solution.py:369
  32.9 0.7 copy-start.3
  33.6 0.7 copy-start.5
  34.3 0.7 copy-start.7
  35.0 2.2 %copy-start.1 = (bf16[1,1,2,1024,1024]{4,3,2,1,0:T(8,128)(2,1)S(1)}, bf16[1,1,2,1024,1024]{4,3,2,1,0:T(8,128)(2,1)}, u32[]{:S(2)}) copy-start(bf16[1,1,2,1024,1024]{4,3,2,1,0:T(8,128)(2,1)} %param.7) | copy-start | bytes 12582916
  37.2 2.2 %copy-start.2 = (bf16[1,1,2,1024,1024]{4,3,2,1,0:T(8,128)(2,1)S(1)}, bf16[1,1,2,1024,1024]{4,3,2,1,0:T(8,128)(2,1)}, u32[]{:S(2)}) copy-start(bf16[1,1,2,1024,1024]{4,3,2,1,0:T(8,128)(2,1)} %param.8) | copy-start | bytes 12582916
  39.4 0.9 copy-start.4
  40.4 0.9 copy-start.6
  41.3 0.9 copy-start.8
  49.6 2.2 %collective-permute-start.11 = (bf16[256,1024]{1,0:T(8,128)(2,1)}, bf16[256,1024]{1,0:T(8,128)(2,1)S(1)}, u32[]{:S(2)}, u32[]{:S(2)}) collective-permute-start(bf16[256,1024]{1,0:T(8,128)(2,1)} %get-tuple-element.9), channel_id=1, source_target_pairs={{0,2},{2,0},{8,10},{10,8},{16,18},{18,16},{24,26},{26,24},{1,3},{3... | collective-permute-start | bytes 1572872 | tf_op jit(solution)/shard_map/ppermute | solution.py:369
  50.3 14.2 %collective-permute-start.7 = (bf16[512,512]{1,0:T(8,128)(2,1)}, bf16[512,512]{1,0:T(8,128)(2,1)S(1)}, u32[]{:S(2)}, u32[]{:S(2)}) collective-permute-start(bf16[512,512]{1,0:T(8,128)(2,1)} %get-tuple-element.7), channel_id=1, source_target_pairs={{0,1},{1,0},{2,3},{3,2},{4,5},{5,4},{6,7},{7,6},{8,9},{9,8},{10,11... | collective-permute-start | bytes 1572872 | tf_op jit(solution)/shard_map/ppermute | solution.py:403
  52.1 15.2 %collective-permute-start.12 = (bf16[256,512]{1,0:T(8,128)(2,1)S(1)}, bf16[256,512]{1,0:T(8,128)(2,1)S(1)}, u32[]{:S(2)}, u32[]{:S(2)}) collective-permute-start(bf16[256,512]{1,0:T(8,128)(2,1)S(1)} %dynamic-slice_convert_fusion), channel_id=1, source_target_pairs={{0,1},{1,0},{2,3},{3,2},{4,5},{5,4},{6,7},{7,6},{8,9},{9,8},{10,11... | collective-permute-start | bytes 786440 | tf_op jit(solution)/shard_map/ppermute | solution.py:403
  64.7 3.4 %collective-permute-start.8 = (bf16[256,512]{1,0:T(8,128)(2,1)S(1)}, bf16[256,512]{1,0:T(8,128)(2,1)S(1)}, u32[]{:S(2)}, u32[]{:S(2)}) collective-permute-start(bf16[256,512]{1,0:T(8,128)(2,1)S(1)} %fusion), channel_id=1, source_target_pairs={{0,2},{2,0},{8,10},{10,8},{16,18},{18,16},{24,26},{26,24},{1,3},{3... | collective-permute-start | bytes 786440 | tf_op jit(solution)/shard_map/ppermute | solution.py:369
  67.4 1.5 %collective-permute-start.13 = (bf16[128,512]{1,0:T(8,128)(2,1)S(1)}, bf16[128,512]{1,0:T(8,128)(2,1)S(1)}, u32[]{:S(2)}, u32[]{:S(2)}) collective-permute-start(bf16[128,512]{1,0:T(8,128)(2,1)S(1)} %fusion.6), channel_id=1, source_target_pairs={{0,16},{2,18},{8,24},{10,26},{16,0},{18,2},{24,8},{26,10},{1,17},{... | collective-permute-start | bytes 393224 | tf_op jit(solution)/shard_map/ppermute | solution.py:369
  68.2 2.0 %collective-permute-start.9 = (bf16[128,512]{1,0:T(8,128)(2,1)S(1)}, bf16[128,512]{1,0:T(8,128)(2,1)S(1)}, u32[]{:S(2)}, u32[]{:S(2)}) collective-permute-start(bf16[128,512]{1,0:T(8,128)(2,1)S(1)} %fusion.5), channel_id=1, source_target_pairs={{0,16},{2,18},{8,24},{10,26},{16,0},{18,2},{24,8},{26,10},{1,17},{... | collective-permute-start | bytes 393224 | tf_op jit(solution)/shard_map/ppermute | solution.py:369
  69.0 32.1 %collective-permute-start.14 = (bf16[128,512]{1,0:T(8,128)(2,1)S(1)}, bf16[128,512]{1,0:T(8,128)(2,1)S(1)}, u32[]{:S(2)}, u32[]{:S(2)}) collective-permute-start(bf16[128,512]{1,0:T(8,128)(2,1)S(1)} %fusion.8), channel_id=1, source_target_pairs={{0,4},{2,6},{8,12},{10,14},{16,20},{18,22},{24,28},{26,30},{1,5},{... | collective-permute-start | bytes 393224 | tf_op jit(solution)/shard_map/ppermute | solution.py:369
  70.3 32.8 %collective-permute-start.10 = (bf16[128,512]{1,0:T(8,128)(2,1)S(1)}, bf16[128,512]{1,0:T(8,128)(2,1)S(1)}, u32[]{:S(2)}, u32[]{:S(2)}) collective-permute-start(bf16[128,512]{1,0:T(8,128)(2,1)S(1)} %fusion.7), channel_id=1, source_target_pairs={{0,4},{2,6},{8,12},{10,14},{16,20},{18,22},{24,28},{26,30},{1,5},{... | collective-permute-start | bytes 393224 | tf_op jit(solution)/shard_map/ppermute | solution.py:369

commit v2 on v1

--- a/solution.py
+++ b/solution.py
@@ -201,7 +201,7 @@
 
 
 def chain_kernel(pick, top_ref, saved_ref, w_in_ref, w_out_ref, grad_ref, q_buf, p_buf, err, pulled, sems):
-    slot = pick[0]
+    slot = pick[6]
     chunks = q_buf.shape[0]
     step = q_buf.shape[1]
     width = p_buf.shape[1]
@@ -240,10 +240,10 @@
             num_scalar_prefetch=1,
             grid=(1,),
             in_specs=[
-                pl.BlockSpec((1, rows, model), lambda i, pick: (pick[1], 0, 0)),
-                pl.BlockSpec((1, rows, model), lambda i, pick: (pick[0], 0, 0)),
-                pl.BlockSpec(memory_space=pl.ANY),
-                pl.BlockSpec(memory_space=pl.ANY),
+                pl.BlockSpec((1, rows, model), lambda i, pick: (pick[3], 0, 0)),
+                pl.BlockSpec((1, rows, model), lambda i, pick: (pick[6], 0, 0)),
+                pl.BlockSpec(memory_space=pltpu.HBM),
+                pl.BlockSpec(memory_space=pltpu.HBM),
             ],
             out_specs=pl.BlockSpec((rows, model), lambda i, pick: (0, 0)),
             scratch_shapes=[
@@ -261,102 +261,216 @@
     )(pick, tops, saved, w_in, w_out)
 
 
-def partial_kernel(
-    pick, e1, e2, e3, late, f1, f2, f3, flate, w_in_ref, w_out_ref,
-    in_send, in_keep, out_send, out_keep,
-    q_buf, p_buf, unit, grads, err, value, unit_part, sems,
+def early_kernel(
+    pick, e1, e2, e3, f1, f2, f3, w_in_ref, w_out_ref,
+    in_acc, out_acc, q_buf, p_buf, early_part,
+    unit, unit_part, grads, err, value, sems,
 ):
-    slot, short, core, half, column = pick[0], pick[1], pick[2], pick[3], pick[4]
+    slot, short, core = pick[0], pick[1], pick[2]
     rows = e1.shape[0]
-    model = e1.shape[1]
-    inner = err.shape[1]
-    lanes = p_buf.shape[2]
-    blocks = p_buf.shape[0]
+    part = p_buf.shape[1]
+    blocks = 4
+    lanes = part // blocks
 
     def first_of(j):
         return pl.multiple_of((2 * j + core) * lanes, lanes)
 
-    q_copy = pltpu.make_async_copy(w_out_ref.at[slot], q_buf, sems.at[0])
-    q_copy.start()
-    p_copies = [
-        pltpu.make_async_copy(w_in_ref.at[slot, :, pl.ds(first_of(j), lanes)], p_buf.at[j], sems.at[1 + j])
-        for j in range(blocks)
-    ]
-    for copy in p_copies:
+    def gather_lanes(target, column):
+        for j in range(blocks):
+            target[:, column + j * lanes : column + (j + 1) * lanes] = unit[:, pl.ds(first_of(j), lanes)]
+
+    copies = [pltpu.make_async_copy(w_out_ref.at[slot], q_buf, sems.at[0])]
+    for j in range(blocks):
+        copies.append(
+            pltpu.make_async_copy(
+                w_in_ref.at[slot, :, pl.ds(first_of(j), lanes)],
+                p_buf.at[:, pl.ds(j * lanes, lanes)],
+                sems.at[1 + j],
+            )
+        )
+    for copy in copies:
         copy.start()
 
-    def put(place, units, tops):
-        for n, (block, top) in enumerate(zip(units, tops)):
-            where = pl.ds((2 * place + n) * rows, rows)
-            unit[where, :] = norm_rows(block[...])[0].astype(jnp.bfloat16)
-            grads[where, :] = top[...]
+    def put_unit(first, second):
+        unit[:rows, :] = norm_rows(first[...])[0].astype(jnp.bfloat16)
+        unit[rows:, :] = norm_rows(second[...])[0].astype(jnp.bfloat16)
 
     @pl.when(short == 0)
     def _():
-        put(0, (e1, e2), (late, e3))
-        put(1, (f1, f2), (flate, f3))
+        put_unit(e2, f2)
 
     @pl.when(short != 0)
     def _():
-        put(0, (late, e1), (e2, e3))
-        put(1, (flate, f1), (f2, f3))
-
-    for j in range(blocks):
-        unit_part[:, j * lanes : (j + 1) * lanes] = unit[:, pl.ds(first_of(j), lanes)]
-    q_copy.wait()
+        put_unit(e1, f1)
+
+    gather_lanes(unit_part, 0)
+    grads[:rows, :] = e3[...]
+    grads[rows:, :] = f3[...]
+    copies[0].wait()
     err[...] = nt_dot(grads[...], q_buf[...]).astype(jnp.bfloat16)
-    for j in range(blocks):
-        p_copies[j].wait()
-        value[:, j * lanes : (j + 1) * lanes] = jnp.dot(
-            unit[...], p_buf[j], preferred_element_type=jnp.float32
+    in_acc[...] = tn_dot(unit_part[...], err[...])
+    for copy in copies[1:]:
+        copy.wait()
+    value[...] = jnp.dot(unit[...], p_buf[...], preferred_element_type=jnp.float32).astype(jnp.bfloat16)
+    out_acc[...] = tn_dot(value[...], grads[...])
+
+    @pl.when(short == 0)
+    def _():
+        put_unit(e1, f1)
+        gather_lanes(early_part, 0)
+        early_part[:, part:] = jnp.dot(
+            unit[...], p_buf[...], preferred_element_type=jnp.float32
         ).astype(jnp.bfloat16)
-    half_cols = inner // 2
+
+    @pl.when(short != 0)
+    def _():
+        grads[:rows, :] = e2[...]
+        grads[rows:, :] = f2[...]
+        early_part[...] = nt_dot(grads[...], q_buf[...]).astype(jnp.bfloat16)
+
+
+def late_kernel(
+    pick, late, flate, e2, f2, early_part, q_buf, p_buf, in_acc, out_acc,
+    in_send, in_keep, out_send, out_keep,
+    unit, unit_part, value, grads, err,
+):
+    short, core, half, column = pick[1], pick[2], pick[3], pick[4]
+    rows = late.shape[0]
+    part = p_buf.shape[1]
+    blocks = 4
+    lanes = part // blocks
+
+    @pl.when(short == 0)
+    def _():
+        grads[:rows, :] = late[...]
+        grads[rows:, :] = flate[...]
+        err[...] = nt_dot(grads[...], q_buf[...]).astype(jnp.bfloat16)
+        unit_part[...] = early_part[:, :part]
+        value[...] = early_part[:, part:]
+
+    @pl.when(short != 0)
+    def _():
+        unit[:rows, :] = norm_rows(late[...])[0].astype(jnp.bfloat16)
+        unit[rows:, :] = norm_rows(flate[...])[0].astype(jnp.bfloat16)
+        for j in range(blocks):
+            first = pl.multiple_of((2 * j + core) * lanes, lanes)
+            unit_part[:, j * lanes : (j + 1) * lanes] = unit[:, pl.ds(first, lanes)]
+        value[...] = jnp.dot(unit[...], p_buf[...], preferred_element_type=jnp.float32).astype(jnp.bfloat16)
+        grads[:rows, :] = e2[...]
+        grads[rows:, :] = f2[...]
+        err[...] = early_part[...]
+
+    half_cols = err.shape[1] // 2
     mine = pl.ds(pl.multiple_of(column * half_cols, half_cols), half_cols)
     other = pl.ds(pl.multiple_of((1 - column) * half_cols, half_cols), half_cols)
-    in_send[...] = tn_dot(unit_part[...], err[:, other]).astype(jnp.bfloat16)
-    in_keep[...] = tn_dot(unit_part[...], err[:, mine])
-    half_rows = value.shape[1] // 2
+    in_send[...] = (in_acc[:, other] + tn_dot(unit_part[...], err[:, other])).astype(jnp.bfloat16)
+    in_keep[...] = in_acc[:, mine] + tn_dot(unit_part[...], err[:, mine])
+    half_rows = part // 2
     upper = pl.ds(pl.multiple_of(half * half_rows, half_rows), half_rows)
     lower = pl.ds(pl.multiple_of((1 - half) * half_rows, half_rows), half_rows)
-    out_send[...] = tn_dot(value[:, lower], grads[...]).astype(jnp.bfloat16)
-    out_keep[...] = tn_dot(value[:, upper], grads[...])
-
-
-def partials(pick, early, late, other_early, other_late, w_in, w_out):
+    out_send[...] = (out_acc[lower, :] + tn_dot(value[:, lower], grads[...])).astype(jnp.bfloat16)
+    out_keep[...] = out_acc[upper, :] + tn_dot(value[:, upper], grads[...])
+
+
+VMEM = pl.BlockSpec(memory_space=pltpu.VMEM)
+SMEM = pl.BlockSpec(memory_space=pltpu.SMEM)
+HBM = pl.BlockSpec(memory_space=pltpu.HBM)
+
+
+def staged_kernel(pick, saved_ref, tops_ref, own_saved, own_top, given, sems):
+    slot, half, give_top = pick[0], pick[3], pick[5]
+    copies = (
+        pltpu.make_async_copy(saved_ref.at[slot], own_saved, sems.at[1]),
+        pltpu.make_async_copy(tops_ref.at[half], own_top, sems.at[2]),
+    )
+
+    @pl.when(give_top != 0)
+    def _():
+        pltpu.make_async_copy(tops_ref.at[half], given, sems.at[0]).start()
+
+    @pl.when(give_top == 0)
+    def _():
+        pltpu.make_async_copy(saved_ref.at[0], given, sems.at[0]).start()
+
+    for copy in copies:
+        copy.start()
+    pltpu.make_async_copy(saved_ref.at[0], given, sems.at[0]).wait()
+    for copy in copies:
+        copy.wait()
+
+
+def staged(pick, saved, tops):
+    block = jax.ShapeDtypeStruct(saved.shape[1:], saved.dtype)
+    return pl.pallas_call(
+        staged_kernel,
+        out_shape=(block,) * 3,
+        in_specs=[SMEM, HBM, HBM],
+        out_specs=(VMEM,) * 3,
+        scratch_shapes=[pltpu.SemaphoreType.DMA((3,))],
+        compiler_params=pltpu.CompilerParams(vmem_limit_bytes=4 * 2**20),
+        name="staged",
+    )(pick, saved, tops)
+
+
+def early_partials(pick, own, partner, w_in, w_out):
+    rows, model = own[0].shape
+    inner = w_in.shape[2]
+    part = model // 2
+    return pl.pallas_call(
+        early_kernel,
+        out_shape=(
+            jax.ShapeDtypeStruct((part, inner), jnp.float32),
+            jax.ShapeDtypeStruct((part, model), jnp.float32),
+            jax.ShapeDtypeStruct((inner, model), jnp.bfloat16),
+            jax.ShapeDtypeStruct((model, part), jnp.bfloat16),
+            jax.ShapeDtypeStruct((2 * rows, model), jnp.bfloat16),
+        ),
+        in_specs=[SMEM] + [VMEM] * 6 + [HBM] * 2,
+        out_specs=(VMEM,) * 5,
+        scratch_shapes=[
+            pltpu.VMEM((2 * rows, model), jnp.bfloat16),
+            pltpu.VMEM((2 * rows, part), jnp.bfloat16),
+            pltpu.VMEM((2 * rows, model), jnp.bfloat16),
+            pltpu.VMEM((2 * rows, inner), jnp.bfloat16),
+            pltpu.VMEM((2 * rows, part), jnp.bfloat16),
+            pltpu.SemaphoreType.DMA((5,)),
+        ],
+        compiler_params=pltpu.CompilerParams(vmem_limit_bytes=24 * 2**20),
+        cost_estimate=pl.CostEstimate(
+            flops=10 * rows * model * inner, bytes_accessed=3 * model * inner, transcendentals=0
+        ),
+        name="early",
+    )(pick, *own, *partner, w_in, w_out)
+
+
+def late_partials(pick, late, other_late, own_top, other_top, early):
+    in_acc, out_acc, q_buf, p_buf, early_part = early
     rows, model = late.shape
-    inner = w_in.shape[2]
-    blocks = 4
-    tokens = 4 * rows
-    lanes = model // (2 * blocks)
-    part = blocks * lanes
-    vmem = pl.BlockSpec(memory_space=pltpu.VMEM)
-    hbm = pl.BlockSpec(memory_space=pl.ANY)
+    inner = q_buf.shape[0]
+    part = p_buf.shape[1]
     return pl.pallas_call(
-        partial_kernel,
+        late_kernel,
         out_shape=(
             jax.ShapeDtypeStruct((part, inner // 2), jnp.bfloat16),
             jax.ShapeDtypeStruct((part, inner // 2), jnp.float32),
             jax.ShapeDtypeStruct((part // 2, model), jnp.bfloat16),
             jax.ShapeDtypeStruct((part // 2, model), jnp.float32),
         ),
-        in_specs=[pl.BlockSpec(memory_space=pltpu.SMEM)] + [vmem] * 8 + [hbm] * 2,
-        out_specs=(vmem,) * 4,
+        in_specs=[SMEM] + [VMEM] * 9,
+        out_specs=(VMEM,) * 4,
         scratch_shapes=[
-            pltpu.VMEM((inner, model), jnp.bfloat16),
-            pltpu.VMEM((blocks, model, lanes), jnp.bfloat16),
-            pltpu.VMEM((tokens, model), jnp.bfloat16),
-            pltpu.VMEM((tokens, model), jnp.bfloat16),
-            pltpu.VMEM((tokens, inner), jnp.bfloat16),
-            pltpu.VMEM((tokens, part), jnp.bfloat16),
-            pltpu.VMEM((tokens, part), jnp.bfloat16),
-            pltpu.SemaphoreType.DMA((1 + blocks,)),
+            pltpu.VMEM((2 * rows, model), jnp.bfloat16),
+            pltpu.VMEM((2 * rows, part), jnp.bfloat16),
+            pltpu.VMEM((2 * rows, part), jnp.bfloat16),
+            pltpu.VMEM((2 * rows, model), jnp.bfloat16),
+            pltpu.VMEM((2 * rows, inner), jnp.bfloat16),
         ],
-        compiler_params=pltpu.CompilerParams(vmem_limit_bytes=40 * 2**20),
+        compiler_params=pltpu.CompilerParams(vmem_limit_bytes=28 * 2**20),
         cost_estimate=pl.CostEstimate(
-            flops=10 * rows * model * inner, bytes_accessed=3 * model * inner, transcendentals=0
-        ),
-        name="partials",
-    )(pick, *early, late, *other_early, other_late, w_in, w_out)
+            flops=8 * rows * model * inner, bytes_accessed=3 * model * inner, transcendentals=0
+        ),
+        name="late",
+    )(pick, late, other_late, own_top, other_top, early_part, q_buf, p_buf, in_acc, out_acc)
 
 
 def moved(value, route):
@@ -385,7 +499,6 @@
     tops = top_grad[0]
     model = saved.shape[2]
     inner = proj_in.shape[2]
-    top_rows = lax.dynamic_index_in_dim(tops, half, 0, keepdims=False)
 
     def across(value):
         return moved(value, lambda p, s: (p ^ 2, s))
@@ -402,21 +515,20 @@
     def column_swap(value):
         return lax.ppermute(value, "tensor", [(0, 1), (1, 0)])
 
-    swapped = across(jnp.where(left & jnp.logical_not(short), top_rows, saved[0]))
-    upper_slot = jnp.where(left, 1, 0).astype(jnp.int32)
-    grad_low = chain(jnp.stack([upper_slot, half.astype(jnp.int32)]), tops, saved, proj_in, proj_out)
+    give_top = left & jnp.logical_not(short)
+    pick = jnp.stack(
+        [part.astype(jnp.int32) for part in (short, short, core, half, column, give_top, left)]
+    )
+    own_saved, own_top, given = staged(pick, saved, tops)
+    swapped = across(given)
+    grad_low = chain(pick, tops, saved, proj_in, proj_out)
+    late = moved(jnp.where(short, swapped, grad_low), lambda p, s: (p, s - 2) if s >= 2 else None)
     grad_other = across_left(grad_low)
-    late = moved(jnp.where(short, swapped, grad_low), lambda p, s: (p, s - 2) if s >= 2 else None)
-    own_saved = jnp.where(short, saved[1], saved[0])
-    early = (own_saved, swapped, jnp.where(short, top_rows, grad_other))
-    other_early = tuple(core_swap(part) for part in early)
+    own = (own_saved, swapped, jnp.where(short, own_top, grad_other))
+    partner = tuple(core_swap(part) for part in own)
+    early = early_partials(pick, own, partner, proj_in, proj_out)
     other_late = core_swap(late)
-    pick = jnp.stack(
-        [part.astype(jnp.int32) for part in (short, short, core, half, column)]
-    )
-    in_send, in_keep, out_send, out_keep = partials(
-        pick, early, late, other_early, other_late, proj_in, proj_out
-    )
+    in_send, in_keep, out_send, out_keep = late_partials(pick, late, other_late, own[1], partner[1], early)
     in_landed = column_swap(in_send)
     out_landed = half_swap(out_send)
     in_sum = (in_keep + in_landed.astype(jnp.float32)).reshape(2, -1, inner // 2)

time: 105 us -> 95.5 us (0.910)
  waiting for transfers between devices: 52.8 us -> 46.6 us
  starting transfers between devices: 21.2 us -> 18.4 us
  other arithmetic: 2.72 us -> 5.16 us
  local copies, waits for them, and re-layouts: 10.2 us -> 8.58 us
    ppermute x13, waiting for transfers between devices: 39.1 us -> 32.9 us  [moved(): return lax.ppermute(value, ('pipe', 'section'), pairs)]
    ppermute x13, starting transfers between devices: 19 us -> 16.3 us  [moved(): return lax.ppermute(value, ('pipe', 'section'), pairs)]
    unnamed x22 -> x16, local copies, waits for them, and re-layouts: 9.35 us -> 7.77 us
    add x1, other arithmetic: 0.16 us -> 1.22 us  [two_section_body(): in_keep + in_landed.astype(jnp.float32)]
    pallas_call x1 -> x3, Pallas kernels: 7.32 us -> 6.59 us  [the longest x1 3.87 us: early_partials(): pl.pallas_call(early_kernel, out_shape=(jax.ShapeDtypeStruct((part, inner...]
  transfers between devices with their start and end apart: 15 -> 15, of which waited for: 6 -> 5; matrix products, arithmetic and copies ran while one was open for 2% -> 5% of each run, Pallas kernels for 0% -> 12%
where the time goes in v2:
time: 95.5 us; the launch traced here: 94.7 us
  waiting for transfers between devices  46.6 us (49%)
  starting transfers between devices  18.4 us (19%)
  Pallas kernels  13.7 us (14%)
  local copies, waits for them, and re-layouts  8.58 us (9%)
  other arithmetic  5.16 us (5%)
  between operations  2.32 us (2%)
    ppermute x13, waiting for transfers between devices, moved(): return lax.ppermute(value, ('pipe', 'section'), pairs)  32.9 us
    ppermute x13, starting transfers between devices, moved(): return lax.ppermute(value, ('pipe', 'section'), pairs)  16.3 us
    ppermute x2, waiting for transfers between devices, column_swap(): return lax.ppermute(value, 'tensor', [(0, 1), (1, 0)])  13.8 us
    unnamed x16, local copies, waits for them, and re-layouts  7.77 us
    pallas_call x1, Pallas kernels, chain(): pl.pallas_call(chain_kernel, out_shape=jax.ShapeDtypeStruct((rows, model)...  7.07 us
    pallas_call x1, Pallas kernels, early_partials(): pl.pallas_call(early_kernel, out_shape=(jax.ShapeDtypeStruct((part, inner...  3.87 us
    ppermute x2, starting transfers between devices, column_swap(): return lax.ppermute(value, 'tensor', [(0, 1), (1, 0)])  2.09 us
    pallas_call x1, Pallas kernels, late_partials(): pl.pallas_call(late_kernel, out_shape=(jax.ShapeDtypeStruct((part, inner...  2.08 us
  transfers between devices with their start and end apart: 15, of which 5 were waited for; matrix products, arithmetic and copies ran while one was open for 5% of the time, Pallas kernels for 12%

profile of v2, /device:TPU:24, one launch (start us, length us, event | category | flops | bytes accessed | tf_op | source)
XLA Modules:
  0.0 94.7 jit_solution(15780782823228881065)
XLA Ops:
  0.6 0.0 copy-start
  0.7 0.6 copy-done
  1.3 0.6 fusion.9
  3.2 0.1 stack.40.pick
  3.3 1.0 %copy-done.3 = bf16[1,1,2,128,1024]{4,3,2,1,0:T(8,128)(2,1)S(1)} copy-done((bf16[1,1,2,128,1024]{4,3,2,1,0:T(8,128)(2,1)S(1)}, bf16[1,1,2,128,1024]{4,3,2,1,0:T(8,128)(2,1)}, u32[]{:S(2)}) %copy-start.3) | copy-done | bytes 524312
  4.4 1.0 %copy-done.4 = bf16[1,2,128,1024]{3,2,1,0:T(8,128)(2,1)S(1)} copy-done((bf16[1,2,128,1024]{3,2,1,0:T(8,128)(2,1)S(1)}, bf16[1,2,128,1024]{3,2,1,0:T(8,128)(2,1)}, u32[]{:S(2)}) %copy-start.4) | copy-done | bytes 524312
  5.4 0.6 staged.1
  6.1 1.6 %collective-permute-start = (bf16[128,1024]{1,0:T(8,128)(2,1)S(1)}, bf16[128,1024]{1,0:T(8,128)(2,1)S(1)}, u32[]{:S(2)}, u32[]{:S(2)}) collective-permute-start(bf16[128,1024]{1,0:T(8,128)(2,1)S(1)} %get-tuple-element.14), channel_id=1, source_target_pairs={{0,16},{2,18},{4,20},{6,22},{8,24},{10,26},{12,28},{14,30},{16,0},... | collective-permute-start | bytes 786440 | tf_op jit(solution)/shard_map/ppermute | solution.py:483
  7.7 7.1 %chain.1 = bf16[128,1024]{1,0:T(8,128)(2,1)} custom-call(s32[7]{0:T(128)} %copy-done.5, bf16[2,128,1024]{2,1,0:T(8,128)(2,1)} %bitcast.50, bf16[2,128,1024]{2,1,0:T(8,128)(2,1)} %bitcast.48, bf16[2,1024,1024]{2,1,0:T(8,128)(2,1)} %bitcast.44, bf16[2,1024,1024]{2,1,0:T(8,128)(2,1)} %bitcast.46), custom_call_target="tpu_custom_call" | custom-call | flops 536870912 | bytes 4194304 | tf_op jit(solution)/shard_map/chain/pallas_call | solution.py:236
  14.7 0.7 collective-permute-start.4
  15.4 0.7 collective-permute-start.5
  16.1 0.0 collective-permute-done.e2
  16.1 1.0 %broadcast_select_fusion.1 = bf16[128,1024]{1,0:T(8,128)(2,1)S(1)} fusion(bf16[128,1024]{1,0:T(8,128)(2,1)S(1)} %collective-permute-done.e2, bf16[128,1024]{1,0:T(8,128)(2,1)} %chain.1, pred[]{:T(512)} %bitcast), kind=kLoop, calls=%fused_computation.18 | loop fusion | flops 131072 | bytes 786433 | tf_op jit(solution)/shard_map/jit(_where)/select_n | solution.py:525
  17.1 5.2 %collective-permute-start.1 = (bf16[128,1024]{1,0:T(8,128)(2,1)S(1)}, bf16[128,1024]{1,0:T(8,128)(2,1)S(1)}, u32[]{:S(2)}, u32[]{:S(2)}) collective-permute-start(bf16[128,1024]{1,0:T(8,128)(2,1)S(1)} %broadcast_select_fusion.1), channel_id=1, source_target_pairs={{4,0},{6,2},{12,8},{14,10},{20,16},{22,18},{28,24},{30,26},{5,1},{... | collective-permute-start | bytes 786440 | tf_op jit(solution)/shard_map/ppermute | solution.py:483
  22.4 0.0 collective-permute-done.4
  22.4 0.0 copy-start.7
  22.4 0.7 collective-permute-start.6
  23.1 0.7 collective-permute-start.3
  23.8 4.8 %collective-permute-done.1.late = bf16[128,1024]{1,0:T(8,128)(2,1)S(1)} collective-permute-done((bf16[128,1024]{1,0:T(8,128)(2,1)S(1)}, bf16[128,1024]{1,0:T(8,128)(2,1)S(1)}, u32[]{:S(2)}, u32[]{:S(2)}) %collective-permute-start.1) | collective-permute-done | bytes 262176 | tf_op jit(solution)/shard_map/ppermute | solution.py:483
  28.6 0.7 collective-permute-start.2
  29.3 0.0 collective-permute-done.5.f1
  29.3 0.0 collective-permute-done.3.f2
  29.3 0.0 copy-start.1
  29.3 2.2 %copy-done.1 = bf16[1,1,2,1024,1024]{4,3,2,1,0:T(8,128)(2,1)S(1)} copy-done((bf16[1,1,2,1024,1024]{4,3,2,1,0:T(8,128)(2,1)S(1)}, bf16[1,1,2,1024,1024]{4,3,2,1,0:T(8,128)(2,1)}, u32[]{:S(2)}) %copy-start.1) | copy-done | bytes 4194328
  31.5 2.2 %copy-done.2 = bf16[1,1,2,1024,1024]{4,3,2,1,0:T(8,128)(2,1)S(1)} copy-done((bf16[1,1,2,1024,1024]{4,3,2,1,0:T(8,128)(2,1)S(1)}, bf16[1,1,2,1024,1024]{4,3,2,1,0:T(8,128)(2,1)}, u32[]{:S(2)}) %copy-start.2) | copy-done | bytes 4194328
  33.7 0.7 copy-done.6
  34.3 3.9 %early.1 = (f32[512,1024]{1,0:T(8,128)S(1)}, f32[512,1024]{1,0:T(8,128)S(1)}, bf16[1024,1024]{1,0:T(8,128)(2,1)S(1)}, bf16[1024,512]{1,0:T(8,128)(2,1)S(1)}, bf16[256,1024]{1,0:T(8,128)(2,1)S(1)}) custom-call(s32[7]{0:T(128)S(1)} %copy-done.6, bf16[128,1024]{1,0:T(8,128)(2,1)S(1)} %get-tuple-element.15.e1, bf16[128,1024]{1,0:T(8,128)(2,1)S(1)} %collective-permute-done.e2, ...), custom_call_target="tpu_custom_call" | custom-call | flops 1342177280 | bytes 3145728 | tf_op jit(solution)/shard_map/early/pallas_call | solution.py:419
  38.2 0.0 collective-permute-done.2.flate
  38.2 2.1 %late.1 = (bf16[512,512]{1,0:T(8,128)(2,1)S(1)}, f32[512,512]{1,0:T(8,128)S(1)}, bf16[256,1024]{1,0:T(8,128)(2,1)S(1)}, f32[256,1024]{1,0:T(8,128)S(1)}) custom-call(s32[7]{0:T(128)S(1)} %copy-done.7, bf16[128,1024]{1,0:T(8,128)(2,1)S(1)} %collective-permute-done.1.late, bf16[128,1024]{1,0:T(8,128)(2,1)S(1)} %collective-permute-done.2.flate, ...), custom_call_target="tpu_custom_call" | custom-call | flops 1073741824 | bytes 3145728 | tf_op jit(solution)/shard_map/late/pallas_call | solution.py:451
  40.3 1.5 %collective-permute-start.11 = (bf16[256,1024]{1,0:T(8,128)(2,1)S(1)}, bf16[256,1024]{1,0:T(8,128)(2,1)}, u32[]{:S(2)}, u32[]{:S(2)}) collective-permute-start(bf16[256,1024]{1,0:T(8,128)(2,1)S(1)} %get-tuple-element.25), channel_id=1, source_target_pairs={{0,2},{2,0},{8,10},{10,8},{16,18},{18,16},{24,26},{26,24},{1,3},{3... | collective-permute-start | bytes 1572872 | tf_op jit(solution)/shard_map/ppermute | solution.py:483
  41.8 1.5 %collective-permute-start.7 = (bf16[512,512]{1,0:T(8,128)(2,1)S(1)}, bf16[512,512]{1,0:T(8,128)(2,1)}, u32[]{:S(2)}, u32[]{:S(2)}) collective-permute-start(bf16[512,512]{1,0:T(8,128)(2,1)S(1)} %get-tuple-element.23), channel_id=1, source_target_pairs={{0,1},{1,0},{2,3},{3,2},{4,5},{5,4},{6,7},{7,6},{8,9},{9,8},{10,11... | collective-permute-start | bytes 1572872 | tf_op jit(solution)/shard_map/ppermute | solution.py:516
  43.3 1.2 %convert_add_fusion = f32[256,1024]{1,0:T(8,128)S(1)} fusion(f32[256,1024]{1,0:T(8,128)S(1)} %get-tuple-element.24, bf16[256,1024]{1,0:T(8,128)(2,1)} %collective-permute-done.11), kind=kLoop, calls=%fused_computation | loop fusion | flops 524288 | bytes 2621440 | tf_op jit(solution)/shard_map/add | solution.py:535
  44.6 0.6 collective-permute-start.12
  45.2 11.5 %collective-permute-done.7 = bf16[512,512]{1,0:T(8,128)(2,1)} collective-permute-done((bf16[512,512]{1,0:T(8,128)(2,1)S(1)}, bf16[512,512]{1,0:T(8,128)(2,1)}, u32[]{:S(2)}, u32[]{:S(2)}) %collective-permute-start.7) | collective-permute-done | bytes 524320 | tf_op jit(solution)/shard_map/ppermute | solution.py:516
  56.7 1.2 %convert_add_fusion.1 = f32[512,512]{1,0:T(8,128)S(1)} fusion(f32[512,512]{1,0:T(8,128)S(1)} %get-tuple-element.22, bf16[512,512]{1,0:T(8,128)(2,1)} %collective-permute-done.7), kind=kLoop, calls=%fused_computation.1 | loop fusion | flops 524288 | bytes 2621440 | tf_op jit(solution)/shard_map/add | solution.py:534
  58.0 0.7 collective-permute-start.8
  58.7 2.2 %collective-permute-done.12 = bf16[256,512]{1,0:T(8,128)(2,1)S(1)} collective-permute-done((bf16[256,512]{1,0:T(8,128)(2,1)S(1)}, bf16[256,512]{1,0:T(8,128)(2,1)S(1)}, u32[]{:S(2)}, u32[]{:S(2)}) %collective-permute-start.12) | collective-permute-done | bytes 262176 | tf_op jit(solution)/shard_map/ppermute | solution.py:516
  60.9 0.1 convert_add_fusion.2
  61.0 0.7 collective-permute-start.13
  61.7 0.1 bitcast_add_fusion
  61.8 0.7 collective-permute-start.9
  62.5 1.3 %collective-permute-start.14 = (bf16[128,512]{1,0:T(8,128)(2,1)S(1)}, bf16[128,512]{1,0:T(8,128)(2,1)S(1)}, u32[]{:S(2)}, u32[]{:S(2)}) collective-permute-start(bf16[128,512]{1,0:T(8,128)(2,1)S(1)} %fusion.8), channel_id=1, source_target_pairs={{0,4},{2,6},{8,12},{10,14},{16,20},{18,22},{24,28},{26,30},{1,5},{... | collective-permute-start | bytes 393224 | tf_op jit(solution)/shard_map/ppermute | solution.py:483
  63.8 0.0 collective-permute-done.9
  63.9 1.3 %collective-permute-start.10 = (bf16[128,512]{1,0:T(8,128)(2,1)S(1)}, bf16[128,512]{1,0:T(8,128)(2,1)S(1)}, u32[]{:S(2)}, u32[]{:S(2)}) collective-permute-start(bf16[128,512]{1,0:T(8,128)(2,1)S(1)} %fusion.7), channel_id=1, source_target_pairs={{0,4},{2,6},{8,12},{10,14},{16,20},{18,22},{24,28},{26,30},{1,5},{... | collective-permute-start | bytes 393224 | tf_op jit(solution)/shard_map/ppermute | solution.py:483
  65.2 26.7 %collective-permute-done.14 = bf16[128,512]{1,0:T(8,128)(2,1)S(1)} collective-permute-done((bf16[128,512]{1,0:T(8,128)(2,1)S(1)}, bf16[128,512]{1,0:T(8,128)(2,1)S(1)}, u32[]{:S(2)}, u32[]{:S(2)}) %collective-permute-start.14) | collective-permute-done | bytes 131104 | tf_op jit(solution)/shard_map/ppermute | solution.py:483
  91.9 0.7 fusion.2
  92.7 1.3 %collective-permute-done.10 = bf16[128,512]{1,0:T(8,128)(2,1)S(1)} collective-permute-done((bf16[128,512]{1,0:T(8,128)(2,1)S(1)}, bf16[128,512]{1,0:T(8,128)(2,1)S(1)}, u32[]{:S(2)}, u32[]{:S(2)}) %collective-permute-start.10) | collective-permute-done | bytes 131104 | tf_op jit(solution)/shard_map/ppermute | solution.py:483
  94.0 0.7 fusion.4
  (19 shorter events, 0.2 us)
Async XLA Ops:
  0.6 0.7 copy-start
  3.3 4.3 %copy-start.5 = (s32[7]{0:T(128)}, s32[7]{0:T(128)S(1)}, u32[]{:S(2)}) copy-start(s32[7]{0:T(128)S(1)} %stack.40.pick) | copy-start | bytes 88
  3.3 1.0 %copy-start.3 = (bf16[1,1,2,128,1024]{4,3,2,1,0:T(8,128)(2,1)S(1)}, bf16[1,1,2,128,1024]{4,3,2,1,0:T(8,128)(2,1)}, u32[]{:S(2)}) copy-start(bf16[1,1,2,128,1024]{4,3,2,1,0:T(8,128)(2,1)} %param.6) | copy-start | bytes 1572868
  4.4 1.0 %copy-start.4 = (bf16[1,2,128,1024]{3,2,1,0:T(8,128)(2,1)S(1)}, bf16[1,2,128,1024]{3,2,1,0:T(8,128)(2,1)}, u32[]{:S(2)}) copy-start(bf16[1,2,128,1024]{3,2,1,0:T(8,128)(2,1)} %param.9) | copy-start | bytes 1572868
  6.1 10.0 %collective-permute-start = (bf16[128,1024]{1,0:T(8,128)(2,1)S(1)}, bf16[128,1024]{1,0:T(8,128)(2,1)S(1)}, u32[]{:S(2)}, u32[]{:S(2)}) collective-permute-start(bf16[128,1024]{1,0:T(8,128)(2,1)S(1)} %get-tuple-element.14), channel_id=1, source_target_pairs={{0,16},{2,18},{4,20},{6,22},{8,24},{10,26},{12,28},{14,30},{16,0},... | collective-permute-start | bytes 786440 | tf_op jit(solution)/shard_map/ppermute | solution.py:483
  14.7 7.6 %collective-permute-start.4 = (bf16[128,1024]{1,0:T(8,128)(2,1)}, bf16[128,1024]{1,0:T(8,128)(2,1)S(1)}, u32[]{:S(2)}, u32[]{:S(2)}) collective-permute-start(bf16[128,1024]{1,0:T(8,128)(2,1)} %chain.1), channel_id=1, source_target_pairs={{0,16},{2,18},{8,24},{10,26},{16,0},{18,2},{24,8},{26,10},{1,17},{... | collective-permute-start | bytes 786440 | tf_op jit(solution)/shard_map/ppermute | solution.py:483
  15.4 13.9 %collective-permute-start.5 = (bf16[128,1024]{1,0:T(8,128)(2,1)S(1)}, bf16[128,1024]{1,0:T(8,128)(2,1)S(1)}, u32[]{:S(2)}, u32[]{:S(2)}) collective-permute-start(bf16[128,1024]{1,0:T(8,128)(2,1)S(1)} %get-tuple-element.15.e1), channel_id=1, source_target_pairs={{0,8},{2,10},{8,0},{10,2},{16,24},{18,26},{24,16},{26,18},{1,9},{3... | collective-permute-start | bytes 786440 | tf_op jit(solution)/shard_map/ppermute | solution.py:483
  17.1 11.5 %collective-permute-start.1 = (bf16[128,1024]{1,0:T(8,128)(2,1)S(1)}, bf16[128,1024]{1,0:T(8,128)(2,1)S(1)}, u32[]{:S(2)}, u32[]{:S(2)}) collective-permute-start(bf16[128,1024]{1,0:T(8,128)(2,1)S(1)} %broadcast_select_fusion.1), channel_id=1, source_target_pairs={{4,0},{6,2},{12,8},{14,10},{20,16},{22,18},{28,24},{30,26},{5,1},{... | collective-permute-start | bytes 786440 | tf_op jit(solution)/shard_map/ppermute | solution.py:483
  22.4 15.9 %copy-start.7 = (s32[7]{0:T(128)S(1)}, s32[7]{0:T(128)}, u32[]{:S(2)}) copy-start(s32[7]{0:T(128)} %copy-done.5) | copy-start | bytes 88
  22.4 6.9 %collective-permute-start.6 = (bf16[128,1024]{1,0:T(8,128)(2,1)S(1)}, bf16[128,1024]{1,0:T(8,128)(2,1)S(1)}, u32[]{:S(2)}, u32[]{:S(2)}) collective-permute-start(bf16[128,1024]{1,0:T(8,128)(2,1)S(1)} %broadcast_select_fusion.e3), channel_id=1, source_target_pairs={{0,8},{2,10},{8,0},{10,2},{16,24},{18,26},{24,16},{26,18},{1,9},{3... | collective-permute-start | bytes 786440 | tf_op jit(solution)/shard_map/ppermute | solution.py:483
  23.1 6.2 %collective-permute-start.3 = (bf16[128,1024]{1,0:T(8,128)(2,1)S(1)}, bf16[128,1024]{1,0:T(8,128)(2,1)S(1)}, u32[]{:S(2)}, u32[]{:S(2)}) collective-permute-start(bf16[128,1024]{1,0:T(8,128)(2,1)S(1)} %collective-permute-done.e2), channel_id=1, source_target_pairs={{0,8},{2,10},{8,0},{10,2},{16,24},{18,26},{24,16},{26,18},{1,9},{3... | collective-permute-start | bytes 786440 | tf_op jit(solution)/shard_map/ppermute | solution.py:483
  28.6 9.6 %collective-permute-start.2 = (bf16[128,1024]{1,0:T(8,128)(2,1)S(1)}, bf16[128,1024]{1,0:T(8,128)(2,1)S(1)}, u32[]{:S(2)}, u32[]{:S(2)}) collective-permute-start(bf16[128,1024]{1,0:T(8,128)(2,1)S(1)} %collective-permute-done.1.late), channel_id=1, source_target_pairs={{0,8},{2,10},{8,0},{10,2},{16,24},{18,26},{24,16},{26,18},{1,9},{3... | collective-permute-start | bytes 786440 | tf_op jit(solution)/shard_map/ppermute | solution.py:483
  29.3 2.2 %copy-start.1 = (bf16[1,1,2,1024,1024]{4,3,2,1,0:T(8,128)(2,1)S(1)}, bf16[1,1,2,1024,1024]{4,3,2,1,0:T(8,128)(2,1)}, u32[]{:S(2)}) copy-start(bf16[1,1,2,1024,1024]{4,3,2,1,0:T(8,128)(2,1)} %param.7) | copy-start | bytes 12582916
  31.5 2.2 %copy-start.2 = (bf16[1,1,2,1024,1024]{4,3,2,1,0:T(8,128)(2,1)S(1)}, bf16[1,1,2,1024,1024]{4,3,2,1,0:T(8,128)(2,1)}, u32[]{:S(2)}) copy-start(bf16[1,1,2,1024,1024]{4,3,2,1,0:T(8,128)(2,1)} %param.8) | copy-start | bytes 12582916
  33.7 0.7 copy-start.6
  40.3 3.0 %collective-permute-start.11 = (bf16[256,1024]{1,0:T(8,128)(2,1)S(1)}, bf16[256,1024]{1,0:T(8,128)(2,1)}, u32[]{:S(2)}, u32[]{:S(2)}) collective-permute-start(bf16[256,1024]{1,0:T(8,128)(2,1)S(1)} %get-tuple-element.25), channel_id=1, source_target_pairs={{0,2},{2,0},{8,10},{10,8},{16,18},{18,16},{24,26},{26,24},{1,3},{3... | collective-permute-start | bytes 1572872 | tf_op jit(solution)/shard_map/ppermute | solution.py:483
  41.8 14.9 %collective-permute-start.7 = (bf16[512,512]{1,0:T(8,128)(2,1)S(1)}, bf16[512,512]{1,0:T(8,128)(2,1)}, u32[]{:S(2)}, u32[]{:S(2)}) collective-permute-start(bf16[512,512]{1,0:T(8,128)(2,1)S(1)} %get-tuple-element.23), channel_id=1, source_target_pairs={{0,1},{1,0},{2,3},{3,2},{4,5},{5,4},{6,7},{7,6},{8,9},{9,8},{10,11... | collective-permute-start | bytes 1572872 | tf_op jit(solution)/shard_map/ppermute | solution.py:516
  44.6 16.3 %collective-permute-start.12 = (bf16[256,512]{1,0:T(8,128)(2,1)S(1)}, bf16[256,512]{1,0:T(8,128)(2,1)S(1)}, u32[]{:S(2)}, u32[]{:S(2)}) collective-permute-start(bf16[256,512]{1,0:T(8,128)(2,1)S(1)} %dynamic-slice_convert_fusion), channel_id=1, source_target_pairs={{0,1},{1,0},{2,3},{3,2},{4,5},{5,4},{6,7},{7,6},{8,9},{9,8},{10,11... | collective-permute-start | bytes 786440 | tf_op jit(solution)/shard_map/ppermute | solution.py:516
  58.0 3.7 %collective-permute-start.8 = (bf16[256,512]{1,0:T(8,128)(2,1)S(1)}, bf16[256,512]{1,0:T(8,128)(2,1)S(1)}, u32[]{:S(2)}, u32[]{:S(2)}) collective-permute-start(bf16[256,512]{1,0:T(8,128)(2,1)S(1)} %fusion), channel_id=1, source_target_pairs={{0,2},{2,0},{8,10},{10,8},{16,18},{18,16},{24,26},{26,24},{1,3},{3... | collective-permute-start | bytes 786440 | tf_op jit(solution)/shard_map/ppermute | solution.py:483
  61.0 1.5 %collective-permute-start.13 = (bf16[128,512]{1,0:T(8,128)(2,1)S(1)}, bf16[128,512]{1,0:T(8,128)(2,1)S(1)}, u32[]{:S(2)}, u32[]{:S(2)}) collective-permute-start(bf16[128,512]{1,0:T(8,128)(2,1)S(1)} %fusion.6), channel_id=1, source_target_pairs={{0,16},{2,18},{8,24},{10,26},{16,0},{18,2},{24,8},{26,10},{1,17},{... | collective-permute-start | bytes 393224 | tf_op jit(solution)/shard_map/ppermute | solution.py:483
  61.8 2.0 %collective-permute-start.9 = (bf16[128,512]{1,0:T(8,128)(2,1)S(1)}, bf16[128,512]{1,0:T(8,128)(2,1)S(1)}, u32[]{:S(2)}, u32[]{:S(2)}) collective-permute-start(bf16[128,512]{1,0:T(8,128)(2,1)S(1)} %fusion.5), channel_id=1, source_target_pairs={{0,16},{2,18},{8,24},{10,26},{16,0},{18,2},{24,8},{26,10},{1,17},{... | collective-permute-start | bytes 393224 | tf_op jit(solution)/shard_map/ppermute | solution.py:483
  62.5 29.4 %collective-permute-start.14 = (bf16[128,512]{1,0:T(8,128)(2,1)S(1)}, bf16[128,512]{1,0:T(8,128)(2,1)S(1)}, u32[]{:S(2)}, u32[]{:S(2)}) collective-permute-start(bf16[128,512]{1,0:T(8,128)(2,1)S(1)} %fusion.8), channel_id=1, source_target_pairs={{0,4},{2,6},{8,12},{10,14},{16,20},{18,22},{24,28},{26,30},{1,5},{... | collective-permute-start | bytes 393224 | tf_op jit(solution)/shard_map/ppermute | solution.py:483
  63.9 30.1 %collective-permute-start.10 = (bf16[128,512]{1,0:T(8,128)(2,1)S(1)}, bf16[128,512]{1,0:T(8,128)(2,1)S(1)}, u32[]{:S(2)}, u32[]{:S(2)}) collective-permute-start(bf16[128,512]{1,0:T(8,128)(2,1)S(1)} %fusion.7), channel_id=1, source_target_pairs={{0,4},{2,6},{8,12},{10,14},{16,20},{18,22},{24,28},{26,30},{1,5},{... | collective-permute-start | bytes 393224 | tf_op jit(solution)/shard_map/ppermute | solution.py:483

commit v3 on v2

--- a/solution.py
+++ b/solution.py
@@ -186,6 +186,25 @@
     return (grad_in_part[None], grad_out_part[None])
 
 
+VMEM = pl.BlockSpec(memory_space=pltpu.VMEM)
+SMEM = pl.BlockSpec(memory_space=pltpu.SMEM)
+HBM = pl.BlockSpec(memory_space=pltpu.HBM)
+
+
+class Place:
+    def __init__(self, bounds):
+        pipe = lax.axis_index("pipe")
+        section = lax.axis_index("section")
+        self.column = lax.axis_index("tensor")
+        self.relay = pipe // 2
+        self.core = pipe % 2
+        self.half = section % 2
+        self.left = section < 2
+        self.short = (bounds[self.relay, 1] - bounds[self.relay, 0]) == 2
+        self.slot = jnp.where(self.short, 1, 0)
+        self.upper_slot = jnp.where(self.left, 1, 0)
+
+
 def norm_rows(saved):
     floats = saved.astype(jnp.float32)
     row_scale = jnp.sqrt(jnp.mean(floats * floats, axis=-1, keepdims=True) + EPS)
@@ -200,8 +219,11 @@
     return lax.dot_general(left, right, (((0,), (0,)), ((), ())), preferred_element_type=jnp.float32)
 
 
-def chain_kernel(pick, top_ref, saved_ref, w_in_ref, w_out_ref, grad_ref, q_buf, p_buf, err, pulled, sems):
-    slot = pick[6]
+def chain_kernel(
+    bounds, top_ref, saved_ref, w_in_ref, w_out_ref, grad_ref, top, saved, q_buf, p_buf, err, pulled, sems
+):
+    place = Place(bounds)
+    slot = place.upper_slot
     chunks = q_buf.shape[0]
     step = q_buf.shape[1]
     width = p_buf.shape[1]
@@ -212,15 +234,21 @@
     def p_copy(j):
         return pltpu.make_async_copy(w_in_ref.at[slot, pl.ds(j * width, width)], p_buf.at[j], sems.at[chunks + j])
 
+    top_copy = pltpu.make_async_copy(top_ref.at[place.half], top, sems.at[2 * chunks])
+    saved_copy = pltpu.make_async_copy(saved_ref.at[slot], saved, sems.at[2 * chunks + 1])
+    top_copy.start()
     for j in range(chunks):
         q_copy(j).start()
+    saved_copy.start()
     for j in range(chunks):
         p_copy(j).start()
-    grad_next = top_ref[0]
+    top_copy.wait()
+    grad_next = top[...]
     for j in range(chunks):
         q_copy(j).wait()
         err[:, j * step : (j + 1) * step] = nt_dot(grad_next, q_buf[j]).astype(jnp.bfloat16)
-    unit, row_scale = norm_rows(saved_ref[0])
+    saved_copy.wait()
+    unit, row_scale = norm_rows(saved[...])
     for j in range(chunks):
         p_copy(j).wait()
         pulled[:, j * width : (j + 1) * width] = nt_dot(err[...], p_buf[j])
@@ -229,44 +257,39 @@
     grad_ref[...] = (grad_next.astype(jnp.float32) + (back - unit * inner_mean) / row_scale).astype(jnp.bfloat16)
 
 
-def chain(pick, tops, saved, w_in, w_out):
+def chain(bounds, tops, saved, w_in, w_out):
     rows, model = saved.shape[1:]
     inner = w_in.shape[2]
     chunks = 4
     return pl.pallas_call(
         chain_kernel,
         out_shape=jax.ShapeDtypeStruct((rows, model), jnp.bfloat16),
-        grid_spec=pltpu.PrefetchScalarGridSpec(
-            num_scalar_prefetch=1,
-            grid=(1,),
-            in_specs=[
-                pl.BlockSpec((1, rows, model), lambda i, pick: (pick[3], 0, 0)),
-                pl.BlockSpec((1, rows, model), lambda i, pick: (pick[6], 0, 0)),
-                pl.BlockSpec(memory_space=pltpu.HBM),
-                pl.BlockSpec(memory_space=pltpu.HBM),
-            ],
-            out_specs=pl.BlockSpec((rows, model), lambda i, pick: (0, 0)),
-            scratch_shapes=[
-                pltpu.VMEM((chunks, inner // chunks, model), jnp.bfloat16),
-                pltpu.VMEM((chunks, model // chunks, inner), jnp.bfloat16),
-                pltpu.VMEM((rows, inner), jnp.bfloat16),
-                pltpu.VMEM((rows, model), jnp.float32),
-                pltpu.SemaphoreType.DMA((2 * chunks,)),
-            ],
-        ),
+        in_specs=[SMEM] + [HBM] * 4,
+        out_specs=VMEM,
+        scratch_shapes=[
+            pltpu.VMEM((rows, model), jnp.bfloat16),
+            pltpu.VMEM((rows, model), jnp.bfloat16),
+            pltpu.VMEM((chunks, inner // chunks, model), jnp.bfloat16),
+            pltpu.VMEM((chunks, model // chunks, inner), jnp.bfloat16),
+            pltpu.VMEM((rows, inner), jnp.bfloat16),
+            pltpu.VMEM((rows, model), jnp.float32),
+            pltpu.SemaphoreType.DMA((2 * chunks + 2,)),
+        ],
+        compiler_params=pltpu.CompilerParams(vmem_limit_bytes=60 * 2**20),
         cost_estimate=pl.CostEstimate(
             flops=4 * rows * model * inner, bytes_accessed=4 * model * inner, transcendentals=0
         ),
         name="chain",
-    )(pick, tops, saved, w_in, w_out)
+    )(bounds, tops, saved, w_in, w_out)
 
 
 def early_kernel(
-    pick, e1, e2, e3, f1, f2, f3, w_in_ref, w_out_ref,
+    bounds, e1, e2, e3, f1, f2, f3, w_in_ref, w_out_ref,
     in_acc, out_acc, q_buf, p_buf, early_part,
     unit, unit_part, grads, err, value, sems,
 ):
-    slot, short, core = pick[0], pick[1], pick[2]
+    place = Place(bounds)
+    slot, short, core = place.slot, place.short, place.core
     rows = e1.shape[0]
     part = p_buf.shape[1]
     blocks = 4
@@ -295,11 +318,11 @@
         unit[:rows, :] = norm_rows(first[...])[0].astype(jnp.bfloat16)
         unit[rows:, :] = norm_rows(second[...])[0].astype(jnp.bfloat16)
 
-    @pl.when(short == 0)
+    @pl.when(jnp.logical_not(short))
     def _():
         put_unit(e2, f2)
 
-    @pl.when(short != 0)
+    @pl.when(short)
     def _():
         put_unit(e1, f1)
 
@@ -314,7 +337,7 @@
     value[...] = jnp.dot(unit[...], p_buf[...], preferred_element_type=jnp.float32).astype(jnp.bfloat16)
     out_acc[...] = tn_dot(value[...], grads[...])
 
-    @pl.when(short == 0)
+    @pl.when(jnp.logical_not(short))
     def _():
         put_unit(e1, f1)
         gather_lanes(early_part, 0)
@@ -322,7 +345,7 @@
             unit[...], p_buf[...], preferred_element_type=jnp.float32
         ).astype(jnp.bfloat16)
 
-    @pl.when(short != 0)
+    @pl.when(short)
     def _():
         grads[:rows, :] = e2[...]
         grads[rows:, :] = f2[...]
@@ -330,17 +353,18 @@
 
 
 def late_kernel(
-    pick, late, flate, e2, f2, early_part, q_buf, p_buf, in_acc, out_acc,
+    bounds, late, flate, e2, f2, early_part, q_buf, p_buf, in_acc, out_acc,
     in_send, in_keep, out_send, out_keep,
     unit, unit_part, value, grads, err,
 ):
-    short, core, half, column = pick[1], pick[2], pick[3], pick[4]
+    place = Place(bounds)
+    short, core, half, column = place.short, place.core, place.half, place.column
     rows = late.shape[0]
     part = p_buf.shape[1]
     blocks = 4
     lanes = part // blocks
 
-    @pl.when(short == 0)
+    @pl.when(jnp.logical_not(short))
     def _():
         grads[:rows, :] = late[...]
         grads[rows:, :] = flate[...]
@@ -348,7 +372,7 @@
         unit_part[...] = early_part[:, :part]
         value[...] = early_part[:, part:]
 
-    @pl.when(short != 0)
+    @pl.when(short)
     def _():
         unit[:rows, :] = norm_rows(late[...])[0].astype(jnp.bfloat16)
         unit[rows:, :] = norm_rows(flate[...])[0].astype(jnp.bfloat16)
@@ -372,23 +396,19 @@
     out_keep[...] = out_acc[upper, :] + tn_dot(value[:, upper], grads[...])
 
 
-VMEM = pl.BlockSpec(memory_space=pltpu.VMEM)
-SMEM = pl.BlockSpec(memory_space=pltpu.SMEM)
-HBM = pl.BlockSpec(memory_space=pltpu.HBM)
-
-
-def staged_kernel(pick, saved_ref, tops_ref, own_saved, own_top, given, sems):
-    slot, half, give_top = pick[0], pick[3], pick[5]
+def staged_kernel(bounds, saved_ref, tops_ref, own_saved, own_top, given, sems):
+    place = Place(bounds)
+    give_top = place.left & jnp.logical_not(place.short)
     copies = (
-        pltpu.make_async_copy(saved_ref.at[slot], own_saved, sems.at[1]),
-        pltpu.make_async_copy(tops_ref.at[half], own_top, sems.at[2]),
-    )
-
-    @pl.when(give_top != 0)
-    def _():
-        pltpu.make_async_copy(tops_ref.at[half], given, sems.at[0]).start()
-
-    @pl.when(give_top == 0)
+        pltpu.make_async_copy(saved_ref.at[place.slot], own_saved, sems.at[1]),
+        pltpu.make_async_copy(tops_ref.at[place.half], own_top, sems.at[2]),
+    )
+
+    @pl.when(give_top)
+    def _():
+        pltpu.make_async_copy(tops_ref.at[place.half], given, sems.at[0]).start()
+
+    @pl.when(jnp.logical_not(give_top))
     def _():
         pltpu.make_async_copy(saved_ref.at[0], given, sems.at[0]).start()
 
@@ -399,7 +419,7 @@
         copy.wait()
 
 
-def staged(pick, saved, tops):
+def staged(bounds, saved, tops):
     block = jax.ShapeDtypeStruct(saved.shape[1:], saved.dtype)
     return pl.pallas_call(
         staged_kernel,
@@ -407,12 +427,12 @@
         in_specs=[SMEM, HBM, HBM],
         out_specs=(VMEM,) * 3,
         scratch_shapes=[pltpu.SemaphoreType.DMA((3,))],
-        compiler_params=pltpu.CompilerParams(vmem_limit_bytes=4 * 2**20),
+        compiler_params=pltpu.CompilerParams(vmem_limit_bytes=60 * 2**20),
         name="staged",
-    )(pick, saved, tops)
-
-
-def early_partials(pick, own, partner, w_in, w_out):
+    )(bounds, saved, tops)
+
+
+def early_partials(bounds, own, partner, w_in, w_out):
     rows, model = own[0].shape
     inner = w_in.shape[2]
     part = model // 2
@@ -435,15 +455,15 @@
             pltpu.VMEM((2 * rows, part), jnp.bfloat16),
             pltpu.SemaphoreType.DMA((5,)),
         ],
-        compiler_params=pltpu.CompilerParams(vmem_limit_bytes=24 * 2**20),
+        compiler_params=pltpu.CompilerParams(vmem_limit_bytes=43 * 2**20),
         cost_estimate=pl.CostEstimate(
             flops=10 * rows * model * inner, bytes_accessed=3 * model * inner, transcendentals=0
         ),
         name="early",
-    )(pick, *own, *partner, w_in, w_out)
-
-
-def late_partials(pick, late, other_late, own_top, other_top, early):
+    )(bounds, *own, *partner, w_in, w_out)
+
+
+def late_partials(bounds, late, other_late, own_top, other_top, early):
     in_acc, out_acc, q_buf, p_buf, early_part = early
     rows, model = late.shape
     inner = q_buf.shape[0]
@@ -470,17 +490,11 @@
             flops=8 * rows * model * inner, bytes_accessed=3 * model * inner, transcendentals=0
         ),
         name="late",
-    )(pick, late, other_late, own_top, other_top, early_part, q_buf, p_buf, in_acc, out_acc)
-
-
-def moved(value, route):
-    sections = lax.axis_size("section")
-    pairs = []
-    for source in range(lax.axis_size("pipe") * sections):
-        target = route(source // sections, source % sections)
-        if target is not None:
-            pairs.append((source, target[0] * sections + target[1]))
-    return lax.ppermute(value, ("pipe", "section"), pairs)
+    )(bounds, late, other_late, own_top, other_top, early_part, q_buf, p_buf, in_acc, out_acc)
+
+
+def flipped(value, axis, bit):
+    return lax.ppermute(value, axis, [(i, i ^ bit) for i in range(lax.axis_size(axis))])
 
 
 def two_section_body(bounds, saved_inputs, w_in, w_out, top_grad):
@@ -488,7 +502,6 @@
     section_index = lax.axis_index("section")
     column = lax.axis_index("tensor")
     relay = pipe_index // 2
-    core = pipe_index % 2
     half = section_index % 2
     left = section_index // 2 == 0
     boundary = lax.dynamic_index_in_dim(bounds, relay, 0, keepdims=False)
@@ -501,34 +514,30 @@
     inner = proj_in.shape[2]
 
     def across(value):
-        return moved(value, lambda p, s: (p ^ 2, s))
-
-    def across_left(value):
-        return moved(value, lambda p, s: (p ^ 2, s) if s < 2 else None)
+        return flipped(value, "pipe", 2)
 
     def core_swap(value):
-        return moved(value, lambda p, s: (p ^ 1, s) if s < 2 else None)
+        return flipped(value, "pipe", 1)
 
     def half_swap(value):
-        return moved(value, lambda p, s: (p, s ^ 1) if s < 2 else None)
+        return flipped(value, "section", 1)
 
     def column_swap(value):
-        return lax.ppermute(value, "tensor", [(0, 1), (1, 0)])
-
-    give_top = left & jnp.logical_not(short)
-    pick = jnp.stack(
-        [part.astype(jnp.int32) for part in (short, short, core, half, column, give_top, left)]
-    )
-    own_saved, own_top, given = staged(pick, saved, tops)
+        return flipped(value, "tensor", 1)
+
+    def section_swap(value):
+        return flipped(value, "section", 2)
+
+    own_saved, own_top, given = staged(bounds, saved, tops)
     swapped = across(given)
-    grad_low = chain(pick, tops, saved, proj_in, proj_out)
-    late = moved(jnp.where(short, swapped, grad_low), lambda p, s: (p, s - 2) if s >= 2 else None)
-    grad_other = across_left(grad_low)
+    grad_low = chain(bounds, tops, saved, proj_in, proj_out)
+    late = section_swap(jnp.where(short, swapped, grad_low))
+    grad_other = across(grad_low)
     own = (own_saved, swapped, jnp.where(short, own_top, grad_other))
     partner = tuple(core_swap(part) for part in own)
-    early = early_partials(pick, own, partner, proj_in, proj_out)
+    early = early_partials(bounds, own, partner, proj_in, proj_out)
     other_late = core_swap(late)
-    in_send, in_keep, out_send, out_keep = late_partials(pick, late, other_late, own[1], partner[1], early)
+    in_send, in_keep, out_send, out_keep = late_partials(bounds, late, other_late, own[1], partner[1], early)
     in_landed = column_swap(in_send)
     out_landed = half_swap(out_send)
     in_sum = (in_keep + in_landed.astype(jnp.float32)).reshape(2, -1, inner // 2)
@@ -544,11 +553,8 @@
         total = (mine + landed.astype(jnp.float32)).reshape(2, -1, mine.shape[1])
         own = lax.dynamic_index_in_dim(total, relay, 0, keepdims=False)
         sent = lax.dynamic_index_in_dim(total, 1 - relay, 0, keepdims=False).astype(jnp.bfloat16)
-        got = across_left(sent)
-        onward = moved(
-            jnp.where(short, got, own.astype(jnp.bfloat16)),
-            lambda p, s: (p, s + 2) if s < 2 else None,
-        )
+        got = across(sent)
+        onward = section_swap(jnp.where(short, got, own.astype(jnp.bfloat16)))
         lower = jnp.where(short, own, got.astype(jnp.float32))
         results.append(jnp.where(left, lower, onward.astype(jnp.float32))[None])
     return tuple(results)

time: 95.5 us -> 82 us (0.86)
  the two profiles are of different devices: /device:TPU:24 before, /device:TPU:0 now
where the time goes in v3:
time: 82 us; the launch traced here: 81.7 us
  waiting for transfers between devices  40.8 us (50%)
  starting transfers between devices  17 us (21%)
  Pallas kernels  16 us (20%)
  other arithmetic  5.08 us (6%)
  between operations  2.04 us (2%)
    ppermute x15, waiting for transfers between devices, flipped(): lax.ppermute(value, axis, [(i, i ^ bit) for i in range(lax.axis_size(axis...  40.8 us
    ppermute x15, starting transfers between devices, flipped(): lax.ppermute(value, axis, [(i, i ^ bit) for i in range(lax.axis_size(axis...  17 us
    pallas_call x1, Pallas kernels, chain(): pl.pallas_call(chain_kernel, out_shape=jax.ShapeDtypeStruct((rows, model)...  6.45 us
    pallas_call x1, Pallas kernels, early_partials(): pl.pallas_call(early_kernel, out_shape=(jax.ShapeDtypeStruct((part, inner...  4.79 us
    pallas_call x1, Pallas kernels, staged(): pl.pallas_call(staged_kernel, out_shape=(block,) * 3, in_specs=[SMEM, HBM...  2.71 us
    pallas_call x1, Pallas kernels, late_partials(): pl.pallas_call(late_kernel, out_shape=(jax.ShapeDtypeStruct((part, inner...  2.07 us
  transfers between devices with their start and end apart: 15, of which 8 were waited for; matrix products, arithmetic and copies ran while one was open for 6% of the time, Pallas kernels for 14%

profile of v3, /device:TPU:0, one launch (start us, length us, event | category | flops | bytes accessed | tf_op | source)
XLA Modules:
  0.0 81.7 jit_solution(3656684810884848711)
XLA Ops:
  0.6 2.7 %staged.1 = (bf16[128,1024]{1,0:T(8,128)(2,1)}, bf16[128,1024]{1,0:T(8,128)(2,1)}, bf16[128,1024]{1,0:T(8,128)(2,1)}) custom-call(s32[2,3]{1,0:T(2,128)} %bounds.7, bf16[2,128,1024]{2,1,0:T(8,128)(2,1)} %bitcast.44, bf16[2,128,1024]{2,1,0:T(8,128)(2,1)} %bitcast.46), custom_call_target="tpu_custom_call" | custom-call | tf_op jit(solution)/shard_map/staged/pallas_call | solution.py:424
  3.3 3.1 %collective-permute-start = (bf16[128,1024]{1,0:T(8,128)(2,1)}, bf16[128,1024]{1,0:T(8,128)(2,1)S(1)}, u32[]{:S(2)}, u32[]{:S(2)}) collective-permute-start(bf16[128,1024]{1,0:T(8,128)(2,1)} %get-tuple-element.14), channel_id=1, source_target_pairs={{0,16},{8,24},{16,0},{24,8},{1,17},{9,25},{17,1},{25,9},{2,18},{10... | collective-permute-start | bytes 786440 | tf_op jit(solution)/shard_map/ppermute | solution.py:497
  6.4 0.0 copy-start
  6.4 0.0 copy-start.1
  6.4 0.0 copy-start.2
  6.4 6.4 %chain.1 = bf16[128,1024]{1,0:T(8,128)(2,1)} custom-call(s32[2,3]{1,0:T(2,128)} %bounds.7, bf16[2,128,1024]{2,1,0:T(8,128)(2,1)} %bitcast.47, bf16[2,128,1024]{2,1,0:T(8,128)(2,1)} %bitcast.45, bf16[2,1024,1024]{2,1,0:T(8,128)(2,1)} %bitcast.38, bf16[2,1024,1024]{2,1,0:T(8,128)(2,1)} %bitcast.40), custom_call_target="tpu_custom_call" | custom-call | flops 536870912 | bytes 4194304 | tf_op jit(solution)/shard_map/chain/pallas_call | solution.py:264
  12.9 0.1 collective-permute-start.4
  13.0 0.0 copy-done
  13.0 0.0 collective-permute-start.5
  13.1 0.0 copy-done.1
  13.1 0.6 fusion.9
  14.9 0.0 collective-permute-done.e2
  14.9 1.0 %broadcast_select_fusion.1 = bf16[128,1024]{1,0:T(8,128)(2,1)S(1)} fusion(bf16[128,1024]{1,0:T(8,128)(2,1)S(1)} %collective-permute-done.e2, bf16[128,1024]{1,0:T(8,128)(2,1)} %chain.1, pred[]{:T(512)} %bitcast), kind=kLoop, calls=%fused_computation.18 | loop fusion | flops 131072 | bytes 786433 | tf_op jit(solution)/shard_map/jit(_where)/select_n | solution.py:534
  15.9 3.0 %collective-permute-start.1 = (bf16[128,1024]{1,0:T(8,128)(2,1)S(1)}, bf16[128,1024]{1,0:T(8,128)(2,1)S(1)}, u32[]{:S(2)}, u32[]{:S(2)}) collective-permute-start(bf16[128,1024]{1,0:T(8,128)(2,1)S(1)} %broadcast_select_fusion.1), channel_id=1, source_target_pairs={{0,4},{2,6},{4,0},{6,2},{1,5},{3,7},{5,1},{7,3},{8,12},{10,14},{12... | collective-permute-start | bytes 786440 | tf_op jit(solution)/shard_map/ppermute | solution.py:497
  18.9 2.0 %collective-permute-done.4 = bf16[128,1024]{1,0:T(8,128)(2,1)S(1)} collective-permute-done((bf16[128,1024]{1,0:T(8,128)(2,1)}, bf16[128,1024]{1,0:T(8,128)(2,1)S(1)}, u32[]{:S(2)}, u32[]{:S(2)}) %collective-permute-start.4) | collective-permute-done | bytes 262176 | tf_op jit(solution)/shard_map/ppermute | solution.py:497
  20.9 0.0 copy-done.2
  20.9 0.1 collective-permute-start.6
  21.0 0.5 collective-permute-start.3
  21.5 10.0 %collective-permute-done.1.late = bf16[128,1024]{1,0:T(8,128)(2,1)S(1)} collective-permute-done((bf16[128,1024]{1,0:T(8,128)(2,1)S(1)}, bf16[128,1024]{1,0:T(8,128)(2,1)S(1)}, u32[]{:S(2)}, u32[]{:S(2)}) %collective-permute-start.1) | collective-permute-done | bytes 262176 | tf_op jit(solution)/shard_map/ppermute | solution.py:497
  31.5 0.0 collective-permute-start.2
  31.5 0.0 collective-permute-done.5.f1
  31.5 0.0 collective-permute-done.6.f3
  31.5 0.0 collective-permute-done.3.f2
  31.5 4.8 %early.1 = (f32[512,1024]{1,0:T(8,128)S(1)}, f32[512,1024]{1,0:T(8,128)S(1)}, bf16[1024,1024]{1,0:T(8,128)(2,1)S(1)}, bf16[1024,512]{1,0:T(8,128)(2,1)S(1)}, bf16[256,1024]{1,0:T(8,128)(2,1)S(1)}) custom-call(s32[2,3]{1,0:T(2,128)S(1)} %copy-done.1, bf16[128,1024]{1,0:T(8,128)(2,1)S(1)} %copy-done, bf16[128,1024]{1,0:T(8,128)(2,1)S(1)} %collective-permute-done.e2, ...), custom_call_target="tpu_custom_call" | custom-call | flops 1342177280 | bytes 3145728 | tf_op jit(solution)/shard_map/early/pallas_call | solution.py:439
  36.3 0.0 collective-permute-done.2.flate
  36.3 2.1 %late.1 = (bf16[512,512]{1,0:T(8,128)(2,1)S(1)}, f32[512,512]{1,0:T(8,128)S(1)}, bf16[256,1024]{1,0:T(8,128)(2,1)S(1)}, f32[256,1024]{1,0:T(8,128)S(1)}) custom-call(s32[2,3]{1,0:T(2,128)S(1)} %copy-done.1, bf16[128,1024]{1,0:T(8,128)(2,1)S(1)} %collective-permute-done.1.late, bf16[128,1024]{1,0:T(8,128)(2,1)S(1)} %collective-permute-done.2.flate, ...), custom_call_target="tpu_custom_call" | custom-call | flops 1073741824 | bytes 3145728 | tf_op jit(solution)/shard_map/late/pallas_call | solution.py:471
  38.4 0.9 %collective-permute-start.11 = (bf16[256,1024]{1,0:T(8,128)(2,1)S(1)}, bf16[256,1024]{1,0:T(8,128)(2,1)}, u32[]{:S(2)}, u32[]{:S(2)}) collective-permute-start(bf16[256,1024]{1,0:T(8,128)(2,1)S(1)} %get-tuple-element.25), channel_id=1, source_target_pairs={{0,2},{2,0},{4,6},{6,4},{1,3},{3,1},{5,7},{7,5},{8,10},{10,8},{12,... | collective-permute-start | bytes 1572872 | tf_op jit(solution)/shard_map/ppermute | solution.py:497
  39.3 1.5 %collective-permute-start.7 = (bf16[512,512]{1,0:T(8,128)(2,1)S(1)}, bf16[512,512]{1,0:T(8,128)(2,1)}, u32[]{:S(2)}, u32[]{:S(2)}) collective-permute-start(bf16[512,512]{1,0:T(8,128)(2,1)S(1)} %get-tuple-element.23), channel_id=1, source_target_pairs={{0,1},{1,0},{2,3},{3,2},{4,5},{5,4},{6,7},{7,6},{8,9},{9,8},{10,11... | collective-permute-start | bytes 1572872 | tf_op jit(solution)/shard_map/ppermute | solution.py:497
  40.8 12.2 %collective-permute-done.11 = bf16[256,1024]{1,0:T(8,128)(2,1)} collective-permute-done((bf16[256,1024]{1,0:T(8,128)(2,1)S(1)}, bf16[256,1024]{1,0:T(8,128)(2,1)}, u32[]{:S(2)}, u32[]{:S(2)}) %collective-permute-start.11) | collective-permute-done | bytes 524320 | tf_op jit(solution)/shard_map/ppermute | solution.py:497
  52.9 1.2 %convert_add_fusion = f32[256,1024]{1,0:T(8,128)S(1)} fusion(f32[256,1024]{1,0:T(8,128)S(1)} %get-tuple-element.24, bf16[256,1024]{1,0:T(8,128)(2,1)} %collective-permute-done.11), kind=kLoop, calls=%fused_computation | loop fusion | flops 524288 | bytes 2621440 | tf_op jit(solution)/shard_map/add | solution.py:544
  54.2 1.6 %collective-permute-start.12 = (bf16[256,512]{1,0:T(8,128)(2,1)S(1)}, bf16[256,512]{1,0:T(8,128)(2,1)S(1)}, u32[]{:S(2)}, u32[]{:S(2)}) collective-permute-start(bf16[256,512]{1,0:T(8,128)(2,1)S(1)} %dynamic-slice_convert_fusion), channel_id=1, source_target_pairs={{0,1},{1,0},{2,3},{3,2},{4,5},{5,4},{6,7},{7,6},{8,9},{9,8},{10,11... | collective-permute-start | bytes 786440 | tf_op jit(solution)/shard_map/ppermute | solution.py:497
  55.8 0.0 collective-permute-done.7
  55.8 1.2 %convert_add_fusion.1 = f32[512,512]{1,0:T(8,128)S(1)} fusion(f32[512,512]{1,0:T(8,128)S(1)} %get-tuple-element.22, bf16[512,512]{1,0:T(8,128)(2,1)} %collective-permute-done.7), kind=kLoop, calls=%fused_computation.1 | loop fusion | flops 524288 | bytes 2621440 | tf_op jit(solution)/shard_map/add | solution.py:543
  57.0 0.8 collective-permute-start.8
  57.8 4.3 %collective-permute-done.12 = bf16[256,512]{1,0:T(8,128)(2,1)S(1)} collective-permute-done((bf16[256,512]{1,0:T(8,128)(2,1)S(1)}, bf16[256,512]{1,0:T(8,128)(2,1)S(1)}, u32[]{:S(2)}, u32[]{:S(2)}) %collective-permute-start.12) | collective-permute-done | bytes 262176 | tf_op jit(solution)/shard_map/ppermute | solution.py:497
  62.1 0.1 convert_add_fusion.2
  62.2 0.7 collective-permute-start.13
  62.9 1.7 %collective-permute-done.8 = bf16[256,512]{1,0:T(8,128)(2,1)S(1)} collective-permute-done((bf16[256,512]{1,0:T(8,128)(2,1)S(1)}, bf16[256,512]{1,0:T(8,128)(2,1)S(1)}, u32[]{:S(2)}, u32[]{:S(2)}) %collective-permute-start.8) | collective-permute-done | bytes 262176 | tf_op jit(solution)/shard_map/ppermute | solution.py:497
  64.7 0.1 bitcast_add_fusion
  64.8 0.7 collective-permute-start.9
  65.4 3.1 %collective-permute-done.13 = bf16[128,512]{1,0:T(8,128)(2,1)S(1)} collective-permute-done((bf16[128,512]{1,0:T(8,128)(2,1)S(1)}, bf16[128,512]{1,0:T(8,128)(2,1)S(1)}, u32[]{:S(2)}, u32[]{:S(2)}) %collective-permute-start.13) | collective-permute-done | bytes 131104 | tf_op jit(solution)/shard_map/ppermute | solution.py:497
  68.6 2.5 %collective-permute-start.14 = (bf16[128,512]{1,0:T(8,128)(2,1)S(1)}, bf16[128,512]{1,0:T(8,128)(2,1)S(1)}, u32[]{:S(2)}, u32[]{:S(2)}) collective-permute-start(bf16[128,512]{1,0:T(8,128)(2,1)S(1)} %fusion.8), channel_id=1, source_target_pairs={{0,4},{2,6},{4,0},{6,2},{1,5},{3,7},{5,1},{7,3},{8,12},{10,14},{12... | collective-permute-start | bytes 393224 | tf_op jit(solution)/shard_map/ppermute | solution.py:497
  71.0 0.0 collective-permute-done.9
  71.0 1.7 %collective-permute-start.10 = (bf16[128,512]{1,0:T(8,128)(2,1)S(1)}, bf16[128,512]{1,0:T(8,128)(2,1)S(1)}, u32[]{:S(2)}, u32[]{:S(2)}) collective-permute-start(bf16[128,512]{1,0:T(8,128)(2,1)S(1)} %fusion.7), channel_id=1, source_target_pairs={{0,4},{2,6},{4,0},{6,2},{1,5},{3,7},{5,1},{7,3},{8,12},{10,14},{12... | collective-permute-start | bytes 393224 | tf_op jit(solution)/shard_map/ppermute | solution.py:497
  72.7 6.9 %collective-permute-done.14 = bf16[128,512]{1,0:T(8,128)(2,1)S(1)} collective-permute-done((bf16[128,512]{1,0:T(8,128)(2,1)S(1)}, bf16[128,512]{1,0:T(8,128)(2,1)S(1)}, u32[]{:S(2)}, u32[]{:S(2)}) %collective-permute-start.14) | collective-permute-done | bytes 131104 | tf_op jit(solution)/shard_map/ppermute | solution.py:497
  79.6 0.7 fusion.2
  80.3 0.7 collective-permute-done.10
  81.0 0.7 fusion.4
  (8 shorter events, 0.2 us)
Async XLA Ops:
  3.3 11.5 %collective-permute-start = (bf16[128,1024]{1,0:T(8,128)(2,1)}, bf16[128,1024]{1,0:T(8,128)(2,1)S(1)}, u32[]{:S(2)}, u32[]{:S(2)}) collective-permute-start(bf16[128,1024]{1,0:T(8,128)(2,1)} %get-tuple-element.14), channel_id=1, source_target_pairs={{0,16},{8,24},{16,0},{24,8},{1,17},{9,25},{17,1},{25,9},{2,18},{10... | collective-permute-start | bytes 786440 | tf_op jit(solution)/shard_map/ppermute | solution.py:497
  6.4 6.6 %copy-start = (bf16[128,1024]{1,0:T(8,128)(2,1)S(1)}, bf16[128,1024]{1,0:T(8,128)(2,1)}, u32[]{:S(2)}) copy-start(bf16[128,1024]{1,0:T(8,128)(2,1)} %get-tuple-element.15.e1) | copy-start | bytes 786436
  6.4 6.6 %copy-start.1 = (s32[2,3]{1,0:T(2,128)S(1)}, s32[2,3]{1,0:T(2,128)}, u32[]{:S(2)}) copy-start(s32[2,3]{1,0:T(2,128)} %bounds.7) | copy-start | bytes 76
  6.4 14.5 %copy-start.2 = (bf16[128,1024]{1,0:T(8,128)(2,1)S(1)}, bf16[128,1024]{1,0:T(8,128)(2,1)}, u32[]{:S(2)}) copy-start(bf16[128,1024]{1,0:T(8,128)(2,1)} %get-tuple-element.16) | copy-start | bytes 786436
  12.9 8.0 %collective-permute-start.4 = (bf16[128,1024]{1,0:T(8,128)(2,1)}, bf16[128,1024]{1,0:T(8,128)(2,1)S(1)}, u32[]{:S(2)}, u32[]{:S(2)}) collective-permute-start(bf16[128,1024]{1,0:T(8,128)(2,1)} %chain.1), channel_id=1, source_target_pairs={{0,16},{8,24},{16,0},{24,8},{1,17},{9,25},{17,1},{25,9},{2,18},{10... | collective-permute-start | bytes 786440 | tf_op jit(solution)/shard_map/ppermute | solution.py:497
  13.0 18.5 %collective-permute-start.5 = (bf16[128,1024]{1,0:T(8,128)(2,1)S(1)}, bf16[128,1024]{1,0:T(8,128)(2,1)S(1)}, u32[]{:S(2)}, u32[]{:S(2)}) collective-permute-start(bf16[128,1024]{1,0:T(8,128)(2,1)S(1)} %copy-done), channel_id=1, source_target_pairs={{0,8},{8,0},{16,24},{24,16},{1,9},{9,1},{17,25},{25,17},{2,10},{10... | collective-permute-start | bytes 786440 | tf_op jit(solution)/shard_map/ppermute | solution.py:497
  15.9 15.6 %collective-permute-start.1 = (bf16[128,1024]{1,0:T(8,128)(2,1)S(1)}, bf16[128,1024]{1,0:T(8,128)(2,1)S(1)}, u32[]{:S(2)}, u32[]{:S(2)}) collective-permute-start(bf16[128,1024]{1,0:T(8,128)(2,1)S(1)} %broadcast_select_fusion.1), channel_id=1, source_target_pairs={{0,4},{2,6},{4,0},{6,2},{1,5},{3,7},{5,1},{7,3},{8,12},{10,14},{12... | collective-permute-start | bytes 786440 | tf_op jit(solution)/shard_map/ppermute | solution.py:497
  20.9 10.6 %collective-permute-start.6 = (bf16[128,1024]{1,0:T(8,128)(2,1)S(1)}, bf16[128,1024]{1,0:T(8,128)(2,1)S(1)}, u32[]{:S(2)}, u32[]{:S(2)}) collective-permute-start(bf16[128,1024]{1,0:T(8,128)(2,1)S(1)} %broadcast_select_fusion.e3), channel_id=1, source_target_pairs={{0,8},{8,0},{16,24},{24,16},{1,9},{9,1},{17,25},{25,17},{2,10},{10... | collective-permute-start | bytes 786440 | tf_op jit(solution)/shard_map/ppermute | solution.py:497
  21.0 10.5 %collective-permute-start.3 = (bf16[128,1024]{1,0:T(8,128)(2,1)S(1)}, bf16[128,1024]{1,0:T(8,128)(2,1)S(1)}, u32[]{:S(2)}, u32[]{:S(2)}) collective-permute-start(bf16[128,1024]{1,0:T(8,128)(2,1)S(1)} %collective-permute-done.e2), channel_id=1, source_target_pairs={{0,8},{8,0},{16,24},{24,16},{1,9},{9,1},{17,25},{25,17},{2,10},{10... | collective-permute-start | bytes 786440 | tf_op jit(solution)/shard_map/ppermute | solution.py:497
  31.5 4.8 %collective-permute-start.2 = (bf16[128,1024]{1,0:T(8,128)(2,1)S(1)}, bf16[128,1024]{1,0:T(8,128)(2,1)S(1)}, u32[]{:S(2)}, u32[]{:S(2)}) collective-permute-start(bf16[128,1024]{1,0:T(8,128)(2,1)S(1)} %collective-permute-done.1.late), channel_id=1, source_target_pairs={{0,8},{8,0},{16,24},{24,16},{1,9},{9,1},{17,25},{25,17},{2,10},{10... | collective-permute-start | bytes 786440 | tf_op jit(solution)/shard_map/ppermute | solution.py:497
  38.4 14.5 %collective-permute-start.11 = (bf16[256,1024]{1,0:T(8,128)(2,1)S(1)}, bf16[256,1024]{1,0:T(8,128)(2,1)}, u32[]{:S(2)}, u32[]{:S(2)}) collective-permute-start(bf16[256,1024]{1,0:T(8,128)(2,1)S(1)} %get-tuple-element.25), channel_id=1, source_target_pairs={{0,2},{2,0},{4,6},{6,4},{1,3},{3,1},{5,7},{7,5},{8,10},{10,8},{12,... | collective-permute-start | bytes 1572872 | tf_op jit(solution)/shard_map/ppermute | solution.py:497
  39.3 16.5 %collective-permute-start.7 = (bf16[512,512]{1,0:T(8,128)(2,1)S(1)}, bf16[512,512]{1,0:T(8,128)(2,1)}, u32[]{:S(2)}, u32[]{:S(2)}) collective-permute-start(bf16[512,512]{1,0:T(8,128)(2,1)S(1)} %get-tuple-element.23), channel_id=1, source_target_pairs={{0,1},{1,0},{2,3},{3,2},{4,5},{5,4},{6,7},{7,6},{8,9},{9,8},{10,11... | collective-permute-start | bytes 1572872 | tf_op jit(solution)/shard_map/ppermute | solution.py:497
  54.2 7.9 %collective-permute-start.12 = (bf16[256,512]{1,0:T(8,128)(2,1)S(1)}, bf16[256,512]{1,0:T(8,128)(2,1)S(1)}, u32[]{:S(2)}, u32[]{:S(2)}) collective-permute-start(bf16[256,512]{1,0:T(8,128)(2,1)S(1)} %dynamic-slice_convert_fusion), channel_id=1, source_target_pairs={{0,1},{1,0},{2,3},{3,2},{4,5},{5,4},{6,7},{7,6},{8,9},{9,8},{10,11... | collective-permute-start | bytes 786440 | tf_op jit(solution)/shard_map/ppermute | solution.py:497
  57.0 7.6 %collective-permute-start.8 = (bf16[256,512]{1,0:T(8,128)(2,1)S(1)}, bf16[256,512]{1,0:T(8,128)(2,1)S(1)}, u32[]{:S(2)}, u32[]{:S(2)}) collective-permute-start(bf16[256,512]{1,0:T(8,128)(2,1)S(1)} %fusion), channel_id=1, source_target_pairs={{0,2},{2,0},{4,6},{6,4},{1,3},{3,1},{5,7},{7,5},{8,10},{10,8},{12,... | collective-permute-start | bytes 786440 | tf_op jit(solution)/shard_map/ppermute | solution.py:497
  62.2 6.3 %collective-permute-start.13 = (bf16[128,512]{1,0:T(8,128)(2,1)S(1)}, bf16[128,512]{1,0:T(8,128)(2,1)S(1)}, u32[]{:S(2)}, u32[]{:S(2)}) collective-permute-start(bf16[128,512]{1,0:T(8,128)(2,1)S(1)} %fusion.6), channel_id=1, source_target_pairs={{0,16},{8,24},{16,0},{24,8},{1,17},{9,25},{17,1},{25,9},{2,18},{10... | collective-permute-start | bytes 393224 | tf_op jit(solution)/shard_map/ppermute | solution.py:497
  64.8 6.2 %collective-permute-start.9 = (bf16[128,512]{1,0:T(8,128)(2,1)S(1)}, bf16[128,512]{1,0:T(8,128)(2,1)S(1)}, u32[]{:S(2)}, u32[]{:S(2)}) collective-permute-start(bf16[128,512]{1,0:T(8,128)(2,1)S(1)} %fusion.5), channel_id=1, source_target_pairs={{0,16},{8,24},{16,0},{24,8},{1,17},{9,25},{17,1},{25,9},{2,18},{10... | collective-permute-start | bytes 393224 | tf_op jit(solution)/shard_map/ppermute | solution.py:497
  68.6 11.0 %collective-permute-start.14 = (bf16[128,512]{1,0:T(8,128)(2,1)S(1)}, bf16[128,512]{1,0:T(8,128)(2,1)S(1)}, u32[]{:S(2)}, u32[]{:S(2)}) collective-permute-start(bf16[128,512]{1,0:T(8,128)(2,1)S(1)} %fusion.8), channel_id=1, source_target_pairs={{0,4},{2,6},{4,0},{6,2},{1,5},{3,7},{5,1},{7,3},{8,12},{10,14},{12... | collective-permute-start | bytes 393224 | tf_op jit(solution)/shard_map/ppermute | solution.py:497
  71.0 9.9 %collective-permute-start.10 = (bf16[128,512]{1,0:T(8,128)(2,1)S(1)}, bf16[128,512]{1,0:T(8,128)(2,1)S(1)}, u32[]{:S(2)}, u32[]{:S(2)}) collective-permute-start(bf16[128,512]{1,0:T(8,128)(2,1)S(1)} %fusion.7), channel_id=1, source_target_pairs={{0,4},{2,6},{4,0},{6,2},{1,5},{3,7},{5,1},{7,3},{8,12},{10,14},{12... | collective-permute-start | bytes 393224 | tf_op jit(solution)/shard_map/ppermute | solution.py:497

commit v4 on v0

--- a/solution.py
+++ b/solution.py
@@ -1,6 +1,8 @@
 import jax
 import jax.numpy as jnp
 from jax import lax
+from jax.experimental import pallas as pl
+from jax.experimental.pallas import tpu as pltpu
 from jax.sharding import PartitionSpec as P
 
 EPS = 1e-05
@@ -72,7 +74,7 @@
     return members
 
 
-def body(bounds, saved_inputs, w_in, w_out, top_grad):
+def general_body(bounds, saved_inputs, w_in, w_out, top_grad):
     sections = lax.axis_size("section") // 2
     tensors = lax.axis_size("tensor")
     pipe_index = lax.axis_index("pipe")
@@ -184,6 +186,373 @@
     return (grad_in_part[None], grad_out_part[None])
 
 
+VMEM = pl.BlockSpec(memory_space=pltpu.VMEM)
+SMEM = pl.BlockSpec(memory_space=pltpu.SMEM)
+KERNEL_BYTES = 14 * 2**20
+STAGE_FLOPS = 8 * 10**9
+
+
+class Place:
+    def __init__(self, bounds):
+        pipe = lax.axis_index("pipe")
+        section = lax.axis_index("section")
+        self.column = lax.axis_index("tensor")
+        self.relay = pipe // 2
+        self.core = pipe % 2
+        self.half = section % 2
+        self.left = section < 2
+        self.short = (bounds[self.relay, 1] - bounds[self.relay, 0]) == 2
+        self.slot = jnp.where(self.short, 1, 0)
+        self.upper_slot = jnp.where(self.left, 1, 0)
+
+
+def norm_rows(saved):
+    floats = saved.astype(jnp.float32)
+    row_scale = jnp.sqrt(jnp.mean(floats * floats, axis=-1, keepdims=True) + EPS)
+    return floats / row_scale, row_scale
+
+
+def nt_dot(left, right):
+    return lax.dot_general(left, right, (((1,), (1,)), ((), ())), preferred_element_type=jnp.float32)
+
+
+def tn_dot(left, right):
+    return lax.dot_general(left, right, (((0,), (0,)), ((), ())), preferred_element_type=jnp.float32)
+
+
+def chain_kernel(bounds, tops, saved, w_in, w_out, grad_out):
+    place = Place(bounds)
+    slot = place.upper_slot
+    grad_next = tops[place.half]
+    err = nt_dot(grad_next, w_out[slot]).astype(jnp.bfloat16)
+    unit, row_scale = norm_rows(saved[slot])
+    pulled = nt_dot(err, w_in[slot])
+    inner_mean = jnp.mean(pulled * unit, axis=-1, keepdims=True)
+    back = grad_next.astype(jnp.float32) + (pulled - unit * inner_mean) / row_scale
+    grad_out[...] = back.astype(jnp.bfloat16)
+
+
+def chain(bounds, tops, saved, w_in, w_out):
+    rows, model = saved.shape[1:]
+    inner = w_in.shape[2]
+    return pl.pallas_call(
+        chain_kernel,
+        out_shape=jax.ShapeDtypeStruct((rows, model), jnp.bfloat16),
+        in_specs=[SMEM] + [VMEM] * 4,
+        out_specs=VMEM,
+        compiler_params=pltpu.CompilerParams(vmem_limit_bytes=KERNEL_BYTES),
+        cost_estimate=pl.CostEstimate(
+            flops=4 * rows * model * inner, bytes_accessed=4 * model * inner, transcendentals=0
+        ),
+        name="chain",
+    )(bounds, tops, saved, w_in, w_out)
+
+
+def opening_kernel(mark):
+    mark[...] = jnp.zeros_like(mark)
+
+
+def opening():
+    return pl.pallas_call(
+        opening_kernel,
+        out_shape=jax.ShapeDtypeStruct((8, 128), jnp.float32),
+        out_specs=VMEM,
+        compiler_params=pltpu.CompilerParams(vmem_limit_bytes=KERNEL_BYTES),
+        cost_estimate=pl.CostEstimate(flops=STAGE_FLOPS, bytes_accessed=4096, transcendentals=0),
+        name="opening",
+    )()
+
+
+def staged_kernel(bounds, mark, saved, tops, own_saved, own_top, given):
+    place = Place(bounds)
+    give_top = place.left & jnp.logical_not(place.short)
+    own_saved[...] = saved[place.slot]
+    own_top[...] = tops[place.half]
+
+    @pl.when(give_top)
+    def _():
+        given[...] = tops[place.half]
+
+    @pl.when(jnp.logical_not(give_top))
+    def _():
+        given[...] = saved[0]
+
+
+def staged(bounds, saved, tops):
+    block = jax.ShapeDtypeStruct(saved.shape[1:], saved.dtype)
+    return pl.pallas_call(
+        staged_kernel,
+        out_shape=(block,) * 3,
+        in_specs=[SMEM, VMEM, VMEM, VMEM],
+        out_specs=(VMEM,) * 3,
+        compiler_params=pltpu.CompilerParams(vmem_limit_bytes=KERNEL_BYTES),
+        cost_estimate=pl.CostEstimate(flops=STAGE_FLOPS, bytes_accessed=8 * saved.size, transcendentals=0),
+        name="staged",
+    )(bounds, opening(), saved, tops)
+
+
+def by_role_kernel(bounds, full_part, short_part, chosen):
+    place = Place(bounds)
+
+    @pl.when(place.short)
+    def _():
+        chosen[...] = short_part[...]
+
+    @pl.when(jnp.logical_not(place.short))
+    def _():
+        chosen[...] = full_part[...]
+
+
+def by_role(bounds, full_part, short_part):
+    return pl.pallas_call(
+        by_role_kernel,
+        out_shape=jax.ShapeDtypeStruct(full_part.shape, full_part.dtype),
+        in_specs=[SMEM, VMEM, VMEM],
+        out_specs=VMEM,
+        compiler_params=pltpu.CompilerParams(vmem_limit_bytes=KERNEL_BYTES),
+        name="by_role",
+    )(bounds, full_part, short_part)
+
+
+BLOCKS = 4
+
+
+def put_unit(unit, first, second):
+    rows = first.shape[0]
+    unit[:rows, :] = norm_rows(first[...])[0].astype(jnp.bfloat16)
+    unit[rows:, :] = norm_rows(second[...])[0].astype(jnp.bfloat16)
+
+
+def lane_block(j, core, lanes):
+    return pl.ds(pl.multiple_of((2 * j + core) * lanes, lanes), lanes)
+
+
+def core_columns(place, unit, w_in, unit_part, value):
+    lanes = unit.shape[1] // (2 * BLOCKS)
+    for j in range(BLOCKS):
+        block = lane_block(j, place.core, lanes)
+        where = pl.ds(j * lanes, lanes)
+        unit_part[:, where] = unit[:, block]
+        value[:, where] = jnp.dot(
+            unit[...], w_in[place.slot, :, block], preferred_element_type=jnp.float32
+        ).astype(jnp.bfloat16)
+
+
+def early_kernel(bounds, e1, e2, f1, f2, w_in, w_out, early_part, unit_part, value, unit):
+    place = Place(bounds)
+    part = unit_part.shape[1]
+
+    @pl.when(jnp.logical_not(place.short))
+    def _():
+        put_unit(unit, e2, f2)
+        core_columns(place, unit, w_in, unit_part, value)
+        put_unit(unit, e1, f1)
+        core_columns(place, unit, w_in, early_part.at[:, :part], early_part.at[:, part:])
+
+    @pl.when(place.short)
+    def _():
+        put_unit(unit, e1, f1)
+        core_columns(place, unit, w_in, unit_part, value)
+        both = jnp.concatenate([e2[...], f2[...]], axis=0)
+        early_part[...] = nt_dot(both, w_out[place.slot]).astype(jnp.bfloat16)
+
+
+def early_factors(bounds, own, partner, w_in, w_out):
+    rows, model = own[0].shape
+    inner = w_in.shape[2]
+    part = model // 2
+    return pl.pallas_call(
+        early_kernel,
+        out_shape=(
+            jax.ShapeDtypeStruct((2 * rows, model), jnp.bfloat16),
+            jax.ShapeDtypeStruct((2 * rows, part), jnp.bfloat16),
+            jax.ShapeDtypeStruct((2 * rows, part), jnp.bfloat16),
+        ),
+        in_specs=[SMEM] + [VMEM] * 6,
+        out_specs=(VMEM,) * 3,
+        scratch_shapes=[pltpu.VMEM((2 * rows, model), jnp.bfloat16)],
+        compiler_params=pltpu.CompilerParams(vmem_limit_bytes=KERNEL_BYTES),
+        cost_estimate=pl.CostEstimate(
+            flops=4 * rows * model * inner, bytes_accessed=3 * model * inner, transcendentals=0
+        ),
+        name="early",
+    )(bounds, *own, *partner, w_in, w_out)
+
+
+def middle_kernel(bounds, e3, f3, unit_part, value, w_out, in_acc, out_acc):
+    place = Place(bounds)
+    grads = jnp.concatenate([e3[...], f3[...]], axis=0)
+    err = nt_dot(grads, w_out[place.slot]).astype(jnp.bfloat16)
+    in_acc[...] = tn_dot(unit_part[...], err)
+    out_acc[...] = tn_dot(value[...], grads)
+
+
+def middle_partials(bounds, e3, f3, unit_part, value, w_out):
+    rows, model = e3.shape
+    inner = w_out.shape[1]
+    part = unit_part.shape[1]
+    return pl.pallas_call(
+        middle_kernel,
+        out_shape=(
+            jax.ShapeDtypeStruct((part, inner), jnp.float32),
+            jax.ShapeDtypeStruct((part, model), jnp.float32),
+        ),
+        in_specs=[SMEM] + [VMEM] * 5,
+        out_specs=(VMEM,) * 2,
+        compiler_params=pltpu.CompilerParams(vmem_limit_bytes=KERNEL_BYTES),
+        cost_estimate=pl.CostEstimate(
+            flops=8 * rows * model * inner, bytes_accessed=3 * model * inner, transcendentals=0
+        ),
+        name="middle",
+    )(bounds, e3, f3, unit_part, value, w_out)
+
+
+def late_kernel(
+    bounds, late, flate, e2, f2, early_part, in_acc, out_acc, w_in, w_out,
+    in_send, in_keep, out_send, out_keep,
+    unit, unit_part, value, grads, err,
+):
+    place = Place(bounds)
+    half, column = place.half, place.column
+    rows = late.shape[0]
+    part = unit_part.shape[1]
+
+    @pl.when(jnp.logical_not(place.short))
+    def _():
+        grads[:rows, :] = late[...]
+        grads[rows:, :] = flate[...]
+        err[...] = nt_dot(grads[...], w_out[place.slot]).astype(jnp.bfloat16)
+        unit_part[...] = early_part[:, :part]
+        value[...] = early_part[:, part:]
+
+    @pl.when(place.short)
+    def _():
+        put_unit(unit, late, flate)
+        core_columns(place, unit, w_in, unit_part, value)
+        grads[:rows, :] = e2[...]
+        grads[rows:, :] = f2[...]
+        err[...] = early_part[...]
+
+    half_cols = err.shape[1] // 2
+    mine = pl.ds(pl.multiple_of(column * half_cols, half_cols), half_cols)
+    other = pl.ds(pl.multiple_of((1 - column) * half_cols, half_cols), half_cols)
+    in_send[...] = (in_acc[:, other] + tn_dot(unit_part[...], err[:, other])).astype(jnp.bfloat16)
+    in_keep[...] = in_acc[:, mine] + tn_dot(unit_part[...], err[:, mine])
+    half_rows = part // 2
+    upper = pl.ds(pl.multiple_of(half * half_rows, half_rows), half_rows)
+    lower = pl.ds(pl.multiple_of((1 - half) * half_rows, half_rows), half_rows)
+    out_send[...] = (out_acc[lower, :] + tn_dot(value[:, lower], grads[...])).astype(jnp.bfloat16)
+    out_keep[...] = out_acc[upper, :] + tn_dot(value[:, upper], grads[...])
+
+
+def late_partials(bounds, late, other_late, own_top, other_top, early_part, accs, w_in, w_out):
+    rows, model = late.shape
+    inner = w_out.shape[1]
+    part = model // 2
+    return pl.pallas_call(
+        late_kernel,
+        out_shape=(
+            jax.ShapeDtypeStruct((part, inner // 2), jnp.bfloat16),
+            jax.ShapeDtypeStruct((part, inner // 2), jnp.float32),
+            jax.ShapeDtypeStruct((part // 2, model), jnp.bfloat16),
+            jax.ShapeDtypeStruct((part // 2, model), jnp.float32),
+        ),
+        in_specs=[SMEM] + [VMEM] * 9,
+        out_specs=(VMEM,) * 4,
+        scratch_shapes=[
+            pltpu.VMEM((2 * rows, model), jnp.bfloat16),
+            pltpu.VMEM((2 * rows, part), jnp.bfloat16),
+            pltpu.VMEM((2 * rows, part), jnp.bfloat16),
+            pltpu.VMEM((2 * rows, model), jnp.bfloat16),
+            pltpu.VMEM((2 * rows, inner), jnp.bfloat16),
+        ],
+        compiler_params=pltpu.CompilerParams(vmem_limit_bytes=KERNEL_BYTES),
+        cost_estimate=pl.CostEstimate(
+            flops=8 * rows * model * inner, bytes_accessed=3 * model * inner, transcendentals=0
+        ),
+        name="late",
+    )(bounds, late, other_late, own_top, other_top, early_part, *accs, w_in, w_out)
+
+
+def flipped(value, axis, bit):
+    return lax.ppermute(value, axis, [(i, i ^ bit) for i in range(lax.axis_size(axis))])
+
+
+def two_section_body(bounds, saved_inputs, w_in, w_out, top_grad):
+    pipe_index = lax.axis_index("pipe")
+    section_index = lax.axis_index("section")
+    column = lax.axis_index("tensor")
+    relay = pipe_index // 2
+    half = section_index % 2
+    left = section_index // 2 == 0
+    boundary = lax.dynamic_index_in_dim(bounds, relay, 0, keepdims=False)
+    short = boundary[1] - boundary[0] == 2
+    saved = saved_inputs[0, 0]
+    proj_in = w_in[0, 0]
+    proj_out = w_out[0, 0]
+    tops = top_grad[0]
+    model = saved.shape[2]
+    inner = proj_in.shape[2]
+
+    def across(value):
+        return flipped(value, "pipe", 2)
+
+    def core_swap(value):
+        return flipped(value, "pipe", 1)
+
+    def half_swap(value):
+        return flipped(value, "section", 1)
+
+    def column_swap(value):
+        return flipped(value, "tensor", 1)
+
+    def section_swap(value):
+        return flipped(value, "section", 2)
+
+    own_saved, own_top, given = staged(bounds, saved, tops)
+    swapped = across(given)
+    grad_low = chain(bounds, tops, saved, proj_in, proj_out)
+    hopping = by_role(bounds, grad_low, swapped)
+    late = section_swap(hopping)
+    grad_other = across(grad_low)
+    own = (own_saved, swapped)
+    partner = tuple(core_swap(part) for part in own)
+    early_part, unit_part, value = early_factors(bounds, own, partner, proj_in, proj_out)
+    grad_early = by_role(bounds, grad_other, own_top)
+    accs = middle_partials(bounds, grad_early, core_swap(grad_early), unit_part, value, proj_out)
+    other_late = core_swap(late)
+    in_send, in_keep, out_send, out_keep = late_partials(
+        bounds, late, other_late, own[1], partner[1], early_part, accs, proj_in, proj_out
+    )
+    in_landed = column_swap(in_send)
+    out_landed = half_swap(out_send)
+    in_sum = (in_keep + in_landed.astype(jnp.float32)).reshape(2, -1, inner // 2)
+    out_sum = out_keep + out_landed.astype(jnp.float32)
+    in_mine = lax.dynamic_index_in_dim(in_sum, half, 0, keepdims=False)
+    in_next = lax.dynamic_index_in_dim(in_sum, 1 - half, 0, keepdims=False)
+    out_mine = lax.dynamic_slice_in_dim(out_sum, column * (model // 2), model // 2, 1)
+    out_next = lax.dynamic_slice_in_dim(out_sum, (1 - column) * (model // 2), model // 2, 1)
+    in_landed = half_swap(in_next.astype(jnp.bfloat16))
+    out_landed = column_swap(out_next.astype(jnp.bfloat16))
+    results = []
+    for mine, landed in ((in_mine, in_landed), (out_mine, out_landed)):
+        total = (mine + landed.astype(jnp.float32)).reshape(2, -1, mine.shape[1])
+        own = lax.dynamic_index_in_dim(total, relay, 0, keepdims=False)
+        sent = lax.dynamic_index_in_dim(total, 1 - relay, 0, keepdims=False).astype(jnp.bfloat16)
+        got = across(sent)
+        onward = section_swap(jnp.where(short, got, own.astype(jnp.bfloat16)))
+        lower = jnp.where(short, own, got.astype(jnp.float32))
+        results.append(jnp.where(left, lower, onward.astype(jnp.float32))[None])
+    return tuple(results)
+
+
+def body(bounds, saved_inputs, w_in, w_out, top_grad):
+    two_sections = lax.axis_size("section") == 4 and lax.axis_size("pipe") == 4
+    if two_sections and lax.axis_size("tensor") == 2:
+        return two_section_body(bounds, saved_inputs, w_in, w_out, top_grad)
+    return general_body(bounds, saved_inputs, w_in, w_out, top_grad)
+
+
 def solution(mesh):
     placed = (
         P(),

time: 234 us -> 76.4 us (0.33)
  the two profiles are of different devices: /device:TPU:24 before, /device:TPU:0 now
where the time goes in v4:
time: 76.4 us; the launch traced here: 76.1 us
  waiting for transfers between devices  36.7 us (48%)
  starting transfers between devices  21 us (27%)
  Pallas kernels  10.3 us (13%)
  other arithmetic  4.1 us (5%)
  between operations  2.14 us (3%)
  local copies, waits for them, and re-layouts  1.9 us (2%)
    ppermute x15, waiting for transfers between devices, flipped(): lax.ppermute(value, axis, [(i, i ^ bit) for i in range(lax.axis_size(axis...  36.7 us
    ppermute x15, starting transfers between devices, flipped(): lax.ppermute(value, axis, [(i, i ^ bit) for i in range(lax.axis_size(axis...  21 us
    pallas_call x1, Pallas kernels, early_factors(): pl.pallas_call(early_kernel, out_shape=(jax.ShapeDtypeStruct((2 * rows, m...  2.32 us
    pallas_call x1, Pallas kernels, chain(): pl.pallas_call(chain_kernel, out_shape=jax.ShapeDtypeStruct((rows, model)...  2.21 us
    pallas_call x1, Pallas kernels, late_partials(): pl.pallas_call(late_kernel, out_shape=(jax.ShapeDtypeStruct((part, inner...  2.09 us
    pallas_call x1, Pallas kernels, middle_partials(): pl.pallas_call(middle_kernel, out_shape=(jax.ShapeDtypeStruct((part, inne...  1.87 us
  transfers between devices with their start and end apart: 15, of which 9 were waited for; matrix products, arithmetic and copies ran while one was open for 5% of the time, Pallas kernels for 10%

profile of v4, /device:TPU:0, one launch (start us, length us, event | category | flops | bytes accessed | tf_op | source)
XLA Modules:
  0.0 76.1 jit_solution(10391085867555214238)
XLA Ops:
  0.7 1.0 %copy-done.2 = bf16[1,2,128,1024]{3,2,1,0:T(8,128)(2,1)S(1)} copy-done((bf16[1,2,128,1024]{3,2,1,0:T(8,128)(2,1)S(1)}, bf16[1,2,128,1024]{3,2,1,0:T(8,128)(2,1)}, u32[]{:S(2)}) %copy-start.2) | copy-done | bytes 524312
  1.7 0.2 copy-done.3
  1.8 0.0 copy-done.4
  1.8 0.6 staged.1
  2.5 3.1 %collective-permute-start = (bf16[128,1024]{1,0:T(8,128)(2,1)S(1)}, bf16[128,1024]{1,0:T(8,128)(2,1)S(1)}, u32[]{:S(2)}, u32[]{:S(2)}) collective-permute-start(bf16[128,1024]{1,0:T(8,128)(2,1)S(1)} %get-tuple-element.14), channel_id=1, source_target_pairs={{0,16},{8,24},{16,0},{24,8},{1,17},{9,25},{17,1},{25,9},{2,18},{10... | collective-permute-start | bytes 786440 | tf_op jit(solution)/shard_map/ppermute | solution.py:478
  5.5 0.0 copy-done.1
  5.5 2.2 %chain.1.full_part = bf16[128,1024]{1,0:T(8,128)(2,1)S(1)} custom-call(s32[2,3]{1,0:T(2,128)S(1)} %copy-done.4, bf16[2,128,1024]{2,1,0:T(8,128)(2,1)S(1)} %bitcast.46, bf16[2,128,1024]{2,1,0:T(8,128)(2,1)S(1)} %bitcast.48, bf16[2,1024,1024]{2,1,0:T(8,128)(2,1)S(1)} %bitcast.42, bf16[2,1024,1024]{2,1,0:T(8,128)(2,1)S(1)} %bitcast.38), custom_call_target="tpu_custom_call" | custom-call | flops 536870912 | bytes 4194304 | tf_op jit(solution)/shard_map/chain/pallas_call | solution.py:238
  7.7 2.8 %collective-permute-start.5 = (bf16[128,1024]{1,0:T(8,128)(2,1)S(1)}, bf16[128,1024]{1,0:T(8,128)(2,1)S(1)}, u32[]{:S(2)}, u32[]{:S(2)}) collective-permute-start(bf16[128,1024]{1,0:T(8,128)(2,1)S(1)} %chain.1.full_part), channel_id=1, source_target_pairs={{0,16},{8,24},{16,0},{24,8},{1,17},{9,25},{17,1},{25,9},{2,18},{10... | collective-permute-start | bytes 786440 | tf_op jit(solution)/shard_map/ppermute | solution.py:478
  10.6 1.8 %collective-permute-done.short_part.e2 = bf16[128,1024]{1,0:T(8,128)(2,1)S(1)} collective-permute-done((bf16[128,1024]{1,0:T(8,128)(2,1)S(1)}, bf16[128,1024]{1,0:T(8,128)(2,1)S(1)}, u32[]{:S(2)}, u32[]{:S(2)}) %collective-permute-start) | collective-permute-done | bytes 262176 | tf_op jit(solution)/shard_map/ppermute | solution.py:478
  12.4 0.6 by_role.2
  13.0 2.9 %collective-permute-start.1 = (bf16[128,1024]{1,0:T(8,128)(2,1)S(1)}, bf16[128,1024]{1,0:T(8,128)(2,1)S(1)}, u32[]{:S(2)}, u32[]{:S(2)}) collective-permute-start(bf16[128,1024]{1,0:T(8,128)(2,1)S(1)} %by_role.2), channel_id=1, source_target_pairs={{0,4},{2,6},{4,0},{6,2},{1,5},{3,7},{5,1},{7,3},{8,12},{10,14},{12... | collective-permute-start | bytes 786440 | tf_op jit(solution)/shard_map/ppermute | solution.py:478
  15.9 0.0 collective-permute-start.4
  15.9 0.5 collective-permute-start.3
  16.4 1.1 %collective-permute-done.5.full_part = bf16[128,1024]{1,0:T(8,128)(2,1)S(1)} collective-permute-done((bf16[128,1024]{1,0:T(8,128)(2,1)S(1)}, bf16[128,1024]{1,0:T(8,128)(2,1)S(1)}, u32[]{:S(2)}, u32[]{:S(2)}) %collective-permute-start.5) | collective-permute-done | bytes 262176 | tf_op jit(solution)/shard_map/ppermute | solution.py:478
  17.5 0.6 by_role.3.e3
  18.1 0.1 collective-permute-start.6
  18.1 8.4 %collective-permute-done.1.late = bf16[128,1024]{1,0:T(8,128)(2,1)S(1)} collective-permute-done((bf16[128,1024]{1,0:T(8,128)(2,1)S(1)}, bf16[128,1024]{1,0:T(8,128)(2,1)S(1)}, u32[]{:S(2)}, u32[]{:S(2)}) %collective-permute-start.1) | collective-permute-done | bytes 262176 | tf_op jit(solution)/shard_map/ppermute | solution.py:478
  26.5 0.0 collective-permute-start.2
  26.5 0.0 collective-permute-done.4.f1
  26.5 0.0 collective-permute-done.3.f2
  26.5 2.3 %early.1 = (bf16[256,1024]{1,0:T(8,128)(2,1)S(1)}, bf16[256,512]{1,0:T(8,128)(2,1)S(1)}, bf16[256,512]{1,0:T(8,128)(2,1)S(1)}) custom-call(s32[2,3]{1,0:T(2,128)S(1)} %copy-done.4, bf16[128,1024]{1,0:T(8,128)(2,1)S(1)} %get-tuple-element.15.e1, bf16[128,1024]{1,0:T(8,128)(2,1)S(1)} %collective-permute-done.short_part.e2, ...), custom_call_target="tpu_custom_call" | custom-call | flops 536870912 | bytes 3145728 | tf_op jit(solution)/shard_map/early/pallas_call | solution.py:364
  28.8 0.0 collective-permute-done.6.f3
  28.8 1.9 %middle.1 = (f32[512,1024]{1,0:T(8,128)S(1)}, f32[512,1024]{1,0:T(8,128)S(1)}) custom-call(s32[2,3]{1,0:T(2,128)S(1)} %copy-done.4, bf16[128,1024]{1,0:T(8,128)(2,1)S(1)} %by_role.3.e3, bf16[128,1024]{1,0:T(8,128)(2,1)S(1)} %collective-permute-done.6.f3, bf16[256,512]{1,0:T(8,128)(2,1)S(1)} %get-tuple-element.18.unit_part, ...), custom_call_target="tpu_custom_call" | custom-call | flops 1073741824 | bytes 3145728 | tf_op jit(solution)/shard_map/middle/pallas_call | solution.py:394
  30.7 0.0 collective-permute-done.2.flate
  30.7 2.1 %late.1 = (bf16[512,512]{1,0:T(8,128)(2,1)S(1)}, f32[512,512]{1,0:T(8,128)S(1)}, bf16[256,1024]{1,0:T(8,128)(2,1)S(1)}, f32[256,1024]{1,0:T(8,128)S(1)}) custom-call(s32[2,3]{1,0:T(2,128)S(1)} %copy-done.4, bf16[128,1024]{1,0:T(8,128)(2,1)S(1)} %collective-permute-done.1.late, bf16[128,1024]{1,0:T(8,128)(2,1)S(1)} %collective-permute-done.2.flate, ...), custom_call_target="tpu_custom_call" | custom-call | flops 1073741824 | bytes 3145728 | tf_op jit(solution)/shard_map/late/pallas_call | solution.py:452
  32.8 0.7 collective-permute-start.11
  33.5 1.5 %collective-permute-start.7 = (bf16[512,512]{1,0:T(8,128)(2,1)S(1)}, bf16[512,512]{1,0:T(8,128)(2,1)}, u32[]{:S(2)}, u32[]{:S(2)}) collective-permute-start(bf16[512,512]{1,0:T(8,128)(2,1)S(1)} %get-tuple-element.23), channel_id=1, source_target_pairs={{0,1},{1,0},{2,3},{3,2},{4,5},{5,4},{6,7},{7,6},{8,9},{9,8},{10,11... | collective-permute-start | bytes 1572872 | tf_op jit(solution)/shard_map/ppermute | solution.py:478
  35.0 0.6 fusion.9
  36.9 10.4 %collective-permute-done.11 = bf16[256,1024]{1,0:T(8,128)(2,1)} collective-permute-done((bf16[256,1024]{1,0:T(8,128)(2,1)S(1)}, bf16[256,1024]{1,0:T(8,128)(2,1)}, u32[]{:S(2)}, u32[]{:S(2)}) %collective-permute-start.11) | collective-permute-done | bytes 524320 | tf_op jit(solution)/shard_map/ppermute | solution.py:478
  47.3 1.2 %convert_add_fusion = f32[256,1024]{1,0:T(8,128)S(1)} fusion(f32[256,1024]{1,0:T(8,128)S(1)} %get-tuple-element.24, bf16[256,1024]{1,0:T(8,128)(2,1)} %collective-permute-done.11), kind=kLoop, calls=%fused_computation | loop fusion | flops 524288 | bytes 2621440 | tf_op jit(solution)/shard_map/add | solution.py:530
  48.6 1.5 %collective-permute-start.12 = (bf16[256,512]{1,0:T(8,128)(2,1)S(1)}, bf16[256,512]{1,0:T(8,128)(2,1)S(1)}, u32[]{:S(2)}, u32[]{:S(2)}) collective-permute-start(bf16[256,512]{1,0:T(8,128)(2,1)S(1)} %dynamic-slice_convert_fusion), channel_id=1, source_target_pairs={{0,1},{1,0},{2,3},{3,2},{4,5},{5,4},{6,7},{7,6},{8,9},{9,8},{10,11... | collective-permute-start | bytes 786440 | tf_op jit(solution)/shard_map/ppermute | solution.py:478
  50.1 0.0 collective-permute-done.7
  50.1 1.2 %convert_add_fusion.1 = f32[512,512]{1,0:T(8,128)S(1)} fusion(f32[512,512]{1,0:T(8,128)S(1)} %get-tuple-element.22, bf16[512,512]{1,0:T(8,128)(2,1)} %collective-permute-done.7), kind=kLoop, calls=%fused_computation.1 | loop fusion | flops 524288 | bytes 2621440 | tf_op jit(solution)/shard_map/add | solution.py:529
  51.4 0.7 collective-permute-start.8
  52.1 4.4 %collective-permute-done.12 = bf16[256,512]{1,0:T(8,128)(2,1)S(1)} collective-permute-done((bf16[256,512]{1,0:T(8,128)(2,1)S(1)}, bf16[256,512]{1,0:T(8,128)(2,1)S(1)}, u32[]{:S(2)}, u32[]{:S(2)}) %collective-permute-start.12) | collective-permute-done | bytes 262176 | tf_op jit(solution)/shard_map/ppermute | solution.py:478
  56.5 0.1 convert_add_fusion.2
  56.6 1.6 %collective-permute-start.13 = (bf16[128,512]{1,0:T(8,128)(2,1)S(1)}, bf16[128,512]{1,0:T(8,128)(2,1)S(1)}, u32[]{:S(2)}, u32[]{:S(2)}) collective-permute-start(bf16[128,512]{1,0:T(8,128)(2,1)S(1)} %fusion.6), channel_id=1, source_target_pairs={{0,16},{8,24},{16,0},{24,8},{1,17},{9,25},{17,1},{25,9},{2,18},{10... | collective-permute-start | bytes 393224 | tf_op jit(solution)/shard_map/ppermute | solution.py:478
  58.2 0.8 %collective-permute-done.8 = bf16[256,512]{1,0:T(8,128)(2,1)S(1)} collective-permute-done((bf16[256,512]{1,0:T(8,128)(2,1)S(1)}, bf16[256,512]{1,0:T(8,128)(2,1)S(1)}, u32[]{:S(2)}, u32[]{:S(2)}) %collective-permute-start.8) | collective-permute-done | bytes 262176 | tf_op jit(solution)/shard_map/ppermute | solution.py:478
  59.0 0.1 bitcast_add_fusion
  59.1 1.6 %collective-permute-start.9 = (bf16[128,512]{1,0:T(8,128)(2,1)S(1)}, bf16[128,512]{1,0:T(8,128)(2,1)S(1)}, u32[]{:S(2)}, u32[]{:S(2)}) collective-permute-start(bf16[128,512]{1,0:T(8,128)(2,1)S(1)} %fusion.5), channel_id=1, source_target_pairs={{0,16},{8,24},{16,0},{24,8},{1,17},{9,25},{17,1},{25,9},{2,18},{10... | collective-permute-start | bytes 393224 | tf_op jit(solution)/shard_map/ppermute | solution.py:478
  60.8 2.3 %collective-permute-done.13 = bf16[128,512]{1,0:T(8,128)(2,1)S(1)} collective-permute-done((bf16[128,512]{1,0:T(8,128)(2,1)S(1)}, bf16[128,512]{1,0:T(8,128)(2,1)S(1)}, u32[]{:S(2)}, u32[]{:S(2)}) %collective-permute-start.13) | collective-permute-done | bytes 131104 | tf_op jit(solution)/shard_map/ppermute | solution.py:478
  63.1 2.2 %collective-permute-start.14 = (bf16[128,512]{1,0:T(8,128)(2,1)S(1)}, bf16[128,512]{1,0:T(8,128)(2,1)S(1)}, u32[]{:S(2)}, u32[]{:S(2)}) collective-permute-start(bf16[128,512]{1,0:T(8,128)(2,1)S(1)} %fusion.8), channel_id=1, source_target_pairs={{0,4},{2,6},{4,0},{6,2},{1,5},{3,7},{5,1},{7,3},{8,12},{10,14},{12... | collective-permute-start | bytes 393224 | tf_op jit(solution)/shard_map/ppermute | solution.py:478
  65.3 0.0 collective-permute-done.9
  65.4 1.7 %collective-permute-start.10 = (bf16[128,512]{1,0:T(8,128)(2,1)S(1)}, bf16[128,512]{1,0:T(8,128)(2,1)S(1)}, u32[]{:S(2)}, u32[]{:S(2)}) collective-permute-start(bf16[128,512]{1,0:T(8,128)(2,1)S(1)} %fusion.7), channel_id=1, source_target_pairs={{0,4},{2,6},{4,0},{6,2},{1,5},{3,7},{5,1},{7,3},{8,12},{10,14},{12... | collective-permute-start | bytes 393224 | tf_op jit(solution)/shard_map/ppermute | solution.py:478
  67.1 6.8 %collective-permute-done.14 = bf16[128,512]{1,0:T(8,128)(2,1)S(1)} collective-permute-done((bf16[128,512]{1,0:T(8,128)(2,1)S(1)}, bf16[128,512]{1,0:T(8,128)(2,1)S(1)}, u32[]{:S(2)}, u32[]{:S(2)}) %collective-permute-start.14) | collective-permute-done | bytes 131104 | tf_op jit(solution)/shard_map/ppermute | solution.py:478
  73.9 0.7 fusion.2
  74.7 0.7 collective-permute-done.10
  75.4 0.7 fusion.4
  (14 shorter events, 0.2 us)
Async XLA Ops:
  0.6 1.0 %copy-start.2 = (bf16[1,2,128,1024]{3,2,1,0:T(8,128)(2,1)S(1)}, bf16[1,2,128,1024]{3,2,1,0:T(8,128)(2,1)}, u32[]{:S(2)}) copy-start(bf16[1,2,128,1024]{3,2,1,0:T(8,128)(2,1)} %param.9) | copy-start | bytes 1572868
  0.6 1.2 %copy-start.3 = (bf16[1,1,2,128,1024]{4,3,2,1,0:T(8,128)(2,1)S(1)}, bf16[1,1,2,128,1024]{4,3,2,1,0:T(8,128)(2,1)}, u32[]{:S(2)}) copy-start(bf16[1,1,2,128,1024]{4,3,2,1,0:T(8,128)(2,1)} %param.6) | copy-start | bytes 1572868
  0.6 1.2 %copy-start.4 = (s32[2,3]{1,0:T(2,128)S(1)}, s32[2,3]{1,0:T(2,128)}, u32[]{:S(2)}) copy-start(s32[2,3]{1,0:T(2,128)} %bounds.13) | copy-start | bytes 76
  1.8 3.7 %copy-start = (bf16[1,1,2,1024,1024]{4,3,2,1,0:T(8,128)(2,1)S(1)}, bf16[1,1,2,1024,1024]{4,3,2,1,0:T(8,128)(2,1)}, u32[]{:S(2)}) copy-start(bf16[1,1,2,1024,1024]{4,3,2,1,0:T(8,128)(2,1)} %param.8) | copy-start | bytes 12582916
  1.8 3.7 %copy-start.1 = (bf16[1,1,2,1024,1024]{4,3,2,1,0:T(8,128)(2,1)S(1)}, bf16[1,1,2,1024,1024]{4,3,2,1,0:T(8,128)(2,1)}, u32[]{:S(2)}) copy-start(bf16[1,1,2,1024,1024]{4,3,2,1,0:T(8,128)(2,1)} %param.7) | copy-start | bytes 12582916
  2.5 9.9 %collective-permute-start = (bf16[128,1024]{1,0:T(8,128)(2,1)S(1)}, bf16[128,1024]{1,0:T(8,128)(2,1)S(1)}, u32[]{:S(2)}, u32[]{:S(2)}) collective-permute-start(bf16[128,1024]{1,0:T(8,128)(2,1)S(1)} %get-tuple-element.14), channel_id=1, source_target_pairs={{0,16},{8,24},{16,0},{24,8},{1,17},{9,25},{17,1},{25,9},{2,18},{10... | collective-permute-start | bytes 786440 | tf_op jit(solution)/shard_map/ppermute | solution.py:478
  7.7 9.7 %collective-permute-start.5 = (bf16[128,1024]{1,0:T(8,128)(2,1)S(1)}, bf16[128,1024]{1,0:T(8,128)(2,1)S(1)}, u32[]{:S(2)}, u32[]{:S(2)}) collective-permute-start(bf16[128,1024]{1,0:T(8,128)(2,1)S(1)} %chain.1.full_part), channel_id=1, source_target_pairs={{0,16},{8,24},{16,0},{24,8},{1,17},{9,25},{17,1},{25,9},{2,18},{10... | collective-permute-start | bytes 786440 | tf_op jit(solution)/shard_map/ppermute | solution.py:478
  13.0 13.5 %collective-permute-start.1 = (bf16[128,1024]{1,0:T(8,128)(2,1)S(1)}, bf16[128,1024]{1,0:T(8,128)(2,1)S(1)}, u32[]{:S(2)}, u32[]{:S(2)}) collective-permute-start(bf16[128,1024]{1,0:T(8,128)(2,1)S(1)} %by_role.2), channel_id=1, source_target_pairs={{0,4},{2,6},{4,0},{6,2},{1,5},{3,7},{5,1},{7,3},{8,12},{10,14},{12... | collective-permute-start | bytes 786440 | tf_op jit(solution)/shard_map/ppermute | solution.py:478
  15.9 10.6 %collective-permute-start.4 = (bf16[128,1024]{1,0:T(8,128)(2,1)S(1)}, bf16[128,1024]{1,0:T(8,128)(2,1)S(1)}, u32[]{:S(2)}, u32[]{:S(2)}) collective-permute-start(bf16[128,1024]{1,0:T(8,128)(2,1)S(1)} %get-tuple-element.15.e1), channel_id=1, source_target_pairs={{0,8},{8,0},{16,24},{24,16},{1,9},{9,1},{17,25},{25,17},{2,10},{10... | collective-permute-start | bytes 786440 | tf_op jit(solution)/shard_map/ppermute | solution.py:478
  15.9 10.6 %collective-permute-start.3 = (bf16[128,1024]{1,0:T(8,128)(2,1)S(1)}, bf16[128,1024]{1,0:T(8,128)(2,1)S(1)}, u32[]{:S(2)}, u32[]{:S(2)}) collective-permute-start(bf16[128,1024]{1,0:T(8,128)(2,1)S(1)} %collective-permute-done.short_part.e2), channel_id=1, source_target_pairs={{0,8},{8,0},{16,24},{24,16},{1,9},{9,1},{17,25},{25,17},{2,10},{10... | collective-permute-start | bytes 786440 | tf_op jit(solution)/shard_map/ppermute | solution.py:478
  18.1 10.8 %collective-permute-start.6 = (bf16[128,1024]{1,0:T(8,128)(2,1)S(1)}, bf16[128,1024]{1,0:T(8,128)(2,1)S(1)}, u32[]{:S(2)}, u32[]{:S(2)}) collective-permute-start(bf16[128,1024]{1,0:T(8,128)(2,1)S(1)} %by_role.3.e3), channel_id=1, source_target_pairs={{0,8},{8,0},{16,24},{24,16},{1,9},{9,1},{17,25},{25,17},{2,10},{10... | collective-permute-start | bytes 786440 | tf_op jit(solution)/shard_map/ppermute | solution.py:478
  26.5 4.2 %collective-permute-start.2 = (bf16[128,1024]{1,0:T(8,128)(2,1)S(1)}, bf16[128,1024]{1,0:T(8,128)(2,1)S(1)}, u32[]{:S(2)}, u32[]{:S(2)}) collective-permute-start(bf16[128,1024]{1,0:T(8,128)(2,1)S(1)} %collective-permute-done.1.late), channel_id=1, source_target_pairs={{0,8},{8,0},{16,24},{24,16},{1,9},{9,1},{17,25},{25,17},{2,10},{10... | collective-permute-start | bytes 786440 | tf_op jit(solution)/shard_map/ppermute | solution.py:478
  32.8 14.5 %collective-permute-start.11 = (bf16[256,1024]{1,0:T(8,128)(2,1)S(1)}, bf16[256,1024]{1,0:T(8,128)(2,1)}, u32[]{:S(2)}, u32[]{:S(2)}) collective-permute-start(bf16[256,1024]{1,0:T(8,128)(2,1)S(1)} %get-tuple-element.25), channel_id=1, source_target_pairs={{0,2},{2,0},{4,6},{6,4},{1,3},{3,1},{5,7},{7,5},{8,10},{10,8},{12,... | collective-permute-start | bytes 1572872 | tf_op jit(solution)/shard_map/ppermute | solution.py:478
  33.5 16.6 %collective-permute-start.7 = (bf16[512,512]{1,0:T(8,128)(2,1)S(1)}, bf16[512,512]{1,0:T(8,128)(2,1)}, u32[]{:S(2)}, u32[]{:S(2)}) collective-permute-start(bf16[512,512]{1,0:T(8,128)(2,1)S(1)} %get-tuple-element.23), channel_id=1, source_target_pairs={{0,1},{1,0},{2,3},{3,2},{4,5},{5,4},{6,7},{7,6},{8,9},{9,8},{10,11... | collective-permute-start | bytes 1572872 | tf_op jit(solution)/shard_map/ppermute | solution.py:478
  48.6 7.9 %collective-permute-start.12 = (bf16[256,512]{1,0:T(8,128)(2,1)S(1)}, bf16[256,512]{1,0:T(8,128)(2,1)S(1)}, u32[]{:S(2)}, u32[]{:S(2)}) collective-permute-start(bf16[256,512]{1,0:T(8,128)(2,1)S(1)} %dynamic-slice_convert_fusion), channel_id=1, source_target_pairs={{0,1},{1,0},{2,3},{3,2},{4,5},{5,4},{6,7},{7,6},{8,9},{9,8},{10,11... | collective-permute-start | bytes 786440 | tf_op jit(solution)/shard_map/ppermute | solution.py:478
  51.4 7.6 %collective-permute-start.8 = (bf16[256,512]{1,0:T(8,128)(2,1)S(1)}, bf16[256,512]{1,0:T(8,128)(2,1)S(1)}, u32[]{:S(2)}, u32[]{:S(2)}) collective-permute-start(bf16[256,512]{1,0:T(8,128)(2,1)S(1)} %fusion), channel_id=1, source_target_pairs={{0,2},{2,0},{4,6},{6,4},{1,3},{3,1},{5,7},{7,5},{8,10},{10,8},{12,... | collective-permute-start | bytes 786440 | tf_op jit(solution)/shard_map/ppermute | solution.py:478
  56.6 6.4 %collective-permute-start.13 = (bf16[128,512]{1,0:T(8,128)(2,1)S(1)}, bf16[128,512]{1,0:T(8,128)(2,1)S(1)}, u32[]{:S(2)}, u32[]{:S(2)}) collective-permute-start(bf16[128,512]{1,0:T(8,128)(2,1)S(1)} %fusion.6), channel_id=1, source_target_pairs={{0,16},{8,24},{16,0},{24,8},{1,17},{9,25},{17,1},{25,9},{2,18},{10... | collective-permute-start | bytes 393224 | tf_op jit(solution)/shard_map/ppermute | solution.py:478
  59.1 6.2 %collective-permute-start.9 = (bf16[128,512]{1,0:T(8,128)(2,1)S(1)}, bf16[128,512]{1,0:T(8,128)(2,1)S(1)}, u32[]{:S(2)}, u32[]{:S(2)}) collective-permute-start(bf16[128,512]{1,0:T(8,128)(2,1)S(1)} %fusion.5), channel_id=1, source_target_pairs={{0,16},{8,24},{16,0},{24,8},{1,17},{9,25},{17,1},{25,9},{2,18},{10... | collective-permute-start | bytes 393224 | tf_op jit(solution)/shard_map/ppermute | solution.py:478
  63.1 10.9 %collective-permute-start.14 = (bf16[128,512]{1,0:T(8,128)(2,1)S(1)}, bf16[128,512]{1,0:T(8,128)(2,1)S(1)}, u32[]{:S(2)}, u32[]{:S(2)}) collective-permute-start(bf16[128,512]{1,0:T(8,128)(2,1)S(1)} %fusion.8), channel_id=1, source_target_pairs={{0,4},{2,6},{4,0},{6,2},{1,5},{3,7},{5,1},{7,3},{8,12},{10,14},{12... | collective-permute-start | bytes 393224 | tf_op jit(solution)/shard_map/ppermute | solution.py:478
  65.4 10.0 %collective-permute-start.10 = (bf16[128,512]{1,0:T(8,128)(2,1)S(1)}, bf16[128,512]{1,0:T(8,128)(2,1)S(1)}, u32[]{:S(2)}, u32[]{:S(2)}) collective-permute-start(bf16[128,512]{1,0:T(8,128)(2,1)S(1)} %fusion.7), channel_id=1, source_target_pairs={{0,4},{2,6},{4,0},{6,2},{1,5},{3,7},{5,1},{7,3},{8,12},{10,14},{12... | collective-permute-start | bytes 393224 | tf_op jit(solution)/shard_map/ppermute | solution.py:478

commit v5 on v4

--- a/solution.py
+++ b/solution.py
@@ -1,3 +1,5 @@
+import functools
+
 import jax
 import jax.numpy as jnp
 from jax import lax
@@ -323,14 +325,15 @@
     unit[rows:, :] = norm_rows(second[...])[0].astype(jnp.bfloat16)
 
 
-def lane_block(j, core, lanes):
-    return pl.ds(pl.multiple_of((2 * j + core) * lanes, lanes), lanes)
+def lane_block(j, place, lanes):
+    owner = place.relay if j // 2 else 1 - place.relay
+    return pl.ds(pl.multiple_of((4 * (j % 2) + 2 * owner + place.core) * lanes, lanes), lanes)
 
 
 def core_columns(place, unit, w_in, unit_part, value):
     lanes = unit.shape[1] // (2 * BLOCKS)
     for j in range(BLOCKS):
-        block = lane_block(j, place.core, lanes)
+        block = lane_block(j, place, lanes)
         where = pl.ds(j * lanes, lanes)
         unit_part[:, where] = unit[:, block]
         value[:, where] = jnp.dot(
@@ -408,10 +411,10 @@
 
 
 def late_kernel(
-    bounds, late, flate, e2, f2, early_part, in_acc, out_acc, w_in, w_out,
-    in_send, in_keep, out_send, out_keep,
-    unit, unit_part, value, grads, err,
+    bounds, late, flate, e2, f2, early_part, in_acc, out_acc, w_in, w_out, *outs
 ):
+    far, near = outs[:4], outs[4:8]
+    unit, unit_part, value, grads, err = outs[8:]
     place = Place(bounds)
     half, column = place.half, place.column
     rows = late.shape[0]
@@ -436,13 +439,16 @@
     half_cols = err.shape[1] // 2
     mine = pl.ds(pl.multiple_of(column * half_cols, half_cols), half_cols)
     other = pl.ds(pl.multiple_of((1 - column) * half_cols, half_cols), half_cols)
-    in_send[...] = (in_acc[:, other] + tn_dot(unit_part[...], err[:, other])).astype(jnp.bfloat16)
-    in_keep[...] = in_acc[:, mine] + tn_dot(unit_part[...], err[:, mine])
-    half_rows = part // 2
-    upper = pl.ds(pl.multiple_of(half * half_rows, half_rows), half_rows)
-    lower = pl.ds(pl.multiple_of((1 - half) * half_rows, half_rows), half_rows)
-    out_send[...] = (out_acc[lower, :] + tn_dot(value[:, lower], grads[...])).astype(jnp.bfloat16)
-    out_keep[...] = out_acc[upper, :] + tn_dot(value[:, upper], grads[...])
+    group = part // 2
+    block = part // 4
+    for k, (in_send, in_keep, out_send, out_keep) in enumerate((far, near)):
+        rows_of = slice(k * group, (k + 1) * group)
+        in_send[...] = (in_acc[rows_of, other] + tn_dot(unit_part[:, rows_of], err[:, other])).astype(jnp.bfloat16)
+        in_keep[...] = in_acc[rows_of, mine] + tn_dot(unit_part[:, rows_of], err[:, mine])
+        kept = pl.ds(pl.multiple_of(k * group + half * block, block), block)
+        sent = pl.ds(pl.multiple_of(k * group + (1 - half) * block, block), block)
+        out_send[...] = (out_acc[sent, :] + tn_dot(value[:, sent], grads[...])).astype(jnp.bfloat16)
+        out_keep[...] = out_acc[kept, :] + tn_dot(value[:, kept], grads[...])
 
 
 def late_partials(bounds, late, other_late, own_top, other_top, early_part, accs, w_in, w_out):
@@ -452,13 +458,14 @@
     return pl.pallas_call(
         late_kernel,
         out_shape=(
-            jax.ShapeDtypeStruct((part, inner // 2), jnp.bfloat16),
-            jax.ShapeDtypeStruct((part, inner // 2), jnp.float32),
-            jax.ShapeDtypeStruct((part // 2, model), jnp.bfloat16),
-            jax.ShapeDtypeStruct((part // 2, model), jnp.float32),
-        ),
+            jax.ShapeDtypeStruct((part // 2, inner // 2), jnp.bfloat16),
+            jax.ShapeDtypeStruct((part // 2, inner // 2), jnp.float32),
+            jax.ShapeDtypeStruct((part // 4, model), jnp.bfloat16),
+            jax.ShapeDtypeStruct((part // 4, model), jnp.float32),
+        )
+        * 2,
         in_specs=[SMEM] + [VMEM] * 9,
-        out_specs=(VMEM,) * 4,
+        out_specs=(VMEM,) * 8,
         scratch_shapes=[
             pltpu.VMEM((2 * rows, model), jnp.bfloat16),
             pltpu.VMEM((2 * rows, part), jnp.bfloat16),
@@ -474,25 +481,86 @@
     )(bounds, late, other_late, own_top, other_top, early_part, *accs, w_in, w_out)
 
 
+def first_add_kernel(bounds, in_keep, in_land, out_keep, out_land, in_mine, in_next, out_mine, out_next):
+    place = Place(bounds)
+    rows = in_mine.shape[0]
+    cols = out_mine.shape[1]
+
+    def row_block(which):
+        return pl.ds(pl.multiple_of(which * rows, rows), rows)
+
+    def col_block(which):
+        return pl.ds(pl.multiple_of(which * cols, cols), cols)
+
+    kept, sent = row_block(place.half), row_block(1 - place.half)
+    in_mine[...] = in_keep[kept, :] + in_land[kept, :].astype(jnp.float32)
+    in_next[...] = (in_keep[sent, :] + in_land[sent, :].astype(jnp.float32)).astype(jnp.bfloat16)
+    kept, sent = col_block(place.column), col_block(1 - place.column)
+    out_mine[...] = out_keep[:, kept] + out_land[:, kept].astype(jnp.float32)
+    out_next[...] = (out_keep[:, sent] + out_land[:, sent].astype(jnp.float32)).astype(jnp.bfloat16)
+
+
+def second_add_kernel(in_mine, in_land, out_mine, out_land, total):
+    total[0] = (in_mine[...] + in_land[...].astype(jnp.float32)).astype(total.dtype)
+    total[1] = (out_mine[...] + out_land[...].astype(jnp.float32)).astype(total.dtype)
+
+
+def hand_on_kernel(bounds, near, got, in_give, out_give, lower):
+    place = Place(bounds)
+
+    @pl.when(place.short)
+    def _():
+        in_give[...] = got[0]
+        out_give[...] = got[1]
+        lower[...] = near[...]
+
+    @pl.when(jnp.logical_not(place.short))
+    def _():
+        in_give[...] = near[0].astype(jnp.bfloat16)
+        out_give[...] = near[1].astype(jnp.bfloat16)
+        lower[...] = got[...].astype(jnp.float32)
+
+
+def result_kernel(which, lower, landed, result):
+    left = lax.axis_index("section") < 2
+
+    @pl.when(left)
+    def _():
+        result[0] = lower[which]
+
+    @pl.when(jnp.logical_not(left))
+    def _():
+        result[0] = landed[...].astype(jnp.float32)
+
+
+def small_call(kernel, operands, shapes, use_bounds=True):
+    return pl.pallas_call(
+        kernel,
+        out_shape=shapes,
+        in_specs=([SMEM] if use_bounds else []) + [VMEM] * (len(operands) - use_bounds),
+        out_specs=jax.tree.map(lambda _: VMEM, shapes),
+        compiler_params=pltpu.CompilerParams(vmem_limit_bytes=KERNEL_BYTES),
+    )(*operands)
+
+
+def low_shape(*dims):
+    return jax.ShapeDtypeStruct(dims, jnp.bfloat16)
+
+
+def full_shape(*dims):
+    return jax.ShapeDtypeStruct(dims, jnp.float32)
+
+
 def flipped(value, axis, bit):
     return lax.ppermute(value, axis, [(i, i ^ bit) for i in range(lax.axis_size(axis))])
 
 
 def two_section_body(bounds, saved_inputs, w_in, w_out, top_grad):
-    pipe_index = lax.axis_index("pipe")
-    section_index = lax.axis_index("section")
-    column = lax.axis_index("tensor")
-    relay = pipe_index // 2
-    half = section_index % 2
-    left = section_index // 2 == 0
-    boundary = lax.dynamic_index_in_dim(bounds, relay, 0, keepdims=False)
-    short = boundary[1] - boundary[0] == 2
     saved = saved_inputs[0, 0]
     proj_in = w_in[0, 0]
     proj_out = w_out[0, 0]
     tops = top_grad[0]
     model = saved.shape[2]
-    inner = proj_in.shape[2]
 
     def across(value):
         return flipped(value, "pipe", 2)
@@ -521,29 +589,47 @@
     grad_early = by_role(bounds, grad_other, own_top)
     accs = middle_partials(bounds, grad_early, core_swap(grad_early), unit_part, value, proj_out)
     other_late = core_swap(late)
-    in_send, in_keep, out_send, out_keep = late_partials(
+    outs = late_partials(
         bounds, late, other_late, own[1], partner[1], early_part, accs, proj_in, proj_out
     )
-    in_landed = column_swap(in_send)
-    out_landed = half_swap(out_send)
-    in_sum = (in_keep + in_landed.astype(jnp.float32)).reshape(2, -1, inner // 2)
-    out_sum = out_keep + out_landed.astype(jnp.float32)
-    in_mine = lax.dynamic_index_in_dim(in_sum, half, 0, keepdims=False)
-    in_next = lax.dynamic_index_in_dim(in_sum, 1 - half, 0, keepdims=False)
-    out_mine = lax.dynamic_slice_in_dim(out_sum, column * (model // 2), model // 2, 1)
-    out_next = lax.dynamic_slice_in_dim(out_sum, (1 - column) * (model // 2), model // 2, 1)
-    in_landed = half_swap(in_next.astype(jnp.bfloat16))
-    out_landed = column_swap(out_next.astype(jnp.bfloat16))
-    results = []
-    for mine, landed in ((in_mine, in_landed), (out_mine, out_landed)):
-        total = (mine + landed.astype(jnp.float32)).reshape(2, -1, mine.shape[1])
-        own = lax.dynamic_index_in_dim(total, relay, 0, keepdims=False)
-        sent = lax.dynamic_index_in_dim(total, 1 - relay, 0, keepdims=False).astype(jnp.bfloat16)
-        got = across(sent)
-        onward = section_swap(jnp.where(short, got, own.astype(jnp.bfloat16)))
-        lower = jnp.where(short, own, got.astype(jnp.float32))
-        results.append(jnp.where(left, lower, onward.astype(jnp.float32))[None])
-    return tuple(results)
+    groups = (outs[:4], outs[4:])
+    landed = [(column_swap(in_send), half_swap(out_send)) for in_send, _, out_send, _ in groups]
+    rows = model // (2 * BLOCKS)
+    block = (rows, model // 2)
+    totals = []
+    for (_, in_keep, _, out_keep), (in_land, out_land), kind in zip(
+        groups, landed, (low_shape, full_shape)
+    ):
+        in_mine, in_next, out_mine, out_next = small_call(
+            first_add_kernel,
+            (bounds, in_keep, in_land, out_keep, out_land),
+            (full_shape(*block), low_shape(*block)) * 2,
+        )
+        in_land, out_land = half_swap(in_next), column_swap(out_next)
+        totals.append(
+            small_call(
+                second_add_kernel,
+                (in_mine, in_land, out_mine, out_land),
+                kind(2, *block),
+                use_bounds=False,
+            )
+        )
+    far, near = totals
+    got = across(far)
+    in_give, out_give, lower = small_call(
+        hand_on_kernel,
+        (bounds, near, got),
+        (low_shape(*block), low_shape(*block), full_shape(2, *block)),
+    )
+    return tuple(
+        small_call(
+            functools.partial(result_kernel, which),
+            (lower, section_swap(give)),
+            full_shape(1, *block),
+            use_bounds=False,
+        )
+        for which, give in enumerate((in_give, out_give))
+    )
 
 
 def body(bounds, saved_inputs, w_in, w_out, top_grad):

time: 76.4 us -> 74.4 us (0.974)
  other arithmetic: 4.1 us -> 0 us
  Pallas kernels: 10.3 us -> 13.8 us
  between operations: 2.14 us -> 0.8 us
    pallas_call x1 -> x8, Pallas kernels: 2.09 us -> 5.62 us  [the longest x7 3.47 us: small_call(): pl.pallas_call(kernel, out_shape=shapes, in_specs=([SMEM] if use_bounds e...]
    add x4 -> x0, other arithmetic: 2.57 us -> none  [the longest x1 1.22 us: two_section_body(): out_sum = out_keep + out_landed.astype(jnp.float32)]
    broadcast_in_dim x2 -> x0, other arithmetic: 1.49 us -> none  [two_section_body(): results.append(jnp.where(left, lower, onward.astype(jnp.float32))[None])]
    ppermute x15 -> x18, waiting for transfers between devices: 36.7 us -> 37.2 us  [flipped(): lax.ppermute(value, axis, [(i, i ^ bit) for i in range(lax.axis_size(axis...]
    ppermute x15 -> x18, starting transfers between devices: 21 us -> 21.2 us  [flipped(): lax.ppermute(value, axis, [(i, i ^ bit) for i in range(lax.axis_size(axis...]
  transfers between devices with their start and end apart: 15 -> 18, of which waited for: 9 -> 10; matrix products, arithmetic and copies ran while one was open for 5% -> 0% of each run, Pallas kernels for 10% -> 13%
where the time goes in v5:
time: 74.4 us; the launch traced here: 74.2 us
  waiting for transfers between devices  37.2 us (50%)
  starting transfers between devices  21.2 us (28%)
  Pallas kernels  13.8 us (19%)
  local copies, waits for them, and re-layouts  1.19 us (2%)
  between operations  0.8 us (1%)
    ppermute x18, waiting for transfers between devices, flipped(): lax.ppermute(value, axis, [(i, i ^ bit) for i in range(lax.axis_size(axis...  37.2 us
    ppermute x18, starting transfers between devices, flipped(): lax.ppermute(value, axis, [(i, i ^ bit) for i in range(lax.axis_size(axis...  21.2 us
    pallas_call x7, Pallas kernels, small_call(): pl.pallas_call(kernel, out_shape=shapes, in_specs=([SMEM] if use_bounds e...  3.47 us
    pallas_call x1, Pallas kernels, early_factors(): pl.pallas_call(early_kernel, out_shape=(jax.ShapeDtypeStruct((2 * rows, m...  2.34 us
    pallas_call x1, Pallas kernels, chain(): pl.pallas_call(chain_kernel, out_shape=jax.ShapeDtypeStruct((rows, model)...  2.21 us
    pallas_call x1, Pallas kernels, late_partials(): pl.pallas_call(late_kernel, out_shape=(jax.ShapeDtypeStruct((part // 2, i...  2.15 us
    pallas_call x1, Pallas kernels, middle_partials(): pl.pallas_call(middle_kernel, out_shape=(jax.ShapeDtypeStruct((part, inne...  1.87 us
  transfers between devices with their start and end apart: 18, of which 10 were waited for; matrix products, arithmetic and copies ran while one was open for 0% of the time, Pallas kernels for 13%

profile of v5, /device:TPU:0, one launch (start us, length us, event | category | flops | bytes accessed | tf_op | source)
XLA Modules:
  0.0 74.2 jit_solution(5227942141924263315)
XLA Ops:
  0.7 0.6 copy-done.4
  1.3 0.4 copy-done.2
  1.7 0.2 copy-done.3
  1.9 0.6 staged.1
  2.5 3.1 %collective-permute-start = (bf16[128,1024]{1,0:T(8,128)(2,1)S(1)}, bf16[128,1024]{1,0:T(8,128)(2,1)S(1)}, u32[]{:S(2)}, u32[]{:S(2)}) collective-permute-start(bf16[128,1024]{1,0:T(8,128)(2,1)S(1)} %get-tuple-element.29), channel_id=1, source_target_pairs={{0,16},{8,24},{16,0},{24,8},{1,17},{9,25},{17,1},{25,9},{2,18},{10... | collective-permute-start | bytes 786440 | tf_op jit(solution)/shard_map/ppermute | solution.py:555
  5.5 2.2 %chain.1.full_part = bf16[128,1024]{1,0:T(8,128)(2,1)S(1)} custom-call(s32[2,3]{1,0:T(2,128)S(1)} %copy-done.4, bf16[2,128,1024]{2,1,0:T(8,128)(2,1)S(1)} %bitcast.12, bf16[2,128,1024]{2,1,0:T(8,128)(2,1)S(1)} %bitcast.14, bf16[2,1024,1024]{2,1,0:T(8,128)(2,1)S(1)} %bitcast.8, bf16[2,1024,1024]{2,1,0:T(8,128)(2,1)S(1)} %bitcast.4), custom_call_target="tpu_custom_call" | custom-call | flops 536870912 | bytes 4194304 | tf_op jit(solution)/shard_map/chain/pallas_call | solution.py:240
  7.8 2.8 %collective-permute-start.5 = (bf16[128,1024]{1,0:T(8,128)(2,1)S(1)}, bf16[128,1024]{1,0:T(8,128)(2,1)S(1)}, u32[]{:S(2)}, u32[]{:S(2)}) collective-permute-start(bf16[128,1024]{1,0:T(8,128)(2,1)S(1)} %chain.1.full_part), channel_id=1, source_target_pairs={{0,16},{8,24},{16,0},{24,8},{1,17},{9,25},{17,1},{25,9},{2,18},{10... | collective-permute-start | bytes 786440 | tf_op jit(solution)/shard_map/ppermute | solution.py:555
  10.6 1.8 %collective-permute-done.short_part.e2 = bf16[128,1024]{1,0:T(8,128)(2,1)S(1)} collective-permute-done((bf16[128,1024]{1,0:T(8,128)(2,1)S(1)}, bf16[128,1024]{1,0:T(8,128)(2,1)S(1)}, u32[]{:S(2)}, u32[]{:S(2)}) %collective-permute-start) | collective-permute-done | bytes 262176 | tf_op jit(solution)/shard_map/ppermute | solution.py:555
  12.4 0.6 by_role.2
  13.0 2.9 %collective-permute-start.1 = (bf16[128,1024]{1,0:T(8,128)(2,1)S(1)}, bf16[128,1024]{1,0:T(8,128)(2,1)S(1)}, u32[]{:S(2)}, u32[]{:S(2)}) collective-permute-start(bf16[128,1024]{1,0:T(8,128)(2,1)S(1)} %by_role.2), channel_id=1, source_target_pairs={{0,4},{2,6},{4,0},{6,2},{1,5},{3,7},{5,1},{7,3},{8,12},{10,14},{12... | collective-permute-start | bytes 786440 | tf_op jit(solution)/shard_map/ppermute | solution.py:555
  15.9 0.0 collective-permute-start.4
  15.9 0.5 collective-permute-start.3
  16.4 1.1 %collective-permute-done.5.full_part = bf16[128,1024]{1,0:T(8,128)(2,1)S(1)} collective-permute-done((bf16[128,1024]{1,0:T(8,128)(2,1)S(1)}, bf16[128,1024]{1,0:T(8,128)(2,1)S(1)}, u32[]{:S(2)}, u32[]{:S(2)}) %collective-permute-start.5) | collective-permute-done | bytes 262176 | tf_op jit(solution)/shard_map/ppermute | solution.py:555
  17.5 0.6 by_role.3.e3
  18.1 0.1 collective-permute-start.6
  18.1 8.4 %collective-permute-done.1.late = bf16[128,1024]{1,0:T(8,128)(2,1)S(1)} collective-permute-done((bf16[128,1024]{1,0:T(8,128)(2,1)S(1)}, bf16[128,1024]{1,0:T(8,128)(2,1)S(1)}, u32[]{:S(2)}, u32[]{:S(2)}) %collective-permute-start.1) | collective-permute-done | bytes 262176 | tf_op jit(solution)/shard_map/ppermute | solution.py:555
  26.5 0.0 collective-permute-start.2
  26.5 0.0 collective-permute-done.4.f1
  26.5 0.0 collective-permute-done.3.f2
  26.5 2.3 %early.1 = (bf16[256,1024]{1,0:T(8,128)(2,1)S(1)}, bf16[256,512]{1,0:T(8,128)(2,1)S(1)}, bf16[256,512]{1,0:T(8,128)(2,1)S(1)}) custom-call(s32[2,3]{1,0:T(2,128)S(1)} %copy-done.4, bf16[128,1024]{1,0:T(8,128)(2,1)S(1)} %get-tuple-element.30.e1, bf16[128,1024]{1,0:T(8,128)(2,1)S(1)} %collective-permute-done.short_part.e2, ...), custom_call_target="tpu_custom_call" | custom-call | flops 536870912 | bytes 3145728 | tf_op jit(solution)/shard_map/early/pallas_call | solution.py:367
  28.9 1.9 %middle.1 = (f32[512,1024]{1,0:T(8,128)S(1)}, f32[512,1024]{1,0:T(8,128)S(1)}) custom-call(s32[2,3]{1,0:T(2,128)S(1)} %copy-done.4, bf16[128,1024]{1,0:T(8,128)(2,1)S(1)} %by_role.3.e3, bf16[128,1024]{1,0:T(8,128)(2,1)S(1)} %collective-permute-done.6.f3, bf16[256,512]{1,0:T(8,128)(2,1)S(1)} %get-tuple-element.33.unit_part, ...), custom_call_target="tpu_custom_call" | custom-call | flops 1073741824 | bytes 3145728 | tf_op jit(solution)/shard_map/middle/pallas_call | solution.py:397
  30.7 0.0 collective-permute-done.2.flate
  30.8 2.2 %late.1 = (bf16[256,512]{1,0:T(8,128)(2,1)S(1)}, f32[256,512]{1,0:T(8,128)S(1)}, bf16[128,1024]{1,0:T(8,128)(2,1)S(1)}, f32[128,1024]{1,0:T(8,128)S(1)}, bf16[25...) custom-call(s32[2,3]{1,0:T(2,128)S(1)} %copy-done.4, ...), custom_call_target="tpu_custom_call" | custom-call | flops 1073741824 | bytes 3145728 | tf_op jit(solution)/shard_map/late/pallas_call | solution.py:458
  32.9 1.5 %collective-permute-start.11 = (bf16[256,512]{1,0:T(8,128)(2,1)S(1)}, bf16[256,512]{1,0:T(8,128)(2,1)S(1)}, u32[]{:S(2)}, u32[]{:S(2)}) collective-permute-start(bf16[256,512]{1,0:T(8,128)(2,1)S(1)} %get-tuple-element.46), channel_id=1, source_target_pairs={{0,1},{1,0},{2,3},{3,2},{4,5},{5,4},{6,7},{7,6},{8,9},{9,8},{10,11... | collective-permute-start | bytes 786440 | tf_op jit(solution)/shard_map/ppermute | solution.py:555
  34.4 0.7 collective-permute-start.12
  35.1 0.5 collective-permute-start.7
  35.6 1.4 %collective-permute-start.8 = (bf16[128,1024]{1,0:T(8,128)(2,1)S(1)}, bf16[128,1024]{1,0:T(8,128)(2,1)S(1)}, u32[]{:S(2)}, u32[]{:S(2)}) collective-permute-start(bf16[128,1024]{1,0:T(8,128)(2,1)S(1)} %get-tuple-element.40), channel_id=1, source_target_pairs={{0,2},{2,0},{4,6},{6,4},{1,3},{3,1},{5,7},{7,5},{8,10},{10,8},{12,... | collective-permute-start | bytes 786440 | tf_op jit(solution)/shard_map/ppermute | solution.py:555
  37.0 5.1 %collective-permute-done.11.in_land = bf16[256,512]{1,0:T(8,128)(2,1)S(1)} collective-permute-done((bf16[256,512]{1,0:T(8,128)(2,1)S(1)}, bf16[256,512]{1,0:T(8,128)(2,1)S(1)}, u32[]{:S(2)}, u32[]{:S(2)}) %collective-permute-start.11) | collective-permute-done | bytes 262176 | tf_op jit(solution)/shard_map/ppermute | solution.py:555
  42.2 1.4 %collective-permute-done.12.out_land = bf16[128,1024]{1,0:T(8,128)(2,1)S(1)} collective-permute-done((bf16[128,1024]{1,0:T(8,128)(2,1)S(1)}, bf16[128,1024]{1,0:T(8,128)(2,1)S(1)}, u32[]{:S(2)}, u32[]{:S(2)}) %collective-permute-start.12) | collective-permute-done | bytes 262176 | tf_op jit(solution)/shard_map/ppermute | solution.py:555
  43.6 0.6 shard_map.70
  44.2 0.7 %collective-permute-start.13 = (bf16[128,512]{1,0:T(8,128)(2,1)S(1)}, bf16[128,512]{1,0:T(8,128)(2,1)S(1)}, u32[]{:S(2)}, u32[]{:S(2)}) collective-permute-start(bf16[128,512]{1,0:T(8,128)(2,1)S(1)} %get-tuple-element.50), channel_id=1, source_target_pairs={{0,2},{2,0},{4,6},{6,4},{1,3},{3,1},{5,7},{7,5},{8,10},{10,8},{12,... | collective-permute-start | bytes 393224 | tf_op jit(solution)/shard_map/ppermute | solution.py:555
  45.0 0.5 collective-permute-start.14
  45.5 5.7 %collective-permute-done.13.in_land = bf16[128,512]{1,0:T(8,128)(2,1)S(1)} collective-permute-done((bf16[128,512]{1,0:T(8,128)(2,1)S(1)}, bf16[128,512]{1,0:T(8,128)(2,1)S(1)}, u32[]{:S(2)}, u32[]{:S(2)}) %collective-permute-start.13) | collective-permute-done | bytes 131104 | tf_op jit(solution)/shard_map/ppermute | solution.py:555
  51.3 0.0 collective-permute-done.14.out_land
  51.3 0.1 shard_map.71
  51.3 1.6 %collective-permute-start.15 = (bf16[2,128,512]{2,1,0:T(8,128)(2,1)S(1)}, bf16[2,128,512]{2,1,0:T(8,128)(2,1)S(1)}, u32[]{:S(2)}, u32[]{:S(2)}) collective-permute-start(bf16[2,128,512]{2,1,0:T(8,128)(2,1)S(1)} %shard_map.71), channel_id=1, source_target_pairs={{0,16},{8,24},{16,0},{24,8},{1,17},{9,25},{17,1},{25,9},{2,18},{10... | collective-permute-start | bytes 786440 | tf_op jit(solution)/shard_map/ppermute | solution.py:555
  53.0 0.6 shard_map.68
  53.6 0.7 collective-permute-start.9
  54.4 0.5 collective-permute-start.10
  54.9 3.8 %collective-permute-done.9.in_land = bf16[128,512]{1,0:T(8,128)(2,1)S(1)} collective-permute-done((bf16[128,512]{1,0:T(8,128)(2,1)S(1)}, bf16[128,512]{1,0:T(8,128)(2,1)S(1)}, u32[]{:S(2)}, u32[]{:S(2)}) %collective-permute-start.9) | collective-permute-done | bytes 131104 | tf_op jit(solution)/shard_map/ppermute | solution.py:555
  58.7 0.7 collective-permute-done.10.out_land
  59.4 0.6 shard_map.72
  60.0 3.4 %collective-permute-start.16 = (bf16[128,512]{1,0:T(8,128)(2,1)S(1)}, bf16[128,512]{1,0:T(8,128)(2,1)S(1)}, u32[]{:S(2)}, u32[]{:S(2)}) collective-permute-start(bf16[128,512]{1,0:T(8,128)(2,1)S(1)} %get-tuple-element.54), channel_id=1, source_target_pairs={{0,4},{2,6},{4,0},{6,2},{1,5},{3,7},{5,1},{7,3},{8,12},{10,14},{12... | collective-permute-start | bytes 393224 | tf_op jit(solution)/shard_map/ppermute | solution.py:555
  63.5 0.1 collective-permute-start.17
  63.6 8.4 %collective-permute-done.16.landed = bf16[128,512]{1,0:T(8,128)(2,1)S(1)} collective-permute-done((bf16[128,512]{1,0:T(8,128)(2,1)S(1)}, bf16[128,512]{1,0:T(8,128)(2,1)S(1)}, u32[]{:S(2)}, u32[]{:S(2)}) %collective-permute-start.16) | collective-permute-done | bytes 131104 | tf_op jit(solution)/shard_map/ppermute | solution.py:555
  72.0 0.7 shard_map.73
  72.7 0.8 %collective-permute-done.17.landed = bf16[128,512]{1,0:T(8,128)(2,1)S(1)} collective-permute-done((bf16[128,512]{1,0:T(8,128)(2,1)S(1)}, bf16[128,512]{1,0:T(8,128)(2,1)S(1)}, u32[]{:S(2)}, u32[]{:S(2)}) %collective-permute-start.17) | collective-permute-done | bytes 131104 | tf_op jit(solution)/shard_map/ppermute | solution.py:555
  73.5 0.7 shard_map.74
  (13 shorter events, 0.1 us)
Async XLA Ops:
  0.6 0.7 copy-start.4
  0.6 1.0 %copy-start.2 = (bf16[1,2,128,1024]{3,2,1,0:T(8,128)(2,1)S(1)}, bf16[1,2,128,1024]{3,2,1,0:T(8,128)(2,1)}, u32[]{:S(2)}) copy-start(bf16[1,2,128,1024]{3,2,1,0:T(8,128)(2,1)} %param.9) | copy-start | bytes 1572868
  0.6 1.2 %copy-start.3 = (bf16[1,1,2,128,1024]{4,3,2,1,0:T(8,128)(2,1)S(1)}, bf16[1,1,2,128,1024]{4,3,2,1,0:T(8,128)(2,1)}, u32[]{:S(2)}) copy-start(bf16[1,1,2,128,1024]{4,3,2,1,0:T(8,128)(2,1)} %param.6) | copy-start | bytes 1572868
  1.8 3.7 %copy-start = (bf16[1,1,2,1024,1024]{4,3,2,1,0:T(8,128)(2,1)S(1)}, bf16[1,1,2,1024,1024]{4,3,2,1,0:T(8,128)(2,1)}, u32[]{:S(2)}) copy-start(bf16[1,1,2,1024,1024]{4,3,2,1,0:T(8,128)(2,1)} %param.8) | copy-start | bytes 12582916
  1.8 3.7 %copy-start.1 = (bf16[1,1,2,1024,1024]{4,3,2,1,0:T(8,128)(2,1)S(1)}, bf16[1,1,2,1024,1024]{4,3,2,1,0:T(8,128)(2,1)}, u32[]{:S(2)}) copy-start(bf16[1,1,2,1024,1024]{4,3,2,1,0:T(8,128)(2,1)} %param.7) | copy-start | bytes 12582916
  2.5 9.9 %collective-permute-start = (bf16[128,1024]{1,0:T(8,128)(2,1)S(1)}, bf16[128,1024]{1,0:T(8,128)(2,1)S(1)}, u32[]{:S(2)}, u32[]{:S(2)}) collective-permute-start(bf16[128,1024]{1,0:T(8,128)(2,1)S(1)} %get-tuple-element.29), channel_id=1, source_target_pairs={{0,16},{8,24},{16,0},{24,8},{1,17},{9,25},{17,1},{25,9},{2,18},{10... | collective-permute-start | bytes 786440 | tf_op jit(solution)/shard_map/ppermute | solution.py:555
  7.8 9.7 %collective-permute-start.5 = (bf16[128,1024]{1,0:T(8,128)(2,1)S(1)}, bf16[128,1024]{1,0:T(8,128)(2,1)S(1)}, u32[]{:S(2)}, u32[]{:S(2)}) collective-permute-start(bf16[128,1024]{1,0:T(8,128)(2,1)S(1)} %chain.1.full_part), channel_id=1, source_target_pairs={{0,16},{8,24},{16,0},{24,8},{1,17},{9,25},{17,1},{25,9},{2,18},{10... | collective-permute-start | bytes 786440 | tf_op jit(solution)/shard_map/ppermute | solution.py:555
  13.0 13.5 %collective-permute-start.1 = (bf16[128,1024]{1,0:T(8,128)(2,1)S(1)}, bf16[128,1024]{1,0:T(8,128)(2,1)S(1)}, u32[]{:S(2)}, u32[]{:S(2)}) collective-permute-start(bf16[128,1024]{1,0:T(8,128)(2,1)S(1)} %by_role.2), channel_id=1, source_target_pairs={{0,4},{2,6},{4,0},{6,2},{1,5},{3,7},{5,1},{7,3},{8,12},{10,14},{12... | collective-permute-start | bytes 786440 | tf_op jit(solution)/shard_map/ppermute | solution.py:555
  15.9 10.6 %collective-permute-start.4 = (bf16[128,1024]{1,0:T(8,128)(2,1)S(1)}, bf16[128,1024]{1,0:T(8,128)(2,1)S(1)}, u32[]{:S(2)}, u32[]{:S(2)}) collective-permute-start(bf16[128,1024]{1,0:T(8,128)(2,1)S(1)} %get-tuple-element.30.e1), channel_id=1, source_target_pairs={{0,8},{8,0},{16,24},{24,16},{1,9},{9,1},{17,25},{25,17},{2,10},{10... | collective-permute-start | bytes 786440 | tf_op jit(solution)/shard_map/ppermute | solution.py:555
  15.9 10.6 %collective-permute-start.3 = (bf16[128,1024]{1,0:T(8,128)(2,1)S(1)}, bf16[128,1024]{1,0:T(8,128)(2,1)S(1)}, u32[]{:S(2)}, u32[]{:S(2)}) collective-permute-start(bf16[128,1024]{1,0:T(8,128)(2,1)S(1)} %collective-permute-done.short_part.e2), channel_id=1, source_target_pairs={{0,8},{8,0},{16,24},{24,16},{1,9},{9,1},{17,25},{25,17},{2,10},{10... | collective-permute-start | bytes 786440 | tf_op jit(solution)/shard_map/ppermute | solution.py:555
  18.1 10.8 %collective-permute-start.6 = (bf16[128,1024]{1,0:T(8,128)(2,1)S(1)}, bf16[128,1024]{1,0:T(8,128)(2,1)S(1)}, u32[]{:S(2)}, u32[]{:S(2)}) collective-permute-start(bf16[128,1024]{1,0:T(8,128)(2,1)S(1)} %by_role.3.e3), channel_id=1, source_target_pairs={{0,8},{8,0},{16,24},{24,16},{1,9},{9,1},{17,25},{25,17},{2,10},{10... | collective-permute-start | bytes 786440 | tf_op jit(solution)/shard_map/ppermute | solution.py:555
  26.5 4.2 %collective-permute-start.2 = (bf16[128,1024]{1,0:T(8,128)(2,1)S(1)}, bf16[128,1024]{1,0:T(8,128)(2,1)S(1)}, u32[]{:S(2)}, u32[]{:S(2)}) collective-permute-start(bf16[128,1024]{1,0:T(8,128)(2,1)S(1)} %collective-permute-done.1.late), channel_id=1, source_target_pairs={{0,8},{8,0},{16,24},{24,16},{1,9},{9,1},{17,25},{25,17},{2,10},{10... | collective-permute-start | bytes 786440 | tf_op jit(solution)/shard_map/ppermute | solution.py:555
  32.9 9.2 %collective-permute-start.11 = (bf16[256,512]{1,0:T(8,128)(2,1)S(1)}, bf16[256,512]{1,0:T(8,128)(2,1)S(1)}, u32[]{:S(2)}, u32[]{:S(2)}) collective-permute-start(bf16[256,512]{1,0:T(8,128)(2,1)S(1)} %get-tuple-element.46), channel_id=1, source_target_pairs={{0,1},{1,0},{2,3},{3,2},{4,5},{5,4},{6,7},{7,6},{8,9},{9,8},{10,11... | collective-permute-start | bytes 786440 | tf_op jit(solution)/shard_map/ppermute | solution.py:555
  34.4 9.2 %collective-permute-start.12 = (bf16[128,1024]{1,0:T(8,128)(2,1)S(1)}, bf16[128,1024]{1,0:T(8,128)(2,1)S(1)}, u32[]{:S(2)}, u32[]{:S(2)}) collective-permute-start(bf16[128,1024]{1,0:T(8,128)(2,1)S(1)} %get-tuple-element.48), channel_id=1, source_target_pairs={{0,2},{2,0},{4,6},{6,4},{1,3},{3,1},{5,7},{7,5},{8,10},{10,8},{12,... | collective-permute-start | bytes 786440 | tf_op jit(solution)/shard_map/ppermute | solution.py:555
  35.1 17.9 %collective-permute-start.7 = (bf16[256,512]{1,0:T(8,128)(2,1)S(1)}, bf16[256,512]{1,0:T(8,128)(2,1)S(1)}, u32[]{:S(2)}, u32[]{:S(2)}) collective-permute-start(bf16[256,512]{1,0:T(8,128)(2,1)S(1)} %get-tuple-element.38), channel_id=1, source_target_pairs={{0,1},{1,0},{2,3},{3,2},{4,5},{5,4},{6,7},{7,6},{8,9},{9,8},{10,11... | collective-permute-start | bytes 786440 | tf_op jit(solution)/shard_map/ppermute | solution.py:555
  35.6 17.4 %collective-permute-start.8 = (bf16[128,1024]{1,0:T(8,128)(2,1)S(1)}, bf16[128,1024]{1,0:T(8,128)(2,1)S(1)}, u32[]{:S(2)}, u32[]{:S(2)}) collective-permute-start(bf16[128,1024]{1,0:T(8,128)(2,1)S(1)} %get-tuple-element.40), channel_id=1, source_target_pairs={{0,2},{2,0},{4,6},{6,4},{1,3},{3,1},{5,7},{7,5},{8,10},{10,8},{12,... | collective-permute-start | bytes 786440 | tf_op jit(solution)/shard_map/ppermute | solution.py:555
  44.2 7.0 %collective-permute-start.13 = (bf16[128,512]{1,0:T(8,128)(2,1)S(1)}, bf16[128,512]{1,0:T(8,128)(2,1)S(1)}, u32[]{:S(2)}, u32[]{:S(2)}) collective-permute-start(bf16[128,512]{1,0:T(8,128)(2,1)S(1)} %get-tuple-element.50), channel_id=1, source_target_pairs={{0,2},{2,0},{4,6},{6,4},{1,3},{3,1},{5,7},{7,5},{8,10},{10,8},{12,... | collective-permute-start | bytes 393224 | tf_op jit(solution)/shard_map/ppermute | solution.py:555
  45.0 6.3 %collective-permute-start.14 = (bf16[128,512]{1,0:T(8,128)(2,1)S(1)}, bf16[128,512]{1,0:T(8,128)(2,1)S(1)}, u32[]{:S(2)}, u32[]{:S(2)}) collective-permute-start(bf16[128,512]{1,0:T(8,128)(2,1)S(1)} %get-tuple-element.52), channel_id=1, source_target_pairs={{0,1},{1,0},{2,3},{3,2},{4,5},{5,4},{6,7},{7,6},{8,9},{9,8},{10,11... | collective-permute-start | bytes 393224 | tf_op jit(solution)/shard_map/ppermute | solution.py:555
  51.3 8.1 %collective-permute-start.15 = (bf16[2,128,512]{2,1,0:T(8,128)(2,1)S(1)}, bf16[2,128,512]{2,1,0:T(8,128)(2,1)S(1)}, u32[]{:S(2)}, u32[]{:S(2)}) collective-permute-start(bf16[2,128,512]{2,1,0:T(8,128)(2,1)S(1)} %shard_map.71), channel_id=1, source_target_pairs={{0,16},{8,24},{16,0},{24,8},{1,17},{9,25},{17,1},{25,9},{2,18},{10... | collective-permute-start | bytes 786440 | tf_op jit(solution)/shard_map/ppermute | solution.py:555
  53.6 5.0 %collective-permute-start.9 = (bf16[128,512]{1,0:T(8,128)(2,1)S(1)}, bf16[128,512]{1,0:T(8,128)(2,1)S(1)}, u32[]{:S(2)}, u32[]{:S(2)}) collective-permute-start(bf16[128,512]{1,0:T(8,128)(2,1)S(1)} %get-tuple-element.42), channel_id=1, source_target_pairs={{0,2},{2,0},{4,6},{6,4},{1,3},{3,1},{5,7},{7,5},{8,10},{10,8},{12,... | collective-permute-start | bytes 393224 | tf_op jit(solution)/shard_map/ppermute | solution.py:555
  54.4 5.0 %collective-permute-start.10 = (bf16[128,512]{1,0:T(8,128)(2,1)S(1)}, bf16[128,512]{1,0:T(8,128)(2,1)S(1)}, u32[]{:S(2)}, u32[]{:S(2)}) collective-permute-start(bf16[128,512]{1,0:T(8,128)(2,1)S(1)} %get-tuple-element.44), channel_id=1, source_target_pairs={{0,1},{1,0},{2,3},{3,2},{4,5},{5,4},{6,7},{7,6},{8,9},{9,8},{10,11... | collective-permute-start | bytes 393224 | tf_op jit(solution)/shard_map/ppermute | solution.py:555
  60.0 11.9 %collective-permute-start.16 = (bf16[128,512]{1,0:T(8,128)(2,1)S(1)}, bf16[128,512]{1,0:T(8,128)(2,1)S(1)}, u32[]{:S(2)}, u32[]{:S(2)}) collective-permute-start(bf16[128,512]{1,0:T(8,128)(2,1)S(1)} %get-tuple-element.54), channel_id=1, source_target_pairs={{0,4},{2,6},{4,0},{6,2},{1,5},{3,7},{5,1},{7,3},{8,12},{10,14},{12... | collective-permute-start | bytes 393224 | tf_op jit(solution)/shard_map/ppermute | solution.py:555
  63.5 10.0 %collective-permute-start.17 = (bf16[128,512]{1,0:T(8,128)(2,1)S(1)}, bf16[128,512]{1,0:T(8,128)(2,1)S(1)}, u32[]{:S(2)}, u32[]{:S(2)}) collective-permute-start(bf16[128,512]{1,0:T(8,128)(2,1)S(1)} %get-tuple-element.55), channel_id=1, source_target_pairs={{0,4},{2,6},{4,0},{6,2},{1,5},{3,7},{5,1},{7,3},{8,12},{10,14},{12... | collective-permute-start | bytes 393224 | tf_op jit(solution)/shard_map/ppermute | solution.py:555

commit v6 on v4

--- a/solution.py
+++ b/solution.py
@@ -314,6 +314,11 @@
     )(bounds, full_part, short_part)
 
 
+def value_kernel(saved, w_in, value):
+    unit = norm_rows(saved[0])[0].astype(jnp.bfloat16)
+    value[...] = jnp.dot(unit, w_in[0], preferred_element_type=jnp.float32).astype(jnp.bfloat16)
+
+
 BLOCKS = 4
 
 
@@ -323,14 +328,21 @@
     unit[rows:, :] = norm_rows(second[...])[0].astype(jnp.bfloat16)
 
 
-def lane_block(j, core, lanes):
-    return pl.ds(pl.multiple_of((2 * j + core) * lanes, lanes), lanes)
+def lane_block(j, place, lanes):
+    owner = place.relay if j // 2 else 1 - place.relay
+    return pl.ds(pl.multiple_of((4 * (j % 2) + 2 * owner + place.core) * lanes, lanes), lanes)
+
+
+def unit_columns(place, unit, unit_part):
+    lanes = unit.shape[1] // (2 * BLOCKS)
+    for j in range(BLOCKS):
+        unit_part[:, j * lanes : (j + 1) * lanes] = unit[:, lane_block(j, place, lanes)]
 
 
 def core_columns(place, unit, w_in, unit_part, value):
     lanes = unit.shape[1] // (2 * BLOCKS)
     for j in range(BLOCKS):
-        block = lane_block(j, place.core, lanes)
+        block = lane_block(j, place, lanes)
         where = pl.ds(j * lanes, lanes)
         unit_part[:, where] = unit[:, block]
         value[:, where] = jnp.dot(
@@ -340,14 +352,14 @@
 
 def early_kernel(bounds, e1, e2, f1, f2, w_in, w_out, early_part, unit_part, value, unit):
     place = Place(bounds)
-    part = unit_part.shape[1]
 
     @pl.when(jnp.logical_not(place.short))
     def _():
         put_unit(unit, e2, f2)
-        core_columns(place, unit, w_in, unit_part, value)
+        unit_columns(place, unit, unit_part)
+        value[...] = jnp.zeros_like(value)
         put_unit(unit, e1, f1)
-        core_columns(place, unit, w_in, early_part.at[:, :part], early_part.at[:, part:])
+        unit_columns(place, unit, early_part)
 
     @pl.when(place.short)
     def _():
@@ -407,71 +419,181 @@
     )(bounds, e3, f3, unit_part, value, w_out)
 
 
-def late_kernel(
-    bounds, late, flate, e2, f2, early_part, in_acc, out_acc, w_in, w_out,
-    in_send, in_keep, out_send, out_keep,
-    unit, unit_part, value, grads, err,
+def split_sums(place, left_part, right_part, acc, x_send, x_keep, z_send, z_keep):
+    group = left_part.shape[1] // 2
+    block = group // 2
+    cols = right_part.shape[1] // 2
+
+    def sums(rows_of, cols_of):
+        new = tn_dot(left_part[:, rows_of], right_part[:, cols_of])
+        return new if acc is None else acc[rows_of, cols_of] + new
+
+    far = slice(0, group)
+    every = slice(None)
+    mine = pl.ds(pl.multiple_of(place.column * cols, cols), cols)
+    other = pl.ds(pl.multiple_of((1 - place.column) * cols, cols), cols)
+    kept = pl.ds(pl.multiple_of(group + place.half * block, block), block)
+    sent = pl.ds(pl.multiple_of(group + (1 - place.half) * block, block), block)
+    x_send[...] = sums(far, other).astype(jnp.bfloat16)
+    x_keep[...] = sums(far, mine)
+    z_send[...] = sums(sent, every).astype(jnp.bfloat16)
+    z_keep[...] = sums(kept, every)
+
+
+def late_in_kernel(
+    bounds, late, flate, early_part, in_acc, w_out, x_send, x_keep, z_send, z_keep, unit, unit_part, err,
 ):
     place = Place(bounds)
-    half, column = place.half, place.column
-    rows = late.shape[0]
     part = unit_part.shape[1]
 
     @pl.when(jnp.logical_not(place.short))
     def _():
-        grads[:rows, :] = late[...]
-        grads[rows:, :] = flate[...]
-        err[...] = nt_dot(grads[...], w_out[place.slot]).astype(jnp.bfloat16)
+        grads = jnp.concatenate([late[...], flate[...]], axis=0)
+        err[...] = nt_dot(grads, w_out[place.slot]).astype(jnp.bfloat16)
         unit_part[...] = early_part[:, :part]
-        value[...] = early_part[:, part:]
 
     @pl.when(place.short)
     def _():
         put_unit(unit, late, flate)
+        unit_columns(place, unit, unit_part)
+        err[...] = early_part[...]
+
+    split_sums(place, unit_part, err, in_acc, x_send, x_keep, z_send, z_keep)
+
+
+def late_out_kernel(
+    bounds, unit, e2, f2, out_acc, w_in, late, flate, low, flow, up, fup,
+    x_send, x_keep, z_send, z_keep, value, grads, unit_part,
+):
+    place = Place(bounds)
+    rows = e2.shape[0]
+    part = value.shape[1]
+    lanes = part // BLOCKS
+    outs = (x_send, x_keep, z_send, z_keep)
+
+    def put_grads(first, second):
+        grads[:rows, :] = first[...]
+        grads[rows:, :] = second[...]
+
+    @pl.when(place.left)
+    def _():
         core_columns(place, unit, w_in, unit_part, value)
-        grads[:rows, :] = e2[...]
-        grads[rows:, :] = f2[...]
-        err[...] = early_part[...]
-
-    half_cols = err.shape[1] // 2
-    mine = pl.ds(pl.multiple_of(column * half_cols, half_cols), half_cols)
-    other = pl.ds(pl.multiple_of((1 - column) * half_cols, half_cols), half_cols)
-    in_send[...] = (in_acc[:, other] + tn_dot(unit_part[...], err[:, other])).astype(jnp.bfloat16)
-    in_keep[...] = in_acc[:, mine] + tn_dot(unit_part[...], err[:, mine])
-    half_rows = part // 2
-    upper = pl.ds(pl.multiple_of(half * half_rows, half_rows), half_rows)
-    lower = pl.ds(pl.multiple_of((1 - half) * half_rows, half_rows), half_rows)
-    out_send[...] = (out_acc[lower, :] + tn_dot(value[:, lower], grads[...])).astype(jnp.bfloat16)
-    out_keep[...] = out_acc[upper, :] + tn_dot(value[:, upper], grads[...])
-
-
-def late_partials(bounds, late, other_late, own_top, other_top, early_part, accs, w_in, w_out):
-    rows, model = late.shape
-    inner = w_out.shape[1]
-    part = model // 2
+        put_grads(e2, f2)
+        split_sums(place, value, grads, out_acc, *outs)
+
+    @pl.when(jnp.logical_not(place.left))
+    def _():
+        for j in range(BLOCKS):
+            block = lane_block(j, place, lanes)
+            where = pl.ds(j * lanes, lanes)
+            value[:rows, where] = up[:, block]
+            value[rows:, where] = fup[:, block]
+
+        @pl.when(place.short)
+        def _():
+            put_grads(late, flate)
+
+        @pl.when(jnp.logical_not(place.short))
+        def _():
+            put_grads(low, flow)
+
+        split_sums(place, value, grads, None, *outs)
+
+
+def split_shapes(part, width):
+    return (
+        low_shape(part // 2, width // 2),
+        full_shape(part // 2, width // 2),
+        low_shape(part // 4, width),
+        full_shape(part // 4, width),
+    )
+
+
+def x_add_kernel(keep, land, mine, following):
+    half = lax.axis_index("section") % 2
+    rows = mine.shape[0]
+    kept = pl.ds(pl.multiple_of(half * rows, rows), rows)
+    sent = pl.ds(pl.multiple_of((1 - half) * rows, rows), rows)
+    mine[...] = keep[kept, :] + land[kept, :].astype(jnp.float32)
+    following[...] = (keep[sent, :] + land[sent, :].astype(jnp.float32)).astype(jnp.bfloat16)
+
+
+def z_add_kernel(keep, land, mine, following):
+    column = lax.axis_index("tensor")
+    cols = mine.shape[1]
+    kept = pl.ds(pl.multiple_of(column * cols, cols), cols)
+    sent = pl.ds(pl.multiple_of((1 - column) * cols, cols), cols)
+    mine[...] = keep[:, kept] + land[:, kept].astype(jnp.float32)
+    following[...] = (keep[:, sent] + land[:, sent].astype(jnp.float32)).astype(jnp.bfloat16)
+
+
+def last_add_kernel(mine, land, total):
+    total[...] = (mine[...] + land[...].astype(jnp.float32)).astype(total.dtype)
+
+
+def hand_on_kernel(bounds, near, got, give, lower):
+    place = Place(bounds)
+
+    @pl.when(place.short)
+    def _():
+        give[...] = got[...]
+        lower[...] = near[...]
+
+    @pl.when(jnp.logical_not(place.short))
+    def _():
+        give[...] = near[...].astype(jnp.bfloat16)
+        lower[...] = got[...].astype(jnp.float32)
+
+
+def in_result_kernel(lower, landed, result):
+    left = lax.axis_index("section") < 2
+
+    @pl.when(left)
+    def _():
+        result[0] = lower[...]
+
+    @pl.when(jnp.logical_not(left))
+    def _():
+        result[0] = landed[...].astype(jnp.float32)
+
+
+def out_result_kernel(bounds, near, got, result):
+    place = Place(bounds)
+    upper = jnp.logical_not(place.left)
+
+    @pl.when(upper)
+    def _():
+        result[0] = near[...] + got[...].astype(jnp.float32)
+
+    @pl.when(place.left & place.short)
+    def _():
+        result[0] = near[...]
+
+    @pl.when(place.left & jnp.logical_not(place.short))
+    def _():
+        result[0] = got[...].astype(jnp.float32)
+
+
+def small_call(kernel, operands, shapes, scratch=(), flops=0):
+    specs = [SMEM if part.ndim == 2 and part.dtype == jnp.int32 else VMEM for part in operands]
+    cost = pl.CostEstimate(flops=flops, bytes_accessed=0, transcendentals=0) if flops else None
     return pl.pallas_call(
-        late_kernel,
-        out_shape=(
-            jax.ShapeDtypeStruct((part, inner // 2), jnp.bfloat16),
-            jax.ShapeDtypeStruct((part, inner // 2), jnp.float32),
-            jax.ShapeDtypeStruct((part // 2, model), jnp.bfloat16),
-            jax.ShapeDtypeStruct((part // 2, model), jnp.float32),
-        ),
-        in_specs=[SMEM] + [VMEM] * 9,
-        out_specs=(VMEM,) * 4,
-        scratch_shapes=[
-            pltpu.VMEM((2 * rows, model), jnp.bfloat16),
-            pltpu.VMEM((2 * rows, part), jnp.bfloat16),
-            pltpu.VMEM((2 * rows, part), jnp.bfloat16),
-            pltpu.VMEM((2 * rows, model), jnp.bfloat16),
-            pltpu.VMEM((2 * rows, inner), jnp.bfloat16),
-        ],
+        kernel,
+        out_shape=shapes,
+        in_specs=specs,
+        out_specs=jax.tree.map(lambda _: VMEM, shapes),
+        scratch_shapes=scratch,
         compiler_params=pltpu.CompilerParams(vmem_limit_bytes=KERNEL_BYTES),
-        cost_estimate=pl.CostEstimate(
-            flops=8 * rows * model * inner, bytes_accessed=3 * model * inner, transcendentals=0
-        ),
-        name="late",
-    )(bounds, late, other_late, own_top, other_top, early_part, *accs, w_in, w_out)
+        cost_estimate=cost,
+    )(*operands)
+
+
+def low_shape(*dims):
+    return jax.ShapeDtypeStruct(dims, jnp.bfloat16)
+
+
+def full_shape(*dims):
+    return jax.ShapeDtypeStruct(dims, jnp.float32)
 
 
 def flipped(value, axis, bit):
@@ -479,14 +601,6 @@
 
 
 def two_section_body(bounds, saved_inputs, w_in, w_out, top_grad):
-    pipe_index = lax.axis_index("pipe")
-    section_index = lax.axis_index("section")
-    column = lax.axis_index("tensor")
-    relay = pipe_index // 2
-    half = section_index % 2
-    left = section_index // 2 == 0
-    boundary = lax.dynamic_index_in_dim(bounds, relay, 0, keepdims=False)
-    short = boundary[1] - boundary[0] == 2
     saved = saved_inputs[0, 0]
     proj_in = w_in[0, 0]
     proj_out = w_out[0, 0]
@@ -506,44 +620,79 @@
     def column_swap(value):
         return flipped(value, "tensor", 1)
 
+    half_axis = lax.axis_size("section") // 2
+
+    def upward(value):
+        return lax.ppermute(value, "section", [(i, i + half_axis) for i in range(half_axis)])
+
+    def downward(value):
+        return lax.ppermute(value, "section", [(i + half_axis, i) for i in range(half_axis)])
+
     def section_swap(value):
         return flipped(value, "section", 2)
 
     own_saved, own_top, given = staged(bounds, saved, tops)
     swapped = across(given)
+    rows = saved.shape[1]
+    row_block = low_shape(rows, model)
+    value_low = small_call(value_kernel, (saved, proj_in), row_block, flops=2 * rows * model * inner)
+    lifted = upward(value_low)
     grad_low = chain(bounds, tops, saved, proj_in, proj_out)
     hopping = by_role(bounds, grad_low, swapped)
-    late = section_swap(hopping)
+    late = downward(hopping)
     grad_other = across(grad_low)
+    raised = upward(grad_low)
     own = (own_saved, swapped)
     partner = tuple(core_swap(part) for part in own)
     early_part, unit_part, value = early_factors(bounds, own, partner, proj_in, proj_out)
     grad_early = by_role(bounds, grad_other, own_top)
-    accs = middle_partials(bounds, grad_early, core_swap(grad_early), unit_part, value, proj_out)
+    in_acc, out_acc = middle_partials(bounds, grad_early, core_swap(grad_early), unit_part, value, proj_out)
+    other_low = core_swap(grad_low)
+    other_lifted = core_swap(lifted)
+    other_raised = core_swap(raised)
     other_late = core_swap(late)
-    in_send, in_keep, out_send, out_keep = late_partials(
-        bounds, late, other_late, own[1], partner[1], early_part, accs, proj_in, proj_out
-    )
-    in_landed = column_swap(in_send)
-    out_landed = half_swap(out_send)
-    in_sum = (in_keep + in_landed.astype(jnp.float32)).reshape(2, -1, inner // 2)
-    out_sum = out_keep + out_landed.astype(jnp.float32)
-    in_mine = lax.dynamic_index_in_dim(in_sum, half, 0, keepdims=False)
-    in_next = lax.dynamic_index_in_dim(in_sum, 1 - half, 0, keepdims=False)
-    out_mine = lax.dynamic_slice_in_dim(out_sum, column * (model // 2), model // 2, 1)
-    out_next = lax.dynamic_slice_in_dim(out_sum, (1 - column) * (model // 2), model // 2, 1)
-    in_landed = half_swap(in_next.astype(jnp.bfloat16))
-    out_landed = column_swap(out_next.astype(jnp.bfloat16))
-    results = []
-    for mine, landed in ((in_mine, in_landed), (out_mine, out_landed)):
-        total = (mine + landed.astype(jnp.float32)).reshape(2, -1, mine.shape[1])
-        own = lax.dynamic_index_in_dim(total, relay, 0, keepdims=False)
-        sent = lax.dynamic_index_in_dim(total, 1 - relay, 0, keepdims=False).astype(jnp.bfloat16)
-        got = across(sent)
-        onward = section_swap(jnp.where(short, got, own.astype(jnp.bfloat16)))
-        lower = jnp.where(short, own, got.astype(jnp.float32))
-        results.append(jnp.where(left, lower, onward.astype(jnp.float32))[None])
-    return tuple(results)
+    part = model // 2
+    pair = 2 * rows
+    *in_parts, unit_late = small_call(
+        late_in_kernel,
+        (bounds, late, other_late, early_part, in_acc, proj_out),
+        split_shapes(part, inner) + (low_shape(pair, model),),
+        scratch=[pltpu.VMEM((pair, part), jnp.bfloat16), pltpu.VMEM((pair, inner), jnp.bfloat16)],
+        flops=6 * rows * model * inner,
+    )
+    out_parts = small_call(
+        late_out_kernel,
+        (bounds, unit_late, own[1], partner[1], out_acc, proj_in)
+        + (raised, other_raised, grad_low, other_low, lifted, other_lifted),
+        split_shapes(part, model),
+        scratch=[
+            pltpu.VMEM((pair, part), jnp.bfloat16),
+            pltpu.VMEM((pair, model), jnp.bfloat16),
+            pltpu.VMEM((pair, part), jnp.bfloat16),
+        ],
+        flops=4 * rows * model * inner,
+    )
+    block = (model // (2 * BLOCKS), model // 2)
+    sums = []
+    for (x_send, x_keep, z_send, z_keep) in (in_parts, out_parts):
+        pair_shapes = (full_shape(*block), low_shape(*block))
+        x_land, z_land = column_swap(x_send), half_swap(z_send)
+        far, far_next = small_call(x_add_kernel, (x_keep, x_land), pair_shapes)
+        near, near_next = small_call(z_add_kernel, (z_keep, z_land), pair_shapes)
+        far_land, near_land = half_swap(far_next), column_swap(near_next)
+        far = small_call(last_add_kernel, (far, far_land), low_shape(*block))
+        got = across(far)
+        near = small_call(last_add_kernel, (near, near_land), full_shape(*block))
+        sums.append((near, got))
+    (in_near, in_got), (out_near, out_got) = sums
+    give, lower = small_call(
+        hand_on_kernel, (bounds, in_near, in_got), (low_shape(*block), full_shape(*block))
+    )
+    landed = section_swap(give)
+    return (
+        small_call(in_result_kernel, (lower, landed), full_shape(1, *block)),
+        small_call(out_result_kernel, (bounds, out_near, out_got), full_shape(1, *block)),
+    )
 
 
 def body(bounds, saved_inputs, w_in, w_out, top_grad):

time: 76.4 us -> 82.3 us (1.077)
  the two profiles are of different devices: /device:TPU:0 before, /device:TPU:24 now
where the time goes in v6:
time: 82.3 us; the launch traced here: 80.6 us
  waiting for transfers between devices  44.8 us (54%)
  starting transfers between devices  19.1 us (23%)
  Pallas kernels  13.4 us (16%)
  local copies, waits for them, and re-layouts  2.42 us (3%)
  between operations  0.87 us (1%)
    ppermute x20, waiting for transfers between devices, flipped(): lax.ppermute(value, axis, [(i, i ^ bit) for i in range(lax.axis_size(axis...  23.4 us
    ppermute x2, waiting for transfers between devices, upward(): lax.ppermute(value, 'section', [(i, i + half_axis) for i in range(half_ax...  21.4 us
    ppermute x20, starting transfers between devices, flipped(): lax.ppermute(value, axis, [(i, i ^ bit) for i in range(lax.axis_size(axis...  14.2 us
    pallas_call x14, Pallas kernels, small_call(): pl.pallas_call(kernel, out_shape=shapes, in_specs=specs, out_specs=jax.tr...  6.42 us
    ppermute x2, starting transfers between devices, upward(): lax.ppermute(value, 'section', [(i, i + half_axis) for i in range(half_ax...  2.58 us
    unnamed x10, local copies, waits for them, and re-layouts  2.42 us
    ppermute x1, starting transfers between devices, downward(): lax.ppermute(value, 'section', [(i + half_axis, i) for i in range(half_ax...  2.26 us
    pallas_call x1, Pallas kernels, chain(): pl.pallas_call(chain_kernel, out_shape=jax.ShapeDtypeStruct((rows, model)...  2.2 us
  transfers between devices with their start and end apart: 23, of which 10 were waited for; matrix products, arithmetic and copies ran while one was open for 0% of the time, Pallas kernels for 15%

profile of v6, /device:TPU:24, one launch (start us, length us, event | category | flops | bytes accessed | tf_op | source)
XLA Modules:
  0.0 80.6 jit_solution(823071948686563832)
XLA Ops:
  0.7 1.0 %copy-done.2 = bf16[1,1,2,128,1024]{4,3,2,1,0:T(8,128)(2,1)S(1)} copy-done((bf16[1,1,2,128,1024]{4,3,2,1,0:T(8,128)(2,1)S(1)}, bf16[1,1,2,128,1024]{4,3,2,1,0:T(8,128)(2,1)}, u32[]{:S(2)}) %copy-start.2) | copy-done | bytes 524312
  1.7 0.2 copy-done.3
  1.8 0.6 staged.1
  2.5 1.6 %collective-permute-start = (bf16[128,1024]{1,0:T(8,128)(2,1)S(1)}, bf16[128,1024]{1,0:T(8,128)(2,1)S(1)}, u32[]{:S(2)}, u32[]{:S(2)}) collective-permute-start(bf16[128,1024]{1,0:T(8,128)(2,1)S(1)} %get-tuple-element.29), channel_id=1, source_target_pairs={{0,16},{8,24},{16,0},{24,8},{1,17},{9,25},{17,1},{25,9},{2,18},{10... | collective-permute-start | bytes 786440 | tf_op jit(solution)/shard_map/ppermute | solution.py:600
  4.1 1.2 %copy-done.1 = bf16[1,1,2,1024,1024]{4,3,2,1,0:T(8,128)(2,1)S(1)} copy-done((bf16[1,1,2,1024,1024]{4,3,2,1,0:T(8,128)(2,1)S(1)}, bf16[1,1,2,1024,1024]{4,3,2,1,0:T(8,128)(2,1)}, u32[]{:S(2)}) %copy-start.1) | copy-done | bytes 4194328
  5.3 2.2 %chain.1.full_part.low = bf16[128,1024]{1,0:T(8,128)(2,1)S(1)} custom-call(s32[2,3]{1,0:T(2,128)S(1)} %copy-done.4, bf16[2,128,1024]{2,1,0:T(8,128)(2,1)S(1)} %bitcast.16, bf16[2,128,1024]{2,1,0:T(8,128)(2,1)S(1)} %bitcast.13, bf16[2,1024,1024]{2,1,0:T(8,128)(2,1)S(1)} %bitcast.8, bf16[2,1024,1024]{2,1,0:T(8,128)(2,1)S(1)} %bitcast.4), custom_call_target="tpu_custom_call" | custom-call | flops 536870912 | bytes 4194304 | tf_op jit(solution)/shard_map/chain/pallas_call | solution.py:238
  7.5 1.6 %collective-permute-start.5 = (bf16[128,1024]{1,0:T(8,128)(2,1)S(1)}, bf16[128,1024]{1,0:T(8,128)(2,1)S(1)}, u32[]{:S(2)}, u32[]{:S(2)}) collective-permute-start(bf16[128,1024]{1,0:T(8,128)(2,1)S(1)} %chain.1.full_part.low), channel_id=1, source_target_pairs={{0,16},{8,24},{16,0},{24,8},{1,17},{9,25},{17,1},{25,9},{2,18},{10... | collective-permute-start | bytes 786440 | tf_op jit(solution)/shard_map/ppermute | solution.py:600
  9.1 2.0 %collective-permute-done.short_part.e2 = bf16[128,1024]{1,0:T(8,128)(2,1)S(1)} collective-permute-done((bf16[128,1024]{1,0:T(8,128)(2,1)S(1)}, bf16[128,1024]{1,0:T(8,128)(2,1)S(1)}, u32[]{:S(2)}, u32[]{:S(2)}) %collective-permute-start) | collective-permute-done | bytes 262176 | tf_op jit(solution)/shard_map/ppermute | solution.py:600
  11.1 0.6 by_role.2
  11.7 2.3 %collective-permute-start.1 = (bf16[128,1024]{1,0:T(8,128)(2,1)S(1)}, bf16[128,1024]{1,0:T(8,128)(2,1)S(1)}, u32[]{:S(2)}, u32[]{:S(2)}) collective-permute-start(bf16[128,1024]{1,0:T(8,128)(2,1)S(1)} %by_role.2), channel_id=1, source_target_pairs={{4,0},{6,2},{5,1},{7,3},{12,8},{14,10},{13,9},{15,11},{20,16},{22,... | collective-permute-start | bytes 786440 | tf_op jit(solution)/shard_map/ppermute | solution.py:629
  14.0 1.3 %collective-permute-start.13 = (bf16[128,1024]{1,0:T(8,128)(2,1)S(1)}, bf16[128,1024]{1,0:T(8,128)(2,1)S(1)}, u32[]{:S(2)}, u32[]{:S(2)}) collective-permute-start(bf16[128,1024]{1,0:T(8,128)(2,1)S(1)} %chain.1.full_part.low), channel_id=1, source_target_pairs={{0,4},{2,6},{1,5},{3,7},{8,12},{10,14},{9,13},{11,15},{16,20},{18,... | collective-permute-start | bytes 786440 | tf_op jit(solution)/shard_map/ppermute | solution.py:626
  15.3 0.5 shard_map.75
  15.8 1.3 %collective-permute-start.16 = (bf16[128,1024]{1,0:T(8,128)(2,1)S(1)}, bf16[128,1024]{1,0:T(8,128)(2,1)S(1)}, u32[]{:S(2)}, u32[]{:S(2)}) collective-permute-start(bf16[128,1024]{1,0:T(8,128)(2,1)S(1)} %shard_map.75), channel_id=1, source_target_pairs={{0,4},{2,6},{1,5},{3,7},{8,12},{10,14},{9,13},{11,15},{16,20},{18,... | collective-permute-start | bytes 786440 | tf_op jit(solution)/shard_map/ppermute | solution.py:626
  17.1 0.0 collective-permute-done.5.full_part
  17.2 0.1 collective-permute-start.4
  17.2 0.6 by_role.3.e3
  17.8 0.6 collective-permute-start.6
  18.4 0.1 collective-permute-start.2
  18.5 15.9 %collective-permute-done.13.late = bf16[128,1024]{1,0:T(8,128)(2,1)S(1)} collective-permute-done((bf16[128,1024]{1,0:T(8,128)(2,1)S(1)}, bf16[128,1024]{1,0:T(8,128)(2,1)S(1)}, u32[]{:S(2)}, u32[]{:S(2)}) %collective-permute-start.13) | collective-permute-done | bytes 262176 | tf_op jit(solution)/shard_map/ppermute | solution.py:626
  34.4 5.5 %collective-permute-done.16.up = bf16[128,1024]{1,0:T(8,128)(2,1)S(1)} collective-permute-done((bf16[128,1024]{1,0:T(8,128)(2,1)S(1)}, bf16[128,1024]{1,0:T(8,128)(2,1)S(1)}, u32[]{:S(2)}, u32[]{:S(2)}) %collective-permute-start.16) | collective-permute-done | bytes 262176 | tf_op jit(solution)/shard_map/ppermute | solution.py:626
  39.9 0.0 collective-permute-start.14
  40.0 0.5 collective-permute-start.17
  40.5 1.1 %early.1 = (bf16[256,1024]{1,0:T(8,128)(2,1)S(1)}, bf16[256,512]{1,0:T(8,128)(2,1)S(1)}, bf16[256,512]{1,0:T(8,128)(2,1)S(1)}) custom-call(s32[2,3]{1,0:T(2,128)S(1)} %copy-done.4, bf16[128,1024]{1,0:T(8,128)(2,1)S(1)} %get-tuple-element.30.e1, bf16[128,1024]{1,0:T(8,128)(2,1)S(1)} %collective-permute-done.short_part.e2, ...), custom_call_target="tpu_custom_call" | custom-call | flops 536870912 | bytes 3145728 | tf_op jit(solution)/shard_map/early/pallas_call | solution.py:376
  41.6 1.9 %middle.1 = (f32[512,1024]{1,0:T(8,128)S(1)}, f32[512,1024]{1,0:T(8,128)S(1)}) custom-call(s32[2,3]{1,0:T(2,128)S(1)} %copy-done.4, bf16[128,1024]{1,0:T(8,128)(2,1)S(1)} %by_role.3.e3, bf16[128,1024]{1,0:T(8,128)(2,1)S(1)} %collective-permute-done.6.f3, bf16[256,512]{1,0:T(8,128)(2,1)S(1)} %get-tuple-element.33.unit_part, ...), custom_call_target="tpu_custom_call" | custom-call | flops 1073741824 | bytes 3145728 | tf_op jit(solution)/shard_map/middle/pallas_call | solution.py:406
  43.5 1.8 %shard_map.68 = (bf16[256,512]{1,0:T(8,128)(2,1)S(1)}, f32[256,512]{1,0:T(8,128)S(1)}, bf16[128,1024]{1,0:T(8,128)(2,1)S(1)}, f32[128,1024]{1,0:T(8,128)S(1)}, bf16[256,1024]{1,0:T(8,128)(2,1)S(1)}) custom-call(s32[2,3]{1,0:T(2,128)S(1)} %copy-done.4, bf16[128,1024]{1,0:T(8,128)(2,1)S(1)} %collective-permute-done.1.late, ...), custom_call_target="tpu_custom_call" | custom-call | flops 805306368 | tf_op jit(solution)/shard_map/pallas_call | solution.py:580
  45.3 1.6 %collective-permute-start.9 = (bf16[256,512]{1,0:T(8,128)(2,1)S(1)}, bf16[256,512]{1,0:T(8,128)(2,1)S(1)}, u32[]{:S(2)}, u32[]{:S(2)}) collective-permute-start(bf16[256,512]{1,0:T(8,128)(2,1)S(1)} %get-tuple-element.41), channel_id=1, source_target_pairs={{0,1},{1,0},{2,3},{3,2},{4,5},{5,4},{6,7},{7,6},{8,9},{9,8},{10,11... | collective-permute-start | bytes 786440 | tf_op jit(solution)/shard_map/ppermute | solution.py:600
  46.9 1.1 %shard_map.76 = (bf16[256,512]{1,0:T(8,128)(2,1)S(1)}, f32[256,512]{1,0:T(8,128)S(1)}, bf16[128,1024]{1,0:T(8,128)(2,1)S(1)}, f32[128,1024]{1,0:T(8,128)S(1)}) custom-call(s32[2,3]{1,0:T(2,128)S(1)} %copy-done.4, bf16[256,1024]{1,0:T(8,128)(2,1)S(1)} %get-tuple-element.46.unit, bf16[128,1024]{1,0:T(8,128)(2,1)S(1)} %collective-permute-done.short_part.e2, ...), custom_call_target="tpu_custom_call" | custom-call | flops 536870912 | tf_op jit(solution)/shard_map/pallas_call | solution.py:580
  48.0 0.6 collective-permute-start.20
  48.6 2.0 %collective-permute-start.18 = (bf16[128,1024]{1,0:T(8,128)(2,1)S(1)}, bf16[128,1024]{1,0:T(8,128)(2,1)S(1)}, u32[]{:S(2)}, u32[]{:S(2)}) collective-permute-start(bf16[128,1024]{1,0:T(8,128)(2,1)S(1)} %get-tuple-element.49), channel_id=1, source_target_pairs={{0,2},{2,0},{4,6},{6,4},{1,3},{3,1},{5,7},{7,5},{8,10},{10,8},{12,... | collective-permute-start | bytes 786440 | tf_op jit(solution)/shard_map/ppermute | solution.py:600
  50.6 3.9 %collective-permute-done.9.land = bf16[256,512]{1,0:T(8,128)(2,1)S(1)} collective-permute-done((bf16[256,512]{1,0:T(8,128)(2,1)S(1)}, bf16[256,512]{1,0:T(8,128)(2,1)S(1)}, u32[]{:S(2)}, u32[]{:S(2)}) %collective-permute-start.9) | collective-permute-done | bytes 262176 | tf_op jit(solution)/shard_map/ppermute | solution.py:600
  54.6 0.1 collective-permute-start.10
  54.7 4.5 %collective-permute-done.20.land = bf16[256,512]{1,0:T(8,128)(2,1)S(1)} collective-permute-done((bf16[256,512]{1,0:T(8,128)(2,1)S(1)}, bf16[256,512]{1,0:T(8,128)(2,1)S(1)}, u32[]{:S(2)}, u32[]{:S(2)}) %collective-permute-start.20) | collective-permute-done | bytes 262176 | tf_op jit(solution)/shard_map/ppermute | solution.py:600
  59.2 0.1 shard_map.79
  59.3 0.1 collective-permute-start.21
  59.4 0.1 shard_map.69
  59.4 1.6 %collective-permute-start.8 = (bf16[128,512]{1,0:T(8,128)(2,1)S(1)}, bf16[128,512]{1,0:T(8,128)(2,1)S(1)}, u32[]{:S(2)}, u32[]{:S(2)}) collective-permute-start(bf16[128,512]{1,0:T(8,128)(2,1)S(1)} %get-tuple-element.39), channel_id=1, source_target_pairs={{0,1},{1,0},{2,3},{3,2},{4,5},{5,4},{6,7},{7,6},{8,9},{9,8},{10,11... | collective-permute-start | bytes 393224 | tf_op jit(solution)/shard_map/ppermute | solution.py:600
  61.0 5.1 %collective-permute-done.10.land = bf16[128,512]{1,0:T(8,128)(2,1)S(1)} collective-permute-done((bf16[128,512]{1,0:T(8,128)(2,1)S(1)}, bf16[128,512]{1,0:T(8,128)(2,1)S(1)}, u32[]{:S(2)}, u32[]{:S(2)}) %collective-permute-start.10) | collective-permute-done | bytes 131104 | tf_op jit(solution)/shard_map/ppermute | solution.py:600
  66.1 2.1 %collective-permute-start.11 = (bf16[128,512]{1,0:T(8,128)(2,1)S(1)}, bf16[128,512]{1,0:T(8,128)(2,1)S(1)}, u32[]{:S(2)}, u32[]{:S(2)}) collective-permute-start(bf16[128,512]{1,0:T(8,128)(2,1)S(1)} %shard_map.72), channel_id=1, source_target_pairs={{0,16},{8,24},{16,0},{24,8},{1,17},{9,25},{17,1},{25,9},{2,18},{10... | collective-permute-start | bytes 393224 | tf_op jit(solution)/shard_map/ppermute | solution.py:600
  68.3 1.6 %collective-permute-start.19 = (bf16[128,512]{1,0:T(8,128)(2,1)S(1)}, bf16[128,512]{1,0:T(8,128)(2,1)S(1)}, u32[]{:S(2)}, u32[]{:S(2)}) collective-permute-start(bf16[128,512]{1,0:T(8,128)(2,1)S(1)} %get-tuple-element.51), channel_id=1, source_target_pairs={{0,1},{1,0},{2,3},{3,2},{4,5},{5,4},{6,7},{7,6},{8,9},{9,8},{10,11... | collective-permute-start | bytes 393224 | tf_op jit(solution)/shard_map/ppermute | solution.py:600
  69.9 0.1 collective-permute-start.22
  70.0 2.0 %collective-permute-done.11.got = bf16[128,512]{1,0:T(8,128)(2,1)S(1)} collective-permute-done((bf16[128,512]{1,0:T(8,128)(2,1)S(1)}, bf16[128,512]{1,0:T(8,128)(2,1)S(1)}, u32[]{:S(2)}, u32[]{:S(2)}) %collective-permute-start.11) | collective-permute-done | bytes 131104 | tf_op jit(solution)/shard_map/ppermute | solution.py:600
  72.0 0.6 shard_map.73
  72.6 0.2 collective-permute-start.12
  72.8 0.5 collective-permute-done.19.land
  73.3 1.6 %collective-permute-done.22.got = bf16[128,512]{1,0:T(8,128)(2,1)S(1)} collective-permute-done((bf16[128,512]{1,0:T(8,128)(2,1)S(1)}, bf16[128,512]{1,0:T(8,128)(2,1)S(1)}, u32[]{:S(2)}, u32[]{:S(2)}) %collective-permute-start.22) | collective-permute-done | bytes 131104 | tf_op jit(solution)/shard_map/ppermute | solution.py:600
  74.9 1.3 %shard_map.81 = f32[1,128,512]{2,1,0:T(8,128)} custom-call(s32[2,3]{1,0:T(2,128)S(1)} %copy-done.4, f32[128,512]{1,0:T(8,128)S(1)} %shard_map.78.near, bf16[128,512]{1,0:T(8,128)(2,1)S(1)} %collective-permute-done.22.got), custom_call_target="tpu_custom_call" | custom-call | tf_op jit(solution)/shard_map/pallas_call | solution.py:580
  76.2 3.7 %collective-permute-done.12.landed = bf16[128,512]{1,0:T(8,128)(2,1)S(1)} collective-permute-done((bf16[128,512]{1,0:T(8,128)(2,1)S(1)}, bf16[128,512]{1,0:T(8,128)(2,1)S(1)}, u32[]{:S(2)}, u32[]{:S(2)}) %collective-permute-start.12) | collective-permute-done | bytes 131104 | tf_op jit(solution)/shard_map/ppermute | solution.py:600
  79.9 0.7 shard_map.74
  (29 shorter events, 0.3 us)
Async XLA Ops:
  0.6 1.0 %copy-start.2 = (bf16[1,1,2,128,1024]{4,3,2,1,0:T(8,128)(2,1)S(1)}, bf16[1,1,2,128,1024]{4,3,2,1,0:T(8,128)(2,1)}, u32[]{:S(2)}) copy-start(bf16[1,1,2,128,1024]{4,3,2,1,0:T(8,128)(2,1)} %param.6) | copy-start | bytes 1572868
  0.6 1.2 %copy-start.3 = (bf16[1,2,128,1024]{3,2,1,0:T(8,128)(2,1)S(1)}, bf16[1,2,128,1024]{3,2,1,0:T(8,128)(2,1)}, u32[]{:S(2)}) copy-start(bf16[1,2,128,1024]{3,2,1,0:T(8,128)(2,1)} %param.9) | copy-start | bytes 1572868
  0.6 1.2 %copy-start.4 = (s32[2,3]{1,0:T(2,128)S(1)}, s32[2,3]{1,0:T(2,128)}, u32[]{:S(2)}) copy-start(s32[2,3]{1,0:T(2,128)} %bounds.19) | copy-start | bytes 76
  1.8 2.2 %copy-start = (bf16[1,1,2,1024,1024]{4,3,2,1,0:T(8,128)(2,1)S(1)}, bf16[1,1,2,1024,1024]{4,3,2,1,0:T(8,128)(2,1)}, u32[]{:S(2)}) copy-start(bf16[1,1,2,1024,1024]{4,3,2,1,0:T(8,128)(2,1)} %param.8) | copy-start | bytes 12582916
  1.8 3.5 %copy-start.1 = (bf16[1,1,2,1024,1024]{4,3,2,1,0:T(8,128)(2,1)S(1)}, bf16[1,1,2,1024,1024]{4,3,2,1,0:T(8,128)(2,1)}, u32[]{:S(2)}) copy-start(bf16[1,1,2,1024,1024]{4,3,2,1,0:T(8,128)(2,1)} %param.7) | copy-start | bytes 12582916
  2.5 8.7 %collective-permute-start = (bf16[128,1024]{1,0:T(8,128)(2,1)S(1)}, bf16[128,1024]{1,0:T(8,128)(2,1)S(1)}, u32[]{:S(2)}, u32[]{:S(2)}) collective-permute-start(bf16[128,1024]{1,0:T(8,128)(2,1)S(1)} %get-tuple-element.29), channel_id=1, source_target_pairs={{0,16},{8,24},{16,0},{24,8},{1,17},{9,25},{17,1},{25,9},{2,18},{10... | collective-permute-start | bytes 786440 | tf_op jit(solution)/shard_map/ppermute | solution.py:600
  7.5 9.6 %collective-permute-start.5 = (bf16[128,1024]{1,0:T(8,128)(2,1)S(1)}, bf16[128,1024]{1,0:T(8,128)(2,1)S(1)}, u32[]{:S(2)}, u32[]{:S(2)}) collective-permute-start(bf16[128,1024]{1,0:T(8,128)(2,1)S(1)} %chain.1.full_part.low), channel_id=1, source_target_pairs={{0,16},{8,24},{16,0},{24,8},{1,17},{9,25},{17,1},{25,9},{2,18},{10... | collective-permute-start | bytes 786440 | tf_op jit(solution)/shard_map/ppermute | solution.py:600
  9.1 8.7 %collective-permute-start.3 = (bf16[128,1024]{1,0:T(8,128)(2,1)S(1)}, bf16[128,1024]{1,0:T(8,128)(2,1)S(1)}, u32[]{:S(2)}, u32[]{:S(2)}) collective-permute-start(bf16[128,1024]{1,0:T(8,128)(2,1)S(1)} %get-tuple-element.30.e1), channel_id=1, source_target_pairs={{0,8},{8,0},{16,24},{24,16},{1,9},{9,1},{17,25},{25,17},{2,10},{10... | collective-permute-start | bytes 786440 | tf_op jit(solution)/shard_map/ppermute | solution.py:600
  11.7 6.7 %collective-permute-start.1 = (bf16[128,1024]{1,0:T(8,128)(2,1)S(1)}, bf16[128,1024]{1,0:T(8,128)(2,1)S(1)}, u32[]{:S(2)}, u32[]{:S(2)}) collective-permute-start(bf16[128,1024]{1,0:T(8,128)(2,1)S(1)} %by_role.2), channel_id=1, source_target_pairs={{4,0},{6,2},{5,1},{7,3},{12,8},{14,10},{13,9},{15,11},{20,16},{22,... | collective-permute-start | bytes 786440 | tf_op jit(solution)/shard_map/ppermute | solution.py:629
  14.0 20.4 %collective-permute-start.13 = (bf16[128,1024]{1,0:T(8,128)(2,1)S(1)}, bf16[128,1024]{1,0:T(8,128)(2,1)S(1)}, u32[]{:S(2)}, u32[]{:S(2)}) collective-permute-start(bf16[128,1024]{1,0:T(8,128)(2,1)S(1)} %chain.1.full_part.low), channel_id=1, source_target_pairs={{0,4},{2,6},{1,5},{3,7},{8,12},{10,14},{9,13},{11,15},{16,20},{18,... | collective-permute-start | bytes 786440 | tf_op jit(solution)/shard_map/ppermute | solution.py:626
  15.8 24.1 %collective-permute-start.16 = (bf16[128,1024]{1,0:T(8,128)(2,1)S(1)}, bf16[128,1024]{1,0:T(8,128)(2,1)S(1)}, u32[]{:S(2)}, u32[]{:S(2)}) collective-permute-start(bf16[128,1024]{1,0:T(8,128)(2,1)S(1)} %shard_map.75), channel_id=1, source_target_pairs={{0,4},{2,6},{1,5},{3,7},{8,12},{10,14},{9,13},{11,15},{16,20},{18,... | collective-permute-start | bytes 786440 | tf_op jit(solution)/shard_map/ppermute | solution.py:626
  17.2 22.8 %collective-permute-start.4 = (bf16[128,1024]{1,0:T(8,128)(2,1)S(1)}, bf16[128,1024]{1,0:T(8,128)(2,1)S(1)}, u32[]{:S(2)}, u32[]{:S(2)}) collective-permute-start(bf16[128,1024]{1,0:T(8,128)(2,1)S(1)} %collective-permute-done.short_part.e2), channel_id=1, source_target_pairs={{0,8},{8,0},{16,24},{24,16},{1,9},{9,1},{17,25},{25,17},{2,10},{10... | collective-permute-start | bytes 786440 | tf_op jit(solution)/shard_map/ppermute | solution.py:600
  17.8 23.7 %collective-permute-start.6 = (bf16[128,1024]{1,0:T(8,128)(2,1)S(1)}, bf16[128,1024]{1,0:T(8,128)(2,1)S(1)}, u32[]{:S(2)}, u32[]{:S(2)}) collective-permute-start(bf16[128,1024]{1,0:T(8,128)(2,1)S(1)} %by_role.3.e3), channel_id=1, source_target_pairs={{0,8},{8,0},{16,24},{24,16},{1,9},{9,1},{17,25},{25,17},{2,10},{10... | collective-permute-start | bytes 786440 | tf_op jit(solution)/shard_map/ppermute | solution.py:600
  18.4 25.1 %collective-permute-start.2 = (bf16[128,1024]{1,0:T(8,128)(2,1)S(1)}, bf16[128,1024]{1,0:T(8,128)(2,1)S(1)}, u32[]{:S(2)}, u32[]{:S(2)}) collective-permute-start(bf16[128,1024]{1,0:T(8,128)(2,1)S(1)} %collective-permute-done.1.late), channel_id=1, source_target_pairs={{0,8},{8,0},{16,24},{24,16},{1,9},{9,1},{17,25},{25,17},{2,10},{10... | collective-permute-start | bytes 786440 | tf_op jit(solution)/shard_map/ppermute | solution.py:600
  34.4 12.4 %collective-permute-start.15 = (bf16[128,1024]{1,0:T(8,128)(2,1)S(1)}, bf16[128,1024]{1,0:T(8,128)(2,1)S(1)}, u32[]{:S(2)}, u32[]{:S(2)}) collective-permute-start(bf16[128,1024]{1,0:T(8,128)(2,1)S(1)} %chain.1.full_part.low), channel_id=1, source_target_pairs={{0,8},{8,0},{16,24},{24,16},{1,9},{9,1},{17,25},{25,17},{2,10},{10... | collective-permute-start | bytes 786440 | tf_op jit(solution)/shard_map/ppermute | solution.py:600
  39.9 6.9 %collective-permute-start.14 = (bf16[128,1024]{1,0:T(8,128)(2,1)S(1)}, bf16[128,1024]{1,0:T(8,128)(2,1)S(1)}, u32[]{:S(2)}, u32[]{:S(2)}) collective-permute-start(bf16[128,1024]{1,0:T(8,128)(2,1)S(1)} %collective-permute-done.13.late), channel_id=1, source_target_pairs={{0,8},{8,0},{16,24},{24,16},{1,9},{9,1},{17,25},{25,17},{2,10},{10... | collective-permute-start | bytes 786440 | tf_op jit(solution)/shard_map/ppermute | solution.py:600
  40.0 6.9 %collective-permute-start.17 = (bf16[128,1024]{1,0:T(8,128)(2,1)S(1)}, bf16[128,1024]{1,0:T(8,128)(2,1)S(1)}, u32[]{:S(2)}, u32[]{:S(2)}) collective-permute-start(bf16[128,1024]{1,0:T(8,128)(2,1)S(1)} %collective-permute-done.16.up), channel_id=1, source_target_pairs={{0,8},{8,0},{16,24},{24,16},{1,9},{9,1},{17,25},{25,17},{2,10},{10... | collective-permute-start | bytes 786440 | tf_op jit(solution)/shard_map/ppermute | solution.py:600
  45.3 9.2 %collective-permute-start.9 = (bf16[256,512]{1,0:T(8,128)(2,1)S(1)}, bf16[256,512]{1,0:T(8,128)(2,1)S(1)}, u32[]{:S(2)}, u32[]{:S(2)}) collective-permute-start(bf16[256,512]{1,0:T(8,128)(2,1)S(1)} %get-tuple-element.41), channel_id=1, source_target_pairs={{0,1},{1,0},{2,3},{3,2},{4,5},{5,4},{6,7},{7,6},{8,9},{9,8},{10,11... | collective-permute-start | bytes 786440 | tf_op jit(solution)/shard_map/ppermute | solution.py:600
  48.0 11.2 %collective-permute-start.20 = (bf16[256,512]{1,0:T(8,128)(2,1)S(1)}, bf16[256,512]{1,0:T(8,128)(2,1)S(1)}, u32[]{:S(2)}, u32[]{:S(2)}) collective-permute-start(bf16[256,512]{1,0:T(8,128)(2,1)S(1)} %get-tuple-element.53), channel_id=1, source_target_pairs={{0,1},{1,0},{2,3},{3,2},{4,5},{5,4},{6,7},{7,6},{8,9},{9,8},{10,11... | collective-permute-start | bytes 786440 | tf_op jit(solution)/shard_map/ppermute | solution.py:600
  48.6 10.7 %collective-permute-start.7 = (bf16[128,1024]{1,0:T(8,128)(2,1)S(1)}, bf16[128,1024]{1,0:T(8,128)(2,1)S(1)}, u32[]{:S(2)}, u32[]{:S(2)}) collective-permute-start(bf16[128,1024]{1,0:T(8,128)(2,1)S(1)} %get-tuple-element.37), channel_id=1, source_target_pairs={{0,2},{2,0},{4,6},{6,4},{1,3},{3,1},{5,7},{7,5},{8,10},{10,8},{12,... | collective-permute-start | bytes 786440 | tf_op jit(solution)/shard_map/ppermute | solution.py:600
  48.6 19.6 %collective-permute-start.18 = (bf16[128,1024]{1,0:T(8,128)(2,1)S(1)}, bf16[128,1024]{1,0:T(8,128)(2,1)S(1)}, u32[]{:S(2)}, u32[]{:S(2)}) collective-permute-start(bf16[128,1024]{1,0:T(8,128)(2,1)S(1)} %get-tuple-element.49), channel_id=1, source_target_pairs={{0,2},{2,0},{4,6},{6,4},{1,3},{3,1},{5,7},{7,5},{8,10},{10,8},{12,... | collective-permute-start | bytes 786440 | tf_op jit(solution)/shard_map/ppermute | solution.py:600
  54.6 11.5 %collective-permute-start.10 = (bf16[128,512]{1,0:T(8,128)(2,1)S(1)}, bf16[128,512]{1,0:T(8,128)(2,1)S(1)}, u32[]{:S(2)}, u32[]{:S(2)}) collective-permute-start(bf16[128,512]{1,0:T(8,128)(2,1)S(1)} %get-tuple-element.43), channel_id=1, source_target_pairs={{0,2},{2,0},{4,6},{6,4},{1,3},{3,1},{5,7},{7,5},{8,10},{10,8},{12,... | collective-permute-start | bytes 393224 | tf_op jit(solution)/shard_map/ppermute | solution.py:600
  59.3 10.6 %collective-permute-start.21 = (bf16[128,512]{1,0:T(8,128)(2,1)S(1)}, bf16[128,512]{1,0:T(8,128)(2,1)S(1)}, u32[]{:S(2)}, u32[]{:S(2)}) collective-permute-start(bf16[128,512]{1,0:T(8,128)(2,1)S(1)} %get-tuple-element.55), channel_id=1, source_target_pairs={{0,2},{2,0},{4,6},{6,4},{1,3},{3,1},{5,7},{7,5},{8,10},{10,8},{12,... | collective-permute-start | bytes 393224 | tf_op jit(solution)/shard_map/ppermute | solution.py:600
  59.4 10.6 %collective-permute-start.8 = (bf16[128,512]{1,0:T(8,128)(2,1)S(1)}, bf16[128,512]{1,0:T(8,128)(2,1)S(1)}, u32[]{:S(2)}, u32[]{:S(2)}) collective-permute-start(bf16[128,512]{1,0:T(8,128)(2,1)S(1)} %get-tuple-element.39), channel_id=1, source_target_pairs={{0,1},{1,0},{2,3},{3,2},{4,5},{5,4},{6,7},{7,6},{8,9},{9,8},{10,11... | collective-permute-start | bytes 393224 | tf_op jit(solution)/shard_map/ppermute | solution.py:600
  66.1 5.8 %collective-permute-start.11 = (bf16[128,512]{1,0:T(8,128)(2,1)S(1)}, bf16[128,512]{1,0:T(8,128)(2,1)S(1)}, u32[]{:S(2)}, u32[]{:S(2)}) collective-permute-start(bf16[128,512]{1,0:T(8,128)(2,1)S(1)} %shard_map.72), channel_id=1, source_target_pairs={{0,16},{8,24},{16,0},{24,8},{1,17},{9,25},{17,1},{25,9},{2,18},{10... | collective-permute-start | bytes 393224 | tf_op jit(solution)/shard_map/ppermute | solution.py:600
  68.3 5.0 %collective-permute-start.19 = (bf16[128,512]{1,0:T(8,128)(2,1)S(1)}, bf16[128,512]{1,0:T(8,128)(2,1)S(1)}, u32[]{:S(2)}, u32[]{:S(2)}) collective-permute-start(bf16[128,512]{1,0:T(8,128)(2,1)S(1)} %get-tuple-element.51), channel_id=1, source_target_pairs={{0,1},{1,0},{2,3},{3,2},{4,5},{5,4},{6,7},{7,6},{8,9},{9,8},{10,11... | collective-permute-start | bytes 393224 | tf_op jit(solution)/shard_map/ppermute | solution.py:600
  69.9 5.0 %collective-permute-start.22 = (bf16[128,512]{1,0:T(8,128)(2,1)S(1)}, bf16[128,512]{1,0:T(8,128)(2,1)S(1)}, u32[]{:S(2)}, u32[]{:S(2)}) collective-permute-start(bf16[128,512]{1,0:T(8,128)(2,1)S(1)} %shard_map.80), channel_id=1, source_target_pairs={{0,16},{8,24},{16,0},{24,8},{1,17},{9,25},{17,1},{25,9},{2,18},{10... | collective-permute-start | bytes 393224 | tf_op jit(solution)/shard_map/ppermute | solution.py:600
  72.6 7.3 %collective-permute-start.12 = (bf16[128,512]{1,0:T(8,128)(2,1)S(1)}, bf16[128,512]{1,0:T(8,128)(2,1)S(1)}, u32[]{:S(2)}, u32[]{:S(2)}) collective-permute-start(bf16[128,512]{1,0:T(8,128)(2,1)S(1)} %get-tuple-element.45), channel_id=1, source_target_pairs={{0,4},{2,6},{4,0},{6,2},{1,5},{3,7},{5,1},{7,3},{8,12},{10,14},{12... | collective-permute-start | bytes 393224 | tf_op jit(solution)/shard_map/ppermute | solution.py:600

commit v7 on v6

--- a/solution.py
+++ b/solution.py
@@ -220,16 +220,20 @@
     return lax.dot_general(left, right, (((0,), (0,)), ((), ())), preferred_element_type=jnp.float32)
 
 
-def chain_kernel(bounds, tops, saved, w_in, w_out, grad_out):
+def chain_kernel(bounds, tops, saved, w_in, w_out, grad_out, upward):
     place = Place(bounds)
     slot = place.upper_slot
+    first_unit = norm_rows(saved[0])[0].astype(jnp.bfloat16)
+    upward[0] = jnp.dot(first_unit, w_in[0], preferred_element_type=jnp.float32).astype(jnp.bfloat16)
     grad_next = tops[place.half]
     err = nt_dot(grad_next, w_out[slot]).astype(jnp.bfloat16)
     unit, row_scale = norm_rows(saved[slot])
     pulled = nt_dot(err, w_in[slot])
     inner_mean = jnp.mean(pulled * unit, axis=-1, keepdims=True)
     back = grad_next.astype(jnp.float32) + (pulled - unit * inner_mean) / row_scale
-    grad_out[...] = back.astype(jnp.bfloat16)
+    grad_low = back.astype(jnp.bfloat16)
+    grad_out[...] = grad_low
+    upward[1] = grad_low
 
 
 def chain(bounds, tops, saved, w_in, w_out):
@@ -237,12 +241,12 @@
     inner = w_in.shape[2]
     return pl.pallas_call(
         chain_kernel,
-        out_shape=jax.ShapeDtypeStruct((rows, model), jnp.bfloat16),
+        out_shape=(low_shape(rows, model), low_shape(2, rows, model)),
         in_specs=[SMEM] + [VMEM] * 4,
-        out_specs=VMEM,
+        out_specs=(VMEM,) * 2,
         compiler_params=pltpu.CompilerParams(vmem_limit_bytes=KERNEL_BYTES),
         cost_estimate=pl.CostEstimate(
-            flops=4 * rows * model * inner, bytes_accessed=4 * model * inner, transcendentals=0
+            flops=6 * rows * model * inner, bytes_accessed=4 * model * inner, transcendentals=0
         ),
         name="chain",
     )(bounds, tops, saved, w_in, w_out)
@@ -312,11 +316,6 @@
         compiler_params=pltpu.CompilerParams(vmem_limit_bytes=KERNEL_BYTES),
         name="by_role",
     )(bounds, full_part, short_part)
-
-
-def value_kernel(saved, w_in, value):
-    unit = norm_rows(saved[0])[0].astype(jnp.bfloat16)
-    value[...] = jnp.dot(unit, w_in[0], preferred_element_type=jnp.float32).astype(jnp.bfloat16)
 
 
 BLOCKS = 4
@@ -462,7 +461,7 @@
 
 
 def late_out_kernel(
-    bounds, unit, e2, f2, out_acc, w_in, late, flate, low, flow, up, fup,
+    bounds, unit, e2, f2, out_acc, w_in, up, fup, low, flow,
     x_send, x_keep, z_send, z_keep, value, grads, unit_part,
 ):
     place = Place(bounds)
@@ -486,12 +485,12 @@
         for j in range(BLOCKS):
             block = lane_block(j, place, lanes)
             where = pl.ds(j * lanes, lanes)
-            value[:rows, where] = up[:, block]
-            value[rows:, where] = fup[:, block]
+            value[:rows, where] = up[0, :, block]
+            value[rows:, where] = fup[0, :, block]
 
         @pl.when(place.short)
         def _():
-            put_grads(late, flate)
+            put_grads(up.at[1], fup.at[1])
 
         @pl.when(jnp.logical_not(place.short))
         def _():
@@ -634,14 +633,11 @@
     own_saved, own_top, given = staged(bounds, saved, tops)
     swapped = across(given)
     rows = saved.shape[1]
-    row_block = low_shape(rows, model)
-    value_low = small_call(value_kernel, (saved, proj_in), row_block, flops=2 * rows * model * inner)
-    lifted = upward(value_low)
-    grad_low = chain(bounds, tops, saved, proj_in, proj_out)
+    grad_low, upload = chain(bounds, tops, saved, proj_in, proj_out)
+    lifted = upward(upload)
     hopping = by_role(bounds, grad_low, swapped)
     late = downward(hopping)
     grad_other = across(grad_low)
-    raised = upward(grad_low)
     own = (own_saved, swapped)
     partner = tuple(core_swap(part) for part in own)
     early_part, unit_part, value = early_factors(bounds, own, partner, proj_in, proj_out)
@@ -649,7 +645,6 @@
     in_acc, out_acc = middle_partials(bounds, grad_early, core_swap(grad_early), unit_part, value, proj_out)
     other_low = core_swap(grad_low)
     other_lifted = core_swap(lifted)
-    other_raised = core_swap(raised)
     other_late = core_swap(late)
     part = model // 2
     pair = 2 * rows
@@ -663,7 +658,7 @@
     out_parts = small_call(
         late_out_kernel,
         (bounds, unit_late, own[1], partner[1], out_acc, proj_in)
-        + (raised, other_raised, grad_low, other_low, lifted, other_lifted),
+        + (lifted, other_lifted, grad_low, other_low),
         split_shapes(part, model),
         scratch=[
             pltpu.VMEM((pair, part), jnp.bfloat16),
@@ -676,10 +671,12 @@
     sums = []
     for (x_send, x_keep, z_send, z_keep) in (in_parts, out_parts):
         pair_shapes = (full_shape(*block), low_shape(*block))
-        x_land, z_land = column_swap(x_send), half_swap(z_send)
+        x_land = column_swap(x_send)
+        z_land = half_swap(z_send)
         far, far_next = small_call(x_add_kernel, (x_keep, x_land), pair_shapes)
         near, near_next = small_call(z_add_kernel, (z_keep, z_land), pair_shapes)
-        far_land, near_land = half_swap(far_next), column_swap(near_next)
+        far_land = half_swap(far_next)
+        near_land = column_swap(near_next)
         far = small_call(last_add_kernel, (far, far_land), low_shape(*block))
         got = across(far)
         near = small_call(last_add_kernel, (near, near_land), full_shape(*block))

time: 82.3 us -> 78 us (0.948)
  the two profiles are of different devices: /device:TPU:24 before, /device:TPU:0 now
where the time goes in v7:
time: 78 us; the launch traced here: 77.6 us
  waiting for transfers between devices  30.3 us (39%)
  starting transfers between devices  25.4 us (33%)
  Pallas kernels  13.9 us (18%)
  local copies, waits for them, and re-layouts  7.15 us (9%)
  between operations  0.85 us (1%)
    ppermute x19, waiting for transfers between devices, flipped(): lax.ppermute(value, axis, [(i, i ^ bit) for i in range(lax.axis_size(axis...  20.7 us
    ppermute x19, starting transfers between devices, flipped(): lax.ppermute(value, axis, [(i, i ^ bit) for i in range(lax.axis_size(axis...  18.1 us
    ppermute x1, waiting for transfers between devices, downward(): lax.ppermute(value, 'section', [(i + half_axis, i) for i in range(half_ax...  9.62 us
    unnamed x16, local copies, waits for them, and re-layouts  7.15 us
    pallas_call x13, Pallas kernels, small_call(): pl.pallas_call(kernel, out_shape=shapes, in_specs=specs, out_specs=jax.tr...  6.49 us
    ppermute x1, starting transfers between devices, upward(): lax.ppermute(value, 'section', [(i, i + half_axis) for i in range(half_ax...  6 us
    pallas_call x1, Pallas kernels, chain(): pl.pallas_call(chain_kernel, out_shape=(low_shape(rows, model), low_shape...  2.57 us
    pallas_call x1, Pallas kernels, middle_partials(): pl.pallas_call(middle_kernel, out_shape=(jax.ShapeDtypeStruct((part, inne...  1.87 us
  transfers between devices with their start and end apart: 21, of which 8 were waited for; matrix products, arithmetic and copies ran while one was open for 0% of the time, Pallas kernels for 13%

profile of v7, /device:TPU:0, one launch (start us, length us, event | category | flops | bytes accessed | tf_op | source)
XLA Modules:
  0.0 77.6 jit_solution(6991753898853102034)
XLA Ops:
  0.6 0.0 copy-start
  0.6 2.2 %copy-done = bf16[1,1,2,1024,1024]{4,3,2,1,0:T(8,128)(2,1)S(1)} copy-done((bf16[1,1,2,1024,1024]{4,3,2,1,0:T(8,128)(2,1)S(1)}, bf16[1,1,2,1024,1024]{4,3,2,1,0:T(8,128)(2,1)}, u32[]{:S(2)}) %copy-start) | copy-done | bytes 4194328
  2.8 2.2 %copy-done.2 = bf16[1,1,2,1024,1024]{4,3,2,1,0:T(8,128)(2,1)S(1)} copy-done((bf16[1,1,2,1024,1024]{4,3,2,1,0:T(8,128)(2,1)S(1)}, bf16[1,1,2,1024,1024]{4,3,2,1,0:T(8,128)(2,1)}, u32[]{:S(2)}) %copy-start.2) | copy-done | bytes 4194328
  5.0 1.0 %copy-done.4 = bf16[1,2,128,1024]{3,2,1,0:T(8,128)(2,1)S(1)} copy-done((bf16[1,2,128,1024]{3,2,1,0:T(8,128)(2,1)S(1)}, bf16[1,2,128,1024]{3,2,1,0:T(8,128)(2,1)}, u32[]{:S(2)}) %copy-start.4) | copy-done | bytes 524312
  6.1 1.0 %copy-done.5 = bf16[1,1,2,128,1024]{4,3,2,1,0:T(8,128)(2,1)S(1)} copy-done((bf16[1,1,2,128,1024]{4,3,2,1,0:T(8,128)(2,1)S(1)}, bf16[1,1,2,128,1024]{4,3,2,1,0:T(8,128)(2,1)}, u32[]{:S(2)}) %copy-start.5) | copy-done | bytes 524312
  7.1 0.7 copy-done.6
  7.8 2.6 %chain.1 = (bf16[128,1024]{1,0:T(8,128)(2,1)S(1)}, bf16[2,128,1024]{2,1,0:T(8,128)(2,1)S(1)}) custom-call(s32[2,3]{1,0:T(2,128)S(1)} %copy-done.6, bf16[2,128,1024]{2,1,0:T(8,128)(2,1)S(1)} %bitcast.11, bf16[2,128,1024]{2,1,0:T(8,128)(2,1)S(1)} %bitcast.13, bf16[2,1024,1024]{2,1,0:T(8,128)(2,1)S(1)} %bitcast.8, bf16[2,1024,1024]{2,1,0:T(8,128)(2,1)S(1)} %bitcast.4), custom_call_target="tpu_custom_call" | custom-call | flops 805306368 | bytes 4194304 | tf_op jit(solution)/shard_map/chain/pallas_call | solution.py:242
  10.4 0.0 copy-start.7
  10.4 6.0 %collective-permute-start.13 = (bf16[2,128,1024]{2,1,0:T(8,128)(2,1)S(1)}, bf16[2,128,1024]{2,1,0:T(8,128)(2,1)S(1)}, u32[]{:S(2)}, u32[]{:S(2)}) collective-permute-start(bf16[2,128,1024]{2,1,0:T(8,128)(2,1)S(1)} %get-tuple-element.51), channel_id=1, source_target_pairs={{0,4},{2,6},{1,5},{3,7},{8,12},{10,14},{9,13},{11,15},{16,20},{18,... | collective-permute-start | bytes 1572872 | tf_op jit(solution)/shard_map/ppermute | solution.py:625
  16.4 0.0 copy-start.1
  16.4 0.0 copy-start.3
  16.4 0.6 staged.1
  17.1 1.6 %collective-permute-start = (bf16[128,1024]{1,0:T(8,128)(2,1)S(1)}, bf16[128,1024]{1,0:T(8,128)(2,1)S(1)}, u32[]{:S(2)}, u32[]{:S(2)}) collective-permute-start(bf16[128,1024]{1,0:T(8,128)(2,1)S(1)} %get-tuple-element.32), channel_id=1, source_target_pairs={{0,16},{8,24},{16,0},{24,8},{1,17},{9,25},{17,1},{25,9},{2,18},{10... | collective-permute-start | bytes 786440 | tf_op jit(solution)/shard_map/ppermute | solution.py:599
  18.6 0.5 collective-permute-start.5
  19.1 7.2 %collective-permute-done.short_part.e2 = bf16[128,1024]{1,0:T(8,128)(2,1)S(1)} collective-permute-done((bf16[128,1024]{1,0:T(8,128)(2,1)S(1)}, bf16[128,1024]{1,0:T(8,128)(2,1)S(1)}, u32[]{:S(2)}, u32[]{:S(2)}) %collective-permute-start) | collective-permute-done | bytes 262176 | tf_op jit(solution)/shard_map/ppermute | solution.py:599
  26.3 0.6 by_role.2
  26.9 1.3 %collective-permute-start.1 = (bf16[128,1024]{1,0:T(8,128)(2,1)S(1)}, bf16[128,1024]{1,0:T(8,128)(2,1)S(1)}, u32[]{:S(2)}, u32[]{:S(2)}) collective-permute-start(bf16[128,1024]{1,0:T(8,128)(2,1)S(1)} %by_role.2), channel_id=1, source_target_pairs={{4,0},{6,2},{5,1},{7,3},{12,8},{14,10},{13,9},{15,11},{20,16},{22,... | collective-permute-start | bytes 786440 | tf_op jit(solution)/shard_map/ppermute | solution.py:628
  28.2 0.1 collective-permute-start.3
  28.3 0.5 collective-permute-start.4
  28.8 0.1 collective-permute-start.14
  28.9 1.6 %collective-permute-done.5.full_part = bf16[128,1024]{1,0:T(8,128)(2,1)S(1)} collective-permute-done((bf16[128,1024]{1,0:T(8,128)(2,1)S(1)}, bf16[128,1024]{1,0:T(8,128)(2,1)S(1)}, u32[]{:S(2)}, u32[]{:S(2)}) %collective-permute-start.5) | collective-permute-done | bytes 262176 | tf_op jit(solution)/shard_map/ppermute | solution.py:599
  30.5 0.6 by_role.3.e3
  31.1 0.1 collective-permute-start.6
  31.2 9.6 %collective-permute-done.1.late = bf16[128,1024]{1,0:T(8,128)(2,1)S(1)} collective-permute-done((bf16[128,1024]{1,0:T(8,128)(2,1)S(1)}, bf16[128,1024]{1,0:T(8,128)(2,1)S(1)}, u32[]{:S(2)}, u32[]{:S(2)}) %collective-permute-start.1) | collective-permute-done | bytes 262176 | tf_op jit(solution)/shard_map/ppermute | solution.py:628
  40.8 0.5 collective-permute-start.15
  41.3 1.1 %early.1 = (bf16[256,1024]{1,0:T(8,128)(2,1)S(1)}, bf16[256,512]{1,0:T(8,128)(2,1)S(1)}, bf16[256,512]{1,0:T(8,128)(2,1)S(1)}) custom-call(s32[2,3]{1,0:T(2,128)S(1)} %copy-done.7, bf16[128,1024]{1,0:T(8,128)(2,1)S(1)} %get-tuple-element.33.e1, bf16[128,1024]{1,0:T(8,128)(2,1)S(1)} %collective-permute-done.short_part.e2, ...), custom_call_target="tpu_custom_call" | custom-call | flops 536870912 | bytes 3145728 | tf_op jit(solution)/shard_map/early/pallas_call | solution.py:375
  42.5 1.9 %middle.1 = (f32[512,1024]{1,0:T(8,128)S(1)}, f32[512,1024]{1,0:T(8,128)S(1)}) custom-call(s32[2,3]{1,0:T(2,128)S(1)} %copy-done.7, bf16[128,1024]{1,0:T(8,128)(2,1)S(1)} %by_role.3.e3, bf16[128,1024]{1,0:T(8,128)(2,1)S(1)} %collective-permute-done.6.f3, bf16[256,512]{1,0:T(8,128)(2,1)S(1)} %get-tuple-element.36.unit_part, ...), custom_call_target="tpu_custom_call" | custom-call | flops 1073741824 | bytes 3145728 | tf_op jit(solution)/shard_map/middle/pallas_call | solution.py:405
  44.4 1.8 %shard_map.68 = (bf16[256,512]{1,0:T(8,128)(2,1)S(1)}, f32[256,512]{1,0:T(8,128)S(1)}, bf16[128,1024]{1,0:T(8,128)(2,1)S(1)}, f32[128,1024]{1,0:T(8,128)S(1)}, bf16[256,1024]{1,0:T(8,128)(2,1)S(1)}) custom-call(s32[2,3]{1,0:T(2,128)S(1)} %copy-done.7, bf16[128,1024]{1,0:T(8,128)(2,1)S(1)} %collective-permute-done.1.late, ...), custom_call_target="tpu_custom_call" | custom-call | flops 805306368 | tf_op jit(solution)/shard_map/pallas_call | solution.py:579
  46.2 1.5 %collective-permute-start.9 = (bf16[256,512]{1,0:T(8,128)(2,1)S(1)}, bf16[256,512]{1,0:T(8,128)(2,1)S(1)}, u32[]{:S(2)}, u32[]{:S(2)}) collective-permute-start(bf16[256,512]{1,0:T(8,128)(2,1)S(1)} %get-tuple-element.44), channel_id=1, source_target_pairs={{0,1},{1,0},{2,3},{3,2},{4,5},{5,4},{6,7},{7,6},{8,9},{9,8},{10,11... | collective-permute-start | bytes 786440 | tf_op jit(solution)/shard_map/ppermute | solution.py:599
  47.7 0.6 collective-permute-start.7
  48.3 1.8 %shard_map.75 = (bf16[256,512]{1,0:T(8,128)(2,1)S(1)}, f32[256,512]{1,0:T(8,128)S(1)}, bf16[128,1024]{1,0:T(8,128)(2,1)S(1)}, f32[128,1024]{1,0:T(8,128)S(1)}) custom-call(s32[2,3]{1,0:T(2,128)S(1)} %copy-done.7, bf16[256,1024]{1,0:T(8,128)(2,1)S(1)} %get-tuple-element.49.unit, bf16[128,1024]{1,0:T(8,128)(2,1)S(1)} %collective-permute-done.short_part.e2, ...), custom_call_target="tpu_custom_call" | custom-call | flops 536870912 | tf_op jit(solution)/shard_map/pallas_call | solution.py:579
  50.1 0.6 collective-permute-start.18
  50.7 4.7 %collective-permute-done.9.land = bf16[256,512]{1,0:T(8,128)(2,1)S(1)} collective-permute-done((bf16[256,512]{1,0:T(8,128)(2,1)S(1)}, bf16[256,512]{1,0:T(8,128)(2,1)S(1)}, u32[]{:S(2)}, u32[]{:S(2)}) %collective-permute-start.9) | collective-permute-done | bytes 262176 | tf_op jit(solution)/shard_map/ppermute | solution.py:599
  55.5 0.7 collective-permute-start.10
  56.1 1.4 %collective-permute-start.16 = (bf16[128,1024]{1,0:T(8,128)(2,1)S(1)}, bf16[128,1024]{1,0:T(8,128)(2,1)S(1)}, u32[]{:S(2)}, u32[]{:S(2)}) collective-permute-start(bf16[128,1024]{1,0:T(8,128)(2,1)S(1)} %get-tuple-element.53), channel_id=1, source_target_pairs={{0,2},{2,0},{4,6},{6,4},{1,3},{3,1},{5,7},{7,5},{8,10},{10,8},{12,... | collective-permute-start | bytes 786440 | tf_op jit(solution)/shard_map/ppermute | solution.py:599
  57.6 1.5 %collective-permute-start.8 = (bf16[128,512]{1,0:T(8,128)(2,1)S(1)}, bf16[128,512]{1,0:T(8,128)(2,1)S(1)}, u32[]{:S(2)}, u32[]{:S(2)}) collective-permute-start(bf16[128,512]{1,0:T(8,128)(2,1)S(1)} %get-tuple-element.42), channel_id=1, source_target_pairs={{0,1},{1,0},{2,3},{3,2},{4,5},{5,4},{6,7},{7,6},{8,9},{9,8},{10,11... | collective-permute-start | bytes 393224 | tf_op jit(solution)/shard_map/ppermute | solution.py:599
  59.2 2.7 %collective-permute-done.10.land = bf16[128,512]{1,0:T(8,128)(2,1)S(1)} collective-permute-done((bf16[128,512]{1,0:T(8,128)(2,1)S(1)}, bf16[128,512]{1,0:T(8,128)(2,1)S(1)}, u32[]{:S(2)}, u32[]{:S(2)}) %collective-permute-start.10) | collective-permute-done | bytes 131104 | tf_op jit(solution)/shard_map/ppermute | solution.py:599
  61.9 2.1 %collective-permute-start.11 = (bf16[128,512]{1,0:T(8,128)(2,1)S(1)}, bf16[128,512]{1,0:T(8,128)(2,1)S(1)}, u32[]{:S(2)}, u32[]{:S(2)}) collective-permute-start(bf16[128,512]{1,0:T(8,128)(2,1)S(1)} %shard_map.72), channel_id=1, source_target_pairs={{0,16},{8,24},{16,0},{24,8},{1,17},{9,25},{17,1},{25,9},{2,18},{10... | collective-permute-start | bytes 393224 | tf_op jit(solution)/shard_map/ppermute | solution.py:599
  64.1 0.6 collective-permute-start.19
  64.8 2.2 %collective-permute-done.11.got = bf16[128,512]{1,0:T(8,128)(2,1)S(1)} collective-permute-done((bf16[128,512]{1,0:T(8,128)(2,1)S(1)}, bf16[128,512]{1,0:T(8,128)(2,1)S(1)}, u32[]{:S(2)}, u32[]{:S(2)}) %collective-permute-start.11) | collective-permute-done | bytes 131104 | tf_op jit(solution)/shard_map/ppermute | solution.py:599
  67.0 0.6 shard_map.73
  67.6 2.0 %collective-permute-start.12 = (bf16[128,512]{1,0:T(8,128)(2,1)S(1)}, bf16[128,512]{1,0:T(8,128)(2,1)S(1)}, u32[]{:S(2)}, u32[]{:S(2)}) collective-permute-start(bf16[128,512]{1,0:T(8,128)(2,1)S(1)} %get-tuple-element.48), channel_id=1, source_target_pairs={{0,4},{2,6},{4,0},{6,2},{1,5},{3,7},{5,1},{7,3},{8,12},{10,14},{12... | collective-permute-start | bytes 393224 | tf_op jit(solution)/shard_map/ppermute | solution.py:599
  69.7 1.6 %collective-permute-start.17 = (bf16[128,512]{1,0:T(8,128)(2,1)S(1)}, bf16[128,512]{1,0:T(8,128)(2,1)S(1)}, u32[]{:S(2)}, u32[]{:S(2)}) collective-permute-start(bf16[128,512]{1,0:T(8,128)(2,1)S(1)} %get-tuple-element.55), channel_id=1, source_target_pairs={{0,1},{1,0},{2,3},{3,2},{4,5},{5,4},{6,7},{7,6},{8,9},{9,8},{10,11... | collective-permute-start | bytes 393224 | tf_op jit(solution)/shard_map/ppermute | solution.py:599
  71.3 2.1 %collective-permute-start.20 = (bf16[128,512]{1,0:T(8,128)(2,1)S(1)}, bf16[128,512]{1,0:T(8,128)(2,1)S(1)}, u32[]{:S(2)}, u32[]{:S(2)}) collective-permute-start(bf16[128,512]{1,0:T(8,128)(2,1)S(1)} %shard_map.79), channel_id=1, source_target_pairs={{0,16},{8,24},{16,0},{24,8},{1,17},{9,25},{17,1},{25,9},{2,18},{10... | collective-permute-start | bytes 393224 | tf_op jit(solution)/shard_map/ppermute | solution.py:599
  73.4 1.6 %collective-permute-done.12.landed = bf16[128,512]{1,0:T(8,128)(2,1)S(1)} collective-permute-done((bf16[128,512]{1,0:T(8,128)(2,1)S(1)}, bf16[128,512]{1,0:T(8,128)(2,1)S(1)}, u32[]{:S(2)}, u32[]{:S(2)}) %collective-permute-start.12) | collective-permute-done | bytes 131104 | tf_op jit(solution)/shard_map/ppermute | solution.py:599
  75.0 0.7 shard_map.74
  75.7 0.6 collective-permute-done.20.got
  76.3 1.3 %shard_map.80 = f32[1,128,512]{2,1,0:T(8,128)} custom-call(s32[2,3]{1,0:T(2,128)S(1)} %copy-done.7, f32[128,512]{1,0:T(8,128)S(1)} %shard_map.77.near, bf16[128,512]{1,0:T(8,128)(2,1)S(1)} %collective-permute-done.20.got), custom_call_target="tpu_custom_call" | custom-call | tf_op jit(solution)/shard_map/pallas_call | solution.py:579
  (30 shorter events, 0.3 us)
Async XLA Ops:
  0.6 2.2 %copy-start = (bf16[1,1,2,1024,1024]{4,3,2,1,0:T(8,128)(2,1)S(1)}, bf16[1,1,2,1024,1024]{4,3,2,1,0:T(8,128)(2,1)}, u32[]{:S(2)}) copy-start(bf16[1,1,2,1024,1024]{4,3,2,1,0:T(8,128)(2,1)} %param.8) | copy-start | bytes 12582916
  2.8 2.2 %copy-start.2 = (bf16[1,1,2,1024,1024]{4,3,2,1,0:T(8,128)(2,1)S(1)}, bf16[1,1,2,1024,1024]{4,3,2,1,0:T(8,128)(2,1)}, u32[]{:S(2)}) copy-start(bf16[1,1,2,1024,1024]{4,3,2,1,0:T(8,128)(2,1)} %param.7) | copy-start | bytes 12582916
  5.0 1.0 %copy-start.4 = (bf16[1,2,128,1024]{3,2,1,0:T(8,128)(2,1)S(1)}, bf16[1,2,128,1024]{3,2,1,0:T(8,128)(2,1)}, u32[]{:S(2)}) copy-start(bf16[1,2,128,1024]{3,2,1,0:T(8,128)(2,1)} %param.9) | copy-start | bytes 1572868
  6.1 1.0 %copy-start.5 = (bf16[1,1,2,128,1024]{4,3,2,1,0:T(8,128)(2,1)S(1)}, bf16[1,1,2,128,1024]{4,3,2,1,0:T(8,128)(2,1)}, u32[]{:S(2)}) copy-start(bf16[1,1,2,128,1024]{4,3,2,1,0:T(8,128)(2,1)} %param.6) | copy-start | bytes 1572868
  7.1 0.7 copy-start.6
  10.4 6.0 %copy-start.7 = (s32[2,3]{1,0:T(2,128)S(1)}, s32[2,3]{1,0:T(2,128)}, u32[]{:S(2)}) copy-start(s32[2,3]{1,0:T(2,128)} %bounds.19) | copy-start | bytes 76
  10.4 18.4 %collective-permute-start.13 = (bf16[2,128,1024]{2,1,0:T(8,128)(2,1)S(1)}, bf16[2,128,1024]{2,1,0:T(8,128)(2,1)S(1)}, u32[]{:S(2)}, u32[]{:S(2)}) collective-permute-start(bf16[2,128,1024]{2,1,0:T(8,128)(2,1)S(1)} %get-tuple-element.51), channel_id=1, source_target_pairs={{0,4},{2,6},{1,5},{3,7},{8,12},{10,14},{9,13},{11,15},{16,20},{18,... | collective-permute-start | bytes 1572872 | tf_op jit(solution)/shard_map/ppermute | solution.py:625
  16.4 24.9 %copy-start.1 = (bf16[1,1,2,1024,1024]{4,3,2,1,0:T(8,128)(2,1)S(1)}, bf16[1,1,2,1024,1024]{4,3,2,1,0:T(8,128)(2,1)}, u32[]{:S(2)}) copy-start(bf16[1,1,2,1024,1024]{4,3,2,1,0:T(8,128)(2,1)} %param.8) | copy-start | bytes 12582916
  16.4 24.9 %copy-start.3 = (bf16[1,1,2,1024,1024]{4,3,2,1,0:T(8,128)(2,1)S(1)}, bf16[1,1,2,1024,1024]{4,3,2,1,0:T(8,128)(2,1)}, u32[]{:S(2)}) copy-start(bf16[1,1,2,1024,1024]{4,3,2,1,0:T(8,128)(2,1)} %param.7) | copy-start | bytes 12582916
  17.1 9.2 %collective-permute-start = (bf16[128,1024]{1,0:T(8,128)(2,1)S(1)}, bf16[128,1024]{1,0:T(8,128)(2,1)S(1)}, u32[]{:S(2)}, u32[]{:S(2)}) collective-permute-start(bf16[128,1024]{1,0:T(8,128)(2,1)S(1)} %get-tuple-element.32), channel_id=1, source_target_pairs={{0,16},{8,24},{16,0},{24,8},{1,17},{9,25},{17,1},{25,9},{2,18},{10... | collective-permute-start | bytes 786440 | tf_op jit(solution)/shard_map/ppermute | solution.py:599
  18.6 11.9 %collective-permute-start.5 = (bf16[128,1024]{1,0:T(8,128)(2,1)S(1)}, bf16[128,1024]{1,0:T(8,128)(2,1)S(1)}, u32[]{:S(2)}, u32[]{:S(2)}) collective-permute-start(bf16[128,1024]{1,0:T(8,128)(2,1)S(1)} %get-tuple-element.31.full_part.low), channel_id=1, source_target_pairs={{0,16},{8,24},{16,0},{24,8},{1,17},{9,25},{17,1},{25,9},{2,18},{10... | collective-permute-start | bytes 786440 | tf_op jit(solution)/shard_map/ppermute | solution.py:599
  26.9 13.9 %collective-permute-start.1 = (bf16[128,1024]{1,0:T(8,128)(2,1)S(1)}, bf16[128,1024]{1,0:T(8,128)(2,1)S(1)}, u32[]{:S(2)}, u32[]{:S(2)}) collective-permute-start(bf16[128,1024]{1,0:T(8,128)(2,1)S(1)} %by_role.2), channel_id=1, source_target_pairs={{4,0},{6,2},{5,1},{7,3},{12,8},{14,10},{13,9},{15,11},{20,16},{22,... | collective-permute-start | bytes 786440 | tf_op jit(solution)/shard_map/ppermute | solution.py:628
  28.2 12.6 %collective-permute-start.3 = (bf16[128,1024]{1,0:T(8,128)(2,1)S(1)}, bf16[128,1024]{1,0:T(8,128)(2,1)S(1)}, u32[]{:S(2)}, u32[]{:S(2)}) collective-permute-start(bf16[128,1024]{1,0:T(8,128)(2,1)S(1)} %get-tuple-element.33.e1), channel_id=1, source_target_pairs={{0,8},{8,0},{16,24},{24,16},{1,9},{9,1},{17,25},{25,17},{2,10},{10... | collective-permute-start | bytes 786440 | tf_op jit(solution)/shard_map/ppermute | solution.py:599
  28.3 13.1 %collective-permute-start.4 = (bf16[128,1024]{1,0:T(8,128)(2,1)S(1)}, bf16[128,1024]{1,0:T(8,128)(2,1)S(1)}, u32[]{:S(2)}, u32[]{:S(2)}) collective-permute-start(bf16[128,1024]{1,0:T(8,128)(2,1)S(1)} %collective-permute-done.short_part.e2), channel_id=1, source_target_pairs={{0,8},{8,0},{16,24},{24,16},{1,9},{9,1},{17,25},{25,17},{2,10},{10... | collective-permute-start | bytes 786440 | tf_op jit(solution)/shard_map/ppermute | solution.py:599
  28.8 19.5 %collective-permute-start.14 = (bf16[2,128,1024]{2,1,0:T(8,128)(2,1)S(1)}, bf16[2,128,1024]{2,1,0:T(8,128)(2,1)S(1)}, u32[]{:S(2)}, u32[]{:S(2)}) collective-permute-start(bf16[2,128,1024]{2,1,0:T(8,128)(2,1)S(1)} %collective-permute-done.13.up), channel_id=1, source_target_pairs={{0,8},{8,0},{16,24},{24,16},{1,9},{9,1},{17,25},{25,17},{2,10},{10... | collective-permute-start | bytes 1572872 | tf_op jit(solution)/shard_map/ppermute | solution.py:599
  31.1 11.4 %collective-permute-start.6 = (bf16[128,1024]{1,0:T(8,128)(2,1)S(1)}, bf16[128,1024]{1,0:T(8,128)(2,1)S(1)}, u32[]{:S(2)}, u32[]{:S(2)}) collective-permute-start(bf16[128,1024]{1,0:T(8,128)(2,1)S(1)} %by_role.3.e3), channel_id=1, source_target_pairs={{0,8},{8,0},{16,24},{24,16},{1,9},{9,1},{17,25},{25,17},{2,10},{10... | collective-permute-start | bytes 786440 | tf_op jit(solution)/shard_map/ppermute | solution.py:599
  40.8 3.5 %collective-permute-start.2 = (bf16[128,1024]{1,0:T(8,128)(2,1)S(1)}, bf16[128,1024]{1,0:T(8,128)(2,1)S(1)}, u32[]{:S(2)}, u32[]{:S(2)}) collective-permute-start(bf16[128,1024]{1,0:T(8,128)(2,1)S(1)} %collective-permute-done.1.late), channel_id=1, source_target_pairs={{0,8},{8,0},{16,24},{24,16},{1,9},{9,1},{17,25},{25,17},{2,10},{10... | collective-permute-start | bytes 786440 | tf_op jit(solution)/shard_map/ppermute | solution.py:599
  40.8 7.5 %collective-permute-start.15 = (bf16[128,1024]{1,0:T(8,128)(2,1)S(1)}, bf16[128,1024]{1,0:T(8,128)(2,1)S(1)}, u32[]{:S(2)}, u32[]{:S(2)}) collective-permute-start(bf16[128,1024]{1,0:T(8,128)(2,1)S(1)} %get-tuple-element.31.full_part.low), channel_id=1, source_target_pairs={{0,8},{8,0},{16,24},{24,16},{1,9},{9,1},{17,25},{25,17},{2,10},{10... | collective-permute-start | bytes 786440 | tf_op jit(solution)/shard_map/ppermute | solution.py:599
  46.2 9.2 %collective-permute-start.9 = (bf16[256,512]{1,0:T(8,128)(2,1)S(1)}, bf16[256,512]{1,0:T(8,128)(2,1)S(1)}, u32[]{:S(2)}, u32[]{:S(2)}) collective-permute-start(bf16[256,512]{1,0:T(8,128)(2,1)S(1)} %get-tuple-element.44), channel_id=1, source_target_pairs={{0,1},{1,0},{2,3},{3,2},{4,5},{5,4},{6,7},{7,6},{8,9},{9,8},{10,11... | collective-permute-start | bytes 786440 | tf_op jit(solution)/shard_map/ppermute | solution.py:599
  47.7 9.8 %collective-permute-start.7 = (bf16[128,1024]{1,0:T(8,128)(2,1)S(1)}, bf16[128,1024]{1,0:T(8,128)(2,1)S(1)}, u32[]{:S(2)}, u32[]{:S(2)}) collective-permute-start(bf16[128,1024]{1,0:T(8,128)(2,1)S(1)} %get-tuple-element.40), channel_id=1, source_target_pairs={{0,2},{2,0},{4,6},{6,4},{1,3},{3,1},{5,7},{7,5},{8,10},{10,8},{12,... | collective-permute-start | bytes 786440 | tf_op jit(solution)/shard_map/ppermute | solution.py:599
  50.1 14.0 %collective-permute-start.18 = (bf16[256,512]{1,0:T(8,128)(2,1)S(1)}, bf16[256,512]{1,0:T(8,128)(2,1)S(1)}, u32[]{:S(2)}, u32[]{:S(2)}) collective-permute-start(bf16[256,512]{1,0:T(8,128)(2,1)S(1)} %get-tuple-element.57), channel_id=1, source_target_pairs={{0,1},{1,0},{2,3},{3,2},{4,5},{5,4},{6,7},{7,6},{8,9},{9,8},{10,11... | collective-permute-start | bytes 786440 | tf_op jit(solution)/shard_map/ppermute | solution.py:599
  55.5 6.4 %collective-permute-start.10 = (bf16[128,512]{1,0:T(8,128)(2,1)S(1)}, bf16[128,512]{1,0:T(8,128)(2,1)S(1)}, u32[]{:S(2)}, u32[]{:S(2)}) collective-permute-start(bf16[128,512]{1,0:T(8,128)(2,1)S(1)} %get-tuple-element.46), channel_id=1, source_target_pairs={{0,2},{2,0},{4,6},{6,4},{1,3},{3,1},{5,7},{7,5},{8,10},{10,8},{12,... | collective-permute-start | bytes 393224 | tf_op jit(solution)/shard_map/ppermute | solution.py:599
  56.1 13.5 %collective-permute-start.16 = (bf16[128,1024]{1,0:T(8,128)(2,1)S(1)}, bf16[128,1024]{1,0:T(8,128)(2,1)S(1)}, u32[]{:S(2)}, u32[]{:S(2)}) collective-permute-start(bf16[128,1024]{1,0:T(8,128)(2,1)S(1)} %get-tuple-element.53), channel_id=1, source_target_pairs={{0,2},{2,0},{4,6},{6,4},{1,3},{3,1},{5,7},{7,5},{8,10},{10,8},{12,... | collective-permute-start | bytes 786440 | tf_op jit(solution)/shard_map/ppermute | solution.py:599
  57.6 7.2 %collective-permute-start.8 = (bf16[128,512]{1,0:T(8,128)(2,1)S(1)}, bf16[128,512]{1,0:T(8,128)(2,1)S(1)}, u32[]{:S(2)}, u32[]{:S(2)}) collective-permute-start(bf16[128,512]{1,0:T(8,128)(2,1)S(1)} %get-tuple-element.42), channel_id=1, source_target_pairs={{0,1},{1,0},{2,3},{3,2},{4,5},{5,4},{6,7},{7,6},{8,9},{9,8},{10,11... | collective-permute-start | bytes 393224 | tf_op jit(solution)/shard_map/ppermute | solution.py:599
  61.9 5.1 %collective-permute-start.11 = (bf16[128,512]{1,0:T(8,128)(2,1)S(1)}, bf16[128,512]{1,0:T(8,128)(2,1)S(1)}, u32[]{:S(2)}, u32[]{:S(2)}) collective-permute-start(bf16[128,512]{1,0:T(8,128)(2,1)S(1)} %shard_map.72), channel_id=1, source_target_pairs={{0,16},{8,24},{16,0},{24,8},{1,17},{9,25},{17,1},{25,9},{2,18},{10... | collective-permute-start | bytes 393224 | tf_op jit(solution)/shard_map/ppermute | solution.py:599
  64.1 7.1 %collective-permute-start.19 = (bf16[128,512]{1,0:T(8,128)(2,1)S(1)}, bf16[128,512]{1,0:T(8,128)(2,1)S(1)}, u32[]{:S(2)}, u32[]{:S(2)}) collective-permute-start(bf16[128,512]{1,0:T(8,128)(2,1)S(1)} %get-tuple-element.59), channel_id=1, source_target_pairs={{0,2},{2,0},{4,6},{6,4},{1,3},{3,1},{5,7},{7,5},{8,10},{10,8},{12,... | collective-permute-start | bytes 393224 | tf_op jit(solution)/shard_map/ppermute | solution.py:599
  67.6 7.3 %collective-permute-start.12 = (bf16[128,512]{1,0:T(8,128)(2,1)S(1)}, bf16[128,512]{1,0:T(8,128)(2,1)S(1)}, u32[]{:S(2)}, u32[]{:S(2)}) collective-permute-start(bf16[128,512]{1,0:T(8,128)(2,1)S(1)} %get-tuple-element.48), channel_id=1, source_target_pairs={{0,4},{2,6},{4,0},{6,2},{1,5},{3,7},{5,1},{7,3},{8,12},{10,14},{12... | collective-permute-start | bytes 393224 | tf_op jit(solution)/shard_map/ppermute | solution.py:599
  69.7 6.0 %collective-permute-start.17 = (bf16[128,512]{1,0:T(8,128)(2,1)S(1)}, bf16[128,512]{1,0:T(8,128)(2,1)S(1)}, u32[]{:S(2)}, u32[]{:S(2)}) collective-permute-start(bf16[128,512]{1,0:T(8,128)(2,1)S(1)} %get-tuple-element.55), channel_id=1, source_target_pairs={{0,1},{1,0},{2,3},{3,2},{4,5},{5,4},{6,7},{7,6},{8,9},{9,8},{10,11... | collective-permute-start | bytes 393224 | tf_op jit(solution)/shard_map/ppermute | solution.py:599
  71.3 5.0 %collective-permute-start.20 = (bf16[128,512]{1,0:T(8,128)(2,1)S(1)}, bf16[128,512]{1,0:T(8,128)(2,1)S(1)}, u32[]{:S(2)}, u32[]{:S(2)}) collective-permute-start(bf16[128,512]{1,0:T(8,128)(2,1)S(1)} %shard_map.79), channel_id=1, source_target_pairs={{0,16},{8,24},{16,0},{24,8},{1,17},{9,25},{17,1},{25,9},{2,18},{10... | collective-permute-start | bytes 393224 | tf_op jit(solution)/shard_map/ppermute | solution.py:599

commit v8 on v7

--- a/solution.py
+++ b/solution.py
@@ -193,7 +193,7 @@
 
 
 class Place:
-    def __init__(self, bounds):
+    def __init__(self, short):
         pipe = lax.axis_index("pipe")
         section = lax.axis_index("section")
         self.column = lax.axis_index("tensor")
@@ -201,7 +201,7 @@
         self.core = pipe % 2
         self.half = section % 2
         self.left = section < 2
-        self.short = (bounds[self.relay, 1] - bounds[self.relay, 0]) == 2
+        self.short = short
         self.slot = jnp.where(self.short, 1, 0)
         self.upper_slot = jnp.where(self.left, 1, 0)
 
@@ -220,8 +220,8 @@
     return lax.dot_general(left, right, (((0,), (0,)), ((), ())), preferred_element_type=jnp.float32)
 
 
-def chain_kernel(bounds, tops, saved, w_in, w_out, grad_out, upward):
-    place = Place(bounds)
+def chain_kernel(flag, tops, saved, w_in, w_out, grad_out, upward):
+    place = Place(flag[0, 0] > 0)
     slot = place.upper_slot
     first_unit = norm_rows(saved[0])[0].astype(jnp.bfloat16)
     upward[0] = jnp.dot(first_unit, w_in[0], preferred_element_type=jnp.float32).astype(jnp.bfloat16)
@@ -236,20 +236,20 @@
     upward[1] = grad_low
 
 
-def chain(bounds, tops, saved, w_in, w_out):
+def chain(flag, tops, saved, w_in, w_out):
     rows, model = saved.shape[1:]
     inner = w_in.shape[2]
     return pl.pallas_call(
         chain_kernel,
         out_shape=(low_shape(rows, model), low_shape(2, rows, model)),
-        in_specs=[SMEM] + [VMEM] * 4,
+        in_specs=[VMEM] * 5,
         out_specs=(VMEM,) * 2,
         compiler_params=pltpu.CompilerParams(vmem_limit_bytes=KERNEL_BYTES),
         cost_estimate=pl.CostEstimate(
             flops=6 * rows * model * inner, bytes_accessed=4 * model * inner, transcendentals=0
         ),
         name="chain",
-    )(bounds, tops, saved, w_in, w_out)
+    )(flag, tops, saved, w_in, w_out)
 
 
 def opening_kernel(mark):
@@ -267,9 +267,11 @@
     )()
 
 
-def staged_kernel(bounds, mark, saved, tops, own_saved, own_top, given):
-    place = Place(bounds)
+def staged_kernel(bounds, mark, saved, tops, own_saved, own_top, given, flag):
+    relay = lax.axis_index("pipe") // 2
+    place = Place(bounds[relay, 1] - bounds[relay, 0] == 2)
     give_top = place.left & jnp.logical_not(place.short)
+    flag[...] = jnp.full_like(flag, jnp.where(place.short, 1, 0))
     own_saved[...] = saved[place.slot]
     own_top[...] = tops[place.half]
 
@@ -286,17 +288,17 @@
     block = jax.ShapeDtypeStruct(saved.shape[1:], saved.dtype)
     return pl.pallas_call(
         staged_kernel,
-        out_shape=(block,) * 3,
+        out_shape=(block,) * 3 + (jax.ShapeDtypeStruct((8, 128), jnp.int32),),
         in_specs=[SMEM, VMEM, VMEM, VMEM],
-        out_specs=(VMEM,) * 3,
+        out_specs=(VMEM,) * 4,
         compiler_params=pltpu.CompilerParams(vmem_limit_bytes=KERNEL_BYTES),
         cost_estimate=pl.CostEstimate(flops=STAGE_FLOPS, bytes_accessed=8 * saved.size, transcendentals=0),
         name="staged",
     )(bounds, opening(), saved, tops)
 
 
-def by_role_kernel(bounds, full_part, short_part, chosen):
-    place = Place(bounds)
+def by_role_kernel(flag, full_part, short_part, chosen):
+    place = Place(flag[0, 0] > 0)
 
     @pl.when(place.short)
     def _():
@@ -307,15 +309,15 @@
         chosen[...] = full_part[...]
 
 
-def by_role(bounds, full_part, short_part):
+def by_role(flag, full_part, short_part):
     return pl.pallas_call(
         by_role_kernel,
         out_shape=jax.ShapeDtypeStruct(full_part.shape, full_part.dtype),
-        in_specs=[SMEM, VMEM, VMEM],
+        in_specs=[VMEM] * 3,
         out_specs=VMEM,
         compiler_params=pltpu.CompilerParams(vmem_limit_bytes=KERNEL_BYTES),
         name="by_role",
-    )(bounds, full_part, short_part)
+    )(flag, full_part, short_part)
 
 
 BLOCKS = 4
@@ -349,8 +351,8 @@
         ).astype(jnp.bfloat16)
 
 
-def early_kernel(bounds, e1, e2, f1, f2, w_in, w_out, early_part, unit_part, value, unit):
-    place = Place(bounds)
+def early_kernel(flag, e1, e2, f1, f2, w_in, w_out, early_part, unit_part, value, unit):
+    place = Place(flag[0, 0] > 0)
 
     @pl.when(jnp.logical_not(place.short))
     def _():
@@ -368,7 +370,7 @@
         early_part[...] = nt_dot(both, w_out[place.slot]).astype(jnp.bfloat16)
 
 
-def early_factors(bounds, own, partner, w_in, w_out):
+def early_factors(flag, own, partner, w_in, w_out):
     rows, model = own[0].shape
     inner = w_in.shape[2]
     part = model // 2
@@ -379,7 +381,7 @@
             jax.ShapeDtypeStruct((2 * rows, part), jnp.bfloat16),
             jax.ShapeDtypeStruct((2 * rows, part), jnp.bfloat16),
         ),
-        in_specs=[SMEM] + [VMEM] * 6,
+        in_specs=[VMEM] * 7,
         out_specs=(VMEM,) * 3,
         scratch_shapes=[pltpu.VMEM((2 * rows, model), jnp.bfloat16)],
         compiler_params=pltpu.CompilerParams(vmem_limit_bytes=KERNEL_BYTES),
@@ -387,18 +389,18 @@
             flops=4 * rows * model * inner, bytes_accessed=3 * model * inner, transcendentals=0
         ),
         name="early",
-    )(bounds, *own, *partner, w_in, w_out)
-
-
-def middle_kernel(bounds, e3, f3, unit_part, value, w_out, in_acc, out_acc):
-    place = Place(bounds)
+    )(flag, *own, *partner, w_in, w_out)
+
+
+def middle_kernel(flag, e3, f3, unit_part, value, w_out, in_acc, out_acc):
+    place = Place(flag[0, 0] > 0)
     grads = jnp.concatenate([e3[...], f3[...]], axis=0)
     err = nt_dot(grads, w_out[place.slot]).astype(jnp.bfloat16)
     in_acc[...] = tn_dot(unit_part[...], err)
     out_acc[...] = tn_dot(value[...], grads)
 
 
-def middle_partials(bounds, e3, f3, unit_part, value, w_out):
+def middle_partials(flag, e3, f3, unit_part, value, w_out):
     rows, model = e3.shape
     inner = w_out.shape[1]
     part = unit_part.shape[1]
@@ -408,14 +410,14 @@
             jax.ShapeDtypeStruct((part, inner), jnp.float32),
             jax.ShapeDtypeStruct((part, model), jnp.float32),
         ),
-        in_specs=[SMEM] + [VMEM] * 5,
+        in_specs=[VMEM] * 6,
         out_specs=(VMEM,) * 2,
         compiler_params=pltpu.CompilerParams(vmem_limit_bytes=KERNEL_BYTES),
         cost_estimate=pl.CostEstimate(
             flops=8 * rows * model * inner, bytes_accessed=3 * model * inner, transcendentals=0
         ),
         name="middle",
-    )(bounds, e3, f3, unit_part, value, w_out)
+    )(flag, e3, f3, unit_part, value, w_out)
 
 
 def split_sums(place, left_part, right_part, acc, x_send, x_keep, z_send, z_keep):
@@ -440,9 +442,9 @@
 
 
 def late_in_kernel(
-    bounds, late, flate, early_part, in_acc, w_out, x_send, x_keep, z_send, z_keep, unit, unit_part, err,
+    flag, late, flate, early_part, in_acc, w_out, x_send, x_keep, z_send, z_keep, unit, unit_part, err,
 ):
-    place = Place(bounds)
+    place = Place(flag[0, 0] > 0)
     part = unit_part.shape[1]
 
     @pl.when(jnp.logical_not(place.short))
@@ -461,10 +463,10 @@
 
 
 def late_out_kernel(
-    bounds, unit, e2, f2, out_acc, w_in, up, fup, low, flow,
+    flag, unit, e2, f2, out_acc, w_in, up, fup, low, flow,
     x_send, x_keep, z_send, z_keep, value, grads, unit_part,
 ):
-    place = Place(bounds)
+    place = Place(flag[0, 0] > 0)
     rows = e2.shape[0]
     part = value.shape[1]
     lanes = part // BLOCKS
@@ -530,8 +532,8 @@
     total[...] = (mine[...] + land[...].astype(jnp.float32)).astype(total.dtype)
 
 
-def hand_on_kernel(bounds, near, got, give, lower):
-    place = Place(bounds)
+def hand_on_kernel(flag, near, got, give, lower):
+    place = Place(flag[0, 0] > 0)
 
     @pl.when(place.short)
     def _():
@@ -556,8 +558,8 @@
         result[0] = landed[...].astype(jnp.float32)
 
 
-def out_result_kernel(bounds, near, got, result):
-    place = Place(bounds)
+def out_result_kernel(flag, near, got, result):
+    place = Place(flag[0, 0] > 0)
     upper = jnp.logical_not(place.left)
 
     @pl.when(upper)
@@ -574,12 +576,11 @@
 
 
 def small_call(kernel, operands, shapes, scratch=(), flops=0):
-    specs = [SMEM if part.ndim == 2 and part.dtype == jnp.int32 else VMEM for part in operands]
     cost = pl.CostEstimate(flops=flops, bytes_accessed=0, transcendentals=0) if flops else None
     return pl.pallas_call(
         kernel,
         out_shape=shapes,
-        in_specs=specs,
+        in_specs=[VMEM] * len(operands),
         out_specs=jax.tree.map(lambda _: VMEM, shapes),
         scratch_shapes=scratch,
         compiler_params=pltpu.CompilerParams(vmem_limit_bytes=KERNEL_BYTES),
@@ -630,19 +631,19 @@
     def section_swap(value):
         return flipped(value, "section", 2)
 
-    own_saved, own_top, given = staged(bounds, saved, tops)
+    own_saved, own_top, given, flag = staged(bounds, saved, tops)
     swapped = across(given)
     rows = saved.shape[1]
-    grad_low, upload = chain(bounds, tops, saved, proj_in, proj_out)
+    grad_low, upload = chain(flag, tops, saved, proj_in, proj_out)
     lifted = upward(upload)
-    hopping = by_role(bounds, grad_low, swapped)
+    hopping = by_role(flag, grad_low, swapped)
     late = downward(hopping)
     grad_other = across(grad_low)
     own = (own_saved, swapped)
     partner = tuple(core_swap(part) for part in own)
-    early_part, unit_part, value = early_factors(bounds, own, partner, proj_in, proj_out)
-    grad_early = by_role(bounds, grad_other, own_top)
-    in_acc, out_acc = middle_partials(bounds, grad_early, core_swap(grad_early), unit_part, value, proj_out)
+    early_part, unit_part, value = early_factors(flag, own, partner, proj_in, proj_out)
+    grad_early = by_role(flag, grad_other, own_top)
+    in_acc, out_acc = middle_partials(flag, grad_early, core_swap(grad_early), unit_part, value, proj_out)
     other_low = core_swap(grad_low)
     other_lifted = core_swap(lifted)
     other_late = core_swap(late)
@@ -650,14 +651,14 @@
     pair = 2 * rows
     *in_parts, unit_late = small_call(
         late_in_kernel,
-        (bounds, late, other_late, early_part, in_acc, proj_out),
+        (flag, late, other_late, early_part, in_acc, proj_out),
         split_shapes(part, inner) + (low_shape(pair, model),),
         scratch=[pltpu.VMEM((pair, part), jnp.bfloat16), pltpu.VMEM((pair, inner), jnp.bfloat16)],
         flops=6 * rows * model * inner,
     )
     out_parts = small_call(
         late_out_kernel,
-        (bounds, unit_late, own[1], partner[1], out_acc, proj_in)
+        (flag, unit_late, own[1], partner[1], out_acc, proj_in)
         + (lifted, other_lifted, grad_low, other_low),
         split_shapes(part, model),
         scratch=[
@@ -683,12 +684,12 @@
         sums.append((near, got))
     (in_near, in_got), (out_near, out_got) = sums
     give, lower = small_call(
-        hand_on_kernel, (bounds, in_near, in_got), (low_shape(*block), full_shape(*block))
+        hand_on_kernel, (flag, in_near, in_got), (low_shape(*block), full_shape(*block))
     )
     landed = section_swap(give)
     return (
         small_call(in_result_kernel, (lower, landed), full_shape(1, *block)),
-        small_call(out_result_kernel, (bounds, out_near, out_got), full_shape(1, *block)),
+        small_call(out_result_kernel, (flag, out_near, out_got), full_shape(1, *block)),
     )
 
 

time: 78 us -> 72 us (0.923)
  Pallas kernels: 13.9 us -> 9.07 us
  local copies, waits for them, and re-layouts: 7.15 us -> 4 us
  starting transfers between devices: 25.4 us -> 28 us
    unnamed x16 -> x10, local copies, waits for them, and re-layouts: 7.15 us -> 4 us
    ppermute x19, starting transfers between devices: 18.1 us -> 20.7 us  [flipped(): lax.ppermute(value, axis, [(i, i ^ bit) for i in range(lax.axis_size(axis...]
    pallas_call x14, Pallas kernels: 7.12 us -> 5.01 us  [the longest x13 4.38 us: small_call(): pl.pallas_call(kernel, out_shape=shapes, in_specs=[VMEM] * len(operands),...]
    pallas_call x2, Pallas kernels: 1.18 us -> 0.11 us  [by_role(): pl.pallas_call(by_role_kernel, out_shape=jax.ShapeDtypeStruct(full_part.s...]
  transfers between devices with their start and end apart: 21 -> 21, of which waited for: 8 -> 8; matrix products, arithmetic and copies ran while one was open for 0% -> 0% of each run, Pallas kernels for 13% -> 8%
where the time goes in v8:
time: 72 us; the launch traced here: 71.8 us
  waiting for transfers between devices  29.9 us (42%)
  starting transfers between devices  28 us (39%)
  Pallas kernels  9.07 us (13%)
  local copies, waits for them, and re-layouts  4 us (6%)
  between operations  0.83 us (1%)
    ppermute x19, starting transfers between devices, flipped(): lax.ppermute(value, axis, [(i, i ^ bit) for i in range(lax.axis_size(axis...  20.7 us
    ppermute x19, waiting for transfers between devices, flipped(): lax.ppermute(value, axis, [(i, i ^ bit) for i in range(lax.axis_size(axis...  20.3 us
    ppermute x1, waiting for transfers between devices, downward(): lax.ppermute(value, 'section', [(i + half_axis, i) for i in range(half_ax...  9.61 us
    ppermute x1, starting transfers between devices, upward(): lax.ppermute(value, 'section', [(i, i + half_axis) for i in range(half_ax...  6 us
    pallas_call x13, Pallas kernels, small_call(): pl.pallas_call(kernel, out_shape=shapes, in_specs=[VMEM] * len(operands),...  4.38 us
    unnamed x10, local copies, waits for them, and re-layouts  4 us
    pallas_call x1, Pallas kernels, chain(): pl.pallas_call(chain_kernel, out_shape=(low_shape(rows, model), low_shape...  2.03 us
  transfers between devices with their start and end apart: 21, of which 8 were waited for; matrix products, arithmetic and copies ran while one was open for 0% of the time, Pallas kernels for 8%

profile of v8, /device:TPU:0, one launch (start us, length us, event | category | flops | bytes accessed | tf_op | source)
XLA Modules:
  0.0 71.8 jit_solution(10730239797774996959)
XLA Ops:
  0.7 1.0 %copy-done.2 = bf16[1,1,2,128,1024]{4,3,2,1,0:T(8,128)(2,1)S(1)} copy-done((bf16[1,1,2,128,1024]{4,3,2,1,0:T(8,128)(2,1)S(1)}, bf16[1,1,2,128,1024]{4,3,2,1,0:T(8,128)(2,1)}, u32[]{:S(2)}) %copy-start.2) | copy-done | bytes 524312
  1.7 0.2 copy-done.3
  1.8 0.6 staged.1
  2.5 1.6 %copy-done = bf16[1,1,2,1024,1024]{4,3,2,1,0:T(8,128)(2,1)S(1)} copy-done((bf16[1,1,2,1024,1024]{4,3,2,1,0:T(8,128)(2,1)S(1)}, bf16[1,1,2,1024,1024]{4,3,2,1,0:T(8,128)(2,1)}, u32[]{:S(2)}) %copy-start) | copy-done | bytes 4194328
  4.0 1.3 %copy-done.1 = bf16[1,1,2,1024,1024]{4,3,2,1,0:T(8,128)(2,1)S(1)} copy-done((bf16[1,1,2,1024,1024]{4,3,2,1,0:T(8,128)(2,1)S(1)}, bf16[1,1,2,1024,1024]{4,3,2,1,0:T(8,128)(2,1)}, u32[]{:S(2)}) %copy-start.1) | copy-done | bytes 4194328
  5.3 2.0 %chain.1 = (bf16[128,1024]{1,0:T(8,128)(2,1)S(1)}, bf16[2,128,1024]{2,1,0:T(8,128)(2,1)S(1)}) custom-call(s32[8,128]{1,0:T(8,128)S(1)} %get-tuple-element.32.flag, bf16[2,128,1024]{2,1,0:T(8,128)(2,1)S(1)} %bitcast.14, bf16[2,128,1024]{2,1,0:T(8,128)(2,1)S(1)} %bitcast.12, bf16[2,1024,1024]{2,1,0:T(8,128)(2,1)S(1)} %bitcast.8, bf16[2,1024,1024]{2,1,0:T(8,128)(2,1)S(1)} %bitcast.4), custom_call_target="tpu_custom_call" | custom-call | flops 805306368 | bytes 4194304 | tf_op jit(solution)/shard_map/chain/pallas_call | solution.py:242
  7.3 6.0 %collective-permute-start.13 = (bf16[2,128,1024]{2,1,0:T(8,128)(2,1)S(1)}, bf16[2,128,1024]{2,1,0:T(8,128)(2,1)S(1)}, u32[]{:S(2)}, u32[]{:S(2)}) collective-permute-start(bf16[2,128,1024]{2,1,0:T(8,128)(2,1)S(1)} %get-tuple-element.53), channel_id=1, source_target_pairs={{0,4},{2,6},{1,5},{3,7},{8,12},{10,14},{9,13},{11,15},{16,20},{18,... | collective-permute-start | bytes 1572872 | tf_op jit(solution)/shard_map/ppermute | solution.py:626
  13.3 1.6 %collective-permute-start = (bf16[128,1024]{1,0:T(8,128)(2,1)S(1)}, bf16[128,1024]{1,0:T(8,128)(2,1)S(1)}, u32[]{:S(2)}, u32[]{:S(2)}) collective-permute-start(bf16[128,1024]{1,0:T(8,128)(2,1)S(1)} %get-tuple-element.34), channel_id=1, source_target_pairs={{0,16},{8,24},{16,0},{24,8},{1,17},{9,25},{17,1},{25,9},{2,18},{10... | collective-permute-start | bytes 786440 | tf_op jit(solution)/shard_map/ppermute | solution.py:600
  14.9 0.5 collective-permute-start.5
  15.4 7.2 %collective-permute-done.short_part.e2 = bf16[128,1024]{1,0:T(8,128)(2,1)S(1)} collective-permute-done((bf16[128,1024]{1,0:T(8,128)(2,1)S(1)}, bf16[128,1024]{1,0:T(8,128)(2,1)S(1)}, u32[]{:S(2)}, u32[]{:S(2)}) %collective-permute-start) | collective-permute-done | bytes 262176 | tf_op jit(solution)/shard_map/ppermute | solution.py:600
  22.6 0.1 by_role.2
  22.7 1.3 %collective-permute-start.1 = (bf16[128,1024]{1,0:T(8,128)(2,1)S(1)}, bf16[128,1024]{1,0:T(8,128)(2,1)S(1)}, u32[]{:S(2)}, u32[]{:S(2)}) collective-permute-start(bf16[128,1024]{1,0:T(8,128)(2,1)S(1)} %by_role.2), channel_id=1, source_target_pairs={{4,0},{6,2},{5,1},{7,3},{12,8},{14,10},{13,9},{15,11},{20,16},{22,... | collective-permute-start | bytes 786440 | tf_op jit(solution)/shard_map/ppermute | solution.py:629
  24.0 0.1 collective-permute-start.3
  24.0 0.5 collective-permute-start.4
  24.5 0.0 collective-permute-done.13.up
  24.5 0.1 collective-permute-start.14
  24.6 2.2 %collective-permute-done.5.full_part = bf16[128,1024]{1,0:T(8,128)(2,1)S(1)} collective-permute-done((bf16[128,1024]{1,0:T(8,128)(2,1)S(1)}, bf16[128,1024]{1,0:T(8,128)(2,1)S(1)}, u32[]{:S(2)}, u32[]{:S(2)}) %collective-permute-start.5) | collective-permute-done | bytes 262176 | tf_op jit(solution)/shard_map/ppermute | solution.py:600
  26.8 0.1 by_role.3.e3
  26.9 0.1 collective-permute-start.6
  26.9 9.6 %collective-permute-done.1.late = bf16[128,1024]{1,0:T(8,128)(2,1)S(1)} collective-permute-done((bf16[128,1024]{1,0:T(8,128)(2,1)S(1)}, bf16[128,1024]{1,0:T(8,128)(2,1)S(1)}, u32[]{:S(2)}, u32[]{:S(2)}) %collective-permute-start.1) | collective-permute-done | bytes 262176 | tf_op jit(solution)/shard_map/ppermute | solution.py:629
  36.6 0.0 collective-permute-done.3.f1
  36.6 0.5 collective-permute-start.15
  37.1 0.0 collective-permute-done.4.f2
  37.1 0.6 early.1
  37.7 1.3 %middle.1 = (f32[512,1024]{1,0:T(8,128)S(1)}, f32[512,1024]{1,0:T(8,128)S(1)}) custom-call(s32[8,128]{1,0:T(8,128)S(1)} %get-tuple-element.32.flag, bf16[128,1024]{1,0:T(8,128)(2,1)S(1)} %by_role.3.e3, bf16[128,1024]{1,0:T(8,128)(2,1)S(1)} %collective-permute-done.6.f3, bf16[256,512]{1,0:T(8,128)(2,1)S(1)} %get-tuple-element.38.unit_part, ...), custom_call_target="tpu_custom_call" | custom-call | flops 1073741824 | bytes 3145728 | tf_op jit(solution)/shard_map/middle/pallas_call | solution.py:407
  39.0 1.3 %shard_map.68 = (bf16[256,512]{1,0:T(8,128)(2,1)S(1)}, f32[256,512]{1,0:T(8,128)S(1)}, bf16[128,1024]{1,0:T(8,128)(2,1)S(1)}, f32[128,1024]{1,0:T(8,128)S(1)}, bf16[256,1024]{1,0:T(8,128)(2,1)S(1)}) custom-call(s32[8,128]{1,0:T(8,128)S(1)} %get-tuple-element.32.flag, bf16[128,1024]{1,0:T(8,128)(2,1)S(1)} %collective-permute-done.1.late, ...), custom_call_target="tpu_custom_call" | custom-call | flops 805306368 | tf_op jit(solution)/shard_map/pallas_call | solution.py:580
  40.3 1.6 %collective-permute-start.9 = (bf16[256,512]{1,0:T(8,128)(2,1)S(1)}, bf16[256,512]{1,0:T(8,128)(2,1)S(1)}, u32[]{:S(2)}, u32[]{:S(2)}) collective-permute-start(bf16[256,512]{1,0:T(8,128)(2,1)S(1)} %get-tuple-element.46), channel_id=1, source_target_pairs={{0,1},{1,0},{2,3},{3,2},{4,5},{5,4},{6,7},{7,6},{8,9},{9,8},{10,11... | collective-permute-start | bytes 786440 | tf_op jit(solution)/shard_map/ppermute | solution.py:600
  41.9 1.8 %collective-permute-start.7 = (bf16[128,1024]{1,0:T(8,128)(2,1)S(1)}, bf16[128,1024]{1,0:T(8,128)(2,1)S(1)}, u32[]{:S(2)}, u32[]{:S(2)}) collective-permute-start(bf16[128,1024]{1,0:T(8,128)(2,1)S(1)} %get-tuple-element.42), channel_id=1, source_target_pairs={{0,2},{2,0},{4,6},{6,4},{1,3},{3,1},{5,7},{7,5},{8,10},{10,8},{12,... | collective-permute-start | bytes 786440 | tf_op jit(solution)/shard_map/ppermute | solution.py:600
  43.6 1.2 %shard_map.75 = (bf16[256,512]{1,0:T(8,128)(2,1)S(1)}, f32[256,512]{1,0:T(8,128)S(1)}, bf16[128,1024]{1,0:T(8,128)(2,1)S(1)}, f32[128,1024]{1,0:T(8,128)S(1)}) custom-call(s32[8,128]{1,0:T(8,128)S(1)} %get-tuple-element.32.flag, bf16[256,1024]{1,0:T(8,128)(2,1)S(1)} %get-tuple-element.51.unit, bf16[128,1024]{1,0:T(8,128)(2,1)S(1)} %collective-permute-done.short_part.e2, ...), custom_call_target="tpu_custom_call" | custom-call | flops 536870912 | tf_op jit(solution)/shard_map/pallas_call | solution.py:580
  44.9 0.6 collective-permute-start.18
  45.5 4.0 %collective-permute-done.9.land = bf16[256,512]{1,0:T(8,128)(2,1)S(1)} collective-permute-done((bf16[256,512]{1,0:T(8,128)(2,1)S(1)}, bf16[256,512]{1,0:T(8,128)(2,1)S(1)}, u32[]{:S(2)}, u32[]{:S(2)}) %collective-permute-start.9) | collective-permute-done | bytes 262176 | tf_op jit(solution)/shard_map/ppermute | solution.py:600
  49.5 0.1 shard_map.71
  49.6 1.9 %collective-permute-start.10 = (bf16[128,512]{1,0:T(8,128)(2,1)S(1)}, bf16[128,512]{1,0:T(8,128)(2,1)S(1)}, u32[]{:S(2)}, u32[]{:S(2)}) collective-permute-start(bf16[128,512]{1,0:T(8,128)(2,1)S(1)} %get-tuple-element.48), channel_id=1, source_target_pairs={{0,2},{2,0},{4,6},{6,4},{1,3},{3,1},{5,7},{7,5},{8,10},{10,8},{12,... | collective-permute-start | bytes 393224 | tf_op jit(solution)/shard_map/ppermute | solution.py:600
  51.4 0.2 collective-permute-start.16
  51.7 0.1 shard_map.69
  51.8 1.6 %collective-permute-start.8 = (bf16[128,512]{1,0:T(8,128)(2,1)S(1)}, bf16[128,512]{1,0:T(8,128)(2,1)S(1)}, u32[]{:S(2)}, u32[]{:S(2)}) collective-permute-start(bf16[128,512]{1,0:T(8,128)(2,1)S(1)} %get-tuple-element.44), channel_id=1, source_target_pairs={{0,1},{1,0},{2,3},{3,2},{4,5},{5,4},{6,7},{7,6},{8,9},{9,8},{10,11... | collective-permute-start | bytes 393224 | tf_op jit(solution)/shard_map/ppermute | solution.py:600
  53.3 2.7 %collective-permute-done.10.land = bf16[128,512]{1,0:T(8,128)(2,1)S(1)} collective-permute-done((bf16[128,512]{1,0:T(8,128)(2,1)S(1)}, bf16[128,512]{1,0:T(8,128)(2,1)S(1)}, u32[]{:S(2)}, u32[]{:S(2)}) %collective-permute-start.10) | collective-permute-done | bytes 131104 | tf_op jit(solution)/shard_map/ppermute | solution.py:600
  56.1 2.2 %collective-permute-start.11 = (bf16[128,512]{1,0:T(8,128)(2,1)S(1)}, bf16[128,512]{1,0:T(8,128)(2,1)S(1)}, u32[]{:S(2)}, u32[]{:S(2)}) collective-permute-start(bf16[128,512]{1,0:T(8,128)(2,1)S(1)} %shard_map.72), channel_id=1, source_target_pairs={{0,16},{8,24},{16,0},{24,8},{1,17},{9,25},{17,1},{25,9},{2,18},{10... | collective-permute-start | bytes 393224 | tf_op jit(solution)/shard_map/ppermute | solution.py:600
  58.3 1.3 %collective-permute-start.19 = (bf16[128,512]{1,0:T(8,128)(2,1)S(1)}, bf16[128,512]{1,0:T(8,128)(2,1)S(1)}, u32[]{:S(2)}, u32[]{:S(2)}) collective-permute-start(bf16[128,512]{1,0:T(8,128)(2,1)S(1)} %get-tuple-element.61), channel_id=1, source_target_pairs={{0,2},{2,0},{4,6},{6,4},{1,3},{3,1},{5,7},{7,5},{8,10},{10,8},{12,... | collective-permute-start | bytes 393224 | tf_op jit(solution)/shard_map/ppermute | solution.py:600
  59.6 1.5 %collective-permute-done.11.got = bf16[128,512]{1,0:T(8,128)(2,1)S(1)} collective-permute-done((bf16[128,512]{1,0:T(8,128)(2,1)S(1)}, bf16[128,512]{1,0:T(8,128)(2,1)S(1)}, u32[]{:S(2)}, u32[]{:S(2)}) %collective-permute-start.11) | collective-permute-done | bytes 131104 | tf_op jit(solution)/shard_map/ppermute | solution.py:600
  61.2 0.1 shard_map.73
  61.2 3.1 %collective-permute-start.12 = (bf16[128,512]{1,0:T(8,128)(2,1)S(1)}, bf16[128,512]{1,0:T(8,128)(2,1)S(1)}, u32[]{:S(2)}, u32[]{:S(2)}) collective-permute-start(bf16[128,512]{1,0:T(8,128)(2,1)S(1)} %get-tuple-element.50), channel_id=1, source_target_pairs={{0,4},{2,6},{4,0},{6,2},{1,5},{3,7},{5,1},{7,3},{8,12},{10,14},{12... | collective-permute-start | bytes 393224 | tf_op jit(solution)/shard_map/ppermute | solution.py:600
  64.4 1.6 %collective-permute-start.17 = (bf16[128,512]{1,0:T(8,128)(2,1)S(1)}, bf16[128,512]{1,0:T(8,128)(2,1)S(1)}, u32[]{:S(2)}, u32[]{:S(2)}) collective-permute-start(bf16[128,512]{1,0:T(8,128)(2,1)S(1)} %get-tuple-element.57), channel_id=1, source_target_pairs={{0,1},{1,0},{2,3},{3,2},{4,5},{5,4},{6,7},{7,6},{8,9},{9,8},{10,11... | collective-permute-start | bytes 393224 | tf_op jit(solution)/shard_map/ppermute | solution.py:600
  66.0 1.6 %collective-permute-start.20 = (bf16[128,512]{1,0:T(8,128)(2,1)S(1)}, bf16[128,512]{1,0:T(8,128)(2,1)S(1)}, u32[]{:S(2)}, u32[]{:S(2)}) collective-permute-start(bf16[128,512]{1,0:T(8,128)(2,1)S(1)} %shard_map.79), channel_id=1, source_target_pairs={{0,16},{8,24},{16,0},{24,8},{1,17},{9,25},{17,1},{25,9},{2,18},{10... | collective-permute-start | bytes 393224 | tf_op jit(solution)/shard_map/ppermute | solution.py:600
  67.7 0.7 %shard_map.74 = f32[1,128,512]{2,1,0:T(8,128)} custom-call(f32[128,512]{1,0:T(8,128)S(1)} %get-tuple-element.49.lower, bf16[128,512]{1,0:T(8,128)(2,1)S(1)} %collective-permute-done.12.landed), custom_call_target="tpu_custom_call" | custom-call | tf_op jit(solution)/shard_map/pallas_call | solution.py:580
  68.4 1.1 %collective-permute-done.17.land = bf16[128,512]{1,0:T(8,128)(2,1)S(1)} collective-permute-done((bf16[128,512]{1,0:T(8,128)(2,1)S(1)}, bf16[128,512]{1,0:T(8,128)(2,1)S(1)}, u32[]{:S(2)}, u32[]{:S(2)}) %collective-permute-start.17) | collective-permute-done | bytes 131104 | tf_op jit(solution)/shard_map/ppermute | solution.py:600
  69.5 1.6 %collective-permute-done.20.got = bf16[128,512]{1,0:T(8,128)(2,1)S(1)} collective-permute-done((bf16[128,512]{1,0:T(8,128)(2,1)S(1)}, bf16[128,512]{1,0:T(8,128)(2,1)S(1)}, u32[]{:S(2)}, u32[]{:S(2)}) %collective-permute-start.20) | collective-permute-done | bytes 131104 | tf_op jit(solution)/shard_map/ppermute | solution.py:600
  71.1 0.8 %shard_map.80 = f32[1,128,512]{2,1,0:T(8,128)} custom-call(s32[8,128]{1,0:T(8,128)S(1)} %get-tuple-element.32.flag, f32[128,512]{1,0:T(8,128)S(1)} %shard_map.77.near, bf16[128,512]{1,0:T(8,128)(2,1)S(1)} %collective-permute-done.20.got), custom_call_target="tpu_custom_call" | custom-call | tf_op jit(solution)/shard_map/pallas_call | solution.py:580
  (24 shorter events, 0.2 us)
Async XLA Ops:
  0.6 1.0 %copy-start.2 = (bf16[1,1,2,128,1024]{4,3,2,1,0:T(8,128)(2,1)S(1)}, bf16[1,1,2,128,1024]{4,3,2,1,0:T(8,128)(2,1)}, u32[]{:S(2)}) copy-start(bf16[1,1,2,128,1024]{4,3,2,1,0:T(8,128)(2,1)} %param.6) | copy-start | bytes 1572868
  0.6 1.2 %copy-start.3 = (bf16[1,2,128,1024]{3,2,1,0:T(8,128)(2,1)S(1)}, bf16[1,2,128,1024]{3,2,1,0:T(8,128)(2,1)}, u32[]{:S(2)}) copy-start(bf16[1,2,128,1024]{3,2,1,0:T(8,128)(2,1)} %param.9) | copy-start | bytes 1572868
  0.6 1.2 %copy-start.4 = (s32[2,3]{1,0:T(2,128)S(1)}, s32[2,3]{1,0:T(2,128)}, u32[]{:S(2)}) copy-start(s32[2,3]{1,0:T(2,128)} %bounds.1) | copy-start | bytes 76
  1.8 2.2 %copy-start = (bf16[1,1,2,1024,1024]{4,3,2,1,0:T(8,128)(2,1)S(1)}, bf16[1,1,2,1024,1024]{4,3,2,1,0:T(8,128)(2,1)}, u32[]{:S(2)}) copy-start(bf16[1,1,2,1024,1024]{4,3,2,1,0:T(8,128)(2,1)} %param.8) | copy-start | bytes 12582916
  1.8 3.5 %copy-start.1 = (bf16[1,1,2,1024,1024]{4,3,2,1,0:T(8,128)(2,1)S(1)}, bf16[1,1,2,1024,1024]{4,3,2,1,0:T(8,128)(2,1)}, u32[]{:S(2)}) copy-start(bf16[1,1,2,1024,1024]{4,3,2,1,0:T(8,128)(2,1)} %param.7) | copy-start | bytes 12582916
  7.3 17.2 %collective-permute-start.13 = (bf16[2,128,1024]{2,1,0:T(8,128)(2,1)S(1)}, bf16[2,128,1024]{2,1,0:T(8,128)(2,1)S(1)}, u32[]{:S(2)}, u32[]{:S(2)}) collective-permute-start(bf16[2,128,1024]{2,1,0:T(8,128)(2,1)S(1)} %get-tuple-element.53), channel_id=1, source_target_pairs={{0,4},{2,6},{1,5},{3,7},{8,12},{10,14},{9,13},{11,15},{16,20},{18,... | collective-permute-start | bytes 1572872 | tf_op jit(solution)/shard_map/ppermute | solution.py:626
  13.3 9.2 %collective-permute-start = (bf16[128,1024]{1,0:T(8,128)(2,1)S(1)}, bf16[128,1024]{1,0:T(8,128)(2,1)S(1)}, u32[]{:S(2)}, u32[]{:S(2)}) collective-permute-start(bf16[128,1024]{1,0:T(8,128)(2,1)S(1)} %get-tuple-element.34), channel_id=1, source_target_pairs={{0,16},{8,24},{16,0},{24,8},{1,17},{9,25},{17,1},{25,9},{2,18},{10... | collective-permute-start | bytes 786440 | tf_op jit(solution)/shard_map/ppermute | solution.py:600
  14.9 11.9 %collective-permute-start.5 = (bf16[128,1024]{1,0:T(8,128)(2,1)S(1)}, bf16[128,1024]{1,0:T(8,128)(2,1)S(1)}, u32[]{:S(2)}, u32[]{:S(2)}) collective-permute-start(bf16[128,1024]{1,0:T(8,128)(2,1)S(1)} %get-tuple-element.33.full_part.low), channel_id=1, source_target_pairs={{0,16},{8,24},{16,0},{24,8},{1,17},{9,25},{17,1},{25,9},{2,18},{10... | collective-permute-start | bytes 786440 | tf_op jit(solution)/shard_map/ppermute | solution.py:600
  22.7 13.9 %collective-permute-start.1 = (bf16[128,1024]{1,0:T(8,128)(2,1)S(1)}, bf16[128,1024]{1,0:T(8,128)(2,1)S(1)}, u32[]{:S(2)}, u32[]{:S(2)}) collective-permute-start(bf16[128,1024]{1,0:T(8,128)(2,1)S(1)} %by_role.2), channel_id=1, source_target_pairs={{4,0},{6,2},{5,1},{7,3},{12,8},{14,10},{13,9},{15,11},{20,16},{22,... | collective-permute-start | bytes 786440 | tf_op jit(solution)/shard_map/ppermute | solution.py:629
  24.0 12.6 %collective-permute-start.3 = (bf16[128,1024]{1,0:T(8,128)(2,1)S(1)}, bf16[128,1024]{1,0:T(8,128)(2,1)S(1)}, u32[]{:S(2)}, u32[]{:S(2)}) collective-permute-start(bf16[128,1024]{1,0:T(8,128)(2,1)S(1)} %get-tuple-element.35.e1), channel_id=1, source_target_pairs={{0,8},{8,0},{16,24},{24,16},{1,9},{9,1},{17,25},{25,17},{2,10},{10... | collective-permute-start | bytes 786440 | tf_op jit(solution)/shard_map/ppermute | solution.py:600
  24.0 13.0 %collective-permute-start.4 = (bf16[128,1024]{1,0:T(8,128)(2,1)S(1)}, bf16[128,1024]{1,0:T(8,128)(2,1)S(1)}, u32[]{:S(2)}, u32[]{:S(2)}) collective-permute-start(bf16[128,1024]{1,0:T(8,128)(2,1)S(1)} %collective-permute-done.short_part.e2), channel_id=1, source_target_pairs={{0,8},{8,0},{16,24},{24,16},{1,9},{9,1},{17,25},{25,17},{2,10},{10... | collective-permute-start | bytes 786440 | tf_op jit(solution)/shard_map/ppermute | solution.py:600
  24.5 19.1 %collective-permute-start.14 = (bf16[2,128,1024]{2,1,0:T(8,128)(2,1)S(1)}, bf16[2,128,1024]{2,1,0:T(8,128)(2,1)S(1)}, u32[]{:S(2)}, u32[]{:S(2)}) collective-permute-start(bf16[2,128,1024]{2,1,0:T(8,128)(2,1)S(1)} %collective-permute-done.13.up), channel_id=1, source_target_pairs={{0,8},{8,0},{16,24},{24,16},{1,9},{9,1},{17,25},{25,17},{2,10},{10... | collective-permute-start | bytes 1572872 | tf_op jit(solution)/shard_map/ppermute | solution.py:600
  26.9 10.8 %collective-permute-start.6 = (bf16[128,1024]{1,0:T(8,128)(2,1)S(1)}, bf16[128,1024]{1,0:T(8,128)(2,1)S(1)}, u32[]{:S(2)}, u32[]{:S(2)}) collective-permute-start(bf16[128,1024]{1,0:T(8,128)(2,1)S(1)} %by_role.3.e3), channel_id=1, source_target_pairs={{0,8},{8,0},{16,24},{24,16},{1,9},{9,1},{17,25},{25,17},{2,10},{10... | collective-permute-start | bytes 786440 | tf_op jit(solution)/shard_map/ppermute | solution.py:600
  36.5 2.5 %collective-permute-start.2 = (bf16[128,1024]{1,0:T(8,128)(2,1)S(1)}, bf16[128,1024]{1,0:T(8,128)(2,1)S(1)}, u32[]{:S(2)}, u32[]{:S(2)}) collective-permute-start(bf16[128,1024]{1,0:T(8,128)(2,1)S(1)} %collective-permute-done.1.late), channel_id=1, source_target_pairs={{0,8},{8,0},{16,24},{24,16},{1,9},{9,1},{17,25},{25,17},{2,10},{10... | collective-permute-start | bytes 786440 | tf_op jit(solution)/shard_map/ppermute | solution.py:600
  36.6 7.1 %collective-permute-start.15 = (bf16[128,1024]{1,0:T(8,128)(2,1)S(1)}, bf16[128,1024]{1,0:T(8,128)(2,1)S(1)}, u32[]{:S(2)}, u32[]{:S(2)}) collective-permute-start(bf16[128,1024]{1,0:T(8,128)(2,1)S(1)} %get-tuple-element.33.full_part.low), channel_id=1, source_target_pairs={{0,8},{8,0},{16,24},{24,16},{1,9},{9,1},{17,25},{25,17},{2,10},{10... | collective-permute-start | bytes 786440 | tf_op jit(solution)/shard_map/ppermute | solution.py:600
  40.3 9.2 %collective-permute-start.9 = (bf16[256,512]{1,0:T(8,128)(2,1)S(1)}, bf16[256,512]{1,0:T(8,128)(2,1)S(1)}, u32[]{:S(2)}, u32[]{:S(2)}) collective-permute-start(bf16[256,512]{1,0:T(8,128)(2,1)S(1)} %get-tuple-element.46), channel_id=1, source_target_pairs={{0,1},{1,0},{2,3},{3,2},{4,5},{5,4},{6,7},{7,6},{8,9},{9,8},{10,11... | collective-permute-start | bytes 786440 | tf_op jit(solution)/shard_map/ppermute | solution.py:600
  41.9 9.8 %collective-permute-start.7 = (bf16[128,1024]{1,0:T(8,128)(2,1)S(1)}, bf16[128,1024]{1,0:T(8,128)(2,1)S(1)}, u32[]{:S(2)}, u32[]{:S(2)}) collective-permute-start(bf16[128,1024]{1,0:T(8,128)(2,1)S(1)} %get-tuple-element.42), channel_id=1, source_target_pairs={{0,2},{2,0},{4,6},{6,4},{1,3},{3,1},{5,7},{7,5},{8,10},{10,8},{12,... | collective-permute-start | bytes 786440 | tf_op jit(solution)/shard_map/ppermute | solution.py:600
  44.9 13.3 %collective-permute-start.18 = (bf16[256,512]{1,0:T(8,128)(2,1)S(1)}, bf16[256,512]{1,0:T(8,128)(2,1)S(1)}, u32[]{:S(2)}, u32[]{:S(2)}) collective-permute-start(bf16[256,512]{1,0:T(8,128)(2,1)S(1)} %get-tuple-element.59), channel_id=1, source_target_pairs={{0,1},{1,0},{2,3},{3,2},{4,5},{5,4},{6,7},{7,6},{8,9},{9,8},{10,11... | collective-permute-start | bytes 786440 | tf_op jit(solution)/shard_map/ppermute | solution.py:600
  49.6 6.4 %collective-permute-start.10 = (bf16[128,512]{1,0:T(8,128)(2,1)S(1)}, bf16[128,512]{1,0:T(8,128)(2,1)S(1)}, u32[]{:S(2)}, u32[]{:S(2)}) collective-permute-start(bf16[128,512]{1,0:T(8,128)(2,1)S(1)} %get-tuple-element.48), channel_id=1, source_target_pairs={{0,2},{2,0},{4,6},{6,4},{1,3},{3,1},{5,7},{7,5},{8,10},{10,8},{12,... | collective-permute-start | bytes 393224 | tf_op jit(solution)/shard_map/ppermute | solution.py:600
  51.4 12.9 %collective-permute-start.16 = (bf16[128,1024]{1,0:T(8,128)(2,1)S(1)}, bf16[128,1024]{1,0:T(8,128)(2,1)S(1)}, u32[]{:S(2)}, u32[]{:S(2)}) collective-permute-start(bf16[128,1024]{1,0:T(8,128)(2,1)S(1)} %get-tuple-element.55), channel_id=1, source_target_pairs={{0,2},{2,0},{4,6},{6,4},{1,3},{3,1},{5,7},{7,5},{8,10},{10,8},{12,... | collective-permute-start | bytes 786440 | tf_op jit(solution)/shard_map/ppermute | solution.py:600
  51.8 7.9 %collective-permute-start.8 = (bf16[128,512]{1,0:T(8,128)(2,1)S(1)}, bf16[128,512]{1,0:T(8,128)(2,1)S(1)}, u32[]{:S(2)}, u32[]{:S(2)}) collective-permute-start(bf16[128,512]{1,0:T(8,128)(2,1)S(1)} %get-tuple-element.44), channel_id=1, source_target_pairs={{0,1},{1,0},{2,3},{3,2},{4,5},{5,4},{6,7},{7,6},{8,9},{9,8},{10,11... | collective-permute-start | bytes 393224 | tf_op jit(solution)/shard_map/ppermute | solution.py:600
  56.1 5.1 %collective-permute-start.11 = (bf16[128,512]{1,0:T(8,128)(2,1)S(1)}, bf16[128,512]{1,0:T(8,128)(2,1)S(1)}, u32[]{:S(2)}, u32[]{:S(2)}) collective-permute-start(bf16[128,512]{1,0:T(8,128)(2,1)S(1)} %shard_map.72), channel_id=1, source_target_pairs={{0,16},{8,24},{16,0},{24,8},{1,17},{9,25},{17,1},{25,9},{2,18},{10... | collective-permute-start | bytes 393224 | tf_op jit(solution)/shard_map/ppermute | solution.py:600
  58.3 7.7 %collective-permute-start.19 = (bf16[128,512]{1,0:T(8,128)(2,1)S(1)}, bf16[128,512]{1,0:T(8,128)(2,1)S(1)}, u32[]{:S(2)}, u32[]{:S(2)}) collective-permute-start(bf16[128,512]{1,0:T(8,128)(2,1)S(1)} %get-tuple-element.61), channel_id=1, source_target_pairs={{0,2},{2,0},{4,6},{6,4},{1,3},{3,1},{5,7},{7,5},{8,10},{10,8},{12,... | collective-permute-start | bytes 393224 | tf_op jit(solution)/shard_map/ppermute | solution.py:600
  61.2 6.4 %collective-permute-start.12 = (bf16[128,512]{1,0:T(8,128)(2,1)S(1)}, bf16[128,512]{1,0:T(8,128)(2,1)S(1)}, u32[]{:S(2)}, u32[]{:S(2)}) collective-permute-start(bf16[128,512]{1,0:T(8,128)(2,1)S(1)} %get-tuple-element.50), channel_id=1, source_target_pairs={{0,4},{2,6},{4,0},{6,2},{1,5},{3,7},{5,1},{7,3},{8,12},{10,14},{12... | collective-permute-start | bytes 393224 | tf_op jit(solution)/shard_map/ppermute | solution.py:600
  64.4 5.0 %collective-permute-start.17 = (bf16[128,512]{1,0:T(8,128)(2,1)S(1)}, bf16[128,512]{1,0:T(8,128)(2,1)S(1)}, u32[]{:S(2)}, u32[]{:S(2)}) collective-permute-start(bf16[128,512]{1,0:T(8,128)(2,1)S(1)} %get-tuple-element.57), channel_id=1, source_target_pairs={{0,1},{1,0},{2,3},{3,2},{4,5},{5,4},{6,7},{7,6},{8,9},{9,8},{10,11... | collective-permute-start | bytes 393224 | tf_op jit(solution)/shard_map/ppermute | solution.py:600
  66.0 5.0 %collective-permute-start.20 = (bf16[128,512]{1,0:T(8,128)(2,1)S(1)}, bf16[128,512]{1,0:T(8,128)(2,1)S(1)}, u32[]{:S(2)}, u32[]{:S(2)}) collective-permute-start(bf16[128,512]{1,0:T(8,128)(2,1)S(1)} %shard_map.79), channel_id=1, source_target_pairs={{0,16},{8,24},{16,0},{24,8},{1,17},{9,25},{17,1},{25,9},{2,18},{10... | collective-permute-start | bytes 393224 | tf_op jit(solution)/shard_map/ppermute | solution.py:600

commit v9 on v8

--- a/solution.py
+++ b/solution.py
@@ -546,33 +546,25 @@
         lower[...] = got[...].astype(jnp.float32)
 
 
-def in_result_kernel(lower, landed, result):
-    left = lax.axis_index("section") < 2
-
-    @pl.when(left)
-    def _():
-        result[0] = lower[...]
-
-    @pl.when(jnp.logical_not(left))
-    def _():
-        result[0] = landed[...].astype(jnp.float32)
-
-
-def out_result_kernel(flag, near, got, result):
+def results_kernel(flag, lower, landed, near, got, in_result, out_result):
     place = Place(flag[0, 0] > 0)
-    upper = jnp.logical_not(place.left)
-
-    @pl.when(upper)
-    def _():
-        result[0] = near[...] + got[...].astype(jnp.float32)
+
+    @pl.when(place.left)
+    def _():
+        in_result[0] = lower[...]
+
+    @pl.when(jnp.logical_not(place.left))
+    def _():
+        in_result[0] = landed[...].astype(jnp.float32)
+        out_result[0] = near[...] + got[...].astype(jnp.float32)
 
     @pl.when(place.left & place.short)
     def _():
-        result[0] = near[...]
+        out_result[0] = near[...]
 
     @pl.when(place.left & jnp.logical_not(place.short))
     def _():
-        result[0] = got[...].astype(jnp.float32)
+        out_result[0] = got[...].astype(jnp.float32)
 
 
 def small_call(kernel, operands, shapes, scratch=(), flops=0):
@@ -687,9 +679,8 @@
         hand_on_kernel, (flag, in_near, in_got), (low_shape(*block), full_shape(*block))
     )
     landed = section_swap(give)
-    return (
-        small_call(in_result_kernel, (lower, landed), full_shape(1, *block)),
-        small_call(out_result_kernel, (flag, out_near, out_got), full_shape(1, *block)),
+    return small_call(
+        results_kernel, (flag, lower, landed, out_near, out_got), (full_shape(1, *block),) * 2
     )
 
 

time: 72 us -> 72.1 us (level)
    ppermute x19, waiting for transfers between devices: 20.3 us -> 21 us  [flipped(): lax.ppermute(value, axis, [(i, i ^ bit) for i in range(lax.axis_size(axis...]
    pallas_call x13 -> x12, Pallas kernels: 4.38 us -> 3.76 us  [small_call(): pl.pallas_call(kernel, out_shape=shapes, in_specs=[VMEM] * len(operands),...]
  transfers between devices with their start and end apart: 21 -> 21, of which waited for: 8 -> 8; matrix products, arithmetic and copies ran while one was open for 0% -> 0% of each run, Pallas kernels for 8% -> 7%
where the time goes in v9:
time: 72.1 us; the launch traced here: 71.9 us
  waiting for transfers between devices  30.6 us (42%)
  starting transfers between devices  28 us (39%)
  Pallas kernels  8.44 us (12%)
  local copies, waits for them, and re-layouts  4 us (6%)
  between operations  0.83 us (1%)
    ppermute x19, waiting for transfers between devices, flipped(): lax.ppermute(value, axis, [(i, i ^ bit) for i in range(lax.axis_size(axis...  21 us
    ppermute x19, starting transfers between devices, flipped(): lax.ppermute(value, axis, [(i, i ^ bit) for i in range(lax.axis_size(axis...  20.7 us
    ppermute x1, waiting for transfers between devices, downward(): lax.ppermute(value, 'section', [(i + half_axis, i) for i in range(half_ax...  9.61 us
    ppermute x1, starting transfers between devices, upward(): lax.ppermute(value, 'section', [(i, i + half_axis) for i in range(half_ax...  6 us
    unnamed x10, local copies, waits for them, and re-layouts  4 us
    pallas_call x12, Pallas kernels, small_call(): pl.pallas_call(kernel, out_shape=shapes, in_specs=[VMEM] * len(operands),...  3.76 us
    pallas_call x1, Pallas kernels, chain(): pl.pallas_call(chain_kernel, out_shape=(low_shape(rows, model), low_shape...  2.03 us
  transfers between devices with their start and end apart: 21, of which 8 were waited for; matrix products, arithmetic and copies ran while one was open for 0% of the time, Pallas kernels for 7%

profile of v9, /device:TPU:0, one launch (start us, length us, event | category | flops | bytes accessed | tf_op | source)
XLA Modules:
  0.0 71.9 jit_solution(6955748500134660130)
XLA Ops:
  0.7 1.0 %copy-done.2 = bf16[1,1,2,128,1024]{4,3,2,1,0:T(8,128)(2,1)S(1)} copy-done((bf16[1,1,2,128,1024]{4,3,2,1,0:T(8,128)(2,1)S(1)}, bf16[1,1,2,128,1024]{4,3,2,1,0:T(8,128)(2,1)}, u32[]{:S(2)}) %copy-start.2) | copy-done | bytes 524312
  1.7 0.2 copy-done.3
  1.8 0.6 staged.1
  2.5 1.6 %copy-done = bf16[1,1,2,1024,1024]{4,3,2,1,0:T(8,128)(2,1)S(1)} copy-done((bf16[1,1,2,1024,1024]{4,3,2,1,0:T(8,128)(2,1)S(1)}, bf16[1,1,2,1024,1024]{4,3,2,1,0:T(8,128)(2,1)}, u32[]{:S(2)}) %copy-start) | copy-done | bytes 4194328
  4.0 1.3 %copy-done.1 = bf16[1,1,2,1024,1024]{4,3,2,1,0:T(8,128)(2,1)S(1)} copy-done((bf16[1,1,2,1024,1024]{4,3,2,1,0:T(8,128)(2,1)S(1)}, bf16[1,1,2,1024,1024]{4,3,2,1,0:T(8,128)(2,1)}, u32[]{:S(2)}) %copy-start.1) | copy-done | bytes 4194328
  5.3 2.0 %chain.1 = (bf16[128,1024]{1,0:T(8,128)(2,1)S(1)}, bf16[2,128,1024]{2,1,0:T(8,128)(2,1)S(1)}) custom-call(s32[8,128]{1,0:T(8,128)S(1)} %get-tuple-element.32.flag, bf16[2,128,1024]{2,1,0:T(8,128)(2,1)S(1)} %bitcast.14, bf16[2,128,1024]{2,1,0:T(8,128)(2,1)S(1)} %bitcast.12, bf16[2,1024,1024]{2,1,0:T(8,128)(2,1)S(1)} %bitcast.8, bf16[2,1024,1024]{2,1,0:T(8,128)(2,1)S(1)} %bitcast.4), custom_call_target="tpu_custom_call" | custom-call | flops 805306368 | bytes 4194304 | tf_op jit(solution)/shard_map/chain/pallas_call | solution.py:242
  7.3 6.0 %collective-permute-start.13 = (bf16[2,128,1024]{2,1,0:T(8,128)(2,1)S(1)}, bf16[2,128,1024]{2,1,0:T(8,128)(2,1)S(1)}, u32[]{:S(2)}, u32[]{:S(2)}) collective-permute-start(bf16[2,128,1024]{2,1,0:T(8,128)(2,1)S(1)} %get-tuple-element.53), channel_id=1, source_target_pairs={{0,4},{2,6},{1,5},{3,7},{8,12},{10,14},{9,13},{11,15},{16,20},{18,... | collective-permute-start | bytes 1572872 | tf_op jit(solution)/shard_map/ppermute | solution.py:618
  13.3 1.6 %collective-permute-start = (bf16[128,1024]{1,0:T(8,128)(2,1)S(1)}, bf16[128,1024]{1,0:T(8,128)(2,1)S(1)}, u32[]{:S(2)}, u32[]{:S(2)}) collective-permute-start(bf16[128,1024]{1,0:T(8,128)(2,1)S(1)} %get-tuple-element.34), channel_id=1, source_target_pairs={{0,16},{8,24},{16,0},{24,8},{1,17},{9,25},{17,1},{25,9},{2,18},{10... | collective-permute-start | bytes 786440 | tf_op jit(solution)/shard_map/ppermute | solution.py:592
  14.9 0.5 collective-permute-start.5
  15.4 7.2 %collective-permute-done.short_part.e2 = bf16[128,1024]{1,0:T(8,128)(2,1)S(1)} collective-permute-done((bf16[128,1024]{1,0:T(8,128)(2,1)S(1)}, bf16[128,1024]{1,0:T(8,128)(2,1)S(1)}, u32[]{:S(2)}, u32[]{:S(2)}) %collective-permute-start) | collective-permute-done | bytes 262176 | tf_op jit(solution)/shard_map/ppermute | solution.py:592
  22.6 0.1 by_role.2
  22.7 1.3 %collective-permute-start.1 = (bf16[128,1024]{1,0:T(8,128)(2,1)S(1)}, bf16[128,1024]{1,0:T(8,128)(2,1)S(1)}, u32[]{:S(2)}, u32[]{:S(2)}) collective-permute-start(bf16[128,1024]{1,0:T(8,128)(2,1)S(1)} %by_role.2), channel_id=1, source_target_pairs={{4,0},{6,2},{5,1},{7,3},{12,8},{14,10},{13,9},{15,11},{20,16},{22,... | collective-permute-start | bytes 786440 | tf_op jit(solution)/shard_map/ppermute | solution.py:621
  24.0 0.1 collective-permute-start.3
  24.0 0.5 collective-permute-start.4
  24.5 0.0 collective-permute-done.13.up
  24.5 0.1 collective-permute-start.14
  24.6 2.2 %collective-permute-done.5.full_part = bf16[128,1024]{1,0:T(8,128)(2,1)S(1)} collective-permute-done((bf16[128,1024]{1,0:T(8,128)(2,1)S(1)}, bf16[128,1024]{1,0:T(8,128)(2,1)S(1)}, u32[]{:S(2)}, u32[]{:S(2)}) %collective-permute-start.5) | collective-permute-done | bytes 262176 | tf_op jit(solution)/shard_map/ppermute | solution.py:592
  26.8 0.1 by_role.3.e3
  26.9 0.1 collective-permute-start.6
  26.9 9.6 %collective-permute-done.1.late = bf16[128,1024]{1,0:T(8,128)(2,1)S(1)} collective-permute-done((bf16[128,1024]{1,0:T(8,128)(2,1)S(1)}, bf16[128,1024]{1,0:T(8,128)(2,1)S(1)}, u32[]{:S(2)}, u32[]{:S(2)}) %collective-permute-start.1) | collective-permute-done | bytes 262176 | tf_op jit(solution)/shard_map/ppermute | solution.py:621
  36.6 0.0 collective-permute-done.3.f1
  36.6 0.5 collective-permute-start.15
  37.1 0.0 collective-permute-done.4.f2
  37.1 0.6 early.1
  37.7 0.0 collective-permute-done.6.f3
  37.7 1.3 %middle.1 = (f32[512,1024]{1,0:T(8,128)S(1)}, f32[512,1024]{1,0:T(8,128)S(1)}) custom-call(s32[8,128]{1,0:T(8,128)S(1)} %get-tuple-element.32.flag, bf16[128,1024]{1,0:T(8,128)(2,1)S(1)} %by_role.3.e3, bf16[128,1024]{1,0:T(8,128)(2,1)S(1)} %collective-permute-done.6.f3, bf16[256,512]{1,0:T(8,128)(2,1)S(1)} %get-tuple-element.38.unit_part, ...), custom_call_target="tpu_custom_call" | custom-call | flops 1073741824 | bytes 3145728 | tf_op jit(solution)/shard_map/middle/pallas_call | solution.py:407
  39.0 1.3 %shard_map.68 = (bf16[256,512]{1,0:T(8,128)(2,1)S(1)}, f32[256,512]{1,0:T(8,128)S(1)}, bf16[128,1024]{1,0:T(8,128)(2,1)S(1)}, f32[128,1024]{1,0:T(8,128)S(1)}, bf16[256,1024]{1,0:T(8,128)(2,1)S(1)}) custom-call(s32[8,128]{1,0:T(8,128)S(1)} %get-tuple-element.32.flag, bf16[128,1024]{1,0:T(8,128)(2,1)S(1)} %collective-permute-done.1.late, ...), custom_call_target="tpu_custom_call" | custom-call | flops 805306368 | tf_op jit(solution)/shard_map/pallas_call | solution.py:572
  40.3 1.6 %collective-permute-start.9 = (bf16[256,512]{1,0:T(8,128)(2,1)S(1)}, bf16[256,512]{1,0:T(8,128)(2,1)S(1)}, u32[]{:S(2)}, u32[]{:S(2)}) collective-permute-start(bf16[256,512]{1,0:T(8,128)(2,1)S(1)} %get-tuple-element.46), channel_id=1, source_target_pairs={{0,1},{1,0},{2,3},{3,2},{4,5},{5,4},{6,7},{7,6},{8,9},{9,8},{10,11... | collective-permute-start | bytes 786440 | tf_op jit(solution)/shard_map/ppermute | solution.py:592
  41.9 1.8 %collective-permute-start.7 = (bf16[128,1024]{1,0:T(8,128)(2,1)S(1)}, bf16[128,1024]{1,0:T(8,128)(2,1)S(1)}, u32[]{:S(2)}, u32[]{:S(2)}) collective-permute-start(bf16[128,1024]{1,0:T(8,128)(2,1)S(1)} %get-tuple-element.42), channel_id=1, source_target_pairs={{0,2},{2,0},{4,6},{6,4},{1,3},{3,1},{5,7},{7,5},{8,10},{10,8},{12,... | collective-permute-start | bytes 786440 | tf_op jit(solution)/shard_map/ppermute | solution.py:592
  43.6 1.2 %shard_map.74 = (bf16[256,512]{1,0:T(8,128)(2,1)S(1)}, f32[256,512]{1,0:T(8,128)S(1)}, bf16[128,1024]{1,0:T(8,128)(2,1)S(1)}, f32[128,1024]{1,0:T(8,128)S(1)}) custom-call(s32[8,128]{1,0:T(8,128)S(1)} %get-tuple-element.32.flag, bf16[256,1024]{1,0:T(8,128)(2,1)S(1)} %get-tuple-element.51.unit, bf16[128,1024]{1,0:T(8,128)(2,1)S(1)} %collective-permute-done.short_part.e2, ...), custom_call_target="tpu_custom_call" | custom-call | flops 536870912 | tf_op jit(solution)/shard_map/pallas_call | solution.py:572
  44.9 0.6 collective-permute-start.18
  45.5 4.0 %collective-permute-done.9.land = bf16[256,512]{1,0:T(8,128)(2,1)S(1)} collective-permute-done((bf16[256,512]{1,0:T(8,128)(2,1)S(1)}, bf16[256,512]{1,0:T(8,128)(2,1)S(1)}, u32[]{:S(2)}, u32[]{:S(2)}) %collective-permute-start.9) | collective-permute-done | bytes 262176 | tf_op jit(solution)/shard_map/ppermute | solution.py:592
  49.5 0.1 shard_map.71
  49.6 1.9 %collective-permute-start.10 = (bf16[128,512]{1,0:T(8,128)(2,1)S(1)}, bf16[128,512]{1,0:T(8,128)(2,1)S(1)}, u32[]{:S(2)}, u32[]{:S(2)}) collective-permute-start(bf16[128,512]{1,0:T(8,128)(2,1)S(1)} %get-tuple-element.48), channel_id=1, source_target_pairs={{0,2},{2,0},{4,6},{6,4},{1,3},{3,1},{5,7},{7,5},{8,10},{10,8},{12,... | collective-permute-start | bytes 393224 | tf_op jit(solution)/shard_map/ppermute | solution.py:592
  51.4 0.2 collective-permute-start.16
  51.7 0.1 shard_map.69
  51.8 1.6 %collective-permute-start.8 = (bf16[128,512]{1,0:T(8,128)(2,1)S(1)}, bf16[128,512]{1,0:T(8,128)(2,1)S(1)}, u32[]{:S(2)}, u32[]{:S(2)}) collective-permute-start(bf16[128,512]{1,0:T(8,128)(2,1)S(1)} %get-tuple-element.44), channel_id=1, source_target_pairs={{0,1},{1,0},{2,3},{3,2},{4,5},{5,4},{6,7},{7,6},{8,9},{9,8},{10,11... | collective-permute-start | bytes 393224 | tf_op jit(solution)/shard_map/ppermute | solution.py:592
  53.3 2.7 %collective-permute-done.10.land = bf16[128,512]{1,0:T(8,128)(2,1)S(1)} collective-permute-done((bf16[128,512]{1,0:T(8,128)(2,1)S(1)}, bf16[128,512]{1,0:T(8,128)(2,1)S(1)}, u32[]{:S(2)}, u32[]{:S(2)}) %collective-permute-start.10) | collective-permute-done | bytes 131104 | tf_op jit(solution)/shard_map/ppermute | solution.py:592
  56.1 2.2 %collective-permute-start.11 = (bf16[128,512]{1,0:T(8,128)(2,1)S(1)}, bf16[128,512]{1,0:T(8,128)(2,1)S(1)}, u32[]{:S(2)}, u32[]{:S(2)}) collective-permute-start(bf16[128,512]{1,0:T(8,128)(2,1)S(1)} %shard_map.72), channel_id=1, source_target_pairs={{0,16},{8,24},{16,0},{24,8},{1,17},{9,25},{17,1},{25,9},{2,18},{10... | collective-permute-start | bytes 393224 | tf_op jit(solution)/shard_map/ppermute | solution.py:592
  58.3 1.3 %collective-permute-start.19 = (bf16[128,512]{1,0:T(8,128)(2,1)S(1)}, bf16[128,512]{1,0:T(8,128)(2,1)S(1)}, u32[]{:S(2)}, u32[]{:S(2)}) collective-permute-start(bf16[128,512]{1,0:T(8,128)(2,1)S(1)} %get-tuple-element.61), channel_id=1, source_target_pairs={{0,2},{2,0},{4,6},{6,4},{1,3},{3,1},{5,7},{7,5},{8,10},{10,8},{12,... | collective-permute-start | bytes 393224 | tf_op jit(solution)/shard_map/ppermute | solution.py:592
  59.7 1.5 %collective-permute-done.11.got = bf16[128,512]{1,0:T(8,128)(2,1)S(1)} collective-permute-done((bf16[128,512]{1,0:T(8,128)(2,1)S(1)}, bf16[128,512]{1,0:T(8,128)(2,1)S(1)}, u32[]{:S(2)}, u32[]{:S(2)}) %collective-permute-start.11) | collective-permute-done | bytes 131104 | tf_op jit(solution)/shard_map/ppermute | solution.py:592
  61.2 0.1 shard_map.73
  61.3 3.1 %collective-permute-start.12 = (bf16[128,512]{1,0:T(8,128)(2,1)S(1)}, bf16[128,512]{1,0:T(8,128)(2,1)S(1)}, u32[]{:S(2)}, u32[]{:S(2)}) collective-permute-start(bf16[128,512]{1,0:T(8,128)(2,1)S(1)} %get-tuple-element.50), channel_id=1, source_target_pairs={{0,4},{2,6},{4,0},{6,2},{1,5},{3,7},{5,1},{7,3},{8,12},{10,14},{12... | collective-permute-start | bytes 393224 | tf_op jit(solution)/shard_map/ppermute | solution.py:592
  64.5 1.6 %collective-permute-start.17 = (bf16[128,512]{1,0:T(8,128)(2,1)S(1)}, bf16[128,512]{1,0:T(8,128)(2,1)S(1)}, u32[]{:S(2)}, u32[]{:S(2)}) collective-permute-start(bf16[128,512]{1,0:T(8,128)(2,1)S(1)} %get-tuple-element.57), channel_id=1, source_target_pairs={{0,1},{1,0},{2,3},{3,2},{4,5},{5,4},{6,7},{7,6},{8,9},{9,8},{10,11... | collective-permute-start | bytes 393224 | tf_op jit(solution)/shard_map/ppermute | solution.py:592
  66.1 1.6 %collective-permute-start.20 = (bf16[128,512]{1,0:T(8,128)(2,1)S(1)}, bf16[128,512]{1,0:T(8,128)(2,1)S(1)}, u32[]{:S(2)}, u32[]{:S(2)}) collective-permute-start(bf16[128,512]{1,0:T(8,128)(2,1)S(1)} %shard_map.78), channel_id=1, source_target_pairs={{0,16},{8,24},{16,0},{24,8},{1,17},{9,25},{17,1},{25,9},{2,18},{10... | collective-permute-start | bytes 393224 | tf_op jit(solution)/shard_map/ppermute | solution.py:592
  67.7 1.8 %collective-permute-done.17.land = bf16[128,512]{1,0:T(8,128)(2,1)S(1)} collective-permute-done((bf16[128,512]{1,0:T(8,128)(2,1)S(1)}, bf16[128,512]{1,0:T(8,128)(2,1)S(1)}, u32[]{:S(2)}, u32[]{:S(2)}) %collective-permute-start.17) | collective-permute-done | bytes 131104 | tf_op jit(solution)/shard_map/ppermute | solution.py:592
  69.5 1.6 %collective-permute-done.20.got = bf16[128,512]{1,0:T(8,128)(2,1)S(1)} collective-permute-done((bf16[128,512]{1,0:T(8,128)(2,1)S(1)}, bf16[128,512]{1,0:T(8,128)(2,1)S(1)}, u32[]{:S(2)}, u32[]{:S(2)}) %collective-permute-start.20) | collective-permute-done | bytes 131104 | tf_op jit(solution)/shard_map/ppermute | solution.py:592
  71.1 0.9 %shard_map.79 = (f32[1,128,512]{2,1,0:T(8,128)}, f32[1,128,512]{2,1,0:T(8,128)}) custom-call(s32[8,128]{1,0:T(8,128)S(1)} %get-tuple-element.32.flag, f32[128,512]{1,0:T(8,128)S(1)} %get-tuple-element.49.lower, bf16[128,512]{1,0:T(8,128)(2,1)S(1)} %collective-permute-done.12.landed, f32[128,512]{1,0:T(8,128)S(1)} %shard_map.76.near, ...), custom_call_target="tpu_custom_call" | custom-call | tf_op jit(solution)/shard_map/pallas_call | solution.py:572
  (23 shorter events, 0.3 us)
Async XLA Ops:
  0.6 1.0 %copy-start.2 = (bf16[1,1,2,128,1024]{4,3,2,1,0:T(8,128)(2,1)S(1)}, bf16[1,1,2,128,1024]{4,3,2,1,0:T(8,128)(2,1)}, u32[]{:S(2)}) copy-start(bf16[1,1,2,128,1024]{4,3,2,1,0:T(8,128)(2,1)} %param.6) | copy-start | bytes 1572868
  0.6 1.2 %copy-start.3 = (bf16[1,2,128,1024]{3,2,1,0:T(8,128)(2,1)S(1)}, bf16[1,2,128,1024]{3,2,1,0:T(8,128)(2,1)}, u32[]{:S(2)}) copy-start(bf16[1,2,128,1024]{3,2,1,0:T(8,128)(2,1)} %param.9) | copy-start | bytes 1572868
  0.6 1.2 %copy-start.4 = (s32[2,3]{1,0:T(2,128)S(1)}, s32[2,3]{1,0:T(2,128)}, u32[]{:S(2)}) copy-start(s32[2,3]{1,0:T(2,128)} %bounds.1) | copy-start | bytes 76
  1.8 2.2 %copy-start = (bf16[1,1,2,1024,1024]{4,3,2,1,0:T(8,128)(2,1)S(1)}, bf16[1,1,2,1024,1024]{4,3,2,1,0:T(8,128)(2,1)}, u32[]{:S(2)}) copy-start(bf16[1,1,2,1024,1024]{4,3,2,1,0:T(8,128)(2,1)} %param.8) | copy-start | bytes 12582916
  1.8 3.5 %copy-start.1 = (bf16[1,1,2,1024,1024]{4,3,2,1,0:T(8,128)(2,1)S(1)}, bf16[1,1,2,1024,1024]{4,3,2,1,0:T(8,128)(2,1)}, u32[]{:S(2)}) copy-start(bf16[1,1,2,1024,1024]{4,3,2,1,0:T(8,128)(2,1)} %param.7) | copy-start | bytes 12582916
  7.3 17.2 %collective-permute-start.13 = (bf16[2,128,1024]{2,1,0:T(8,128)(2,1)S(1)}, bf16[2,128,1024]{2,1,0:T(8,128)(2,1)S(1)}, u32[]{:S(2)}, u32[]{:S(2)}) collective-permute-start(bf16[2,128,1024]{2,1,0:T(8,128)(2,1)S(1)} %get-tuple-element.53), channel_id=1, source_target_pairs={{0,4},{2,6},{1,5},{3,7},{8,12},{10,14},{9,13},{11,15},{16,20},{18,... | collective-permute-start | bytes 1572872 | tf_op jit(solution)/shard_map/ppermute | solution.py:618
  13.3 9.2 %collective-permute-start = (bf16[128,1024]{1,0:T(8,128)(2,1)S(1)}, bf16[128,1024]{1,0:T(8,128)(2,1)S(1)}, u32[]{:S(2)}, u32[]{:S(2)}) collective-permute-start(bf16[128,1024]{1,0:T(8,128)(2,1)S(1)} %get-tuple-element.34), channel_id=1, source_target_pairs={{0,16},{8,24},{16,0},{24,8},{1,17},{9,25},{17,1},{25,9},{2,18},{10... | collective-permute-start | bytes 786440 | tf_op jit(solution)/shard_map/ppermute | solution.py:592
  14.9 11.9 %collective-permute-start.5 = (bf16[128,1024]{1,0:T(8,128)(2,1)S(1)}, bf16[128,1024]{1,0:T(8,128)(2,1)S(1)}, u32[]{:S(2)}, u32[]{:S(2)}) collective-permute-start(bf16[128,1024]{1,0:T(8,128)(2,1)S(1)} %get-tuple-element.33.full_part.low), channel_id=1, source_target_pairs={{0,16},{8,24},{16,0},{24,8},{1,17},{9,25},{17,1},{25,9},{2,18},{10... | collective-permute-start | bytes 786440 | tf_op jit(solution)/shard_map/ppermute | solution.py:592
  22.7 13.9 %collective-permute-start.1 = (bf16[128,1024]{1,0:T(8,128)(2,1)S(1)}, bf16[128,1024]{1,0:T(8,128)(2,1)S(1)}, u32[]{:S(2)}, u32[]{:S(2)}) collective-permute-start(bf16[128,1024]{1,0:T(8,128)(2,1)S(1)} %by_role.2), channel_id=1, source_target_pairs={{4,0},{6,2},{5,1},{7,3},{12,8},{14,10},{13,9},{15,11},{20,16},{22,... | collective-permute-start | bytes 786440 | tf_op jit(solution)/shard_map/ppermute | solution.py:621
  24.0 12.6 %collective-permute-start.3 = (bf16[128,1024]{1,0:T(8,128)(2,1)S(1)}, bf16[128,1024]{1,0:T(8,128)(2,1)S(1)}, u32[]{:S(2)}, u32[]{:S(2)}) collective-permute-start(bf16[128,1024]{1,0:T(8,128)(2,1)S(1)} %get-tuple-element.35.e1), channel_id=1, source_target_pairs={{0,8},{8,0},{16,24},{24,16},{1,9},{9,1},{17,25},{25,17},{2,10},{10... | collective-permute-start | bytes 786440 | tf_op jit(solution)/shard_map/ppermute | solution.py:592
  24.0 13.0 %collective-permute-start.4 = (bf16[128,1024]{1,0:T(8,128)(2,1)S(1)}, bf16[128,1024]{1,0:T(8,128)(2,1)S(1)}, u32[]{:S(2)}, u32[]{:S(2)}) collective-permute-start(bf16[128,1024]{1,0:T(8,128)(2,1)S(1)} %collective-permute-done.short_part.e2), channel_id=1, source_target_pairs={{0,8},{8,0},{16,24},{24,16},{1,9},{9,1},{17,25},{25,17},{2,10},{10... | collective-permute-start | bytes 786440 | tf_op jit(solution)/shard_map/ppermute | solution.py:592
  24.5 19.1 %collective-permute-start.14 = (bf16[2,128,1024]{2,1,0:T(8,128)(2,1)S(1)}, bf16[2,128,1024]{2,1,0:T(8,128)(2,1)S(1)}, u32[]{:S(2)}, u32[]{:S(2)}) collective-permute-start(bf16[2,128,1024]{2,1,0:T(8,128)(2,1)S(1)} %collective-permute-done.13.up), channel_id=1, source_target_pairs={{0,8},{8,0},{16,24},{24,16},{1,9},{9,1},{17,25},{25,17},{2,10},{10... | collective-permute-start | bytes 1572872 | tf_op jit(solution)/shard_map/ppermute | solution.py:592
  26.9 10.8 %collective-permute-start.6 = (bf16[128,1024]{1,0:T(8,128)(2,1)S(1)}, bf16[128,1024]{1,0:T(8,128)(2,1)S(1)}, u32[]{:S(2)}, u32[]{:S(2)}) collective-permute-start(bf16[128,1024]{1,0:T(8,128)(2,1)S(1)} %by_role.3.e3), channel_id=1, source_target_pairs={{0,8},{8,0},{16,24},{24,16},{1,9},{9,1},{17,25},{25,17},{2,10},{10... | collective-permute-start | bytes 786440 | tf_op jit(solution)/shard_map/ppermute | solution.py:592
  36.5 2.5 %collective-permute-start.2 = (bf16[128,1024]{1,0:T(8,128)(2,1)S(1)}, bf16[128,1024]{1,0:T(8,128)(2,1)S(1)}, u32[]{:S(2)}, u32[]{:S(2)}) collective-permute-start(bf16[128,1024]{1,0:T(8,128)(2,1)S(1)} %collective-permute-done.1.late), channel_id=1, source_target_pairs={{0,8},{8,0},{16,24},{24,16},{1,9},{9,1},{17,25},{25,17},{2,10},{10... | collective-permute-start | bytes 786440 | tf_op jit(solution)/shard_map/ppermute | solution.py:592
  36.6 7.1 %collective-permute-start.15 = (bf16[128,1024]{1,0:T(8,128)(2,1)S(1)}, bf16[128,1024]{1,0:T(8,128)(2,1)S(1)}, u32[]{:S(2)}, u32[]{:S(2)}) collective-permute-start(bf16[128,1024]{1,0:T(8,128)(2,1)S(1)} %get-tuple-element.33.full_part.low), channel_id=1, source_target_pairs={{0,8},{8,0},{16,24},{24,16},{1,9},{9,1},{17,25},{25,17},{2,10},{10... | collective-permute-start | bytes 786440 | tf_op jit(solution)/shard_map/ppermute | solution.py:592
  40.3 9.2 %collective-permute-start.9 = (bf16[256,512]{1,0:T(8,128)(2,1)S(1)}, bf16[256,512]{1,0:T(8,128)(2,1)S(1)}, u32[]{:S(2)}, u32[]{:S(2)}) collective-permute-start(bf16[256,512]{1,0:T(8,128)(2,1)S(1)} %get-tuple-element.46), channel_id=1, source_target_pairs={{0,1},{1,0},{2,3},{3,2},{4,5},{5,4},{6,7},{7,6},{8,9},{9,8},{10,11... | collective-permute-start | bytes 786440 | tf_op jit(solution)/shard_map/ppermute | solution.py:592
  41.9 9.8 %collective-permute-start.7 = (bf16[128,1024]{1,0:T(8,128)(2,1)S(1)}, bf16[128,1024]{1,0:T(8,128)(2,1)S(1)}, u32[]{:S(2)}, u32[]{:S(2)}) collective-permute-start(bf16[128,1024]{1,0:T(8,128)(2,1)S(1)} %get-tuple-element.42), channel_id=1, source_target_pairs={{0,2},{2,0},{4,6},{6,4},{1,3},{3,1},{5,7},{7,5},{8,10},{10,8},{12,... | collective-permute-start | bytes 786440 | tf_op jit(solution)/shard_map/ppermute | solution.py:592
  44.9 13.3 %collective-permute-start.18 = (bf16[256,512]{1,0:T(8,128)(2,1)S(1)}, bf16[256,512]{1,0:T(8,128)(2,1)S(1)}, u32[]{:S(2)}, u32[]{:S(2)}) collective-permute-start(bf16[256,512]{1,0:T(8,128)(2,1)S(1)} %get-tuple-element.59), channel_id=1, source_target_pairs={{0,1},{1,0},{2,3},{3,2},{4,5},{5,4},{6,7},{7,6},{8,9},{9,8},{10,11... | collective-permute-start | bytes 786440 | tf_op jit(solution)/shard_map/ppermute | solution.py:592
  49.6 6.4 %collective-permute-start.10 = (bf16[128,512]{1,0:T(8,128)(2,1)S(1)}, bf16[128,512]{1,0:T(8,128)(2,1)S(1)}, u32[]{:S(2)}, u32[]{:S(2)}) collective-permute-start(bf16[128,512]{1,0:T(8,128)(2,1)S(1)} %get-tuple-element.48), channel_id=1, source_target_pairs={{0,2},{2,0},{4,6},{6,4},{1,3},{3,1},{5,7},{7,5},{8,10},{10,8},{12,... | collective-permute-start | bytes 393224 | tf_op jit(solution)/shard_map/ppermute | solution.py:592
  51.4 12.9 %collective-permute-start.16 = (bf16[128,1024]{1,0:T(8,128)(2,1)S(1)}, bf16[128,1024]{1,0:T(8,128)(2,1)S(1)}, u32[]{:S(2)}, u32[]{:S(2)}) collective-permute-start(bf16[128,1024]{1,0:T(8,128)(2,1)S(1)} %get-tuple-element.55), channel_id=1, source_target_pairs={{0,2},{2,0},{4,6},{6,4},{1,3},{3,1},{5,7},{7,5},{8,10},{10,8},{12,... | collective-permute-start | bytes 786440 | tf_op jit(solution)/shard_map/ppermute | solution.py:592
  51.8 7.9 %collective-permute-start.8 = (bf16[128,512]{1,0:T(8,128)(2,1)S(1)}, bf16[128,512]{1,0:T(8,128)(2,1)S(1)}, u32[]{:S(2)}, u32[]{:S(2)}) collective-permute-start(bf16[128,512]{1,0:T(8,128)(2,1)S(1)} %get-tuple-element.44), channel_id=1, source_target_pairs={{0,1},{1,0},{2,3},{3,2},{4,5},{5,4},{6,7},{7,6},{8,9},{9,8},{10,11... | collective-permute-start | bytes 393224 | tf_op jit(solution)/shard_map/ppermute | solution.py:592
  56.1 5.1 %collective-permute-start.11 = (bf16[128,512]{1,0:T(8,128)(2,1)S(1)}, bf16[128,512]{1,0:T(8,128)(2,1)S(1)}, u32[]{:S(2)}, u32[]{:S(2)}) collective-permute-start(bf16[128,512]{1,0:T(8,128)(2,1)S(1)} %shard_map.72), channel_id=1, source_target_pairs={{0,16},{8,24},{16,0},{24,8},{1,17},{9,25},{17,1},{25,9},{2,18},{10... | collective-permute-start | bytes 393224 | tf_op jit(solution)/shard_map/ppermute | solution.py:592
  58.3 7.7 %collective-permute-start.19 = (bf16[128,512]{1,0:T(8,128)(2,1)S(1)}, bf16[128,512]{1,0:T(8,128)(2,1)S(1)}, u32[]{:S(2)}, u32[]{:S(2)}) collective-permute-start(bf16[128,512]{1,0:T(8,128)(2,1)S(1)} %get-tuple-element.61), channel_id=1, source_target_pairs={{0,2},{2,0},{4,6},{6,4},{1,3},{3,1},{5,7},{7,5},{8,10},{10,8},{12,... | collective-permute-start | bytes 393224 | tf_op jit(solution)/shard_map/ppermute | solution.py:592
  61.3 8.3 %collective-permute-start.12 = (bf16[128,512]{1,0:T(8,128)(2,1)S(1)}, bf16[128,512]{1,0:T(8,128)(2,1)S(1)}, u32[]{:S(2)}, u32[]{:S(2)}) collective-permute-start(bf16[128,512]{1,0:T(8,128)(2,1)S(1)} %get-tuple-element.50), channel_id=1, source_target_pairs={{0,4},{2,6},{4,0},{6,2},{1,5},{3,7},{5,1},{7,3},{8,12},{10,14},{12... | collective-permute-start | bytes 393224 | tf_op jit(solution)/shard_map/ppermute | solution.py:592
  64.5 5.0 %collective-permute-start.17 = (bf16[128,512]{1,0:T(8,128)(2,1)S(1)}, bf16[128,512]{1,0:T(8,128)(2,1)S(1)}, u32[]{:S(2)}, u32[]{:S(2)}) collective-permute-start(bf16[128,512]{1,0:T(8,128)(2,1)S(1)} %get-tuple-element.57), channel_id=1, source_target_pairs={{0,1},{1,0},{2,3},{3,2},{4,5},{5,4},{6,7},{7,6},{8,9},{9,8},{10,11... | collective-permute-start | bytes 393224 | tf_op jit(solution)/shard_map/ppermute | solution.py:592
  66.1 5.0 %collective-permute-start.20 = (bf16[128,512]{1,0:T(8,128)(2,1)S(1)}, bf16[128,512]{1,0:T(8,128)(2,1)S(1)}, u32[]{:S(2)}, u32[]{:S(2)}) collective-permute-start(bf16[128,512]{1,0:T(8,128)(2,1)S(1)} %shard_map.78), channel_id=1, source_target_pairs={{0,16},{8,24},{16,0},{24,8},{1,17},{9,25},{17,1},{25,9},{2,18},{10... | collective-permute-start | bytes 393224 | tf_op jit(solution)/shard_map/ppermute | solution.py:592

commit v10 on v9

--- a/solution.py
+++ b/solution.py
@@ -420,30 +420,24 @@
     )(flag, e3, f3, unit_part, value, w_out)
 
 
-def split_sums(place, left_part, right_part, acc, x_send, x_keep, z_send, z_keep):
+def split_sums(place, left_part, right_part, acc, x_sum, z_sum, keep):
     group = left_part.shape[1] // 2
     block = group // 2
     cols = right_part.shape[1] // 2
+    column = place.column if keep else 1 - place.column
+    half = place.half if keep else 1 - place.half
 
     def sums(rows_of, cols_of):
         new = tn_dot(left_part[:, rows_of], right_part[:, cols_of])
         return new if acc is None else acc[rows_of, cols_of] + new
 
-    far = slice(0, group)
-    every = slice(None)
-    mine = pl.ds(pl.multiple_of(place.column * cols, cols), cols)
-    other = pl.ds(pl.multiple_of((1 - place.column) * cols, cols), cols)
-    kept = pl.ds(pl.multiple_of(group + place.half * block, block), block)
-    sent = pl.ds(pl.multiple_of(group + (1 - place.half) * block, block), block)
-    x_send[...] = sums(far, other).astype(jnp.bfloat16)
-    x_keep[...] = sums(far, mine)
-    z_send[...] = sums(sent, every).astype(jnp.bfloat16)
-    z_keep[...] = sums(kept, every)
-
-
-def late_in_kernel(
-    flag, late, flate, early_part, in_acc, w_out, x_send, x_keep, z_send, z_keep, unit, unit_part, err,
-):
+    cols_of = pl.ds(pl.multiple_of(column * cols, cols), cols)
+    rows_of = pl.ds(pl.multiple_of(group + half * block, block), block)
+    x_sum[...] = sums(slice(0, group), cols_of).astype(x_sum.dtype)
+    z_sum[...] = sums(rows_of, slice(None)).astype(z_sum.dtype)
+
+
+def late_in_kernel(flag, late, flate, early_part, in_acc, w_out, x_send, z_send, unit_part, err, unit):
     place = Place(flag[0, 0] > 0)
     part = unit_part.shape[1]
 
@@ -459,18 +453,20 @@
         unit_columns(place, unit, unit_part)
         err[...] = early_part[...]
 
-    split_sums(place, unit_part, err, in_acc, x_send, x_keep, z_send, z_keep)
+    split_sums(place, unit_part, err, in_acc, x_send, z_send, False)
+
+
+def in_keep_kernel(flag, unit_part, err, in_acc, x_keep, z_keep):
+    split_sums(Place(flag[0, 0] > 0), unit_part, err, in_acc, x_keep, z_keep, True)
 
 
 def late_out_kernel(
-    flag, unit, e2, f2, out_acc, w_in, up, fup, low, flow,
-    x_send, x_keep, z_send, z_keep, value, grads, unit_part,
+    flag, unit, e2, f2, out_acc, w_in, up, fup, low, flow, x_send, z_send, value, grads, unit_part,
 ):
     place = Place(flag[0, 0] > 0)
     rows = e2.shape[0]
     part = value.shape[1]
     lanes = part // BLOCKS
-    outs = (x_send, x_keep, z_send, z_keep)
 
     def put_grads(first, second):
         grads[:rows, :] = first[...]
@@ -480,7 +476,7 @@
     def _():
         core_columns(place, unit, w_in, unit_part, value)
         put_grads(e2, f2)
-        split_sums(place, value, grads, out_acc, *outs)
+        split_sums(place, value, grads, out_acc, x_send, z_send, False)
 
     @pl.when(jnp.logical_not(place.left))
     def _():
@@ -498,16 +494,23 @@
         def _():
             put_grads(low, flow)
 
-        split_sums(place, value, grads, None, *outs)
-
-
-def split_shapes(part, width):
-    return (
-        low_shape(part // 2, width // 2),
-        full_shape(part // 2, width // 2),
-        low_shape(part // 4, width),
-        full_shape(part // 4, width),
-    )
+        split_sums(place, value, grads, None, x_send, z_send, False)
+
+
+def out_keep_kernel(flag, value, grads, out_acc, x_keep, z_keep):
+    place = Place(flag[0, 0] > 0)
+
+    @pl.when(place.left)
+    def _():
+        split_sums(place, value, grads, out_acc, x_keep, z_keep, True)
+
+    @pl.when(jnp.logical_not(place.left))
+    def _():
+        split_sums(place, value, grads, None, x_keep, z_keep, True)
+
+
+def split_shapes(part, width, kind):
+    return (kind(part // 2, width // 2), kind(part // 4, width))
 
 
 def x_add_kernel(keep, land, mine, following):
@@ -641,28 +644,29 @@
     other_late = core_swap(late)
     part = model // 2
     pair = 2 * rows
-    *in_parts, unit_late = small_call(
+    *in_sends, unit_part, err, unit_late = small_call(
         late_in_kernel,
         (flag, late, other_late, early_part, in_acc, proj_out),
-        split_shapes(part, inner) + (low_shape(pair, model),),
-        scratch=[pltpu.VMEM((pair, part), jnp.bfloat16), pltpu.VMEM((pair, inner), jnp.bfloat16)],
-        flops=6 * rows * model * inner,
-    )
-    out_parts = small_call(
+        split_shapes(part, inner, low_shape) + (low_shape(pair, part), low_shape(pair, inner), low_shape(pair, model)),
+        flops=5 * rows * model * inner,
+    )
+    in_keeps = small_call(
+        in_keep_kernel, (flag, unit_part, err, in_acc), split_shapes(part, inner, full_shape)
+    )
+    *out_sends, value, grads = small_call(
         late_out_kernel,
         (flag, unit_late, own[1], partner[1], out_acc, proj_in)
         + (lifted, other_lifted, grad_low, other_low),
-        split_shapes(part, model),
-        scratch=[
-            pltpu.VMEM((pair, part), jnp.bfloat16),
-            pltpu.VMEM((pair, model), jnp.bfloat16),
-            pltpu.VMEM((pair, part), jnp.bfloat16),
-        ],
-        flops=4 * rows * model * inner,
+        split_shapes(part, model, low_shape) + (low_shape(pair, part), low_shape(pair, model)),
+        scratch=[pltpu.VMEM((pair, part), jnp.bfloat16)],
+        flops=3 * rows * model * inner,
+    )
+    out_keeps = small_call(
+        out_keep_kernel, (flag, value, grads, out_acc), split_shapes(part, model, full_shape)
     )
     block = (model // (2 * BLOCKS), model // 2)
     sums = []
-    for (x_send, x_keep, z_send, z_keep) in (in_parts, out_parts):
+    for (x_send, z_send), (x_keep, z_keep) in ((in_sends, in_keeps), (out_sends, out_keeps)):
         pair_shapes = (full_shape(*block), low_shape(*block))
         x_land = column_swap(x_send)
         z_land = half_swap(z_send)

time: 72.1 us -> 72 us (level)
    pallas_call x12 -> x14, Pallas kernels: 3.76 us -> 4.2 us  [small_call(): pl.pallas_call(kernel, out_shape=shapes, in_specs=[VMEM] * len(operands),...]
where the time goes in v10:
time: 72 us; the launch traced here: 71.8 us
  waiting for transfers between devices  30 us (42%)
  starting transfers between devices  28 us (39%)
  Pallas kernels  8.88 us (12%)
  local copies, waits for them, and re-layouts  4.01 us (6%)
  between operations  0.86 us (1%)
    ppermute x19, starting transfers between devices, flipped(): lax.ppermute(value, axis, [(i, i ^ bit) for i in range(lax.axis_size(axis...  20.7 us
    ppermute x19, waiting for transfers between devices, flipped(): lax.ppermute(value, axis, [(i, i ^ bit) for i in range(lax.axis_size(axis...  20.4 us
    ppermute x1, waiting for transfers between devices, downward(): lax.ppermute(value, 'section', [(i + half_axis, i) for i in range(half_ax...  9.62 us
    ppermute x1, starting transfers between devices, upward(): lax.ppermute(value, 'section', [(i, i + half_axis) for i in range(half_ax...  6 us
    pallas_call x14, Pallas kernels, small_call(): pl.pallas_call(kernel, out_shape=shapes, in_specs=[VMEM] * len(operands),...  4.2 us
    unnamed x10, local copies, waits for them, and re-layouts  4.01 us
    pallas_call x1, Pallas kernels, chain(): pl.pallas_call(chain_kernel, out_shape=(low_shape(rows, model), low_shape...  2.03 us
  transfers between devices with their start and end apart: 21, of which 8 were waited for; matrix products, arithmetic and copies ran while one was open for 0% of the time, Pallas kernels for 7%

profile of v10, /device:TPU:0, one launch (start us, length us, event | category | flops | bytes accessed | tf_op | source)
XLA Modules:
  0.0 71.8 jit_solution(16228075544097042218)
XLA Ops:
  0.7 0.6 copy-done.4
  1.3 0.4 copy-done.2
  1.7 0.2 copy-done.3
  1.9 0.6 staged.1
  2.5 1.6 %copy-done = bf16[1,1,2,1024,1024]{4,3,2,1,0:T(8,128)(2,1)S(1)} copy-done((bf16[1,1,2,1024,1024]{4,3,2,1,0:T(8,128)(2,1)S(1)}, bf16[1,1,2,1024,1024]{4,3,2,1,0:T(8,128)(2,1)}, u32[]{:S(2)}) %copy-start) | copy-done | bytes 4194328
  4.0 1.3 %copy-done.1 = bf16[1,1,2,1024,1024]{4,3,2,1,0:T(8,128)(2,1)S(1)} copy-done((bf16[1,1,2,1024,1024]{4,3,2,1,0:T(8,128)(2,1)S(1)}, bf16[1,1,2,1024,1024]{4,3,2,1,0:T(8,128)(2,1)}, u32[]{:S(2)}) %copy-start.1) | copy-done | bytes 4194328
  5.3 2.0 %chain.1 = (bf16[128,1024]{1,0:T(8,128)(2,1)S(1)}, bf16[2,128,1024]{2,1,0:T(8,128)(2,1)S(1)}) custom-call(s32[8,128]{1,0:T(8,128)S(1)} %get-tuple-element.36.flag, bf16[2,128,1024]{2,1,0:T(8,128)(2,1)S(1)} %bitcast.14, bf16[2,128,1024]{2,1,0:T(8,128)(2,1)S(1)} %bitcast.12, bf16[2,1024,1024]{2,1,0:T(8,128)(2,1)S(1)} %bitcast.8, bf16[2,1024,1024]{2,1,0:T(8,128)(2,1)S(1)} %bitcast.4), custom_call_target="tpu_custom_call" | custom-call | flops 805306368 | bytes 4194304 | tf_op jit(solution)/shard_map/chain/pallas_call | solution.py:242
  7.3 6.0 %collective-permute-start.13 = (bf16[2,128,1024]{2,1,0:T(8,128)(2,1)S(1)}, bf16[2,128,1024]{2,1,0:T(8,128)(2,1)S(1)}, u32[]{:S(2)}, u32[]{:S(2)}) collective-permute-start(bf16[2,128,1024]{2,1,0:T(8,128)(2,1)S(1)} %get-tuple-element.59), channel_id=1, source_target_pairs={{0,4},{2,6},{1,5},{3,7},{8,12},{10,14},{9,13},{11,15},{16,20},{18,... | collective-permute-start | bytes 1572872 | tf_op jit(solution)/shard_map/ppermute | solution.py:621
  13.4 1.6 %collective-permute-start = (bf16[128,1024]{1,0:T(8,128)(2,1)S(1)}, bf16[128,1024]{1,0:T(8,128)(2,1)S(1)}, u32[]{:S(2)}, u32[]{:S(2)}) collective-permute-start(bf16[128,1024]{1,0:T(8,128)(2,1)S(1)} %get-tuple-element.38), channel_id=1, source_target_pairs={{0,16},{8,24},{16,0},{24,8},{1,17},{9,25},{17,1},{25,9},{2,18},{10... | collective-permute-start | bytes 786440 | tf_op jit(solution)/shard_map/ppermute | solution.py:595
  14.9 0.5 collective-permute-start.5
  15.4 7.2 %collective-permute-done.short_part.e2 = bf16[128,1024]{1,0:T(8,128)(2,1)S(1)} collective-permute-done((bf16[128,1024]{1,0:T(8,128)(2,1)S(1)}, bf16[128,1024]{1,0:T(8,128)(2,1)S(1)}, u32[]{:S(2)}, u32[]{:S(2)}) %collective-permute-start) | collective-permute-done | bytes 262176 | tf_op jit(solution)/shard_map/ppermute | solution.py:595
  22.6 0.1 by_role.2
  22.7 1.3 %collective-permute-start.1 = (bf16[128,1024]{1,0:T(8,128)(2,1)S(1)}, bf16[128,1024]{1,0:T(8,128)(2,1)S(1)}, u32[]{:S(2)}, u32[]{:S(2)}) collective-permute-start(bf16[128,1024]{1,0:T(8,128)(2,1)S(1)} %by_role.2), channel_id=1, source_target_pairs={{4,0},{6,2},{5,1},{7,3},{12,8},{14,10},{13,9},{15,11},{20,16},{22,... | collective-permute-start | bytes 786440 | tf_op jit(solution)/shard_map/ppermute | solution.py:624
  24.0 0.1 collective-permute-start.3
  24.0 0.5 collective-permute-start.4
  24.5 0.1 collective-permute-start.14
  24.6 2.2 %collective-permute-done.5.full_part = bf16[128,1024]{1,0:T(8,128)(2,1)S(1)} collective-permute-done((bf16[128,1024]{1,0:T(8,128)(2,1)S(1)}, bf16[128,1024]{1,0:T(8,128)(2,1)S(1)}, u32[]{:S(2)}, u32[]{:S(2)}) %collective-permute-start.5) | collective-permute-done | bytes 262176 | tf_op jit(solution)/shard_map/ppermute | solution.py:595
  26.8 0.1 by_role.3.e3
  26.9 0.1 collective-permute-start.6
  27.0 9.6 %collective-permute-done.1.late = bf16[128,1024]{1,0:T(8,128)(2,1)S(1)} collective-permute-done((bf16[128,1024]{1,0:T(8,128)(2,1)S(1)}, bf16[128,1024]{1,0:T(8,128)(2,1)S(1)}, u32[]{:S(2)}, u32[]{:S(2)}) %collective-permute-start.1) | collective-permute-done | bytes 262176 | tf_op jit(solution)/shard_map/ppermute | solution.py:624
  36.6 0.5 collective-permute-start.15
  37.1 0.6 early.1
  37.7 1.3 %middle.1 = (f32[512,1024]{1,0:T(8,128)S(1)}, f32[512,1024]{1,0:T(8,128)S(1)}) custom-call(s32[8,128]{1,0:T(8,128)S(1)} %get-tuple-element.36.flag, bf16[128,1024]{1,0:T(8,128)(2,1)S(1)} %by_role.3.e3, bf16[128,1024]{1,0:T(8,128)(2,1)S(1)} %collective-permute-done.6.f3, bf16[256,512]{1,0:T(8,128)(2,1)S(1)} %get-tuple-element.42.unit_part, ...), custom_call_target="tpu_custom_call" | custom-call | flops 1073741824 | bytes 3145728 | tf_op jit(solution)/shard_map/middle/pallas_call | solution.py:407
  39.0 1.1 %shard_map.68 = (bf16[256,512]{1,0:T(8,128)(2,1)S(1)}, bf16[128,1024]{1,0:T(8,128)(2,1)S(1)}, bf16[256,512]{1,0:T(8,128)(2,1)S(1)}, bf16[256,1024]{1,0:T(8,128)(2,1)S(1)}, bf16[256,1024]{1,0:T(8,128)(2,1)S(1)}) custom-call(s32[8,128]{1,0:T(8,128)S(1)} %get-tuple-element.36.flag, bf16[128,1024]{1,0:T(8,128)(2,1)S(1)} %collective-permute-done.1.late, ...), custom_call_target="tpu_custom_call" | custom-call | flops 671088640 | tf_op jit(solution)/shard_map/pallas_call | solution.py:575
  40.2 1.6 %collective-permute-start.9 = (bf16[256,512]{1,0:T(8,128)(2,1)S(1)}, bf16[256,512]{1,0:T(8,128)(2,1)S(1)}, u32[]{:S(2)}, u32[]{:S(2)}) collective-permute-start(bf16[256,512]{1,0:T(8,128)(2,1)S(1)} %get-tuple-element.52), channel_id=1, source_target_pairs={{0,1},{1,0},{2,3},{3,2},{4,5},{5,4},{6,7},{7,6},{8,9},{9,8},{10,11... | collective-permute-start | bytes 786440 | tf_op jit(solution)/shard_map/ppermute | solution.py:595
  41.7 1.8 %collective-permute-start.7 = (bf16[128,1024]{1,0:T(8,128)(2,1)S(1)}, bf16[128,1024]{1,0:T(8,128)(2,1)S(1)}, u32[]{:S(2)}, u32[]{:S(2)}) collective-permute-start(bf16[128,1024]{1,0:T(8,128)(2,1)S(1)} %get-tuple-element.48), channel_id=1, source_target_pairs={{0,2},{2,0},{4,6},{6,4},{1,3},{3,1},{5,7},{7,5},{8,10},{10,8},{12,... | collective-permute-start | bytes 786440 | tf_op jit(solution)/shard_map/ppermute | solution.py:595
  43.5 1.2 %shard_map.75 = (bf16[256,512]{1,0:T(8,128)(2,1)S(1)}, bf16[128,1024]{1,0:T(8,128)(2,1)S(1)}, bf16[256,512]{1,0:T(8,128)(2,1)S(1)}, bf16[256,1024]{1,0:T(8,128)(2,1)S(1)}) custom-call(s32[8,128]{1,0:T(8,128)S(1)} %get-tuple-element.36.flag, bf16[256,1024]{1,0:T(8,128)(2,1)S(1)} %get-tuple-element.57.unit, ...), custom_call_target="tpu_custom_call" | custom-call | flops 402653184 | tf_op jit(solution)/shard_map/pallas_call | solution.py:575
  44.7 0.6 collective-permute-start.18
  45.3 0.3 shard_map.69
  45.6 3.8 %collective-permute-done.9.land = bf16[256,512]{1,0:T(8,128)(2,1)S(1)} collective-permute-done((bf16[256,512]{1,0:T(8,128)(2,1)S(1)}, bf16[256,512]{1,0:T(8,128)(2,1)S(1)}, u32[]{:S(2)}, u32[]{:S(2)}) %collective-permute-start.9) | collective-permute-done | bytes 262176 | tf_op jit(solution)/shard_map/ppermute | solution.py:595
  49.5 1.8 %collective-permute-start.10 = (bf16[128,512]{1,0:T(8,128)(2,1)S(1)}, bf16[128,512]{1,0:T(8,128)(2,1)S(1)}, u32[]{:S(2)}, u32[]{:S(2)}) collective-permute-start(bf16[128,512]{1,0:T(8,128)(2,1)S(1)} %get-tuple-element.54), channel_id=1, source_target_pairs={{0,2},{2,0},{4,6},{6,4},{1,3},{3,1},{5,7},{7,5},{8,10},{10,8},{12,... | collective-permute-start | bytes 393224 | tf_op jit(solution)/shard_map/ppermute | solution.py:595
  51.3 0.2 collective-permute-start.16
  51.6 0.1 shard_map.70
  51.6 1.5 %collective-permute-start.8 = (bf16[128,512]{1,0:T(8,128)(2,1)S(1)}, bf16[128,512]{1,0:T(8,128)(2,1)S(1)}, u32[]{:S(2)}, u32[]{:S(2)}) collective-permute-start(bf16[128,512]{1,0:T(8,128)(2,1)S(1)} %get-tuple-element.50), channel_id=1, source_target_pairs={{0,1},{1,0},{2,3},{3,2},{4,5},{5,4},{6,7},{7,6},{8,9},{9,8},{10,11... | collective-permute-start | bytes 393224 | tf_op jit(solution)/shard_map/ppermute | solution.py:595
  53.2 2.7 %collective-permute-done.10.land = bf16[128,512]{1,0:T(8,128)(2,1)S(1)} collective-permute-done((bf16[128,512]{1,0:T(8,128)(2,1)S(1)}, bf16[128,512]{1,0:T(8,128)(2,1)S(1)}, u32[]{:S(2)}, u32[]{:S(2)}) %collective-permute-start.10) | collective-permute-done | bytes 131104 | tf_op jit(solution)/shard_map/ppermute | solution.py:595
  55.9 2.1 %collective-permute-start.11 = (bf16[128,512]{1,0:T(8,128)(2,1)S(1)}, bf16[128,512]{1,0:T(8,128)(2,1)S(1)}, u32[]{:S(2)}, u32[]{:S(2)}) collective-permute-start(bf16[128,512]{1,0:T(8,128)(2,1)S(1)} %shard_map.73), channel_id=1, source_target_pairs={{0,16},{8,24},{16,0},{24,8},{1,17},{9,25},{17,1},{25,9},{2,18},{10... | collective-permute-start | bytes 393224 | tf_op jit(solution)/shard_map/ppermute | solution.py:595
  58.1 0.3 shard_map.76
  58.4 0.1 shard_map.79
  58.5 1.3 %collective-permute-start.19 = (bf16[128,512]{1,0:T(8,128)(2,1)S(1)}, bf16[128,512]{1,0:T(8,128)(2,1)S(1)}, u32[]{:S(2)}, u32[]{:S(2)}) collective-permute-start(bf16[128,512]{1,0:T(8,128)(2,1)S(1)} %get-tuple-element.69), channel_id=1, source_target_pairs={{0,2},{2,0},{4,6},{6,4},{1,3},{3,1},{5,7},{7,5},{8,10},{10,8},{12,... | collective-permute-start | bytes 393224 | tf_op jit(solution)/shard_map/ppermute | solution.py:595
  59.8 1.2 %collective-permute-done.11.got = bf16[128,512]{1,0:T(8,128)(2,1)S(1)} collective-permute-done((bf16[128,512]{1,0:T(8,128)(2,1)S(1)}, bf16[128,512]{1,0:T(8,128)(2,1)S(1)}, u32[]{:S(2)}, u32[]{:S(2)}) %collective-permute-start.11) | collective-permute-done | bytes 131104 | tf_op jit(solution)/shard_map/ppermute | solution.py:595
  61.0 0.1 shard_map.74
  61.1 3.1 %collective-permute-start.12 = (bf16[128,512]{1,0:T(8,128)(2,1)S(1)}, bf16[128,512]{1,0:T(8,128)(2,1)S(1)}, u32[]{:S(2)}, u32[]{:S(2)}) collective-permute-start(bf16[128,512]{1,0:T(8,128)(2,1)S(1)} %get-tuple-element.56), channel_id=1, source_target_pairs={{0,4},{2,6},{4,0},{6,2},{1,5},{3,7},{5,1},{7,3},{8,12},{10,14},{12... | collective-permute-start | bytes 393224 | tf_op jit(solution)/shard_map/ppermute | solution.py:595
  64.2 0.1 shard_map.77
  64.3 1.5 %collective-permute-start.17 = (bf16[128,512]{1,0:T(8,128)(2,1)S(1)}, bf16[128,512]{1,0:T(8,128)(2,1)S(1)}, u32[]{:S(2)}, u32[]{:S(2)}) collective-permute-start(bf16[128,512]{1,0:T(8,128)(2,1)S(1)} %get-tuple-element.65), channel_id=1, source_target_pairs={{0,1},{1,0},{2,3},{3,2},{4,5},{5,4},{6,7},{7,6},{8,9},{9,8},{10,11... | collective-permute-start | bytes 393224 | tf_op jit(solution)/shard_map/ppermute | solution.py:595
  65.9 1.6 %collective-permute-start.20 = (bf16[128,512]{1,0:T(8,128)(2,1)S(1)}, bf16[128,512]{1,0:T(8,128)(2,1)S(1)}, u32[]{:S(2)}, u32[]{:S(2)}) collective-permute-start(bf16[128,512]{1,0:T(8,128)(2,1)S(1)} %shard_map.80), channel_id=1, source_target_pairs={{0,16},{8,24},{16,0},{24,8},{1,17},{9,25},{17,1},{25,9},{2,18},{10... | collective-permute-start | bytes 393224 | tf_op jit(solution)/shard_map/ppermute | solution.py:595
  67.5 1.8 %collective-permute-done.17.land = bf16[128,512]{1,0:T(8,128)(2,1)S(1)} collective-permute-done((bf16[128,512]{1,0:T(8,128)(2,1)S(1)}, bf16[128,512]{1,0:T(8,128)(2,1)S(1)}, u32[]{:S(2)}, u32[]{:S(2)}) %collective-permute-start.17) | collective-permute-done | bytes 131104 | tf_op jit(solution)/shard_map/ppermute | solution.py:595
  69.4 1.5 %collective-permute-done.20.got = bf16[128,512]{1,0:T(8,128)(2,1)S(1)} collective-permute-done((bf16[128,512]{1,0:T(8,128)(2,1)S(1)}, bf16[128,512]{1,0:T(8,128)(2,1)S(1)}, u32[]{:S(2)}, u32[]{:S(2)}) %collective-permute-start.20) | collective-permute-done | bytes 131104 | tf_op jit(solution)/shard_map/ppermute | solution.py:595
  70.9 0.9 %shard_map.81 = (f32[1,128,512]{2,1,0:T(8,128)}, f32[1,128,512]{2,1,0:T(8,128)}) custom-call(s32[8,128]{1,0:T(8,128)S(1)} %get-tuple-element.36.flag, f32[128,512]{1,0:T(8,128)S(1)} %get-tuple-element.55.lower, bf16[128,512]{1,0:T(8,128)(2,1)S(1)} %collective-permute-done.12.landed, f32[128,512]{1,0:T(8,128)S(1)} %shard_map.78.near, ...), custom_call_target="tpu_custom_call" | custom-call | tf_op jit(solution)/shard_map/pallas_call | solution.py:575
  (25 shorter events, 0.2 us)
Async XLA Ops:
  0.6 0.7 copy-start.4
  0.6 1.0 %copy-start.2 = (bf16[1,1,2,128,1024]{4,3,2,1,0:T(8,128)(2,1)S(1)}, bf16[1,1,2,128,1024]{4,3,2,1,0:T(8,128)(2,1)}, u32[]{:S(2)}) copy-start(bf16[1,1,2,128,1024]{4,3,2,1,0:T(8,128)(2,1)} %param.6) | copy-start | bytes 1572868
  0.6 1.2 %copy-start.3 = (bf16[1,2,128,1024]{3,2,1,0:T(8,128)(2,1)S(1)}, bf16[1,2,128,1024]{3,2,1,0:T(8,128)(2,1)}, u32[]{:S(2)}) copy-start(bf16[1,2,128,1024]{3,2,1,0:T(8,128)(2,1)} %param.9) | copy-start | bytes 1572868
  1.8 2.2 %copy-start = (bf16[1,1,2,1024,1024]{4,3,2,1,0:T(8,128)(2,1)S(1)}, bf16[1,1,2,1024,1024]{4,3,2,1,0:T(8,128)(2,1)}, u32[]{:S(2)}) copy-start(bf16[1,1,2,1024,1024]{4,3,2,1,0:T(8,128)(2,1)} %param.8) | copy-start | bytes 12582916
  1.8 3.5 %copy-start.1 = (bf16[1,1,2,1024,1024]{4,3,2,1,0:T(8,128)(2,1)S(1)}, bf16[1,1,2,1024,1024]{4,3,2,1,0:T(8,128)(2,1)}, u32[]{:S(2)}) copy-start(bf16[1,1,2,1024,1024]{4,3,2,1,0:T(8,128)(2,1)} %param.7) | copy-start | bytes 12582916
  7.3 17.2 %collective-permute-start.13 = (bf16[2,128,1024]{2,1,0:T(8,128)(2,1)S(1)}, bf16[2,128,1024]{2,1,0:T(8,128)(2,1)S(1)}, u32[]{:S(2)}, u32[]{:S(2)}) collective-permute-start(bf16[2,128,1024]{2,1,0:T(8,128)(2,1)S(1)} %get-tuple-element.59), channel_id=1, source_target_pairs={{0,4},{2,6},{1,5},{3,7},{8,12},{10,14},{9,13},{11,15},{16,20},{18,... | collective-permute-start | bytes 1572872 | tf_op jit(solution)/shard_map/ppermute | solution.py:621
  13.4 9.2 %collective-permute-start = (bf16[128,1024]{1,0:T(8,128)(2,1)S(1)}, bf16[128,1024]{1,0:T(8,128)(2,1)S(1)}, u32[]{:S(2)}, u32[]{:S(2)}) collective-permute-start(bf16[128,1024]{1,0:T(8,128)(2,1)S(1)} %get-tuple-element.38), channel_id=1, source_target_pairs={{0,16},{8,24},{16,0},{24,8},{1,17},{9,25},{17,1},{25,9},{2,18},{10... | collective-permute-start | bytes 786440 | tf_op jit(solution)/shard_map/ppermute | solution.py:595
  14.9 11.9 %collective-permute-start.5 = (bf16[128,1024]{1,0:T(8,128)(2,1)S(1)}, bf16[128,1024]{1,0:T(8,128)(2,1)S(1)}, u32[]{:S(2)}, u32[]{:S(2)}) collective-permute-start(bf16[128,1024]{1,0:T(8,128)(2,1)S(1)} %get-tuple-element.37.full_part.low), channel_id=1, source_target_pairs={{0,16},{8,24},{16,0},{24,8},{1,17},{9,25},{17,1},{25,9},{2,18},{10... | collective-permute-start | bytes 786440 | tf_op jit(solution)/shard_map/ppermute | solution.py:595
  22.7 13.9 %collective-permute-start.1 = (bf16[128,1024]{1,0:T(8,128)(2,1)S(1)}, bf16[128,1024]{1,0:T(8,128)(2,1)S(1)}, u32[]{:S(2)}, u32[]{:S(2)}) collective-permute-start(bf16[128,1024]{1,0:T(8,128)(2,1)S(1)} %by_role.2), channel_id=1, source_target_pairs={{4,0},{6,2},{5,1},{7,3},{12,8},{14,10},{13,9},{15,11},{20,16},{22,... | collective-permute-start | bytes 786440 | tf_op jit(solution)/shard_map/ppermute | solution.py:624
  24.0 12.6 %collective-permute-start.3 = (bf16[128,1024]{1,0:T(8,128)(2,1)S(1)}, bf16[128,1024]{1,0:T(8,128)(2,1)S(1)}, u32[]{:S(2)}, u32[]{:S(2)}) collective-permute-start(bf16[128,1024]{1,0:T(8,128)(2,1)S(1)} %get-tuple-element.39.e1), channel_id=1, source_target_pairs={{0,8},{8,0},{16,24},{24,16},{1,9},{9,1},{17,25},{25,17},{2,10},{10... | collective-permute-start | bytes 786440 | tf_op jit(solution)/shard_map/ppermute | solution.py:595
  24.0 13.1 %collective-permute-start.4 = (bf16[128,1024]{1,0:T(8,128)(2,1)S(1)}, bf16[128,1024]{1,0:T(8,128)(2,1)S(1)}, u32[]{:S(2)}, u32[]{:S(2)}) collective-permute-start(bf16[128,1024]{1,0:T(8,128)(2,1)S(1)} %collective-permute-done.short_part.e2), channel_id=1, source_target_pairs={{0,8},{8,0},{16,24},{24,16},{1,9},{9,1},{17,25},{25,17},{2,10},{10... | collective-permute-start | bytes 786440 | tf_op jit(solution)/shard_map/ppermute | solution.py:595
  24.5 19.0 %collective-permute-start.14 = (bf16[2,128,1024]{2,1,0:T(8,128)(2,1)S(1)}, bf16[2,128,1024]{2,1,0:T(8,128)(2,1)S(1)}, u32[]{:S(2)}, u32[]{:S(2)}) collective-permute-start(bf16[2,128,1024]{2,1,0:T(8,128)(2,1)S(1)} %collective-permute-done.13.up), channel_id=1, source_target_pairs={{0,8},{8,0},{16,24},{24,16},{1,9},{9,1},{17,25},{25,17},{2,10},{10... | collective-permute-start | bytes 1572872 | tf_op jit(solution)/shard_map/ppermute | solution.py:595
  26.9 10.8 %collective-permute-start.6 = (bf16[128,1024]{1,0:T(8,128)(2,1)S(1)}, bf16[128,1024]{1,0:T(8,128)(2,1)S(1)}, u32[]{:S(2)}, u32[]{:S(2)}) collective-permute-start(bf16[128,1024]{1,0:T(8,128)(2,1)S(1)} %by_role.3.e3), channel_id=1, source_target_pairs={{0,8},{8,0},{16,24},{24,16},{1,9},{9,1},{17,25},{25,17},{2,10},{10... | collective-permute-start | bytes 786440 | tf_op jit(solution)/shard_map/ppermute | solution.py:595
  36.6 2.5 %collective-permute-start.2 = (bf16[128,1024]{1,0:T(8,128)(2,1)S(1)}, bf16[128,1024]{1,0:T(8,128)(2,1)S(1)}, u32[]{:S(2)}, u32[]{:S(2)}) collective-permute-start(bf16[128,1024]{1,0:T(8,128)(2,1)S(1)} %collective-permute-done.1.late), channel_id=1, source_target_pairs={{0,8},{8,0},{16,24},{24,16},{1,9},{9,1},{17,25},{25,17},{2,10},{10... | collective-permute-start | bytes 786440 | tf_op jit(solution)/shard_map/ppermute | solution.py:595
  36.6 6.9 %collective-permute-start.15 = (bf16[128,1024]{1,0:T(8,128)(2,1)S(1)}, bf16[128,1024]{1,0:T(8,128)(2,1)S(1)}, u32[]{:S(2)}, u32[]{:S(2)}) collective-permute-start(bf16[128,1024]{1,0:T(8,128)(2,1)S(1)} %get-tuple-element.37.full_part.low), channel_id=1, source_target_pairs={{0,8},{8,0},{16,24},{24,16},{1,9},{9,1},{17,25},{25,17},{2,10},{10... | collective-permute-start | bytes 786440 | tf_op jit(solution)/shard_map/ppermute | solution.py:595
  40.2 9.2 %collective-permute-start.9 = (bf16[256,512]{1,0:T(8,128)(2,1)S(1)}, bf16[256,512]{1,0:T(8,128)(2,1)S(1)}, u32[]{:S(2)}, u32[]{:S(2)}) collective-permute-start(bf16[256,512]{1,0:T(8,128)(2,1)S(1)} %get-tuple-element.52), channel_id=1, source_target_pairs={{0,1},{1,0},{2,3},{3,2},{4,5},{5,4},{6,7},{7,6},{8,9},{9,8},{10,11... | collective-permute-start | bytes 786440 | tf_op jit(solution)/shard_map/ppermute | solution.py:595
  41.7 9.8 %collective-permute-start.7 = (bf16[128,1024]{1,0:T(8,128)(2,1)S(1)}, bf16[128,1024]{1,0:T(8,128)(2,1)S(1)}, u32[]{:S(2)}, u32[]{:S(2)}) collective-permute-start(bf16[128,1024]{1,0:T(8,128)(2,1)S(1)} %get-tuple-element.48), channel_id=1, source_target_pairs={{0,2},{2,0},{4,6},{6,4},{1,3},{3,1},{5,7},{7,5},{8,10},{10,8},{12,... | collective-permute-start | bytes 786440 | tf_op jit(solution)/shard_map/ppermute | solution.py:595
  44.7 13.7 %collective-permute-start.18 = (bf16[256,512]{1,0:T(8,128)(2,1)S(1)}, bf16[256,512]{1,0:T(8,128)(2,1)S(1)}, u32[]{:S(2)}, u32[]{:S(2)}) collective-permute-start(bf16[256,512]{1,0:T(8,128)(2,1)S(1)} %get-tuple-element.67), channel_id=1, source_target_pairs={{0,1},{1,0},{2,3},{3,2},{4,5},{5,4},{6,7},{7,6},{8,9},{9,8},{10,11... | collective-permute-start | bytes 786440 | tf_op jit(solution)/shard_map/ppermute | solution.py:595
  49.5 6.4 %collective-permute-start.10 = (bf16[128,512]{1,0:T(8,128)(2,1)S(1)}, bf16[128,512]{1,0:T(8,128)(2,1)S(1)}, u32[]{:S(2)}, u32[]{:S(2)}) collective-permute-start(bf16[128,512]{1,0:T(8,128)(2,1)S(1)} %get-tuple-element.54), channel_id=1, source_target_pairs={{0,2},{2,0},{4,6},{6,4},{1,3},{3,1},{5,7},{7,5},{8,10},{10,8},{12,... | collective-permute-start | bytes 393224 | tf_op jit(solution)/shard_map/ppermute | solution.py:595
  51.3 12.9 %collective-permute-start.16 = (bf16[128,1024]{1,0:T(8,128)(2,1)S(1)}, bf16[128,1024]{1,0:T(8,128)(2,1)S(1)}, u32[]{:S(2)}, u32[]{:S(2)}) collective-permute-start(bf16[128,1024]{1,0:T(8,128)(2,1)S(1)} %get-tuple-element.63), channel_id=1, source_target_pairs={{0,2},{2,0},{4,6},{6,4},{1,3},{3,1},{5,7},{7,5},{8,10},{10,8},{12,... | collective-permute-start | bytes 786440 | tf_op jit(solution)/shard_map/ppermute | solution.py:595
  51.6 8.2 %collective-permute-start.8 = (bf16[128,512]{1,0:T(8,128)(2,1)S(1)}, bf16[128,512]{1,0:T(8,128)(2,1)S(1)}, u32[]{:S(2)}, u32[]{:S(2)}) collective-permute-start(bf16[128,512]{1,0:T(8,128)(2,1)S(1)} %get-tuple-element.50), channel_id=1, source_target_pairs={{0,1},{1,0},{2,3},{3,2},{4,5},{5,4},{6,7},{7,6},{8,9},{9,8},{10,11... | collective-permute-start | bytes 393224 | tf_op jit(solution)/shard_map/ppermute | solution.py:595
  55.9 5.1 %collective-permute-start.11 = (bf16[128,512]{1,0:T(8,128)(2,1)S(1)}, bf16[128,512]{1,0:T(8,128)(2,1)S(1)}, u32[]{:S(2)}, u32[]{:S(2)}) collective-permute-start(bf16[128,512]{1,0:T(8,128)(2,1)S(1)} %shard_map.73), channel_id=1, source_target_pairs={{0,16},{8,24},{16,0},{24,8},{1,17},{9,25},{17,1},{25,9},{2,18},{10... | collective-permute-start | bytes 393224 | tf_op jit(solution)/shard_map/ppermute | solution.py:595
  58.5 7.4 %collective-permute-start.19 = (bf16[128,512]{1,0:T(8,128)(2,1)S(1)}, bf16[128,512]{1,0:T(8,128)(2,1)S(1)}, u32[]{:S(2)}, u32[]{:S(2)}) collective-permute-start(bf16[128,512]{1,0:T(8,128)(2,1)S(1)} %get-tuple-element.69), channel_id=1, source_target_pairs={{0,2},{2,0},{4,6},{6,4},{1,3},{3,1},{5,7},{7,5},{8,10},{10,8},{12,... | collective-permute-start | bytes 393224 | tf_op jit(solution)/shard_map/ppermute | solution.py:595
  61.1 8.3 %collective-permute-start.12 = (bf16[128,512]{1,0:T(8,128)(2,1)S(1)}, bf16[128,512]{1,0:T(8,128)(2,1)S(1)}, u32[]{:S(2)}, u32[]{:S(2)}) collective-permute-start(bf16[128,512]{1,0:T(8,128)(2,1)S(1)} %get-tuple-element.56), channel_id=1, source_target_pairs={{0,4},{2,6},{4,0},{6,2},{1,5},{3,7},{5,1},{7,3},{8,12},{10,14},{12... | collective-permute-start | bytes 393224 | tf_op jit(solution)/shard_map/ppermute | solution.py:595
  64.3 5.0 %collective-permute-start.17 = (bf16[128,512]{1,0:T(8,128)(2,1)S(1)}, bf16[128,512]{1,0:T(8,128)(2,1)S(1)}, u32[]{:S(2)}, u32[]{:S(2)}) collective-permute-start(bf16[128,512]{1,0:T(8,128)(2,1)S(1)} %get-tuple-element.65), channel_id=1, source_target_pairs={{0,1},{1,0},{2,3},{3,2},{4,5},{5,4},{6,7},{7,6},{8,9},{9,8},{10,11... | collective-permute-start | bytes 393224 | tf_op jit(solution)/shard_map/ppermute | solution.py:595
  65.9 5.0 %collective-permute-start.20 = (bf16[128,512]{1,0:T(8,128)(2,1)S(1)}, bf16[128,512]{1,0:T(8,128)(2,1)S(1)}, u32[]{:S(2)}, u32[]{:S(2)}) collective-permute-start(bf16[128,512]{1,0:T(8,128)(2,1)S(1)} %shard_map.80), channel_id=1, source_target_pairs={{0,16},{8,24},{16,0},{24,8},{1,17},{9,25},{17,1},{25,9},{2,18},{10... | collective-permute-start | bytes 393224 | tf_op jit(solution)/shard_map/ppermute | solution.py:595
